TPU v7x, 128 devices: a whole 4x4x4 slice. The times are simulated.
128 devices in a mesh: dp: 32 (over x, y, core), tensor: 4 (over z).
Axes of the slice: x: 4, y: 4, z: 4, core: 2. Of those that a mesh axis runs over, the one named last changes fastest.
Arguments:
- patch_rows: bfloat16 [256, 512, 1280], P('dp', None, 'tensor'), may hold values from -6 to 6
- out_grads: bfloat16 [256, 512, 1280], P('dp', None, 'tensor'), may hold values from -0.29882812 to 0.29882812
- basis_a: bfloat16 [27, 1280, 128], P(None, 'tensor', 'dp'), may hold values from -0.03125 to 0.03125
- basis_g: bfloat16 [1280, 1280], P('tensor', 'dp'), may hold values from -0.15625 to 0.15625
Outputs:
- corrections: float32 [128, 1280], P(('dp', 'tensor'))
All inputs are finite; a program needn't handle non-finite values.
Results may differ from a plain program's by a relative error of at most 0.00054.
Values may be sent and summed in bfloat16 or wider, within the bound.
No kernel may reach another device: no remote copies, remote signals or barrier semaphores. Data moves between devices by JAX's collectives and lax.ppermute only.
A program may use at most 256 MiB of HBM per device.

v0:
```python
import jax
import jax.numpy as jnp
from jax import lax
from jax.sharding import PartitionSpec as P

CIN = 1280
COUT = 1280
SIDE = 8


def padded_grid(rows):
    examples_here = rows.shape[0]
    channels = rows.shape[2]
    volume = rows.reshape(examples_here, SIDE, SIDE, SIDE, channels)
    return jnp.pad(volume, ((0, 0), (1, 1), (1, 1), (1, 1), (0, 0)))


def project_taps(padded, basis, examples_here, channels):
    summed = None
    for offset_x in range(3):
        for offset_y in range(3):
            for offset_z in range(3):
                tap_index = offset_x * 9 + offset_y * 3 + offset_z
                window = padded[
                    :,
                    offset_x : offset_x + SIDE,
                    offset_y : offset_y + SIDE,
                    offset_z : offset_z + SIDE,
                    :,
                ]
                window = window.reshape(examples_here * SIDE * SIDE * SIDE, channels)
                tap_term = jnp.dot(window, basis[tap_index], preferred_element_type=jnp.float32)
                summed = tap_term if summed is None else summed + tap_term
    return summed


def squared_sums(coeff_a, coeff_g):
    products = jnp.einsum("epr,epj->erj", coeff_a, coeff_g, preferred_element_type=jnp.float32)
    return jnp.sum(products * products, axis=0)


def grad_coeffs(grads_own, basis_full):
    owned = grads_own.shape[0]
    flat = grads_own.reshape(owned * SIDE * SIDE * SIDE, COUT)
    projected = jnp.dot(flat, basis_full, preferred_element_type=jnp.float32).astype(jnp.bfloat16)
    return projected.reshape(owned, SIDE * SIDE * SIDE, COUT)


def body(patch_rows, out_grads, basis_a, basis_g):
    basis_cols = lax.all_gather(basis_g, "dp", axis=1, tiled=True)
    basis_full = lax.all_gather(basis_cols, "tensor", axis=0, tiled=True)
    rows_own, grads_own = (
        lax.all_to_all(patch_rows, "tensor", split_axis=0, concat_axis=2, tiled=True),
        lax.all_to_all(out_grads, "tensor", split_axis=0, concat_axis=2, tiled=True),
    )
    coeff_g = grad_coeffs(grads_own, basis_full)
    owned = rows_own.shape[0]
    padded = padded_grid(rows_own)
    basis_wide = lax.all_gather(basis_a, "tensor", axis=1, tiled=True)
    piece = lax.all_gather(basis_wide, "dp", axis=2, tiled=True)
    width_here = piece.shape[2]
    coeff_a = project_taps(padded, piece, owned, CIN).astype(jnp.bfloat16)
    coeff_a = coeff_a.reshape(owned, SIDE * SIDE * SIDE, width_here)
    partial_value = squared_sums(coeff_a, coeff_g)
    summed = lax.psum_scatter(partial_value, ("dp", "tensor"), scatter_dimension=0, tiled=True)
    examples_all = grads_own.shape[0] * lax.axis_size("dp") * lax.axis_size("tensor")
    return summed / examples_all


def solution(mesh):
    in_specs = (
        P("dp", None, "tensor"),
        P("dp", None, "tensor"),
        P(None, "tensor", "dp"),
        P("tensor", "dp"),
    )
    out_specs = P(("dp", "tensor"), None)
    return jax.shard_map(body, mesh=mesh, in_specs=in_specs, out_specs=out_specs, check_vma=False)
```

profile of v0, /device:TPU:1, one launch (start us, length us, event | category | flops | bytes accessed | tf_op | source)
XLA Modules:
  0.0 476.8 jit_solution(9286829090334482958)
XLA Ops:
  6.5 26.7 %all_gather.14 = bf16[320,1280]{0,1:T(8,128)(2,1)S(1)} all-gather(bf16[320,40]{0,1:T(8,128)(2,1)} %param.7), channel_id=1, replica_groups=mesh['dp'=32,'tensor'=4] {'dp'}, dimensions={1}, use_global_device_ids=true | all-gather | bytes 844800 | tf_op jit(solution)/shard_map/all_gather | solution.py:50
  34.9 20.0 %all_gather.12 = bf16[27,1280,4]{0,2,1:T(4,128)(2,1)S(1)} all-gather(bf16[27,320,4]{0,2,1:T(4,128)(2,1)S(1)} %copy.53), channel_id=1, replica_groups=mesh['dp'=32,'tensor'=4] {'tensor'}, dimensions={1}, use_global_device_ids=true | all-gather | bytes 345600 | tf_op jit(solution)/shard_map/all_gather | solution.py:59
  56.4 49.0 %all_to_all.30 = bf16[8,512,320]{1,2,0:T(8,128)(2,1)} all-to-all(bf16[8,512,320]{1,2,0:T(8,128)(2,1)} %param.4), channel_id=1, replica_groups=mesh['dp'=32,'tensor'=4] {'tensor'}, dimensions={0} | all-to-all | bytes 5242880 | tf_op jit(solution)/shard_map/all_to_all | solution.py:53
  105.4 4.6 all-to-all-start.1
  110.0 4.4 copy.117
  114.5 25.4 %all-to-all-done.1 = bf16[8,512,320]{1,2,0:T(8,128)(2,1)} async-done(((bf16[8,512,320]{1,2,0:T(8,128)(2,1)}), bf16[8,512,320]{1,2,0:T(8,128)(2,1)}, u32[]{:S(2)}, u32[]{:S(2)}) %all-to-all-start.1) | async-done | bytes 2621472 | tf_op jit(solution)/shard_map/all_to_all | solution.py:54
  139.9 4.4 copy.82
  144.3 2.2 copy.114
  146.6 2.2 copy.113
  148.7 7.5 %copy.52 = bf16[2,512,4,320]{3,2,1,0:T(4,128)(2,1)} copy(bf16[2,512,4,320]{1,0,3,2:T(2,128)(2,1)S(1)} %bitcast.156) | data formatting | bytes 5242880 | tf_op jit(solution)/shard_map/all_to_all | solution.py:53
  156.2 5.3 %reshape.96 = bf16[2,8,8,8,1280]{4,3,2,1,0:T(8,128)(2,1)S(1)} reshape(bf16[2,512,4,320]{3,2,1,0:T(4,128)(2,1)} %copy.52) | data formatting | bytes 5242880 | tf_op jit(solution)/shard_map/reshape | solution.py:14
  161.5 6.6 %pad_slice_fusion.1 = (bf16[2,8,8,8,1280]{4,3,2,1,0:T(8,128)(2,1)}, bf16[2,8,8,8,1280]{4,3,2,1,0:T(8,128)(2,1)}, bf16[2,8,8,8,1280]{4,3,2,1,0:T(8,128)(2,1)}, bf...) fusion(bf16[2,8,8,8,1280]{4,3,2,1,0:T(8,128)(2,1)S(1)} %reshape.96), kind=kLoop, calls=%fused_computation.1 | loop fusion | bytes 20971520 | tf_op jit(solution)/shard_map/slice | solution.py:24
  168.1 16.0 %pad_slice_fusion = (bf16[2,8,8,8,1280]{4,3,2,1,0:T(8,128)(2,1)}, bf16[2,8,8,8,1280]{4,3,2,1,0:T(8,128)(2,1)}, bf16[2,8,8,8,1280]{4,3,2,1,0:T(8,128)(2,1)}, bf16...) fusion(bf16[2,8,8,8,1280]{4,3,2,1,0:T(8,128)(2,1)S(1)} %reshape.96), kind=kLoop, calls=%fused_computation | loop fusion | bytes 52428800 | tf_op jit(solution)/shard_map/slice | solution.py:24
  184.1 7.9 %convolution_convert_fusion = bf16[1024,1280]{1,0:T(8,128)(2,1)} fusion(bf16[1024,1280]{0,1:T(8,128)(2,1)} %bitcast.187, bf16[1280,1280]{1,0:T(8,128)(2,1)} %all-gather.5.cloned.1.call-done), kind=kOutput, calls=%fused_computation.26 | convolution fusion | flops 3356753920 | bytes 8519680 | tf_op jit(solution)/shard_map/dot_general | solution.py:45
  192.0 13.4 %fusion.31 = (bf16[1,1280,128]{1,0,2:T(2,128)(2,1)}, bf16[1,1280,128]{1,0,2:T(2,128)(2,1)}, bf16[1,1280,128]{1,0,2:T(2,128)(2,1)}, bf16[1,1280,128]{1,0,2:T(2,12...) fusion(bf16[27,1280,128]{1,0,2:T(8,128)(2,1)} %all-gather.3.clo, ...), kind=kLoop, calls=%fused_computation.87 | loop fusion | bytes 5242880 | tf_op jit(solution)/shard_map/slice | solution.py:32
  209.4 2.0 copy.91
  216.9 23.6 %fusion.30 = (bf16[1,1280,128]{1,0,2:T(2,128)(2,1)}, bf16[1,1280,128]{1,0,2:T(2,128)(2,1)}, bf16[1,1280,128]{1,0,2:T(2,128)(2,1)}, bf16[1,1280,128]{1,0,2:T(2,12...) fusion(bf16[27,1280,128]{1,0,2:T(8,128)(2,1)} %all-gather.3.clo, ...), kind=kLoop, calls=%fused_computation.86 | loop fusion | bytes 12451840 | tf_op jit(solution)/shard_map/slice | solution.py:32
  240.5 2.0 copy.112
  244.5 2.0 copy.110
  254.3 2.0 copy.105
  256.3 2.0 copy.104
  264.7 2.1 copy.98
  270.8 2.0 copy.95
  322.8 146.0 %all-reduce.4.cloned.1.call-done = f32[128,1280]{1,0:T(8,128)} async-done(((f32[128,1280]{1,0:T(8,128)}), f32[128,1280]{1,0:T(8,128)}) %all-reduce.4.cloned.1.call-update) | async-done | bytes 655376
  (170 shorter events, 84.0 us)
Async XLA Ops:
  6.5 28.1 %copy-start.54 = (bf16[27,320,4]{1,2,0:T(4,128)(2,1)S(1)}, bf16[27,320,4]{1,2,0:T(4,128)(2,1)}, u32[]{:S(2)}) copy-start(bf16[27,320,4]{1,2,0:T(4,128)(2,1)} %param.6) | copy-start | bytes 207364
  6.5 177.6 %all-gather.5.cloned.1.call-start = ((), (), s32[]{:S(2)}) async-start(), calls=%async_computation.3 | async-start | bytes 4096000 | tf_op jit(solution)/shard_map/all_gather | solution.py:51
  34.5 157.5 %all-gather.3.cloned.1.call-start = ((), (), s32[]{:S(2)}) async-start(), calls=%async_computation.2 | async-start | bytes 10813440 | tf_op jit(solution)/shard_map/all_gather | solution.py:60
  105.4 34.5 %all-to-all-start.1 = ((bf16[8,512,320]{1,2,0:T(8,128)(2,1)}), bf16[8,512,320]{1,2,0:T(8,128)(2,1)}, u32[]{:S(2)}, u32[]{:S(2)}) async-start(bf16[8,512,320]{1,2,0:T(8,128)(2,1)} %param.5), calls=%async_computation.1 | async-start | bytes 5242880 | tf_op jit(solution)/shard_map/all_to_all | solution.py:54
  110.0 358.8 %all-reduce.4.cloned.1.call-start = ((), (), s32[]{:S(2)}) async-start(), calls=%async_computation.4 | async-start | bytes 1310720
  264.7 9.6 %copy-start.25 = (bf16[2,8,8,8,1280]{4,3,2,1,0:T(8,128)(2,1)S(1)}, bf16[2,8,8,8,1280]{4,3,2,1,0:T(8,128)(2,1)}, u32[]{:S(2)}) copy-start(bf16[2,8,8,8,1280]{4,3,2,1,0:T(8,128)(2,1)} %get-tuple-element.57) | copy-start | bytes 7864324
  274.2 2.0 copy-start.18
  274.2 2.0 copy-start.47
  278.0 1.8 copy-start.43
  279.8 1.8 copy-start.41
  281.5 1.8 copy-start.39
  283.3 1.8 copy-start.37
  285.1 1.8 copy-start.35
  286.8 1.8 copy-start.53
  288.6 1.8 copy-start.52
  290.3 1.8 copy-start.51
  292.1 1.8 copy-start.50
  293.9 1.8 copy-start.49
  295.6 1.8 copy-start.48
  296.5 2.0 copy-start.6
  296.5 2.0 copy-start.46
  298.5 1.8 copy-start.44
  300.2 1.8 copy-start.42
  302.0 1.8 copy-start.40
  (35 other events, 61.1 us)
Sparse Core Ops, SparseCore 0:
  34.7 70.6 all-gather.4
  107.6 57.5 all-gather.2
  322.9 145.7 all-reduce.3
where the time goes:
time: 486 us; the launch traced here: 477 us
  waiting for transfers between devices  171 us (35%)
  local copies, waits for them, and re-layouts  156 us (32%)
  blocking collectives  95.7 us (20%)
  matrix products  33.5 us (7%)
  between operations  13.6 us (3%)
    unnamed x4, waiting for transfers between devices  146 us
    unnamed x140, local copies, waits for them, and re-layouts  72.5 us
    all_to_all x1, blocking collectives, body(): lax.all_to_all(patch_rows, 'tensor', split_axis=0, concat_axis=2, tiled=T...  49 us
    slice x2, local copies, waits for them, and re-layouts, project_taps(): basis[tap_index]  37.1 us
    all_gather x1, blocking collectives, body(): basis_cols = lax.all_gather(basis_g, 'dp', axis=1, tiled=True)  26.7 us
    all_to_all x1, waiting for transfers between devices, body(): lax.all_to_all(out_grads, 'tensor', split_axis=0, concat_axis=2, tiled=True)  25.4 us
    dot_general x27, matrix products, project_taps(): jnp.dot(window, basis[tap_index], preferred_element_type=jnp.float32)  24.2 us
    slice x2, local copies, waits for them, and re-layouts, project_taps(): padded[:, offset_x:offset_x + SIDE, offset_y:offset_y + SIDE, offset_z:of...  22.6 us
  transfers between devices with their start and end apart: 4, of which 2 were waited for; matrix products, arithmetic and copies ran while one was open for 12% of the time, Pallas kernels for 0%

commit v1 on v0

v1 whole, which is shorter than its diff:
```python
import functools

import jax
import jax.numpy as jnp
from jax import lax
from jax.experimental import pallas as pl
from jax.experimental.pallas import tpu as pltpu
from jax.sharding import Mesh, PartitionSpec as P

SIDE = 8
POS = SIDE * SIDE * SIDE
AB = 9
HALF = 512
CHIPS = ("x", "y")
ALL = ("x", "y", "core", "z")


def lane_coords():
    p = lax.broadcasted_iota(jnp.int32, (1, POS), 1)
    return p // 64, (p // 8) % 8, p % 8


def shifted(y, ab, i, j):
    a, b = ab // 3 - 1, ab % 3 - 1
    s = a * 64 + b * 8
    if s == 0:
        return y
    ok = None
    for v, o in ((i, a), (j, b)):
        if o != 0:
            m = (v + o >= 0) & (v + o < SIDE)
            ok = m if ok is None else ok & m
    return jnp.where(ok, pltpu.roll(y, (-s) % POS, 1), 0.0)


def conv_kernel(idx_ref, b_own_ref, b_oth_ref, x_ref, o_ref, xc_ref, *, per):
    i, j, k = lane_coords()
    core = idx_ref[0]
    block = idx_ref[1]
    h = x_ref.shape[1]
    b = jnp.concatenate([b_own_ref[...], b_oth_ref[...]], axis=1)

    def put(row, v):
        at = pl.multiple_of((row + core * HALF) % (2 * HALF), 64)
        xc_ref[pl.ds(at, v.shape[0]), :] = v

    for n in range(per):
        x = x_ref[block * per + n]
        xf = x.astype(jnp.float32)
        before = jnp.where(k >= 1, pltpu.roll(xf, 1, 1), 0.0).astype(x.dtype)
        after = jnp.where(k <= SIDE - 2, pltpu.roll(xf, POS - 1, 1), 0.0).astype(x.dtype)
        put(0, before)
        put(h, x[: HALF - h])
        put(HALF, x[HALF - h :])
        put(2 * h, after)
        put(3 * h, jnp.zeros((2 * HALF - 3 * h, POS), x.dtype))
        y = jnp.dot(b, xc_ref[...], preferred_element_type=jnp.float32)
        y = y.reshape(y.shape[0] // (8 * AB), AB, 8, POS)
        acc = None
        for ab in range(AB):
            t = shifted(y[:, ab].reshape(-1, POS), ab, i, j)
            acc = t if acc is None else acc + t
        o_ref[n] = acc.astype(o_ref.dtype)


def conv(idx, b_own, b_oth, x, per, dtype):
    ranks = b_own.shape[0] // AB
    return pl.pallas_call(
        functools.partial(conv_kernel, per=per),
        out_shape=jax.ShapeDtypeStruct((per, ranks, POS), dtype),
        in_specs=[pl.BlockSpec(memory_space=pltpu.SMEM)] + [pl.BlockSpec(memory_space=pltpu.VMEM)] * 3,
        out_specs=pl.BlockSpec(memory_space=pltpu.VMEM),
        scratch_shapes=[pltpu.VMEM((2 * HALF, POS), jnp.bfloat16)],
        compiler_params=pltpu.CompilerParams(vmem_limit_bytes=40 << 20),
        name="conv_taps",
    )(idx, b_own, b_oth, x)


NT = (((1,), (1,)), ((), ()))


def squares_kernel(own_ref, r1_ref, r2_ref, r3_ref, g_ref, bg_ref, o_ref, *, scale):
    per, ranks = own_ref.shape[0], own_ref.shape[1]
    tensor = bg_ref.shape[1]
    total = None
    for n in range(per):
        c = own_ref[n] + r1_ref[n].astype(jnp.float32) + r2_ref[n].astype(jnp.float32) + r3_ref[n].astype(jnp.float32)
        hi = c.astype(jnp.bfloat16)
        lo = (c - hi.astype(jnp.float32)).astype(jnp.bfloat16)
        both = jnp.concatenate([hi, lo], axis=0)
        prod = None
        for z in range(tensor):
            m = lax.dot_general(both, g_ref[z * per + n], NT, preferred_element_type=jnp.float32)
            m = (m[:ranks] + m[ranks:]).astype(jnp.bfloat16)
            bg = bg_ref[:, z].reshape(-1, bg_ref.shape[3])
            t = lax.dot_general(m, bg, NT, preferred_element_type=jnp.float32)
            prod = t if prod is None else prod + t
        sq = prod * prod
        total = sq if total is None else total + sq
    o_ref[...] = total * scale


def squares(own, received, grads, bg, scale):
    return pl.pallas_call(
        functools.partial(squares_kernel, scale=scale),
        out_shape=jax.ShapeDtypeStruct((own.shape[1], bg.shape[0] * bg.shape[2]), jnp.float32),
        in_specs=[pl.BlockSpec(memory_space=pltpu.VMEM)] * 6,
        out_specs=pl.BlockSpec(memory_space=pltpu.VMEM),
        compiler_params=pltpu.CompilerParams(vmem_limit_bytes=40 << 20),
        name="squared_sums",
    )(own, *received, grads, bg)


def shift(v, axis, s):
    n = lax.axis_size(axis)
    return lax.ppermute(v, axis, [(i, (i + s) % n) for i in range(n)])


def body(patch_rows, out_grads, basis_a, basis_g):
    core, z = lax.axis_index("core"), lax.axis_index("z")
    x = patch_rows.transpose(0, 2, 1)
    grads = out_grads.transpose(0, 2, 1)
    here, channels = x.shape[0], x.shape[1]
    tensor = lax.axis_size("z")
    per = here // tensor
    chips = lax.axis_size(CHIPS)

    with jax.named_scope("gather_basis_a"):
        own = basis_a.reshape(AB, 3, channels, -1).transpose(0, 3, 1, 2)
        own = own.reshape(AB, own.shape[1], 3 * channels)
        own = jnp.pad(own, ((0, 0), (0, 0), (0, 2 * HALF - 3 * channels)))
        oth = shift(own, "core", 1)
        rows = jnp.where(core == 0, jnp.concatenate([own, oth], axis=1), jnp.concatenate([oth, own], axis=1))
        half = jnp.where(core == 0, rows[:, :, :HALF], rows[:, :, HALF:])
        spread = jnp.broadcast_to(half[None], (chips, *half.shape))
        b_own = lax.all_to_all(spread, CHIPS, 0, 0, tiled=True)
        b_own = b_own.reshape(-1, HALF)
        b_oth = shift(b_own, "core", 1)

    with jax.named_scope("gather_basis_g"):
        bg = lax.all_gather(basis_g.T, ALL, axis=0)
        bg = bg.reshape(-1, tensor, *bg.shape[1:])

    with jax.named_scope("exchange_grads"):
        grads_all = lax.all_to_all(grads, "z", 0, 0, tiled=True)

    def part(s, dtype):
        idx = jnp.stack([core, (z + s) % tensor]).astype(jnp.int32)
        return conv(idx, b_own, b_oth, x, per, dtype)

    received = []
    for s in (2, 1, 3):
        with jax.named_scope("coeff_part"):
            received.append(shift(part(s, jnp.bfloat16), "z", s))
    mine = part(0, jnp.float32)

    examples = here * lax.axis_size(("x", "y", "core"))
    total = squares(mine, received, grads_all, bg, 1.0 / examples)

    with jax.named_scope("sum_examples"):
        rows = total.reshape(chips, 2, -1, total.shape[1])
        keep = jnp.where(core == 0, rows[:, 0], rows[:, 1])
        give = jnp.where(core == 0, rows[:, 1], rows[:, 0])
        keep = keep + shift(give, "core", 1)
        keep = keep.astype(jnp.bfloat16).reshape(chips * tensor, 1, -1)
        got = lax.all_to_all(keep, ("x", "y", "z"), 0, 0, tiled=True)
        return jnp.sum(got.astype(jnp.float32), axis=0)


def solution(mesh):
    tensor = mesh.shape["tensor"]
    fine = Mesh(mesh.devices.reshape(4, -1, 2, tensor), ALL)
    dp = ("x", "y", "core")
    in_specs = (P(dp, None, "z"), P(dp, None, "z"), P(None, "z", dp), P("z", dp))
    return jax.shard_map(body, mesh=fine, in_specs=in_specs, out_specs=P(ALL, None), check_vma=False)
```

time: 486 us -> 131 us (0.27); the launches traced: 477 us -> 130 us
  waiting for transfers between devices: 171 us -> 22.4 us
  local copies, waits for them, and re-layouts: 156 us -> 12.5 us
  blocking collectives: 95.7 us -> 38.1 us
  matrix products: 33.5 us -> 0 us
  Pallas kernels: 0 us -> 26.8 us
  starting transfers between devices: 4.64 us -> 13.7 us
    unnamed x4 -> x1, waiting for transfers between devices: 146 us -> 0.71 us
    unnamed x140 -> x22, local copies, waits for them, and re-layouts: 72.5 us -> 9.96 us
    slice x4 -> x0, local copies, waits for them, and re-layouts: 59.6 us -> none  [the longest x2 37.1 us: project_taps(): basis[tap_index]]
    all_gather x2 -> x0, blocking collectives: 46.8 us -> none  [the longest x1 26.7 us: body(): basis_cols = lax.all_gather(basis_g, 'dp', axis=1, tiled=True)]
    dot_general x29 -> x0, matrix products: 33.5 us -> none  [the longest x27 24.2 us: project_taps(): jnp.dot(window, basis[tap_index], preferred_element_type=jnp.float32)]
    pallas_call x0 -> x5, Pallas kernels: none -> 26.8 us  [the longest x4 20.9 us: conv(): pl.pallas_call(functools.partial(conv_kernel, per=per), out_shape=jax.Sha...]
    all_to_all x1, waiting for transfers between devices: 25.4 us -> 0.01 us  [body(): grads_all = lax.all_to_all(grads, 'z', 0, 0, tiled=True)]
    ppermute x0 -> x6, waiting for transfers between devices: none -> 21.7 us  [shift(): return lax.ppermute(v, axis, [(i, (i + s) % n) for i in range(n)])]
  transfers between devices with their start and end apart: 4 -> 8, of which waited for: 2 -> 5; matrix products, arithmetic and copies ran while one was open for 12% -> 1% of each run, Pallas kernels for 0% -> 16%
where the time goes in v1:
time: 131 us; the launch traced here: 130 us
  blocking collectives  38.1 us (29%)
  Pallas kernels  26.8 us (20%)
  waiting for transfers between devices  22.4 us (17%)
  starting transfers between devices  13.7 us (10%)
  between operations  13.5 us (10%)
  local copies, waits for them, and re-layouts  12.5 us (10%)
  other arithmetic  2.55 us (2%)
    all_to_all x1, blocking collectives, body(): b_own = lax.all_to_all(spread, CHIPS, 0, 0, tiled=True)  24.5 us
    ppermute x6, waiting for transfers between devices, shift(): return lax.ppermute(v, axis, [(i, (i + s) % n) for i in range(n)])  21.7 us
    pallas_call x4, Pallas kernels, conv(): pl.pallas_call(functools.partial(conv_kernel, per=per), out_shape=jax.Sha...  20.9 us
    all_to_all x1, blocking collectives, body(): got = lax.all_to_all(keep, ('x', 'y', 'z'), 0, 0, tiled=True)  13.5 us
    unnamed x22, local copies, waits for them, and re-layouts  9.96 us
    ppermute x6, starting transfers between devices, shift(): return lax.ppermute(v, axis, [(i, (i + s) % n) for i in range(n)])  8.33 us
    pallas_call x1, Pallas kernels, squares(): pl.pallas_call(functools.partial(squares_kernel, scale=scale), out_shape=...  5.91 us
    all_to_all x1, starting transfers between devices, body(): grads_all = lax.all_to_all(grads, 'z', 0, 0, tiled=True)  5.35 us
  transfers between devices with their start and end apart: 8, of which 5 were waited for; matrix products, arithmetic and copies ran while one was open for 1% of the time, Pallas kernels for 16%

profile of v1, /device:TPU:1, one launch (start us, length us, event | category | flops | bytes accessed | tf_op | source)
XLA Modules:
  0.0 129.6 jit_solution(4430898396872952424)
XLA Ops:
  7.3 0.9 copy.26
  8.4 1.5 %collective-permute-start = (bf16[9,4,1024]{2,1,0:T(4,128)(2,1)S(1)}, bf16[9,4,1024]{2,1,0:T(4,128)(2,1)S(1)}, u32[]{:S(2)}, u32[]{:S(2)}) collective-permute-start(bf16[9,4,1024]{2,1,0:T(4,128)(2,1)S(1)} %pad.4), channel_id=1, source_target_pairs={{0,4},{4,0},{1,5},{5,1},{2,6},{6,2},{3,7},{7,3},{8,12},{12,8},{9,1... | collective-permute-start | bytes 221192 | tf_op jit(solution)/shard_map/gather_basis_a/ppermute | solution.py:116
  11.0 24.5 %all_to_all.15 = bf16[16,9,8,512]{3,2,1,0:T(8,128)(2,1)} all-to-all(bf16[16,9,8,512]{3,2,1,0:T(8,128)(2,1)S(1)} %broadcast_in_dim.2), channel_id=1, replica_groups=mesh['x'=4,'y'=4,'core'=2,'z'=4] {'x','y'}, dimensions={0} | all-to-all | bytes 2359296 | tf_op jit(solution)/shard_map/gather_basis_a/all_to_all | solution.py:136
  35.6 5.3 %all-to-all-start.1 = ((bf16[8,320,512]{2,1,0:T(8,128)(2,1)}), bf16[8,320,512]{2,1,0:T(8,128)(2,1)}, u32[]{:S(2)}, u32[]{:S(2)}) async-start(bf16[8,320,512]{2,1,0:T(8,128)(2,1)} %bitcast.42), calls=%async_computation.1 | async-start | bytes 5242880 | tf_op jit(solution)/shard_map/exchange_grads/all_to_all | solution.py:145
  40.9 2.0 %collective-permute-start.1 = (bf16[1152,512]{1,0:T(8,128)(2,1)}, bf16[1152,512]{1,0:T(8,128)(2,1)}, u32[]{:S(2)}, u32[]{:S(2)}) collective-permute-start(bf16[1152,512]{1,0:T(8,128)(2,1)} %bitcast.36), channel_id=1, source_target_pairs={{0,4},{4,0},{1,5},{5,1},{2,6},{6,2},{3,7},{7,3},{8,12},{12,8},{9,1... | collective-permute-start | bytes 3538952 | tf_op jit(solution)/shard_map/gather_basis_a/ppermute | solution.py:116
  43.2 2.6 %collective-permute-done.1.b_oth_ref = bf16[1152,512]{1,0:T(8,128)(2,1)} collective-permute-done((bf16[1152,512]{1,0:T(8,128)(2,1)}, bf16[1152,512]{1,0:T(8,128)(2,1)}, u32[]{:S(2)}, u32[]{:S(2)}) %collective-permute-start.1) | collective-permute-done | bytes 1179680 | tf_op jit(solution)/shard_map/gather_basis_a/ppermute | solution.py:116
  45.8 1.3 copy-done.1
  47.0 5.4 %conv_taps.7 = bf16[2,128,512]{2,1,0:T(8,128)(2,1)} custom-call(s32[2]{0:T(128)S(1)} %pad_add_fusion.3.idx_ref, bf16[1152,512]{1,0:T(8,128)(2,1)S(1)} %bitcast.37, bf16[1152,512]{1,0:T(8,128)(2,1)} %collective-permute-done.1.b_oth_ref, bf16[8,320,512]{2,1,0:T(8,128)(2,1)S(1)} %bitcast.32), custom_call_target="tpu_custom_call" | custom-call | tf_op jit(solution)/shard_map/coeff_part/conv_taps/pallas_call | solution.py:68
  52.4 3.1 %collective-permute-start.4 = (bf16[2,128,512]{2,1,0:T(8,128)(2,1)}, bf16[2,128,512]{2,1,0:T(8,128)(2,1)S(1)}, u32[]{:S(2)}, u32[]{:S(2)}) collective-permute-start(bf16[2,128,512]{2,1,0:T(8,128)(2,1)} %conv_taps.7), channel_id=1, source_target_pairs={{0,3},{1,0},{2,1},{3,2},{4,7},{5,4},{6,5},{7,6},{8,11},{9,8},{10,9... | collective-permute-start | bytes 786440 | tf_op jit(solution)/shard_map/coeff_part/ppermute | solution.py:116
  55.5 5.4 %conv_taps.6 = bf16[2,128,512]{2,1,0:T(8,128)(2,1)} custom-call(s32[2]{0:T(128)S(1)} %pad_add_fusion.2.idx_ref, bf16[1152,512]{1,0:T(8,128)(2,1)S(1)} %bitcast.38, bf16[1152,512]{1,0:T(8,128)(2,1)} %collective-permute-done.1.b_oth_ref, bf16[8,320,512]{2,1,0:T(8,128)(2,1)S(1)} %bitcast.33), custom_call_target="tpu_custom_call" | custom-call | tf_op jit(solution)/shard_map/coeff_part/conv_taps/pallas_call | solution.py:68
  60.9 5.4 %conv_taps.5 = bf16[2,128,512]{2,1,0:T(8,128)(2,1)} custom-call(s32[2]{0:T(128)S(1)} %pad_add_fusion.1.idx_ref, bf16[1152,512]{1,0:T(8,128)(2,1)S(1)} %bitcast.39, bf16[1152,512]{1,0:T(8,128)(2,1)} %collective-permute-done.1.b_oth_ref, bf16[8,320,512]{2,1,0:T(8,128)(2,1)S(1)} %bitcast.34), custom_call_target="tpu_custom_call" | custom-call | tf_op jit(solution)/shard_map/coeff_part/conv_taps/pallas_call | solution.py:68
  66.4 1.6 %collective-permute-start.2 = (bf16[2,128,512]{2,1,0:T(8,128)(2,1)}, bf16[2,128,512]{2,1,0:T(8,128)(2,1)S(1)}, u32[]{:S(2)}, u32[]{:S(2)}) collective-permute-start(bf16[2,128,512]{2,1,0:T(8,128)(2,1)} %conv_taps.5), channel_id=1, source_target_pairs={{0,2},{1,3},{2,0},{3,1},{4,6},{5,7},{6,4},{7,5},{8,10},{9,11},{10,... | collective-permute-start | bytes 786440 | tf_op jit(solution)/shard_map/coeff_part/ppermute | solution.py:116
  68.1 1.3 copy-done.2
  69.3 4.7 %conv_taps.4.own_ref = f32[2,128,512]{2,1,0:T(8,128)S(1)} custom-call(s32[2]{0:T(128)S(1)} %pad_add_fusion.idx_ref, bf16[1152,512]{1,0:T(8,128)(2,1)S(1)} %bitcast.40, bf16[1152,512]{1,0:T(8,128)(2,1)} %collective-permute-done.1.b_oth_ref, bf16[8,320,512]{2,1,0:T(8,128)(2,1)S(1)} %bitcast.35), custom_call_target="tpu_custom_call" | custom-call | tf_op jit(solution)/shard_map/conv_taps/pallas_call | solution.py:68
  74.9 4.3 %collective-permute-done.4.r3_ref = bf16[2,128,512]{2,1,0:T(8,128)(2,1)S(1)} collective-permute-done((bf16[2,128,512]{2,1,0:T(8,128)(2,1)}, bf16[2,128,512]{2,1,0:T(8,128)(2,1)S(1)}, u32[]{:S(2)}, u32[]{:S(2)}) %collective-permute-start.4) | collective-permute-done | bytes 262176 | tf_op jit(solution)/shard_map/coeff_part/ppermute | solution.py:116
  79.1 12.3 %collective-permute-done.3.r2_ref = bf16[2,128,512]{2,1,0:T(8,128)(2,1)S(1)} collective-permute-done((bf16[2,128,512]{2,1,0:T(8,128)(2,1)}, bf16[2,128,512]{2,1,0:T(8,128)(2,1)S(1)}, u32[]{:S(2)}, u32[]{:S(2)}) %collective-permute-start.3) | collective-permute-done | bytes 262176 | tf_op jit(solution)/shard_map/coeff_part/ppermute | solution.py:116
  92.9 2.1 %copy-done.3 = bf16[5120,320]{1,0:T(8,128)(2,1)S(1)} copy-done((bf16[5120,320]{1,0:T(8,128)(2,1)S(1)}, bf16[5120,320]{1,0:T(8,128)(2,1)}, u32[]{:S(2)}) %copy-start.3) | copy-done | bytes 3276824
  95.0 1.0 copy-done.5
  96.0 0.9 copy-done.7
  97.0 0.9 copy-done.9
  97.9 5.9 %squared_sums.1 = f32[128,1280]{1,0:T(8,128)S(1)} custom-call(f32[2,128,512]{2,1,0:T(8,128)S(1)} %copy-done.5, bf16[2,128,512]{2,1,0:T(8,128)(2,1)S(1)} %copy-done.9, bf16[2,128,512]{2,1,0:T(8,128)(2,1)S(1)} %copy-done.7, bf16[2,128,512]{2,1,0:T(8,128)(2,1)S(1)} %collective-permute-done.4.r3_ref, bf16[8,320,512]{2,1,0:T(8,128)(2,1)} %all-to-all-done.1.g_ref, ...), custom_call_target="tpu_custom_call" | custom-call | tf_op jit(solution)/shard_map/squared_sums/pallas_call | solution.py:104
  104.2 1.6 %collective-permute-done.5 = f32[16,4,1280]{2,1,0:T(4,128)S(1)} collective-permute-done((f32[16,4,1280]{2,1,0:T(4,128)S(1)}, f32[16,4,1280]{2,1,0:T(4,128)S(1)}, u32[]{:S(2)}, u32[]{:S(2)}) %collective-permute-start.5) | collective-permute-done | bytes 327712 | tf_op jit(solution)/shard_map/sum_examples/ppermute | solution.py:116
  106.5 1.6 %reduce.1 = bf16[64,1280]{1,0:T(8,128)(2,1)S(1)} reduce(bf16[64,1,1280]{2,1,0:T(2,128)(2,1)S(1)} %reshape.32, bf16[]{:T(256)} %broadcast.10), dimensions={1}, to_apply=%reshape.32.reduce_sub_computation | reduce | bytes 327682 | tf_op jit(solution)/shard_map/sum_examples/reshape | solution.py:165
  108.2 13.5 %all_to_all.16 = bf16[64,2,640]{2,1,0:T(2,128)(2,1)S(1)} all-to-all(bf16[64,2,640]{2,1,0:T(2,128)(2,1)S(1)} %reshape.33), channel_id=1, replica_groups=mesh['x'=4,'y'=4,'core'=2,'z'=4] {'x','y','z'}, dimensions={0} | all-to-all | bytes 327680 | tf_op jit(solution)/shard_map/sum_examples/all_to_all | solution.py:166
  (40 shorter events, 6.7 us)
Async XLA Ops:
  6.5 86.3 %all-gather.3.cloned.1.call-start = ((), (), s32[]{:S(2)}) async-start(), calls=%async_computation.3 | async-start | bytes 3962880 | tf_op jit(solution)/shard_map/gather_basis_g/all_gather | solution.py:141
  8.4 2.4 %collective-permute-start = (bf16[9,4,1024]{2,1,0:T(4,128)(2,1)S(1)}, bf16[9,4,1024]{2,1,0:T(4,128)(2,1)S(1)}, u32[]{:S(2)}, u32[]{:S(2)}) collective-permute-start(bf16[9,4,1024]{2,1,0:T(4,128)(2,1)S(1)} %pad.4), channel_id=1, source_target_pairs={{0,4},{4,0},{1,5},{5,1},{2,6},{6,2},{3,7},{7,3},{8,12},{12,8},{9,1... | collective-permute-start | bytes 221192 | tf_op jit(solution)/shard_map/gather_basis_a/ppermute | solution.py:116
  35.5 10.2 %copy-start = (bf16[8,512,320]{1,2,0:T(8,128)(2,1)S(1)}, bf16[8,512,320]{1,2,0:T(8,128)(2,1)}, u32[]{:S(2)}) copy-start(bf16[8,512,320]{1,2,0:T(8,128)(2,1)} %param.4) | copy-start | bytes 7864324
  35.6 39.3 %all-to-all-start.1 = ((bf16[8,320,512]{2,1,0:T(8,128)(2,1)}), bf16[8,320,512]{2,1,0:T(8,128)(2,1)}, u32[]{:S(2)}, u32[]{:S(2)}) async-start(bf16[8,320,512]{2,1,0:T(8,128)(2,1)} %bitcast.42), calls=%async_computation.1 | async-start | bytes 5242880 | tf_op jit(solution)/shard_map/exchange_grads/all_to_all | solution.py:145
  40.9 4.8 %collective-permute-start.1 = (bf16[1152,512]{1,0:T(8,128)(2,1)}, bf16[1152,512]{1,0:T(8,128)(2,1)}, u32[]{:S(2)}, u32[]{:S(2)}) collective-permute-start(bf16[1152,512]{1,0:T(8,128)(2,1)} %bitcast.36), channel_id=1, source_target_pairs={{0,4},{4,0},{1,5},{5,1},{2,6},{6,2},{3,7},{7,3},{8,12},{12,8},{9,1... | collective-permute-start | bytes 3538952 | tf_op jit(solution)/shard_map/gather_basis_a/ppermute | solution.py:116
  45.7 1.3 copy-start.1
  52.4 26.7 %collective-permute-start.4 = (bf16[2,128,512]{2,1,0:T(8,128)(2,1)}, bf16[2,128,512]{2,1,0:T(8,128)(2,1)S(1)}, u32[]{:S(2)}, u32[]{:S(2)}) collective-permute-start(bf16[2,128,512]{2,1,0:T(8,128)(2,1)} %conv_taps.7), channel_id=1, source_target_pairs={{0,3},{1,0},{2,1},{3,2},{4,7},{5,4},{6,5},{7,6},{8,11},{9,8},{10,9... | collective-permute-start | bytes 786440 | tf_op jit(solution)/shard_map/coeff_part/ppermute | solution.py:116
  60.9 30.5 %collective-permute-start.3 = (bf16[2,128,512]{2,1,0:T(8,128)(2,1)}, bf16[2,128,512]{2,1,0:T(8,128)(2,1)S(1)}, u32[]{:S(2)}, u32[]{:S(2)}) collective-permute-start(bf16[2,128,512]{2,1,0:T(8,128)(2,1)} %conv_taps.6), channel_id=1, source_target_pairs={{0,1},{1,2},{2,3},{3,0},{4,5},{5,6},{6,7},{7,4},{8,9},{9,10},{10,1... | collective-permute-start | bytes 786440 | tf_op jit(solution)/shard_map/coeff_part/ppermute | solution.py:116
  66.4 25.8 %collective-permute-start.2 = (bf16[2,128,512]{2,1,0:T(8,128)(2,1)}, bf16[2,128,512]{2,1,0:T(8,128)(2,1)S(1)}, u32[]{:S(2)}, u32[]{:S(2)}) collective-permute-start(bf16[2,128,512]{2,1,0:T(8,128)(2,1)} %conv_taps.5), channel_id=1, source_target_pairs={{0,2},{1,3},{2,0},{3,1},{4,6},{5,7},{6,4},{7,5},{8,10},{9,11},{10,... | collective-permute-start | bytes 786440 | tf_op jit(solution)/shard_map/coeff_part/ppermute | solution.py:116
  68.1 1.3 copy-start.2
  74.0 0.8 copy-start.4
  91.5 0.7 copy-start.6
  92.2 0.7 copy-start.8
  92.9 2.1 %copy-start.3 = (bf16[5120,320]{1,0:T(8,128)(2,1)S(1)}, bf16[5120,320]{1,0:T(8,128)(2,1)}, u32[]{:S(2)}) copy-start(bf16[5120,320]{1,0:T(8,128)(2,1)} %all-gather.3.cloned.1.call-done) | copy-start | bytes 9830404
  95.0 1.0 copy-start.5
  96.0 0.9 copy-start.7
  97.0 0.9 copy-start.9
  104.1 1.7 %collective-permute-start.5 = (f32[16,4,1280]{2,1,0:T(4,128)S(1)}, f32[16,4,1280]{2,1,0:T(4,128)S(1)}, u32[]{:S(2)}, u32[]{:S(2)}) collective-permute-start(f32[16,4,1280]{2,1,0:T(4,128)S(1)} %select_bitcast_fusion), channel_id=1, source_target_pairs={{0,4},{4,0},{1,5},{5,1},{2,6},{6,2},{3,7},{7,3},{8,12},{12,8},{9,1... | collective-permute-start | bytes 983048 | tf_op jit(solution)/shard_map/sum_examples/ppermute | solution.py:116
Sparse Core Ops, SparseCore 0:
  10.3 79.2 all-gather.2

commit v2 on v1

v2 whole, which is shorter than its diff:
```python
import jax
import jax.numpy as jnp
from jax import lax
from jax.experimental import pallas as pl
from jax.experimental.pallas import tpu as pltpu
from jax.sharding import Mesh, PartitionSpec as P

SIDE = 8
POS = SIDE * SIDE * SIDE
AB = 9
ALL = ("x", "y", "core", "z")
NT = (((1,), (1,)), ((), ()))
VMEM = pl.BlockSpec(memory_space=pltpu.VMEM)
SMEM = pl.BlockSpec(memory_space=pltpu.SMEM)
HBM = pl.BlockSpec(memory_space=pltpu.HBM)


def lane_coords():
    p = lax.broadcasted_iota(jnp.int32, (1, POS), 1)
    return p // 64, (p // 8) % 8, p % 8


def shifted(y, ab, i, j):
    a, b = ab // 3 - 1, ab % 3 - 1
    s = a * 64 + b * 8
    if s == 0:
        return y
    ok = None
    for v, o in ((i, a), (j, b)):
        if o != 0:
            m = (v + o >= 0) & (v + o < SIDE)
            ok = m if ok is None else ok & m
    return jnp.where(ok, pltpu.roll(y, (-s) % POS, 1), 0.0)


def conv_kernel(idx_ref, *refs):
    *b_refs, x_ref, x_oth_ref, o_ref, b_buf, x_buf, xc_ref, o_buf, sem = refs
    i, j, k = lane_coords()
    block = idx_ref[0]
    h = x_ref.shape[1]
    per = o_ref.shape[0] // 2
    parts, rows = len(b_refs), b_refs[0].shape[1]
    copies = [
        pltpu.make_async_copy(ref.at[block * per + n], x_buf.at[m * per + n], sem.at[m * per + n])
        for m, ref in enumerate((x_ref, x_oth_ref))
        for n in range(per)
    ]
    loads = [pltpu.make_async_copy(ref, b_buf.at[m], sem.at[2 * per + m]) for m, ref in enumerate(b_refs)]
    for c in copies[:1] + loads + copies[1:]:
        c.start()
    b, stores = None, []
    for n in range(2 * per):
        copies[n].wait()
        x = x_buf[n]
        xf = x.astype(jnp.float32)
        xc_ref[:h] = jnp.where(k >= 1, pltpu.roll(xf, 1, 1), 0.0).astype(x.dtype)
        xc_ref[h : 2 * h] = x
        xc_ref[2 * h :] = jnp.where(k <= SIDE - 2, pltpu.roll(xf, POS - 1, 1), 0.0).astype(x.dtype)
        if b is None:
            for c in loads:
                c.wait()
            b = b_buf[...].reshape(parts * AB * rows, 3 * h)
        y = jnp.dot(b, xc_ref[...], preferred_element_type=jnp.float32)
        y = y.reshape(parts, AB, rows, POS)
        acc = None
        for ab in range(AB):
            t = shifted(y[:, ab].reshape(-1, POS), ab, i, j)
            acc = t if acc is None else acc + t
        o_buf[n] = acc.astype(o_ref.dtype)
        stores.append(pltpu.make_async_copy(o_buf.at[n], o_ref.at[n], sem.at[2 * per + parts + n]))
        stores[-1].start()
    for c in stores:
        c.wait()


def conv(idx, blocks, x, x_oth, per, dtype):
    rows = blocks[0].shape[1]
    ranks = len(blocks) * rows
    return pl.pallas_call(
        conv_kernel,
        out_shape=jax.ShapeDtypeStruct((2 * per, ranks, POS), dtype),
        in_specs=[SMEM] + [HBM] * (len(blocks) + 2),
        out_specs=HBM,
        scratch_shapes=[
            pltpu.VMEM((len(blocks), *blocks[0].shape), jnp.bfloat16),
            pltpu.VMEM((2 * per, x.shape[1], POS), jnp.bfloat16),
            pltpu.VMEM((3 * x.shape[1], POS), jnp.bfloat16),
            pltpu.VMEM((2 * per, ranks, POS), dtype),
            pltpu.SemaphoreType.DMA((4 * per + len(blocks),)),
        ],
        compiler_params=pltpu.CompilerParams(vmem_limit_bytes=40 << 20),
        name="conv_taps",
    )(idx, *blocks, x, x_oth)


def squares_kernel(idx_ref, own_ref, r1_ref, r2_ref, r3_ref, g_ref, g_oth_ref, bg_ref, bg_oth_ref, o_ref, own_buf, r_buf, g_buf, bg_buf, hi_ref, m_ref, sem, *, scale):
    x, y, core, z = idx_ref[0], idx_ref[1], idx_ref[2], idx_ref[3]
    chips, width = bg_ref.shape[0], bg_ref.shape[1]
    examples, ranks = own_ref.shape[0], own_ref.shape[1]
    per = examples // 2
    tensor = g_ref.shape[0] // per
    side = 4

    def chip(rx, ry):
        return ((x + side - rx) % side) * side + (y + side - ry) % side

    pairs = [(own_ref, own_buf), (r1_ref, r_buf.at[0]), (r2_ref, r_buf.at[1]), (r3_ref, r_buf.at[2])]
    for n in range(examples):
        src = g_ref if n < per else g_oth_ref
        for t in range(tensor):
            pairs.append((src.at[((z + tensor - t) % tensor) * per + n % per], g_buf.at[n, t]))
    late = len(pairs)
    for b in range(chips):
        at = chip(b // side, b % side) * 2
        pairs.append((bg_ref.at[b], bg_buf.at[at + core]))
        pairs.append((bg_oth_ref.at[b], bg_buf.at[at + 1 - core]))
    copies = [pltpu.make_async_copy(a, b, sem.at[i]) for i, (a, b) in enumerate(pairs)]
    for c in copies:
        c.start()
    for c in copies[:4]:
        c.wait()
    for n in range(examples):
        c = own_buf[n] + r_buf[0, n].astype(jnp.float32) + r_buf[1, n].astype(jnp.float32) + r_buf[2, n].astype(jnp.float32)
        hi_ref[n] = c.astype(jnp.bfloat16)
        hi = hi_ref[n]
        lo = (c - hi.astype(jnp.float32)).astype(jnp.bfloat16)
        both = jnp.concatenate([hi, lo], axis=0)
        for c in copies[4 + n * tensor : 4 + (n + 1) * tensor]:
            c.wait()
        g = g_buf[n].reshape(-1, POS)
        m = lax.dot_general(both, g, NT, preferred_element_type=jnp.float32)
        m_ref[n * ranks : (n + 1) * ranks] = (m[:ranks] + m[ranks:]).astype(jnp.bfloat16)
    for c in copies[late:]:
        c.wait()
    bg = bg_buf[...].reshape(2 * chips * width, bg_buf.shape[2])
    prod = lax.dot_general(m_ref[...], bg, NT, preferred_element_type=jnp.float32)
    sq = None
    for n in range(examples):
        t = prod[n * ranks : (n + 1) * ranks]
        sq = t * t if sq is None else sq + t * t
    sq = sq * scale
    low = ranks // chips
    for b in range(chips):
        o_ref[chip(b % side, b // side)] = sq[b * low : (b + 1) * low]


def squares(idx, own, received, g, g_oth, bg, bg_oth, scale):
    examples, ranks = own.shape[0], own.shape[1]
    chips, width, hidden = bg.shape
    tensor = g.shape[0] // (examples // 2)

    def kernel(*refs):
        squares_kernel(*refs, scale=scale)

    return pl.pallas_call(
        kernel,
        out_shape=jax.ShapeDtypeStruct((chips, ranks // chips, 2 * chips * width), jnp.float32),
        in_specs=[SMEM] + [HBM] * 8,
        out_specs=VMEM,
        scratch_shapes=[
            pltpu.VMEM(own.shape, jnp.float32),
            pltpu.VMEM((3, *own.shape), jnp.bfloat16),
            pltpu.VMEM((examples, tensor, *g.shape[1:]), jnp.bfloat16),
            pltpu.VMEM((2 * chips, width, hidden), jnp.bfloat16),
            pltpu.VMEM((examples, ranks, POS), jnp.bfloat16),
            pltpu.VMEM((examples * ranks, hidden), jnp.bfloat16),
            pltpu.SemaphoreType.DMA((4 + examples * tensor + 2 * chips,)),
        ],
        compiler_params=pltpu.CompilerParams(vmem_limit_bytes=48 << 20),
        name="squared_sums",
    )(idx, own, *received, g, g_oth, bg, bg_oth)


def shift(v, axis, s):
    n = lax.axis_size(axis)
    return lax.ppermute(v, axis, [(i, (i + s) % n) for i in range(n)])


def around(v, axis):
    return [v] + [shift(v, axis, s) for s in range(1, lax.axis_size(axis))]


def body(patch_rows, out_grads, basis_a, basis_g):
    coords = [lax.axis_index(a).astype(jnp.int32) for a in ALL]
    z = coords[3]
    x = patch_rows.transpose(0, 2, 1)
    grads = out_grads.transpose(0, 2, 1)
    here, channels = x.shape[0], x.shape[1]
    tensor = lax.axis_size("z")
    per = here // tensor

    with jax.named_scope("basis_g_z"):
        bg = around(basis_g.T, "z")
    with jax.named_scope("basis_a_x"):
        own = basis_a.reshape(AB, 3, channels, -1).transpose(0, 3, 1, 2)
        ba = around(own.reshape(AB, own.shape[1], 3 * channels), "x")
    with jax.named_scope("exchange_grads"):
        g = lax.all_to_all(grads, "z", 0, 0, tiled=True)
    with jax.named_scope("exchange_inputs"):
        x_oth = shift(x, "core", 1)

    ba, bg, x_oth = lax.optimization_barrier((ba, bg, x_oth))
    with jax.named_scope("basis_a_y"):
        ba = around(jnp.concatenate(ba, axis=1), "y")
    with jax.named_scope("basis_g_y"):
        bg = around(jnp.concatenate(bg, axis=1), "y")

    ba, bg = lax.optimization_barrier((ba, bg))
    with jax.named_scope("basis_g_x"):
        bg = around(jnp.stack(bg), "x")

    parts = []

    def part(s, dtype):
        idx = ((z + s) % tensor).reshape(1)
        if parts:
            idx, _ = lax.optimization_barrier((idx, parts[-1]))
        return conv(idx, ba, x, x_oth, per, dtype)

    received = []
    for s in (2, 1, 3):
        with jax.named_scope("coeff_part"):
            parts.append(part(s, jnp.bfloat16))
            received.append(shift(parts[-1], "z", s))
    parts.append(received[0])
    mine = part(0, jnp.float32)
    with jax.named_scope("exchange_cores"):
        g, bg, _ = lax.optimization_barrier((g, bg, parts[2]))
        g_oth = shift(g, "core", 1)
        bg = jnp.concatenate(bg, axis=0)
        bg_oth = shift(bg, "core", 1)

    examples = here * lax.axis_size(("x", "y", "core"))
    total = squares(jnp.stack(coords), mine, received, g, g_oth, bg, bg_oth, 1.0 / examples)

    with jax.named_scope("sum_examples"):
        rows = total.reshape(-1, 1, total.shape[2])
        got = lax.all_to_all(rows, ("x", "y", "z"), 0, 0, tiled=True)
        return jnp.sum(got, axis=0)


def solution(mesh):
    tensor = mesh.shape["tensor"]
    fine = Mesh(mesh.devices.reshape(4, -1, 2, tensor), ALL)
    dp = ("x", "y", "core")
    in_specs = (P(dp, None, "z"), P(dp, None, "z"), P(None, "z", dp), P("z", dp))
    return jax.shard_map(body, mesh=fine, in_specs=in_specs, out_specs=P(ALL, None), check_vma=False)
```

time: 131 us -> 149 us (1.14)
  waiting for transfers between devices: 22.4 us -> 50.5 us
  starting transfers between devices: 13.7 us -> 35.5 us
  blocking collectives: 38.1 us -> 16.9 us
  between operations: 13.5 us -> 0.15 us
  Pallas kernels: 26.8 us -> 30.7 us
  local copies, waits for them, and re-layouts: 12.5 us -> 10.5 us
    ppermute x6 -> x21, waiting for transfers between devices: 21.7 us -> 50.5 us  [shift(): return lax.ppermute(v, axis, [(i, (i + s) % n) for i in range(n)])]
    ppermute x6 -> x21, starting transfers between devices: 8.33 us -> 30.1 us  [shift(): return lax.ppermute(v, axis, [(i, (i + s) % n) for i in range(n)])]
    all_to_all x2 -> x1, blocking collectives: 38.1 us -> 16.9 us  [body(): got = lax.all_to_all(rows, ('x', 'y', 'z'), 0, 0, tiled=True)]
    unnamed x22 -> x15, local copies, waits for them, and re-layouts: 9.96 us -> 5.99 us
    pallas_call x5, Pallas kernels: 26.8 us -> 30.7 us  [the longest x4 24.4 us: conv(): pl.pallas_call(conv_kernel, out_shape=jax.ShapeDtypeStruct((2 * per, rank...]
    concatenate x0 -> x2, local copies, waits for them, and re-layouts: none -> 3.33 us  [the longest x1 1.79 us: body(): bg = jnp.concatenate(bg, axis=0)]
    reshape x1 -> x0, other arithmetic: 1.59 us -> none  [body(): keep = keep.astype(jnp.bfloat16).reshape(chips * tensor, 1, -1)]
    another operation x4 -> x2, other arithmetic: 0.3 us -> 1.8 us  [the longest x1 1.72 us: body(): bg = around(jnp.stack(bg), 'x')]
  transfers between devices with their start and end apart: 8 -> 22, of which waited for: 5 -> 9; matrix products, arithmetic and copies ran while one was open for 1% -> 7% of each run, Pallas kernels for 16% -> 17%
where the time goes in v2:
time: 149 us; the launch traced here: 146 us
  waiting for transfers between devices  50.5 us (34%)
  starting transfers between devices  35.5 us (24%)
  Pallas kernels  30.7 us (21%)
  blocking collectives  16.9 us (11%)
  local copies, waits for them, and re-layouts  10.5 us (7%)
  other arithmetic  2.22 us (1%)
    ppermute x21, waiting for transfers between devices, shift(): return lax.ppermute(v, axis, [(i, (i + s) % n) for i in range(n)])  50.5 us
    ppermute x21, starting transfers between devices, shift(): return lax.ppermute(v, axis, [(i, (i + s) % n) for i in range(n)])  30.1 us
    pallas_call x4, Pallas kernels, conv(): pl.pallas_call(conv_kernel, out_shape=jax.ShapeDtypeStruct((2 * per, rank...  24.4 us
    all_to_all x1, blocking collectives, body(): got = lax.all_to_all(rows, ('x', 'y', 'z'), 0, 0, tiled=True)  16.9 us
    pallas_call x1, Pallas kernels, squares(): pl.pallas_call(kernel, out_shape=jax.ShapeDtypeStruct((chips, ranks // ch...  6.33 us
    unnamed x15, local copies, waits for them, and re-layouts  5.99 us
    all_to_all x1, starting transfers between devices, body(): g = lax.all_to_all(grads, 'z', 0, 0, tiled=True)  5.37 us
  transfers between devices with their start and end apart: 22, of which 9 were waited for; matrix products, arithmetic and copies ran while one was open for 7% of the time, Pallas kernels for 17%

profile of v2, /device:TPU:1, one launch (start us, length us, event | category | flops | bytes accessed | tf_op | source)
XLA Modules:
  0.0 146.4 jit_solution(12158586001243260920)
XLA Ops:
  1.4 5.4 %all-to-all-start = ((bf16[8,320,512]{2,1,0:T(8,128)(2,1)}), bf16[8,320,512]{2,1,0:T(8,128)(2,1)}, u32[]{:S(2)}, u32[]{:S(2)}) async-start(bf16[8,320,512]{2,1,0:T(8,128)(2,1)} %bitcast.24), calls=%async_computation | async-start | bytes 5242880 | tf_op jit(solution)/shard_map/exchange_grads/all_to_all | solution.py:198
  6.8 3.4 %collective-permute-start.5 = (bf16[40,320]{1,0:T(8,128)(2,1)S(1)}, bf16[40,320]{1,0:T(8,128)(2,1)S(1)}, u32[]{:S(2)}, u32[]{:S(2)}) collective-permute-start(bf16[40,320]{1,0:T(8,128)(2,1)S(1)} %bitcast.31), channel_id=1, source_target_pairs={{0,3},{1,0},{2,1},{3,2},{4,7},{5,4},{6,5},{7,6},{8,11},{9,8},{10,9... | collective-permute-start | bytes 76808 | tf_op jit(solution)/shard_map/basis_g_z/ppermute | solution.py:176
  10.3 2.5 %collective-permute-start.2 = (bf16[9,4,960]{2,1,0:T(4,128)(2,1)S(1)}, bf16[9,4,960]{2,1,0:T(4,128)(2,1)S(1)}, u32[]{:S(2)}, u32[]{:S(2)}) collective-permute-start(bf16[9,4,960]{2,1,0:T(4,128)(2,1)S(1)} %reshape.25), channel_id=1, source_target_pairs={{0,96},{32,0},{64,32},{96,64},{1,97},{33,1},{65,33},{97,65},{2,98}... | collective-permute-start | bytes 207368 | tf_op jit(solution)/shard_map/basis_a_x/ppermute | solution.py:176
  14.0 23.8 %collective-permute-done.5 = bf16[40,320]{1,0:T(8,128)(2,1)S(1)} collective-permute-done((bf16[40,320]{1,0:T(8,128)(2,1)S(1)}, bf16[40,320]{1,0:T(8,128)(2,1)S(1)}, u32[]{:S(2)}, u32[]{:S(2)}) %collective-permute-start.5) | collective-permute-done | bytes 25632 | tf_op jit(solution)/shard_map/basis_g_z/ppermute | solution.py:176
  37.8 3.4 %collective-permute-start.4 = (bf16[40,320]{1,0:T(8,128)(2,1)S(1)}, bf16[40,320]{1,0:T(8,128)(2,1)S(1)}, u32[]{:S(2)}, u32[]{:S(2)}) collective-permute-start(bf16[40,320]{1,0:T(8,128)(2,1)S(1)} %bitcast.32), channel_id=1, source_target_pairs={{0,2},{1,3},{2,0},{3,1},{4,6},{5,7},{6,4},{7,5},{8,10},{9,11},{10,... | collective-permute-start | bytes 76808 | tf_op jit(solution)/shard_map/basis_g_z/ppermute | solution.py:176
  42.5 4.0 %collective-permute-done.3 = bf16[40,320]{1,0:T(8,128)(2,1)S(1)} collective-permute-done((bf16[40,320]{1,0:T(8,128)(2,1)S(1)}, bf16[40,320]{1,0:T(8,128)(2,1)S(1)}, u32[]{:S(2)}, u32[]{:S(2)}) %collective-permute-start.3) | collective-permute-done | bytes 25632 | tf_op jit(solution)/shard_map/basis_g_z/ppermute | solution.py:176
  47.3 2.8 %collective-permute-start.9 = (bf16[9,16,960]{2,1,0:T(8,128)(2,1)S(1)}, bf16[9,16,960]{2,1,0:T(8,128)(2,1)S(1)}, u32[]{:S(2)}, u32[]{:S(2)}) collective-permute-start(bf16[9,16,960]{2,1,0:T(8,128)(2,1)S(1)} %pad_maximum_fusion.1.refs_0_), channel_id=1, source_target_pairs={{0,24},{8,0},{16,8},{24,16},{1,25},{9,1},{17,9},{25,17},{2,26},{10... | collective-permute-start | bytes 829448 | tf_op jit(solution)/shard_map/basis_a_y/ppermute | solution.py:176
  52.7 2.0 %collective-permute-start.12 = (bf16[40,1280]{1,0:T(8,128)(2,1)}, bf16[40,1280]{1,0:T(8,128)(2,1)S(1)}, u32[]{:S(2)}, u32[]{:S(2)}) collective-permute-start(bf16[40,1280]{1,0:T(8,128)(2,1)} %concatenate.10), channel_id=1, source_target_pairs={{0,24},{8,0},{16,8},{24,16},{1,25},{9,1},{17,9},{25,17},{2,26},{10... | collective-permute-start | bytes 307208 | tf_op jit(solution)/shard_map/basis_g_y/ppermute | solution.py:176
  56.1 5.5 %collective-permute-done.12 = bf16[40,1280]{1,0:T(8,128)(2,1)S(1)} collective-permute-done((bf16[40,1280]{1,0:T(8,128)(2,1)}, bf16[40,1280]{1,0:T(8,128)(2,1)S(1)}, u32[]{:S(2)}, u32[]{:S(2)}) %collective-permute-start.12) | collective-permute-done | bytes 102432 | tf_op jit(solution)/shard_map/basis_g_y/ppermute | solution.py:176
  61.7 3.6 %collective-permute-done.11 = bf16[40,1280]{1,0:T(8,128)(2,1)S(1)} collective-permute-done((bf16[40,1280]{1,0:T(8,128)(2,1)}, bf16[40,1280]{1,0:T(8,128)(2,1)S(1)}, u32[]{:S(2)}, u32[]{:S(2)}) %collective-permute-start.11) | collective-permute-done | bytes 102432 | tf_op jit(solution)/shard_map/basis_g_y/ppermute | solution.py:176
  65.2 4.8 %collective-permute-done.10 = bf16[40,1280]{1,0:T(8,128)(2,1)S(1)} collective-permute-done((bf16[40,1280]{1,0:T(8,128)(2,1)}, bf16[40,1280]{1,0:T(8,128)(2,1)S(1)}, u32[]{:S(2)}, u32[]{:S(2)}) %collective-permute-start.10) | collective-permute-done | bytes 102432 | tf_op jit(solution)/shard_map/basis_g_y/ppermute | solution.py:176
  71.7 2.5 %collective-permute-start.18 = (bf16[4,40,1280]{2,1,0:T(8,128)(2,1)}, bf16[4,40,1280]{2,1,0:T(8,128)(2,1)}, u32[]{:S(2)}, u32[]{:S(2)}) collective-permute-start(bf16[4,40,1280]{2,1,0:T(8,128)(2,1)} %pad_maximum_fusion), channel_id=1, source_target_pairs={{0,96},{32,0},{64,32},{96,64},{1,97},{33,1},{65,33},{97,65},{2,98}... | collective-permute-start | bytes 1228808 | tf_op jit(solution)/shard_map/basis_g_x/ppermute | solution.py:176
  75.3 6.1 %conv_taps.4 = bf16[4,64,512]{2,1,0:T(8,128)(2,1)} custom-call(s32[1]{0:T(128)} %bitcast.5.idx_ref, bf16[9,16,960]{2,1,0:T(8,128)(2,1)S(1)} %pad_maximum_fusion.1.refs_0_, bf16[9,16,960]{2,1,0:T(8,128)(2,1)} %collective-permute-done.7.refs_1_, bf16[9,16,960]{2,1,0:T(8,128)(2,1)S(1)} %collective-permute-done.8.refs_2_, ...), custom_call_target="tpu_custom_call" | custom-call | tf_op jit(solution)/shard_map/coeff_part/conv_taps/pallas_call | solution.py:79
  81.4 6.1 %conv_taps.6 = bf16[4,64,512]{2,1,0:T(8,128)(2,1)} custom-call(s32[1]{0:T(128)} %bitcast.10.idx_ref, bf16[9,16,960]{2,1,0:T(8,128)(2,1)S(1)} %pad_maximum_fusion.1.refs_0_, bf16[9,16,960]{2,1,0:T(8,128)(2,1)} %collective-permute-done.7.refs_1_, bf16[9,16,960]{2,1,0:T(8,128)(2,1)S(1)} %collective-permute-done.8.refs_2_, ...), custom_call_target="tpu_custom_call" | custom-call | tf_op jit(solution)/shard_map/coeff_part/conv_taps/pallas_call | solution.py:79
  87.5 6.1 %conv_taps.7 = bf16[4,64,512]{2,1,0:T(8,128)(2,1)} custom-call(s32[1]{0:T(128)} %bitcast.11.idx_ref, bf16[9,16,960]{2,1,0:T(8,128)(2,1)S(1)} %pad_maximum_fusion.1.refs_0_, bf16[9,16,960]{2,1,0:T(8,128)(2,1)} %collective-permute-done.7.refs_1_, bf16[9,16,960]{2,1,0:T(8,128)(2,1)S(1)} %collective-permute-done.8.refs_2_, ...), custom_call_target="tpu_custom_call" | custom-call | tf_op jit(solution)/shard_map/coeff_part/conv_taps/pallas_call | solution.py:79
  95.0 4.1 %collective-permute-start.19 = (bf16[8,320,512]{2,1,0:T(8,128)(2,1)}, bf16[8,320,512]{2,1,0:T(8,128)(2,1)}, u32[]{:S(2)}, u32[]{:S(2)}) collective-permute-start(bf16[8,320,512]{2,1,0:T(8,128)(2,1)} %all-to-all-done.refs_5_), channel_id=1, source_target_pairs={{0,4},{4,0},{1,5},{5,1},{2,6},{6,2},{3,7},{7,3},{8,12},{12,8},{9,1... | collective-permute-start | bytes 7864328 | tf_op jit(solution)/shard_map/exchange_cores/ppermute | solution.py:176
  99.1 1.8 %constant_dynamic-update-slice_fusion.3 = bf16[16,40,1280]{2,1,0:T(8,128)(2,1)} fusion(bf16[4,40,1280]{2,1,0:T(8,128)(2,1)} %pad_maximum_fusion), kind=kLoop, calls=%fused_computation.6 | loop fusion | bytes 819200
  100.9 1.8 %constant_dynamic-update-slice_fusion.2 = bf16[16,40,1280]{2,1,0:T(8,128)(2,1)} fusion(bf16[16,40,1280]{2,1,0:T(8,128)(2,1)} %constant_dynamic-update-slice_fusion.3, bf16[4,40,1280]{2,1,0:T(8,128)(2,1)} %collective-permute-done.16), kind=kLoop, calls=%fused_computation.5 | loop fusion | bytes 819200
  102.7 1.8 %constant_dynamic-update-slice_fusion.1 = bf16[16,40,1280]{2,1,0:T(8,128)(2,1)} fusion(bf16[16,40,1280]{2,1,0:T(8,128)(2,1)} %constant_dynamic-update-slice_fusion.2, bf16[4,40,1280]{2,1,0:T(8,128)(2,1)} %collective-permute-done.17), kind=kLoop, calls=%fused_computation.4 | loop fusion | bytes 819200
  104.5 1.8 %constant_dynamic-update-slice_fusion.refs_7_ = bf16[16,40,1280]{2,1,0:T(8,128)(2,1)} fusion(bf16[16,40,1280]{2,1,0:T(8,128)(2,1)} %constant_dynamic-update-slice_fusion.1, bf16[4,40,1280]{2,1,0:T(8,128)(2,1)} %collective-permute-done.18), kind=kLoop, calls=%fused_computation.3 | loop fusion | bytes 819200 | tf_op jit(solution)/shard_map/exchange_cores/concatenate | solution.py:230
  109.6 5.9 %collective-permute-done.13.refs_2_ = bf16[4,64,512]{2,1,0:T(8,128)(2,1)} collective-permute-done((bf16[4,64,512]{2,1,0:T(8,128)(2,1)}, bf16[4,64,512]{2,1,0:T(8,128)(2,1)}, u32[]{:S(2)}, u32[]{:S(2)}) %collective-permute-start.13) | collective-permute-done | bytes 262176 | tf_op jit(solution)/shard_map/coeff_part/ppermute | solution.py:176
  115.5 6.2 %conv_taps.5.refs_1_ = f32[4,64,512]{2,1,0:T(8,128)S(1)} custom-call(s32[1]{0:T(128)} %bitcast.4.idx_ref, bf16[9,16,960]{2,1,0:T(8,128)(2,1)S(1)} %pad_maximum_fusion.1.refs_0_, bf16[9,16,960]{2,1,0:T(8,128)(2,1)} %collective-permute-done.7.refs_1_, bf16[9,16,960]{2,1,0:T(8,128)(2,1)S(1)} %collective-permute-done.8.refs_2_, ...), custom_call_target="tpu_custom_call" | custom-call | tf_op jit(solution)/shard_map/conv_taps/pallas_call | solution.py:79
  122.0 6.3 %squared_sums.1 = f32[16,4,1280]{2,1,0:T(4,128)S(1)} custom-call(s32[4]{0:T(128)S(1)} %pad_add_fusion.refs_0_, f32[4,64,512]{2,1,0:T(8,128)S(1)} %conv_taps.5.refs_1_, bf16[4,64,512]{2,1,0:T(8,128)(2,1)} %collective-permute-done.13.refs_2_, bf16[4,64,512]{2,1,0:T(8,128)(2,1)} %collective-permute-done.14.refs_3_, ...), custom_call_target="tpu_custom_call" | custom-call | tf_op jit(solution)/shard_map/squared_sums/pallas_call | solution.py:155
  128.7 16.9 %all_to_all.10 = f32[64,1,1280]{2,1,0:T(1,128)S(1)} all-to-all(f32[64,1,1280]{2,1,0:T(1,128)S(1)} %reshape.29), channel_id=1, replica_groups=mesh['x'=4,'y'=4,'core'=2,'z'=4] {'x','y','z'}, dimensions={0} | all-to-all | bytes 655360 | tf_op jit(solution)/shard_map/sum_examples/all_to_all | solution.py:238
  (51 shorter events, 17.9 us)
Async XLA Ops:
  0.0 47.1 %collective-permute-start.6 = (bf16[8,320,512]{2,1,0:T(8,128)(2,1)}, bf16[8,320,512]{2,1,0:T(8,128)(2,1)}, u32[]{:S(2)}, u32[]{:S(2)}) collective-permute-start(bf16[8,320,512]{2,1,0:T(8,128)(2,1)} %bitcast.19), channel_id=1, source_target_pairs={{0,4},{4,0},{1,5},{5,1},{2,6},{6,2},{3,7},{7,3},{8,12},{12,8},{9,1... | collective-permute-start | bytes 7864328 | tf_op jit(solution)/shard_map/exchange_inputs/ppermute | solution.py:176
  1.4 8.7 %copy-start.1 = (bf16[27,320,4]{1,2,0:T(4,128)(2,1)S(1)}, bf16[27,320,4]{1,2,0:T(4,128)(2,1)}, u32[]{:S(2)}) copy-start(bf16[27,320,4]{1,2,0:T(4,128)(2,1)} %param.6) | copy-start | bytes 207364
  1.4 73.9 %copy-start = (bf16[8,512,320]{1,2,0:T(8,128)(2,1)S(1)}, bf16[8,512,320]{1,2,0:T(8,128)(2,1)}, u32[]{:S(2)}) copy-start(bf16[8,512,320]{1,2,0:T(8,128)(2,1)} %param.4) | copy-start | bytes 7864324
  1.4 92.1 %all-to-all-start = ((bf16[8,320,512]{2,1,0:T(8,128)(2,1)}), bf16[8,320,512]{2,1,0:T(8,128)(2,1)}, u32[]{:S(2)}, u32[]{:S(2)}) async-start(bf16[8,320,512]{2,1,0:T(8,128)(2,1)} %bitcast.24), calls=%async_computation | async-start | bytes 5242880 | tf_op jit(solution)/shard_map/exchange_grads/all_to_all | solution.py:198
  6.8 31.0 %collective-permute-start.5 = (bf16[40,320]{1,0:T(8,128)(2,1)S(1)}, bf16[40,320]{1,0:T(8,128)(2,1)S(1)}, u32[]{:S(2)}, u32[]{:S(2)}) collective-permute-start(bf16[40,320]{1,0:T(8,128)(2,1)S(1)} %bitcast.31), channel_id=1, source_target_pairs={{0,3},{1,0},{2,1},{3,2},{4,7},{5,4},{6,5},{7,6},{8,11},{9,8},{10,9... | collective-permute-start | bytes 76808 | tf_op jit(solution)/shard_map/basis_g_z/ppermute | solution.py:176
  10.3 36.2 %collective-permute-start.2 = (bf16[9,4,960]{2,1,0:T(4,128)(2,1)S(1)}, bf16[9,4,960]{2,1,0:T(4,128)(2,1)S(1)}, u32[]{:S(2)}, u32[]{:S(2)}) collective-permute-start(bf16[9,4,960]{2,1,0:T(4,128)(2,1)S(1)} %reshape.25), channel_id=1, source_target_pairs={{0,96},{32,0},{64,32},{96,64},{1,97},{33,1},{65,33},{97,65},{2,98}... | collective-permute-start | bytes 207368 | tf_op jit(solution)/shard_map/basis_a_x/ppermute | solution.py:176
  12.9 33.6 %collective-permute-start.1 = (bf16[9,4,960]{2,1,0:T(4,128)(2,1)S(1)}, bf16[9,4,960]{2,1,0:T(4,128)(2,1)S(1)}, u32[]{:S(2)}, u32[]{:S(2)}) collective-permute-start(bf16[9,4,960]{2,1,0:T(4,128)(2,1)S(1)} %reshape.25), channel_id=1, source_target_pairs={{0,64},{32,96},{64,0},{96,32},{1,65},{33,97},{65,1},{97,33},{2,66}... | collective-permute-start | bytes 207368 | tf_op jit(solution)/shard_map/basis_a_x/ppermute | solution.py:176
  13.4 33.1 %collective-permute-start = (bf16[9,4,960]{2,1,0:T(4,128)(2,1)S(1)}, bf16[9,4,960]{2,1,0:T(4,128)(2,1)S(1)}, u32[]{:S(2)}, u32[]{:S(2)}) collective-permute-start(bf16[9,4,960]{2,1,0:T(4,128)(2,1)S(1)} %reshape.25), channel_id=1, source_target_pairs={{0,32},{32,64},{64,96},{96,0},{1,33},{33,65},{65,97},{97,1},{2,34}... | collective-permute-start | bytes 207368 | tf_op jit(solution)/shard_map/basis_a_x/ppermute | solution.py:176
  37.8 4.7 %collective-permute-start.4 = (bf16[40,320]{1,0:T(8,128)(2,1)S(1)}, bf16[40,320]{1,0:T(8,128)(2,1)S(1)}, u32[]{:S(2)}, u32[]{:S(2)}) collective-permute-start(bf16[40,320]{1,0:T(8,128)(2,1)S(1)} %bitcast.32), channel_id=1, source_target_pairs={{0,2},{1,3},{2,0},{3,1},{4,6},{5,7},{6,4},{7,5},{8,10},{9,11},{10,... | collective-permute-start | bytes 76808 | tf_op jit(solution)/shard_map/basis_g_z/ppermute | solution.py:176
  42.5 4.0 %collective-permute-start.3 = (bf16[40,320]{1,0:T(8,128)(2,1)S(1)}, bf16[40,320]{1,0:T(8,128)(2,1)S(1)}, u32[]{:S(2)}, u32[]{:S(2)}) collective-permute-start(bf16[40,320]{1,0:T(8,128)(2,1)S(1)} %bitcast.33), channel_id=1, source_target_pairs={{0,1},{1,2},{2,3},{3,0},{4,5},{5,6},{6,7},{7,4},{8,9},{9,10},{10,1... | collective-permute-start | bytes 76808 | tf_op jit(solution)/shard_map/basis_g_z/ppermute | solution.py:176
  47.3 22.7 %collective-permute-start.9 = (bf16[9,16,960]{2,1,0:T(8,128)(2,1)S(1)}, bf16[9,16,960]{2,1,0:T(8,128)(2,1)S(1)}, u32[]{:S(2)}, u32[]{:S(2)}) collective-permute-start(bf16[9,16,960]{2,1,0:T(8,128)(2,1)S(1)} %pad_maximum_fusion.1.refs_0_), channel_id=1, source_target_pairs={{0,24},{8,0},{16,8},{24,16},{1,25},{9,1},{17,9},{25,17},{2,26},{10... | collective-permute-start | bytes 829448 | tf_op jit(solution)/shard_map/basis_a_y/ppermute | solution.py:176
  50.1 19.9 %collective-permute-start.8 = (bf16[9,16,960]{2,1,0:T(8,128)(2,1)S(1)}, bf16[9,16,960]{2,1,0:T(8,128)(2,1)S(1)}, u32[]{:S(2)}, u32[]{:S(2)}) collective-permute-start(bf16[9,16,960]{2,1,0:T(8,128)(2,1)S(1)} %pad_maximum_fusion.1.refs_0_), channel_id=1, source_target_pairs={{0,16},{8,24},{16,0},{24,8},{1,17},{9,25},{17,1},{25,9},{2,18},{10... | collective-permute-start | bytes 829448 | tf_op jit(solution)/shard_map/basis_a_y/ppermute | solution.py:176
  50.4 19.6 %collective-permute-start.7 = (bf16[9,16,960]{2,1,0:T(8,128)(2,1)S(1)}, bf16[9,16,960]{2,1,0:T(8,128)(2,1)}, u32[]{:S(2)}, u32[]{:S(2)}) collective-permute-start(bf16[9,16,960]{2,1,0:T(8,128)(2,1)S(1)} %pad_maximum_fusion.1.refs_0_), channel_id=1, source_target_pairs={{0,8},{8,16},{16,24},{24,0},{1,9},{9,17},{17,25},{25,1},{2,10},{10... | collective-permute-start | bytes 829448 | tf_op jit(solution)/shard_map/basis_a_y/ppermute | solution.py:176
  52.7 8.9 %collective-permute-start.12 = (bf16[40,1280]{1,0:T(8,128)(2,1)}, bf16[40,1280]{1,0:T(8,128)(2,1)S(1)}, u32[]{:S(2)}, u32[]{:S(2)}) collective-permute-start(bf16[40,1280]{1,0:T(8,128)(2,1)} %concatenate.10), channel_id=1, source_target_pairs={{0,24},{8,0},{16,8},{24,16},{1,25},{9,1},{17,9},{25,17},{2,26},{10... | collective-permute-start | bytes 307208 | tf_op jit(solution)/shard_map/basis_g_y/ppermute | solution.py:176
  54.7 10.6 %collective-permute-start.11 = (bf16[40,1280]{1,0:T(8,128)(2,1)}, bf16[40,1280]{1,0:T(8,128)(2,1)S(1)}, u32[]{:S(2)}, u32[]{:S(2)}) collective-permute-start(bf16[40,1280]{1,0:T(8,128)(2,1)} %concatenate.10), channel_id=1, source_target_pairs={{0,16},{8,24},{16,0},{24,8},{1,17},{9,25},{17,1},{25,9},{2,18},{10... | collective-permute-start | bytes 307208 | tf_op jit(solution)/shard_map/basis_g_y/ppermute | solution.py:176
  61.6 8.4 %collective-permute-start.10 = (bf16[40,1280]{1,0:T(8,128)(2,1)}, bf16[40,1280]{1,0:T(8,128)(2,1)S(1)}, u32[]{:S(2)}, u32[]{:S(2)}) collective-permute-start(bf16[40,1280]{1,0:T(8,128)(2,1)} %concatenate.10), channel_id=1, source_target_pairs={{0,8},{8,16},{16,24},{24,0},{1,9},{9,17},{17,25},{25,1},{2,10},{10... | collective-permute-start | bytes 307208 | tf_op jit(solution)/shard_map/basis_g_y/ppermute | solution.py:176
  71.7 21.8 %collective-permute-start.18 = (bf16[4,40,1280]{2,1,0:T(8,128)(2,1)}, bf16[4,40,1280]{2,1,0:T(8,128)(2,1)}, u32[]{:S(2)}, u32[]{:S(2)}) collective-permute-start(bf16[4,40,1280]{2,1,0:T(8,128)(2,1)} %pad_maximum_fusion), channel_id=1, source_target_pairs={{0,96},{32,0},{64,32},{96,64},{1,97},{33,1},{65,33},{97,65},{2,98}... | collective-permute-start | bytes 1228808 | tf_op jit(solution)/shard_map/basis_g_x/ppermute | solution.py:176
  74.2 19.4 %collective-permute-start.17 = (bf16[4,40,1280]{2,1,0:T(8,128)(2,1)}, bf16[4,40,1280]{2,1,0:T(8,128)(2,1)}, u32[]{:S(2)}, u32[]{:S(2)}) collective-permute-start(bf16[4,40,1280]{2,1,0:T(8,128)(2,1)} %pad_maximum_fusion), channel_id=1, source_target_pairs={{0,64},{32,96},{64,0},{96,32},{1,65},{33,97},{65,1},{97,33},{2,66}... | collective-permute-start | bytes 1228808 | tf_op jit(solution)/shard_map/basis_g_x/ppermute | solution.py:176
  74.7 20.3 %collective-permute-start.16 = (bf16[4,40,1280]{2,1,0:T(8,128)(2,1)}, bf16[4,40,1280]{2,1,0:T(8,128)(2,1)}, u32[]{:S(2)}, u32[]{:S(2)}) collective-permute-start(bf16[4,40,1280]{2,1,0:T(8,128)(2,1)} %pad_maximum_fusion), channel_id=1, source_target_pairs={{0,32},{32,64},{64,96},{96,0},{1,33},{33,65},{65,97},{97,1},{2,34}... | collective-permute-start | bytes 1228808 | tf_op jit(solution)/shard_map/basis_g_x/ppermute | solution.py:176
  95.0 27.0 %collective-permute-start.19 = (bf16[8,320,512]{2,1,0:T(8,128)(2,1)}, bf16[8,320,512]{2,1,0:T(8,128)(2,1)}, u32[]{:S(2)}, u32[]{:S(2)}) collective-permute-start(bf16[8,320,512]{2,1,0:T(8,128)(2,1)} %all-to-all-done.refs_5_), channel_id=1, source_target_pairs={{0,4},{4,0},{1,5},{5,1},{2,6},{6,2},{3,7},{7,3},{8,12},{12,8},{9,1... | collective-permute-start | bytes 7864328 | tf_op jit(solution)/shard_map/exchange_cores/ppermute | solution.py:176
  106.3 15.7 %collective-permute-start.20 = (bf16[16,40,1280]{2,1,0:T(8,128)(2,1)}, bf16[16,40,1280]{2,1,0:T(8,128)(2,1)}, u32[]{:S(2)}, u32[]{:S(2)}) collective-permute-start(bf16[16,40,1280]{2,1,0:T(8,128)(2,1)} %constant_dynamic-update-slice_fusion.refs_7_), channel_id=1, source_target_pairs={{0,4},{4,0},{1,5},{5,1},{2,6},{6,2},{3,7},{7,3},{8,12},{12,8},{9,1... | collective-permute-start | bytes 4915208 | tf_op jit(solution)/shard_map/exchange_cores/ppermute | solution.py:176
  106.3 9.2 %collective-permute-start.13 = (bf16[4,64,512]{2,1,0:T(8,128)(2,1)}, bf16[4,64,512]{2,1,0:T(8,128)(2,1)}, u32[]{:S(2)}, u32[]{:S(2)}) collective-permute-start(bf16[4,64,512]{2,1,0:T(8,128)(2,1)} %conv_taps.4), channel_id=1, source_target_pairs={{0,2},{1,3},{2,0},{3,1},{4,6},{5,7},{6,4},{7,5},{8,10},{9,11},{10,... | collective-permute-start | bytes 786440 | tf_op jit(solution)/shard_map/coeff_part/ppermute | solution.py:176
  108.1 13.7 %collective-permute-start.15 = (bf16[4,64,512]{2,1,0:T(8,128)(2,1)}, bf16[4,64,512]{2,1,0:T(8,128)(2,1)}, u32[]{:S(2)}, u32[]{:S(2)}) collective-permute-start(bf16[4,64,512]{2,1,0:T(8,128)(2,1)} %conv_taps.7), channel_id=1, source_target_pairs={{0,3},{1,0},{2,1},{3,2},{4,7},{5,4},{6,5},{7,6},{8,11},{9,8},{10,9... | collective-permute-start | bytes 786440 | tf_op jit(solution)/shard_map/coeff_part/ppermute | solution.py:176
  108.4 13.6 %collective-permute-start.14 = (bf16[4,64,512]{2,1,0:T(8,128)(2,1)}, bf16[4,64,512]{2,1,0:T(8,128)(2,1)}, u32[]{:S(2)}, u32[]{:S(2)}) collective-permute-start(bf16[4,64,512]{2,1,0:T(8,128)(2,1)} %conv_taps.6), channel_id=1, source_target_pairs={{0,1},{1,2},{2,3},{3,0},{4,5},{5,6},{6,7},{7,4},{8,9},{9,10},{10,1... | collective-permute-start | bytes 786440 | tf_op jit(solution)/shard_map/coeff_part/ppermute | solution.py:176
  (4 other events, 18.6 us)

commit v3 on v2

--- a/solution.py
+++ b/solution.py
@@ -34,87 +34,93 @@
 
 
 def conv_kernel(idx_ref, *refs):
-    *b_refs, x_ref, x_oth_ref, o_ref, b_buf, x_buf, xc_ref, o_buf, sem = refs
+    *b_refs, x_ref, x_oth_ref, o_ref, xc_ref, o_buf, sem = refs
     i, j, k = lane_coords()
     block = idx_ref[0]
     h = x_ref.shape[1]
     per = o_ref.shape[0] // 2
-    parts, rows = len(b_refs), b_refs[0].shape[1]
-    copies = [
-        pltpu.make_async_copy(ref.at[block * per + n], x_buf.at[m * per + n], sem.at[m * per + n])
-        for m, ref in enumerate((x_ref, x_oth_ref))
-        for n in range(per)
-    ]
-    loads = [pltpu.make_async_copy(ref, b_buf.at[m], sem.at[2 * per + m]) for m, ref in enumerate(b_refs)]
-    for c in copies[:1] + loads + copies[1:]:
-        c.start()
-    b, stores = None, []
+    rows = b_refs[0].shape[1]
+    zero = jnp.zeros((), x_ref.dtype)
+    b = jnp.concatenate([r[...].reshape(AB * rows, 3 * h) for r in b_refs], axis=0)
     for n in range(2 * per):
-        copies[n].wait()
-        x = x_buf[n]
-        xf = x.astype(jnp.float32)
-        xc_ref[:h] = jnp.where(k >= 1, pltpu.roll(xf, 1, 1), 0.0).astype(x.dtype)
-        xc_ref[h : 2 * h] = x
-        xc_ref[2 * h :] = jnp.where(k <= SIDE - 2, pltpu.roll(xf, POS - 1, 1), 0.0).astype(x.dtype)
-        if b is None:
-            for c in loads:
-                c.wait()
-            b = b_buf[...].reshape(parts * AB * rows, 3 * h)
-        y = jnp.dot(b, xc_ref[...], preferred_element_type=jnp.float32)
-        y = y.reshape(parts, AB, rows, POS)
+        x = (x_ref if n < per else x_oth_ref)[block * per + n % per]
+        xc_ref[n, :h] = jnp.where(k >= 1, pltpu.roll(x, 1, 1), zero)
+        xc_ref[n, h : 2 * h] = x
+        xc_ref[n, 2 * h :] = jnp.where(k <= SIDE - 2, pltpu.roll(x, POS - 1, 1), zero)
+    stores = []
+    for n in range(2 * per):
+        y = jnp.dot(b, xc_ref[n], preferred_element_type=jnp.float32)
+        y = y.reshape(len(b_refs), AB, rows, POS)
         acc = None
         for ab in range(AB):
             t = shifted(y[:, ab].reshape(-1, POS), ab, i, j)
             acc = t if acc is None else acc + t
         o_buf[n] = acc.astype(o_ref.dtype)
-        stores.append(pltpu.make_async_copy(o_buf.at[n], o_ref.at[n], sem.at[2 * per + parts + n]))
+        stores.append(pltpu.make_async_copy(o_buf.at[n], o_ref.at[n], sem.at[n]))
         stores[-1].start()
     for c in stores:
         c.wait()
 
 
 def conv(idx, blocks, x, x_oth, per, dtype):
-    rows = blocks[0].shape[1]
-    ranks = len(blocks) * rows
+    ranks = len(blocks) * blocks[0].shape[1]
     return pl.pallas_call(
         conv_kernel,
         out_shape=jax.ShapeDtypeStruct((2 * per, ranks, POS), dtype),
-        in_specs=[SMEM] + [HBM] * (len(blocks) + 2),
+        in_specs=[SMEM] + [VMEM] * (len(blocks) + 2),
         out_specs=HBM,
         scratch_shapes=[
-            pltpu.VMEM((len(blocks), *blocks[0].shape), jnp.bfloat16),
-            pltpu.VMEM((2 * per, x.shape[1], POS), jnp.bfloat16),
-            pltpu.VMEM((3 * x.shape[1], POS), jnp.bfloat16),
+            pltpu.VMEM((2 * per, 3 * x.shape[1], POS), jnp.bfloat16),
             pltpu.VMEM((2 * per, ranks, POS), dtype),
-            pltpu.SemaphoreType.DMA((4 * per + len(blocks),)),
+            pltpu.SemaphoreType.DMA((2 * per,)),
         ],
-        compiler_params=pltpu.CompilerParams(vmem_limit_bytes=40 << 20),
+        compiler_params=pltpu.CompilerParams(vmem_limit_bytes=18 << 20),
         name="conv_taps",
     )(idx, *blocks, x, x_oth)
 
 
+def merge_kernel(*refs):
+    *parts, o_ref, sem = refs
+    copies = [pltpu.make_async_copy(p, o_ref.at[i], sem.at[i]) for i, p in enumerate(parts)]
+    for c in copies:
+        c.start()
+    for c in copies:
+        c.wait()
+
+
+def merge(parts):
+    return pl.pallas_call(
+        merge_kernel,
+        out_shape=jax.ShapeDtypeStruct((len(parts), *parts[0].shape), parts[0].dtype),
+        in_specs=[HBM] * len(parts),
+        out_specs=HBM,
+        scratch_shapes=[pltpu.SemaphoreType.DMA((len(parts),))],
+        name="stack_copies",
+    )(*parts)
+
+
 def squares_kernel(idx_ref, own_ref, r1_ref, r2_ref, r3_ref, g_ref, g_oth_ref, bg_ref, bg_oth_ref, o_ref, own_buf, r_buf, g_buf, bg_buf, hi_ref, m_ref, sem, *, scale):
     x, y, core, z = idx_ref[0], idx_ref[1], idx_ref[2], idx_ref[3]
-    chips, width = bg_ref.shape[0], bg_ref.shape[1]
+    side, width = bg_ref.shape[0], bg_ref.shape[2]
     examples, ranks = own_ref.shape[0], own_ref.shape[1]
     per = examples // 2
     tensor = g_ref.shape[0] // per
-    side = 4
 
     def chip(rx, ry):
         return ((x + side - rx) % side) * side + (y + side - ry) % side
 
-    pairs = [(own_ref, own_buf), (r1_ref, r_buf.at[0]), (r2_ref, r_buf.at[1]), (r3_ref, r_buf.at[2])]
+    pairs = [(own_ref, own_buf)] + [(r, r_buf.at[i]) for i, r in enumerate((r1_ref, r2_ref, r3_ref))]
     for n in range(examples):
         src = g_ref if n < per else g_oth_ref
         for t in range(tensor):
             pairs.append((src.at[((z + tensor - t) % tensor) * per + n % per], g_buf.at[n, t]))
     late = len(pairs)
-    for b in range(chips):
-        at = chip(b // side, b % side) * 2
-        pairs.append((bg_ref.at[b], bg_buf.at[at + core]))
-        pairs.append((bg_oth_ref.at[b], bg_buf.at[at + 1 - core]))
-    copies = [pltpu.make_async_copy(a, b, sem.at[i]) for i, (a, b) in enumerate(pairs)]
+    for rx in range(side):
+        for ry in range(side):
+            at = chip(rx, ry) * 2
+            pairs.append((bg_ref.at[rx, ry], bg_buf.at[at + core]))
+            pairs.append((bg_oth_ref.at[rx, ry], bg_buf.at[at + 1 - core]))
+    copies = [pltpu.make_async_copy(p, q, sem.at[i]) for i, (p, q) in enumerate(pairs)]
     for c in copies:
         c.start()
     for c in copies[:4]:
@@ -127,26 +133,26 @@
         both = jnp.concatenate([hi, lo], axis=0)
         for c in copies[4 + n * tensor : 4 + (n + 1) * tensor]:
             c.wait()
-        g = g_buf[n].reshape(-1, POS)
-        m = lax.dot_general(both, g, NT, preferred_element_type=jnp.float32)
+        m = lax.dot_general(both, g_buf[n].reshape(-1, POS), NT, preferred_element_type=jnp.float32)
         m_ref[n * ranks : (n + 1) * ranks] = (m[:ranks] + m[ranks:]).astype(jnp.bfloat16)
     for c in copies[late:]:
         c.wait()
-    bg = bg_buf[...].reshape(2 * chips * width, bg_buf.shape[2])
+    bg = bg_buf[...].reshape(bg_buf.shape[0] * width, bg_buf.shape[2])
     prod = lax.dot_general(m_ref[...], bg, NT, preferred_element_type=jnp.float32)
     sq = None
     for n in range(examples):
         t = prod[n * ranks : (n + 1) * ranks]
         sq = t * t if sq is None else sq + t * t
     sq = sq * scale
-    low = ranks // chips
-    for b in range(chips):
+    low = ranks // (side * side)
+    for b in range(side * side):
         o_ref[chip(b % side, b // side)] = sq[b * low : (b + 1) * low]
 
 
 def squares(idx, own, received, g, g_oth, bg, bg_oth, scale):
     examples, ranks = own.shape[0], own.shape[1]
-    chips, width, hidden = bg.shape
+    side, _, width, hidden = bg.shape
+    chips = side * side
     tensor = g.shape[0] // (examples // 2)
 
     def kernel(*refs):
@@ -166,7 +172,7 @@
             pltpu.VMEM((examples * ranks, hidden), jnp.bfloat16),
             pltpu.SemaphoreType.DMA((4 + examples * tensor + 2 * chips,)),
         ],
-        compiler_params=pltpu.CompilerParams(vmem_limit_bytes=48 << 20),
+        compiler_params=pltpu.CompilerParams(vmem_limit_bytes=28 << 20),
         name="squared_sums",
     )(idx, own, *received, g, g_oth, bg, bg_oth)
 
@@ -193,15 +199,18 @@
         bg = around(basis_g.T, "z")
     with jax.named_scope("basis_a_x"):
         own = basis_a.reshape(AB, 3, channels, -1).transpose(0, 3, 1, 2)
-        ba = around(own.reshape(AB, own.shape[1], 3 * channels), "x")
+        own = own.reshape(AB, own.shape[1], 3 * channels)
+        grads, bg, own = lax.optimization_barrier((grads, bg, own))
+        ba = around(own, "x")
     with jax.named_scope("exchange_grads"):
         g = lax.all_to_all(grads, "z", 0, 0, tiled=True)
     with jax.named_scope("exchange_inputs"):
         x_oth = shift(x, "core", 1)
 
-    ba, bg, x_oth = lax.optimization_barrier((ba, bg, x_oth))
     with jax.named_scope("basis_a_y"):
-        ba = around(jnp.concatenate(ba, axis=1), "y")
+        ba = jnp.concatenate(ba, axis=1)
+        ba, bg, x_oth = lax.optimization_barrier((ba, bg, x_oth))
+        ba = around(ba, "y")
     with jax.named_scope("basis_g_y"):
         bg = around(jnp.concatenate(bg, axis=1), "y")
 
@@ -222,12 +231,12 @@
         with jax.named_scope("coeff_part"):
             parts.append(part(s, jnp.bfloat16))
             received.append(shift(parts[-1], "z", s))
-    parts.append(received[0])
+    parts.append((parts[-1], received[0]))
     mine = part(0, jnp.float32)
     with jax.named_scope("exchange_cores"):
-        g, bg, _ = lax.optimization_barrier((g, bg, parts[2]))
+        g, bg, mine = lax.optimization_barrier((g, bg, mine))
         g_oth = shift(g, "core", 1)
-        bg = jnp.concatenate(bg, axis=0)
+        bg = merge(bg)
         bg_oth = shift(bg, "core", 1)
 
     examples = here * lax.axis_size(("x", "y", "core"))

time: 149 us -> 180 us (1.21)
  Pallas kernels: 30.7 us -> 83.9 us
  waiting for transfers between devices: 50.5 us -> 29.2 us
  local copies, waits for them, and re-layouts: 10.5 us -> 12.8 us
  starting transfers between devices: 35.5 us -> 33.2 us
    pallas_call x0 -> x1, Pallas kernels: none -> 50.8 us  [merge(): pl.pallas_call(merge_kernel, out_shape=jax.ShapeDtypeStruct((len(parts),...]
    ppermute x21, waiting for transfers between devices: 50.5 us -> 29.1 us  [shift(): return lax.ppermute(v, axis, [(i, (i + s) % n) for i in range(n)])]
    unnamed x15 -> x28, local copies, waits for them, and re-layouts: 5.99 us -> 9.19 us
    pallas_call x1, Pallas kernels: 6.33 us -> 8.34 us  [squares(): pl.pallas_call(kernel, out_shape=jax.ShapeDtypeStruct((chips, ranks // ch...]
  transfers between devices with their start and end apart: 22 -> 22, of which waited for: 9 -> 9; matrix products, arithmetic and copies ran while one was open for 7% -> 3% of each run, Pallas kernels for 17% -> 42%
where the time goes in v3:
time: 180 us; the launch traced here: 178 us
  Pallas kernels  83.9 us (47%)
  starting transfers between devices  33.2 us (18%)
  waiting for transfers between devices  29.2 us (16%)
  blocking collectives  16.9 us (9%)
  local copies, waits for them, and re-layouts  12.8 us (7%)
  other arithmetic  2.19 us (1%)
    pallas_call x1, Pallas kernels, merge(): pl.pallas_call(merge_kernel, out_shape=jax.ShapeDtypeStruct((len(parts),...  50.8 us
    ppermute x21, waiting for transfers between devices, shift(): return lax.ppermute(v, axis, [(i, (i + s) % n) for i in range(n)])  29.1 us
    ppermute x21, starting transfers between devices, shift(): return lax.ppermute(v, axis, [(i, (i + s) % n) for i in range(n)])  28.5 us
    pallas_call x4, Pallas kernels, conv(): pl.pallas_call(conv_kernel, out_shape=jax.ShapeDtypeStruct((2 * per, rank...  24.8 us
    all_to_all x1, blocking collectives, body(): got = lax.all_to_all(rows, ('x', 'y', 'z'), 0, 0, tiled=True)  16.9 us
    unnamed x28, local copies, waits for them, and re-layouts  9.19 us
    pallas_call x1, Pallas kernels, squares(): pl.pallas_call(kernel, out_shape=jax.ShapeDtypeStruct((chips, ranks // ch...  8.34 us
    all_to_all x1, starting transfers between devices, body(): g = lax.all_to_all(grads, 'z', 0, 0, tiled=True)  4.67 us
  transfers between devices with their start and end apart: 22, of which 9 were waited for; matrix products, arithmetic and copies ran while one was open for 3% of the time, Pallas kernels for 42%

profile of v3, /device:TPU:1, one launch (start us, length us, event | category | flops | bytes accessed | tf_op | source)
XLA Modules:
  0.0 178.3 jit_solution(12670586079043068188)
XLA Ops:
  1.4 3.8 %collective-permute-start.2 = (bf16[40,320]{1,0:T(8,128)(2,1)}, bf16[40,320]{1,0:T(8,128)(2,1)S(1)}, u32[]{:S(2)}, u32[]{:S(2)}) collective-permute-start(bf16[40,320]{1,0:T(8,128)(2,1)} %bitcast.31), channel_id=1, source_target_pairs={{0,3},{1,0},{2,1},{3,2},{4,7},{5,4},{6,5},{7,6},{8,11},{9,8},{10,9... | collective-permute-start | bytes 76808 | tf_op jit(solution)/shard_map/basis_g_z/ppermute | solution.py:182
  7.0 2.7 %collective-permute-done.1 = bf16[40,320]{1,0:T(8,128)(2,1)S(1)} collective-permute-done((bf16[40,320]{1,0:T(8,128)(2,1)}, bf16[40,320]{1,0:T(8,128)(2,1)S(1)}, u32[]{:S(2)}, u32[]{:S(2)}) %collective-permute-start.1) | collective-permute-done | bytes 25632 | tf_op jit(solution)/shard_map/basis_g_z/ppermute | solution.py:182
  10.4 4.7 %all-to-all-start = ((bf16[8,320,512]{2,1,0:T(8,128)(2,1)}), bf16[8,320,512]{2,1,0:T(8,128)(2,1)}, u32[]{:S(2)}, u32[]{:S(2)}) async-start(bf16[8,320,512]{2,1,0:T(8,128)(2,1)} %bitcast.24), calls=%async_computation | async-start | bytes 5242880 | tf_op jit(solution)/shard_map/exchange_grads/all_to_all | solution.py:206
  15.1 2.5 %collective-permute-start.5 = (bf16[9,4,960]{2,1,0:T(4,128)(2,1)S(1)}, bf16[9,4,960]{2,1,0:T(4,128)(2,1)S(1)}, u32[]{:S(2)}, u32[]{:S(2)}) collective-permute-start(bf16[9,4,960]{2,1,0:T(4,128)(2,1)S(1)} %reshape.23), channel_id=1, source_target_pairs={{0,96},{32,0},{64,32},{96,64},{1,97},{33,1},{65,33},{97,65},{2,98}... | collective-permute-start | bytes 207368 | tf_op jit(solution)/shard_map/basis_a_x/ppermute | solution.py:182
  19.0 3.4 %collective-permute-done.4 = bf16[9,4,960]{2,1,0:T(4,128)(2,1)S(1)} collective-permute-done((bf16[9,4,960]{2,1,0:T(4,128)(2,1)S(1)}, bf16[9,4,960]{2,1,0:T(4,128)(2,1)S(1)}, u32[]{:S(2)}, u32[]{:S(2)}) %collective-permute-start.4) | collective-permute-done | bytes 69152 | tf_op jit(solution)/shard_map/basis_a_x/ppermute | solution.py:182
  23.7 2.8 %collective-permute-start.9 = (bf16[9,16,960]{2,1,0:T(8,128)(2,1)S(1)}, bf16[9,16,960]{2,1,0:T(8,128)(2,1)S(1)}, u32[]{:S(2)}, u32[]{:S(2)}) collective-permute-start(bf16[9,16,960]{2,1,0:T(8,128)(2,1)S(1)} %pad_maximum_fusion.1.refs_0_), channel_id=1, source_target_pairs={{0,24},{8,0},{16,8},{24,16},{1,25},{9,1},{17,9},{25,17},{2,26},{10... | collective-permute-start | bytes 829448 | tf_op jit(solution)/shard_map/basis_a_y/ppermute | solution.py:182
  27.6 1.5 concatenate.7
  29.1 2.0 %collective-permute-start.12 = (bf16[40,1280]{1,0:T(8,128)(2,1)}, bf16[40,1280]{1,0:T(8,128)(2,1)S(1)}, u32[]{:S(2)}, u32[]{:S(2)}) collective-permute-start(bf16[40,1280]{1,0:T(8,128)(2,1)} %concatenate.7), channel_id=1, source_target_pairs={{0,24},{8,0},{16,8},{24,16},{1,25},{9,1},{17,9},{25,17},{2,26},{10... | collective-permute-start | bytes 307208 | tf_op jit(solution)/shard_map/basis_g_y/ppermute | solution.py:182
  32.5 6.0 %collective-permute-done.12 = bf16[40,1280]{1,0:T(8,128)(2,1)S(1)} collective-permute-done((bf16[40,1280]{1,0:T(8,128)(2,1)}, bf16[40,1280]{1,0:T(8,128)(2,1)S(1)}, u32[]{:S(2)}, u32[]{:S(2)}) %collective-permute-start.12) | collective-permute-done | bytes 102432 | tf_op jit(solution)/shard_map/basis_g_y/ppermute | solution.py:182
  38.5 4.0 %collective-permute-done.11 = bf16[40,1280]{1,0:T(8,128)(2,1)S(1)} collective-permute-done((bf16[40,1280]{1,0:T(8,128)(2,1)}, bf16[40,1280]{1,0:T(8,128)(2,1)S(1)}, u32[]{:S(2)}, u32[]{:S(2)}) %collective-permute-start.11) | collective-permute-done | bytes 102432 | tf_op jit(solution)/shard_map/basis_g_y/ppermute | solution.py:182
  42.5 4.3 %collective-permute-done.10 = bf16[40,1280]{1,0:T(8,128)(2,1)S(1)} collective-permute-done((bf16[40,1280]{1,0:T(8,128)(2,1)}, bf16[40,1280]{1,0:T(8,128)(2,1)S(1)}, u32[]{:S(2)}, u32[]{:S(2)}) %collective-permute-start.10) | collective-permute-done | bytes 102432 | tf_op jit(solution)/shard_map/basis_g_y/ppermute | solution.py:182
  46.8 1.7 pad_maximum_fusion.refs_0_
  50.1 5.5 %conv_taps.4 = bf16[4,64,512]{2,1,0:T(8,128)(2,1)} custom-call(s32[1]{0:T(128)} %bitcast.16.idx_ref, bf16[9,16,960]{2,1,0:T(8,128)(2,1)S(1)} %pad_maximum_fusion.1.refs_0_, bf16[9,16,960]{2,1,0:T(8,128)(2,1)} %collective-permute-done.7.refs_1_, bf16[9,16,960]{2,1,0:T(8,128)(2,1)S(1)} %collective-permute-done.8.refs_2_, ...), custom_call_target="tpu_custom_call" | custom-call | tf_op jit(solution)/shard_map/coeff_part/conv_taps/pallas_call | solution.py:67
  55.5 3.0 %collective-permute-start.16 = (bf16[4,64,512]{2,1,0:T(8,128)(2,1)}, bf16[4,64,512]{2,1,0:T(8,128)(2,1)}, u32[]{:S(2)}, u32[]{:S(2)}) collective-permute-start(bf16[4,64,512]{2,1,0:T(8,128)(2,1)} %conv_taps.4), channel_id=1, source_target_pairs={{0,2},{1,3},{2,0},{3,1},{4,6},{5,7},{6,4},{7,5},{8,10},{9,11},{10,... | collective-permute-start | bytes 786440 | tf_op jit(solution)/shard_map/coeff_part/ppermute | solution.py:182
  58.5 6.3 %conv_taps.5 = bf16[4,64,512]{2,1,0:T(8,128)(2,1)S(1)} custom-call(s32[1]{0:T(128)} %bitcast.15.idx_ref, bf16[9,16,960]{2,1,0:T(8,128)(2,1)S(1)} %pad_maximum_fusion.1.refs_0_, bf16[9,16,960]{2,1,0:T(8,128)(2,1)} %collective-permute-done.7.refs_1_, bf16[9,16,960]{2,1,0:T(8,128)(2,1)S(1)} %collective-permute-done.8.refs_2_, ...), custom_call_target="tpu_custom_call" | custom-call | tf_op jit(solution)/shard_map/coeff_part/conv_taps/pallas_call | solution.py:67
  65.5 6.3 %conv_taps.6 = bf16[4,64,512]{2,1,0:T(8,128)(2,1)S(1)} custom-call(s32[1]{0:T(128)} %bitcast.14.idx_ref, bf16[9,16,960]{2,1,0:T(8,128)(2,1)S(1)} %pad_maximum_fusion.1.refs_0_, bf16[9,16,960]{2,1,0:T(8,128)(2,1)} %collective-permute-done.7.refs_1_, bf16[9,16,960]{2,1,0:T(8,128)(2,1)S(1)} %collective-permute-done.8.refs_2_, ...), custom_call_target="tpu_custom_call" | custom-call | tf_op jit(solution)/shard_map/coeff_part/conv_taps/pallas_call | solution.py:67
  72.6 6.7 %conv_taps.7.refs_1_ = f32[4,64,512]{2,1,0:T(8,128)S(1)} custom-call(s32[1]{0:T(128)} %bitcast.13.idx_ref, bf16[9,16,960]{2,1,0:T(8,128)(2,1)S(1)} %pad_maximum_fusion.1.refs_0_, bf16[9,16,960]{2,1,0:T(8,128)(2,1)} %collective-permute-done.7.refs_1_, bf16[9,16,960]{2,1,0:T(8,128)(2,1)S(1)} %collective-permute-done.8.refs_2_, ...), custom_call_target="tpu_custom_call" | custom-call | tf_op jit(solution)/shard_map/conv_taps/pallas_call | solution.py:67
  80.1 5.5 %collective-permute-start.19 = (bf16[8,320,512]{2,1,0:T(8,128)(2,1)}, bf16[8,320,512]{2,1,0:T(8,128)(2,1)S(1)}, u32[]{:S(2)}, u32[]{:S(2)}) collective-permute-start(bf16[8,320,512]{2,1,0:T(8,128)(2,1)} %all-to-all-done.refs_5_), channel_id=1, source_target_pairs={{0,4},{4,0},{1,5},{5,1},{2,6},{6,2},{3,7},{7,3},{8,12},{12,8},{9,1... | collective-permute-start | bytes 7864328 | tf_op jit(solution)/shard_map/exchange_cores/ppermute | solution.py:182
  85.7 50.8 %stack_copies.1.refs_7_ = bf16[4,4,40,1280]{3,2,1,0:T(8,128)(2,1)} custom-call(bf16[4,40,1280]{2,1,0:T(8,128)(2,1)} %pad_maximum_fusion.refs_0_, bf16[4,40,1280]{2,1,0:T(8,128)(2,1)} %collective-permute-done.13.refs_1_, bf16[4,40,1280]{2,1,0:T(8,128)(2,1)} %collective-permute-done.14.refs_2_, bf16[4,40,1280]{2,1,0:T(8,128)(2,1)} %collective-permute-done.15.refs_3_), custom_call_target="tpu_custom_call" | custom-call | tf_op jit(solution)/shard_map/exchange_cores/stack_copies/pallas_call | solution.py:92
  138.2 6.2 %collective-permute-done.18.refs_4_ = bf16[4,64,512]{2,1,0:T(8,128)(2,1)S(1)} collective-permute-done((bf16[4,64,512]{2,1,0:T(8,128)(2,1)}, bf16[4,64,512]{2,1,0:T(8,128)(2,1)S(1)}, u32[]{:S(2)}, u32[]{:S(2)}) %collective-permute-start.18) | collective-permute-done | bytes 262176 | tf_op jit(solution)/shard_map/coeff_part/ppermute | solution.py:182
  146.2 1.5 copy-done.2
  149.1 1.7 copy-done.3
  151.8 8.3 %squared_sums.1 = f32[16,4,1280]{2,1,0:T(4,128)S(1)} custom-call(s32[4]{0:T(128)S(1)} %pad_add_fusion.refs_0_, f32[4,64,512]{2,1,0:T(8,128)S(1)} %copy-done.5, bf16[4,64,512]{2,1,0:T(8,128)(2,1)} %collective-permute-done.16.refs_2_, bf16[4,64,512]{2,1,0:T(8,128)(2,1)} %collective-permute-done.17.refs_3_, bf16[4,64,512]{2,1,0:T(8,128)(2,1)S(1)} %copy-done.7, ...), custom_call_target="tpu_custom_call" | custom-call | tf_op jit(solution)/shard_map/squared_sums/pallas_call | solution.py:161
  160.6 16.9 %all_to_all.10 = f32[64,1,1280]{2,1,0:T(1,128)S(1)} all-to-all(f32[64,1,1280]{2,1,0:T(1,128)S(1)} %reshape.29), channel_id=1, replica_groups=mesh['x'=4,'y'=4,'core'=2,'z'=4] {'x','y','z'}, dimensions={0} | all-to-all | bytes 655360 | tf_op jit(solution)/shard_map/sum_examples/all_to_all | solution.py:247
  (64 shorter events, 19.8 us)
Async XLA Ops:
  0.0 23.7 %collective-permute-start.6 = (bf16[8,320,512]{2,1,0:T(8,128)(2,1)}, bf16[8,320,512]{2,1,0:T(8,128)(2,1)}, u32[]{:S(2)}, u32[]{:S(2)}) collective-permute-start(bf16[8,320,512]{2,1,0:T(8,128)(2,1)} %bitcast.19), channel_id=1, source_target_pairs={{0,4},{4,0},{1,5},{5,1},{2,6},{6,2},{3,7},{7,3},{8,12},{12,8},{9,1... | collective-permute-start | bytes 7864328 | tf_op jit(solution)/shard_map/exchange_inputs/ppermute | solution.py:182
  1.4 5.6 %collective-permute-start.2 = (bf16[40,320]{1,0:T(8,128)(2,1)}, bf16[40,320]{1,0:T(8,128)(2,1)S(1)}, u32[]{:S(2)}, u32[]{:S(2)}) collective-permute-start(bf16[40,320]{1,0:T(8,128)(2,1)} %bitcast.31), channel_id=1, source_target_pairs={{0,3},{1,0},{2,1},{3,2},{4,7},{5,4},{6,5},{7,6},{8,11},{9,8},{10,9... | collective-permute-start | bytes 76808 | tf_op jit(solution)/shard_map/basis_g_z/ppermute | solution.py:182
  5.3 4.5 %collective-permute-start.1 = (bf16[40,320]{1,0:T(8,128)(2,1)}, bf16[40,320]{1,0:T(8,128)(2,1)S(1)}, u32[]{:S(2)}, u32[]{:S(2)}) collective-permute-start(bf16[40,320]{1,0:T(8,128)(2,1)} %bitcast.32), channel_id=1, source_target_pairs={{0,2},{1,3},{2,0},{3,1},{4,6},{5,7},{6,4},{7,5},{8,10},{9,11},{10,... | collective-permute-start | bytes 76808 | tf_op jit(solution)/shard_map/basis_g_z/ppermute | solution.py:182
  5.3 4.5 %collective-permute-start = (bf16[40,320]{1,0:T(8,128)(2,1)}, bf16[40,320]{1,0:T(8,128)(2,1)S(1)}, u32[]{:S(2)}, u32[]{:S(2)}) collective-permute-start(bf16[40,320]{1,0:T(8,128)(2,1)} %bitcast.33), channel_id=1, source_target_pairs={{0,1},{1,2},{2,3},{3,0},{4,5},{5,6},{6,7},{7,4},{8,9},{9,10},{10,1... | collective-permute-start | bytes 76808 | tf_op jit(solution)/shard_map/basis_g_z/ppermute | solution.py:182
  9.8 40.3 %copy-start = (bf16[8,512,320]{1,2,0:T(8,128)(2,1)S(1)}, bf16[8,512,320]{1,2,0:T(8,128)(2,1)}, u32[]{:S(2)}) copy-start(bf16[8,512,320]{1,2,0:T(8,128)(2,1)} %param.4) | copy-start | bytes 7864324
  10.4 69.7 %all-to-all-start = ((bf16[8,320,512]{2,1,0:T(8,128)(2,1)}), bf16[8,320,512]{2,1,0:T(8,128)(2,1)}, u32[]{:S(2)}, u32[]{:S(2)}) async-start(bf16[8,320,512]{2,1,0:T(8,128)(2,1)} %bitcast.24), calls=%async_computation | async-start | bytes 5242880 | tf_op jit(solution)/shard_map/exchange_grads/all_to_all | solution.py:206
  15.1 4.0 %collective-permute-start.5 = (bf16[9,4,960]{2,1,0:T(4,128)(2,1)S(1)}, bf16[9,4,960]{2,1,0:T(4,128)(2,1)S(1)}, u32[]{:S(2)}, u32[]{:S(2)}) collective-permute-start(bf16[9,4,960]{2,1,0:T(4,128)(2,1)S(1)} %reshape.23), channel_id=1, source_target_pairs={{0,96},{32,0},{64,32},{96,64},{1,97},{33,1},{65,33},{97,65},{2,98}... | collective-permute-start | bytes 207368 | tf_op jit(solution)/shard_map/basis_a_x/ppermute | solution.py:182
  17.6 4.8 %collective-permute-start.4 = (bf16[9,4,960]{2,1,0:T(4,128)(2,1)S(1)}, bf16[9,4,960]{2,1,0:T(4,128)(2,1)S(1)}, u32[]{:S(2)}, u32[]{:S(2)}) collective-permute-start(bf16[9,4,960]{2,1,0:T(4,128)(2,1)S(1)} %reshape.23), channel_id=1, source_target_pairs={{0,64},{32,96},{64,0},{96,32},{1,65},{33,97},{65,1},{97,33},{2,66}... | collective-permute-start | bytes 207368 | tf_op jit(solution)/shard_map/basis_a_x/ppermute | solution.py:182
  18.1 5.4 %collective-permute-start.3 = (bf16[9,4,960]{2,1,0:T(4,128)(2,1)S(1)}, bf16[9,4,960]{2,1,0:T(4,128)(2,1)S(1)}, u32[]{:S(2)}, u32[]{:S(2)}) collective-permute-start(bf16[9,4,960]{2,1,0:T(4,128)(2,1)S(1)} %reshape.23), channel_id=1, source_target_pairs={{0,32},{32,64},{64,96},{96,0},{1,33},{33,65},{65,97},{97,1},{2,34}... | collective-permute-start | bytes 207368 | tf_op jit(solution)/shard_map/basis_a_x/ppermute | solution.py:182
  23.7 23.1 %collective-permute-start.9 = (bf16[9,16,960]{2,1,0:T(8,128)(2,1)S(1)}, bf16[9,16,960]{2,1,0:T(8,128)(2,1)S(1)}, u32[]{:S(2)}, u32[]{:S(2)}) collective-permute-start(bf16[9,16,960]{2,1,0:T(8,128)(2,1)S(1)} %pad_maximum_fusion.1.refs_0_), channel_id=1, source_target_pairs={{0,24},{8,0},{16,8},{24,16},{1,25},{9,1},{17,9},{25,17},{2,26},{10... | collective-permute-start | bytes 829448 | tf_op jit(solution)/shard_map/basis_a_y/ppermute | solution.py:182
  26.5 20.3 %collective-permute-start.8 = (bf16[9,16,960]{2,1,0:T(8,128)(2,1)S(1)}, bf16[9,16,960]{2,1,0:T(8,128)(2,1)S(1)}, u32[]{:S(2)}, u32[]{:S(2)}) collective-permute-start(bf16[9,16,960]{2,1,0:T(8,128)(2,1)S(1)} %pad_maximum_fusion.1.refs_0_), channel_id=1, source_target_pairs={{0,16},{8,24},{16,0},{24,8},{1,17},{9,25},{17,1},{25,9},{2,18},{10... | collective-permute-start | bytes 829448 | tf_op jit(solution)/shard_map/basis_a_y/ppermute | solution.py:182
  26.9 20.0 %collective-permute-start.7 = (bf16[9,16,960]{2,1,0:T(8,128)(2,1)S(1)}, bf16[9,16,960]{2,1,0:T(8,128)(2,1)}, u32[]{:S(2)}, u32[]{:S(2)}) collective-permute-start(bf16[9,16,960]{2,1,0:T(8,128)(2,1)S(1)} %pad_maximum_fusion.1.refs_0_), channel_id=1, source_target_pairs={{0,8},{8,16},{16,24},{24,0},{1,9},{9,17},{17,25},{25,1},{2,10},{10... | collective-permute-start | bytes 829448 | tf_op jit(solution)/shard_map/basis_a_y/ppermute | solution.py:182
  29.1 9.4 %collective-permute-start.12 = (bf16[40,1280]{1,0:T(8,128)(2,1)}, bf16[40,1280]{1,0:T(8,128)(2,1)S(1)}, u32[]{:S(2)}, u32[]{:S(2)}) collective-permute-start(bf16[40,1280]{1,0:T(8,128)(2,1)} %concatenate.7), channel_id=1, source_target_pairs={{0,24},{8,0},{16,8},{24,16},{1,25},{9,1},{17,9},{25,17},{2,26},{10... | collective-permute-start | bytes 307208 | tf_op jit(solution)/shard_map/basis_g_y/ppermute | solution.py:182
  31.1 11.4 %collective-permute-start.11 = (bf16[40,1280]{1,0:T(8,128)(2,1)}, bf16[40,1280]{1,0:T(8,128)(2,1)S(1)}, u32[]{:S(2)}, u32[]{:S(2)}) collective-permute-start(bf16[40,1280]{1,0:T(8,128)(2,1)} %concatenate.7), channel_id=1, source_target_pairs={{0,16},{8,24},{16,0},{24,8},{1,17},{9,25},{17,1},{25,9},{2,18},{10... | collective-permute-start | bytes 307208 | tf_op jit(solution)/shard_map/basis_g_y/ppermute | solution.py:182
  38.5 8.4 %collective-permute-start.10 = (bf16[40,1280]{1,0:T(8,128)(2,1)}, bf16[40,1280]{1,0:T(8,128)(2,1)S(1)}, u32[]{:S(2)}, u32[]{:S(2)}) collective-permute-start(bf16[40,1280]{1,0:T(8,128)(2,1)} %concatenate.7), channel_id=1, source_target_pairs={{0,8},{8,16},{16,24},{24,0},{1,9},{9,17},{17,25},{25,1},{2,10},{10... | collective-permute-start | bytes 307208 | tf_op jit(solution)/shard_map/basis_g_y/ppermute | solution.py:182
  48.5 31.6 %collective-permute-start.15 = (bf16[4,40,1280]{2,1,0:T(8,128)(2,1)}, bf16[4,40,1280]{2,1,0:T(8,128)(2,1)}, u32[]{:S(2)}, u32[]{:S(2)}) collective-permute-start(bf16[4,40,1280]{2,1,0:T(8,128)(2,1)} %pad_maximum_fusion.refs_0_), channel_id=1, source_target_pairs={{0,96},{32,0},{64,32},{96,64},{1,97},{33,1},{65,33},{97,65},{2,98}... | collective-permute-start | bytes 1228808 | tf_op jit(solution)/shard_map/basis_g_x/ppermute | solution.py:182
  48.8 31.3 %collective-permute-start.14 = (bf16[4,40,1280]{2,1,0:T(8,128)(2,1)}, bf16[4,40,1280]{2,1,0:T(8,128)(2,1)}, u32[]{:S(2)}, u32[]{:S(2)}) collective-permute-start(bf16[4,40,1280]{2,1,0:T(8,128)(2,1)} %pad_maximum_fusion.refs_0_), channel_id=1, source_target_pairs={{0,64},{32,96},{64,0},{96,32},{1,65},{33,97},{65,1},{97,33},{2,66}... | collective-permute-start | bytes 1228808 | tf_op jit(solution)/shard_map/basis_g_x/ppermute | solution.py:182
  49.3 30.8 %collective-permute-start.13 = (bf16[4,40,1280]{2,1,0:T(8,128)(2,1)}, bf16[4,40,1280]{2,1,0:T(8,128)(2,1)}, u32[]{:S(2)}, u32[]{:S(2)}) collective-permute-start(bf16[4,40,1280]{2,1,0:T(8,128)(2,1)} %pad_maximum_fusion.refs_0_), channel_id=1, source_target_pairs={{0,32},{32,64},{64,96},{96,0},{1,33},{33,65},{65,97},{97,1},{2,34}... | collective-permute-start | bytes 1228808 | tf_op jit(solution)/shard_map/basis_g_x/ppermute | solution.py:182
  55.5 17.0 %collective-permute-start.16 = (bf16[4,64,512]{2,1,0:T(8,128)(2,1)}, bf16[4,64,512]{2,1,0:T(8,128)(2,1)}, u32[]{:S(2)}, u32[]{:S(2)}) collective-permute-start(bf16[4,64,512]{2,1,0:T(8,128)(2,1)} %conv_taps.4), channel_id=1, source_target_pairs={{0,2},{1,3},{2,0},{3,1},{4,6},{5,7},{6,4},{7,5},{8,10},{9,11},{10,... | collective-permute-start | bytes 786440 | tf_op jit(solution)/shard_map/coeff_part/ppermute | solution.py:182
  80.1 67.6 %copy-start.5 = (f32[4,64,512]{2,1,0:T(8,128)S(1)}, f32[4,64,512]{2,1,0:T(8,128)}, u32[]{:S(2)}) copy-start(f32[4,64,512]{2,1,0:T(8,128)} %copy-done.4) | copy-start | bytes 1572868
  80.1 66.0 %collective-permute-start.19 = (bf16[8,320,512]{2,1,0:T(8,128)(2,1)}, bf16[8,320,512]{2,1,0:T(8,128)(2,1)S(1)}, u32[]{:S(2)}, u32[]{:S(2)}) collective-permute-start(bf16[8,320,512]{2,1,0:T(8,128)(2,1)} %all-to-all-done.refs_5_), channel_id=1, source_target_pairs={{0,4},{4,0},{1,5},{5,1},{2,6},{6,2},{3,7},{7,3},{8,12},{12,8},{9,1... | collective-permute-start | bytes 7864328 | tf_op jit(solution)/shard_map/exchange_cores/ppermute | solution.py:182
  136.5 9.7 %collective-permute-start.20 = (bf16[4,4,40,1280]{3,2,1,0:T(8,128)(2,1)}, bf16[4,4,40,1280]{3,2,1,0:T(8,128)(2,1)}, u32[]{:S(2)}, u32[]{:S(2)}) collective-permute-start(bf16[4,4,40,1280]{3,2,1,0:T(8,128)(2,1)} %stack_copies.1.refs_7_), channel_id=1, source_target_pairs={{0,4},{4,0},{1,5},{5,1},{2,6},{6,2},{3,7},{7,3},{8,12},{12,8},{9,1... | collective-permute-start | bytes 4915208 | tf_op jit(solution)/shard_map/exchange_cores/ppermute | solution.py:182
  136.5 7.8 %collective-permute-start.18 = (bf16[4,64,512]{2,1,0:T(8,128)(2,1)}, bf16[4,64,512]{2,1,0:T(8,128)(2,1)S(1)}, u32[]{:S(2)}, u32[]{:S(2)}) collective-permute-start(bf16[4,64,512]{2,1,0:T(8,128)(2,1)} %copy-done.9), channel_id=1, source_target_pairs={{0,3},{1,0},{2,1},{3,2},{4,7},{5,4},{6,5},{7,6},{8,11},{9,8},{10,9... | collective-permute-start | bytes 786440 | tf_op jit(solution)/shard_map/coeff_part/ppermute | solution.py:182
  137.5 8.7 %collective-permute-start.17 = (bf16[4,64,512]{2,1,0:T(8,128)(2,1)}, bf16[4,64,512]{2,1,0:T(8,128)(2,1)}, u32[]{:S(2)}, u32[]{:S(2)}) collective-permute-start(bf16[4,64,512]{2,1,0:T(8,128)(2,1)} %copy-done.8), channel_id=1, source_target_pairs={{0,1},{1,2},{2,3},{3,0},{4,5},{5,6},{6,7},{7,4},{8,9},{9,10},{10,1... | collective-permute-start | bytes 786440 | tf_op jit(solution)/shard_map/coeff_part/ppermute | solution.py:182
  (12 other events, 30.4 us)

commit v4 on v3

v4 whole, which is shorter than its diff:
```python
import jax
import jax.numpy as jnp
from jax import lax
from jax.experimental import pallas as pl
from jax.experimental.pallas import tpu as pltpu
from jax.sharding import Mesh, PartitionSpec as P

SIDE = 8
POS = SIDE * SIDE * SIDE
AB = 9
ALL = ("x", "y", "core", "z")
NT = (((1,), (1,)), ((), ()))
VMEM = pl.BlockSpec(memory_space=pltpu.VMEM)
SMEM = pl.BlockSpec(memory_space=pltpu.SMEM)
ANY = pl.BlockSpec(memory_space=pl.ANY)


def lane_coords():
    p = lax.broadcasted_iota(jnp.int32, (1, POS), 1)
    return p // 64, (p // 8) % 8, p % 8


def shifted(y, ab, i, j):
    a, b = ab // 3 - 1, ab % 3 - 1
    s = a * 64 + b * 8
    if s == 0:
        return y
    ok = None
    for v, o in ((i, a), (j, b)):
        if o != 0:
            m = (v + o >= 0) & (v + o < SIDE)
            ok = m if ok is None else ok & m
    return jnp.where(ok, pltpu.roll(y, (-s) % POS, 1), 0.0)


def conv_kernel(idx_ref, *refs, outs):
    b_refs, (x_ref, x_oth_ref), o_refs = refs[:-6 - outs], refs[-6 - outs : -4 - outs], refs[-4 - outs : -4]
    b_buf, x_buf, xc_ref, sem = refs[-4:]
    i, j, k = lane_coords()
    h = x_ref.shape[1]
    per = o_refs[0].shape[0] // 2
    parts, rows = len(b_refs), b_refs[0].shape[1]
    zero = jnp.zeros((), x_ref.dtype)
    pairs = [(r, b_buf.at[m]) for m, r in enumerate(b_refs)]
    for o in range(outs):
        for m, ref in enumerate((x_ref, x_oth_ref)):
            for n in range(per):
                pairs.append((ref.at[idx_ref[o] * per + n], x_buf.at[(2 * o + m) * per + n]))
    copies = [pltpu.make_async_copy(p, q, sem.at[t]) for t, (p, q) in enumerate(pairs)]
    for c in copies:
        c.start()
    b = None
    for n in range(2 * per * outs):
        copies[parts + n].wait()
        x = x_buf[n]
        xc_ref[n % 2, :h] = jnp.where(k >= 1, pltpu.roll(x, 1, 1), zero)
        xc_ref[n % 2, h : 2 * h] = x
        xc_ref[n % 2, 2 * h :] = jnp.where(k <= SIDE - 2, pltpu.roll(x, POS - 1, 1), zero)
        if b is None:
            for c in copies[:parts]:
                c.wait()
            b = b_buf[...].reshape(parts * AB * rows, 3 * h)
        y = jnp.dot(b, xc_ref[n % 2], preferred_element_type=jnp.float32)
        y = y.reshape(parts, AB, rows, POS)
        acc = None
        for ab in range(AB):
            t = shifted(y[:, ab].reshape(-1, POS), ab, i, j)
            acc = t if acc is None else acc + t
        o_ref = o_refs[n // (2 * per)]
        o_ref[n % (2 * per)] = acc.astype(o_ref.dtype)


def conv(idx, blocks, x, x_oth, per, dtypes):
    ranks = len(blocks) * blocks[0].shape[1]
    outs = len(dtypes)
    examples = 2 * per * outs

    def kernel(*refs):
        conv_kernel(*refs, outs=outs)

    return pl.pallas_call(
        kernel,
        out_shape=[jax.ShapeDtypeStruct((2 * per, ranks, POS), d) for d in dtypes],
        in_specs=[SMEM] + [ANY] * (len(blocks) + 2),
        out_specs=[VMEM] * outs,
        scratch_shapes=[
            pltpu.VMEM((len(blocks), *blocks[0].shape), jnp.bfloat16),
            pltpu.VMEM((examples, *x.shape[1:]), jnp.bfloat16),
            pltpu.VMEM((2, 3 * x.shape[1], POS), jnp.bfloat16),
            pltpu.SemaphoreType.DMA((len(blocks) + examples,)),
        ],
        compiler_params=pltpu.CompilerParams(vmem_limit_bytes=48 << 20),
        name="conv_taps",
    )(idx, *blocks, x, x_oth)


def squares_kernel(idx_ref, own_ref, r1_ref, r2_ref, r3_ref, g_ref, g_oth_ref, *refs, scale):
    *bg_refs, o_ref, own_buf, r_buf, g_buf, bg_buf, hi_ref, m_ref, sem = refs
    x, y, core, z = idx_ref[0], idx_ref[1], idx_ref[2], idx_ref[3]
    side, width = len(bg_refs) // 2, bg_refs[0].shape[1]
    examples, ranks = own_ref.shape[0], own_ref.shape[1]
    per = examples // 2
    tensor = g_ref.shape[0] // per

    def chip(rx, ry):
        return ((x + side - rx) % side) * side + (y + side - ry) % side

    pairs = [(own_ref, own_buf)] + [(r, r_buf.at[i]) for i, r in enumerate((r1_ref, r2_ref, r3_ref))]
    for n in range(examples):
        src = g_ref if n < per else g_oth_ref
        for t in range(tensor):
            pairs.append((src.at[((z + tensor - t) % tensor) * per + n % per], g_buf.at[n, t]))
    late = len(pairs)
    for rx in range(side):
        for ry in range(side):
            at = chip(rx, ry) * 2
            pairs.append((bg_refs[ry].at[rx], bg_buf.at[at + core]))
            pairs.append((bg_refs[side + ry].at[rx], bg_buf.at[at + 1 - core]))
    copies = [pltpu.make_async_copy(p, q, sem.at[i]) for i, (p, q) in enumerate(pairs)]
    for c in copies:
        c.start()
    for c in copies[:4]:
        c.wait()
    for n in range(examples):
        c = own_buf[n] + r_buf[0, n].astype(jnp.float32) + r_buf[1, n].astype(jnp.float32) + r_buf[2, n].astype(jnp.float32)
        hi_ref[n] = c.astype(jnp.bfloat16)
        hi = hi_ref[n]
        lo = (c - hi.astype(jnp.float32)).astype(jnp.bfloat16)
        both = jnp.concatenate([hi, lo], axis=0)
        for c in copies[4 + n * tensor : 4 + (n + 1) * tensor]:
            c.wait()
        m = lax.dot_general(both, g_buf[n].reshape(-1, POS), NT, preferred_element_type=jnp.float32)
        m_ref[n * ranks : (n + 1) * ranks] = (m[:ranks] + m[ranks:]).astype(jnp.bfloat16)
    for c in copies[late:]:
        c.wait()
    bg = bg_buf[...].reshape(bg_buf.shape[0] * width, bg_buf.shape[2])
    prod = lax.dot_general(m_ref[...], bg, NT, preferred_element_type=jnp.float32)
    sq = None
    for n in range(examples):
        t = prod[n * ranks : (n + 1) * ranks]
        sq = t * t if sq is None else sq + t * t
    sq = sq * scale
    low = ranks // (side * side)
    for b in range(side * side):
        o_ref[chip(b % side, b // side)] = sq[b * low : (b + 1) * low]


def squares(idx, own, received, g, g_oth, bg, bg_oth, scale):
    examples, ranks = own.shape[0], own.shape[1]
    side, width, hidden = bg[0].shape
    chips = side * side
    tensor = g.shape[0] // (examples // 2)

    def kernel(*refs):
        squares_kernel(*refs, scale=scale)

    return pl.pallas_call(
        kernel,
        out_shape=jax.ShapeDtypeStruct((chips, ranks // chips, 2 * chips * width), jnp.float32),
        in_specs=[SMEM] + [ANY] * (6 + 2 * side),
        out_specs=VMEM,
        scratch_shapes=[
            pltpu.VMEM(own.shape, jnp.float32),
            pltpu.VMEM((3, *own.shape), jnp.bfloat16),
            pltpu.VMEM((examples, tensor, *g.shape[1:]), jnp.bfloat16),
            pltpu.VMEM((2 * chips, width, hidden), jnp.bfloat16),
            pltpu.VMEM((examples, ranks, POS), jnp.bfloat16),
            pltpu.VMEM((examples * ranks, hidden), jnp.bfloat16),
            pltpu.SemaphoreType.DMA((4 + examples * tensor + 2 * chips,)),
        ],
        compiler_params=pltpu.CompilerParams(vmem_limit_bytes=48 << 20),
        name="squared_sums",
    )(idx, own, *received, g, g_oth, *bg, *bg_oth)


def shift(v, axis, s):
    n = lax.axis_size(axis)
    return lax.ppermute(v, axis, [(i, (i + s) % n) for i in range(n)])


def around(v, axis):
    return [v] + [shift(v, axis, s) for s in range(1, lax.axis_size(axis))]


def body(patch_rows, out_grads, basis_a, basis_g):
    coords = [lax.axis_index(a).astype(jnp.int32) for a in ALL]
    z = coords[3]
    x = patch_rows.transpose(0, 2, 1)
    grads = out_grads.transpose(0, 2, 1)
    here, channels = x.shape[0], x.shape[1]
    tensor = lax.axis_size("z")
    per = here // tensor

    with jax.named_scope("basis_a_x"):
        own = basis_a.reshape(AB, 3, channels, -1).transpose(0, 3, 1, 2)
        own = own.reshape(AB, own.shape[1], 3 * channels)
        ba = around(own, "x")
    with jax.named_scope("basis_g_z"):
        bg, _ = lax.optimization_barrier((basis_g.T, own))
        bg = around(bg, "z")
    with jax.named_scope("exchange_grads"):
        grads, bg, ba = lax.optimization_barrier((grads, bg, ba))
        g = lax.all_to_all(grads, "z", 0, 0, tiled=True)
    with jax.named_scope("basis_a_y"):
        ba = jnp.concatenate(ba, axis=1)
        bg, give, _ = lax.optimization_barrier((bg, x, ba))
        x_oth = shift(give, "core", 1)
        ba = around(ba, "y")
    with jax.named_scope("basis_g_x"):
        bg = around(jnp.concatenate(bg, axis=1), "x")

    def parts(shifts, dtypes, after=None):
        idx = jnp.stack([(z + s) % tensor for s in shifts])
        if after is not None:
            idx, _ = lax.optimization_barrier((idx, after))
        return conv(idx, ba, x, x_oth, per, dtypes)

    ba, bg = lax.optimization_barrier((ba, bg))
    with jax.named_scope("basis_g_y"):
        bg = around(jnp.stack(bg), "y")
    with jax.named_scope("coeff_parts"):
        far, near = parts((2, 1), (jnp.bfloat16, jnp.bfloat16))
        received = [shift(far, "z", 2), shift(near, "z", 1)]
        last, mine = parts((3, 0), (jnp.bfloat16, jnp.float32), far)
    with jax.named_scope("exchange_cores"):
        g, bg, received, mine = lax.optimization_barrier((g, bg, received, mine))
        g_oth = shift(g, "core", 1)
        bg_oth = [shift(v, "core", 1) for v in bg]
    received.append(shift(last, "z", 3))

    examples = here * lax.axis_size(("x", "y", "core"))
    total = squares(jnp.stack(coords), mine, received, g, g_oth, bg, bg_oth, 1.0 / examples)

    with jax.named_scope("sum_examples"):
        rows = total.reshape(-1, 1, total.shape[2])
        got = lax.all_to_all(rows, ("x", "y", "z"), 0, 0, tiled=True)
        return jnp.sum(got, axis=0)


def solution(mesh):
    tensor = mesh.shape["tensor"]
    fine = Mesh(mesh.devices.reshape(4, -1, 2, tensor), ALL)
    dp = ("x", "y", "core")
    in_specs = (P(dp, None, "z"), P(dp, None, "z"), P(None, "z", dp), P("z", dp))
    return jax.shard_map(body, mesh=fine, in_specs=in_specs, out_specs=P(ALL, None), check_vma=False)
```

time: 180 us -> 122 us (0.68)
  Pallas kernels: 83.9 us -> 28.9 us
  waiting for transfers between devices: 29.2 us -> 26.1 us
    pallas_call x5 -> x2, Pallas kernels: 75.6 us -> 20.7 us  [conv(): pl.pallas_call(kernel, out_shape=[jax.ShapeDtypeStruct((2 * per, ranks, P...]
    ppermute x21 -> x24, waiting for transfers between devices: 29.1 us -> 26.1 us  [shift(): return lax.ppermute(v, axis, [(i, (i + s) % n) for i in range(n)])]
    ppermute x21 -> x24, starting transfers between devices: 28.5 us -> 30 us  [shift(): return lax.ppermute(v, axis, [(i, (i + s) % n) for i in range(n)])]
  transfers between devices with their start and end apart: 22 -> 25, of which waited for: 9 -> 9; matrix products, arithmetic and copies ran while one was open for 3% -> 0% of each run, Pallas kernels for 42% -> 17%
where the time goes in v4:
time: 122 us
  starting transfers between devices  34.5 us (28%)
  Pallas kernels  28.9 us (24%)
  waiting for transfers between devices  26.1 us (21%)
  blocking collectives  18.5 us (15%)
  local copies, waits for them, and re-layouts  12.7 us (10%)
    ppermute x24, starting transfers between devices, shift(): return lax.ppermute(v, axis, [(i, (i + s) % n) for i in range(n)])  30 us
    ppermute x24, waiting for transfers between devices, shift(): return lax.ppermute(v, axis, [(i, (i + s) % n) for i in range(n)])  26.1 us
    pallas_call x2, Pallas kernels, conv(): pl.pallas_call(kernel, out_shape=[jax.ShapeDtypeStruct((2 * per, ranks, P...  20.7 us
    all_to_all x1, blocking collectives, body(): got = lax.all_to_all(rows, ('x', 'y', 'z'), 0, 0, tiled=True)  18.5 us
    unnamed x28, local copies, waits for them, and re-layouts  10.5 us
    pallas_call x1, Pallas kernels, squares(): pl.pallas_call(kernel, out_shape=jax.ShapeDtypeStruct((chips, ranks // ch...  8.16 us
    all_to_all x1, starting transfers between devices, body(): g = lax.all_to_all(grads, 'z', 0, 0, tiled=True)  4.56 us
  transfers between devices with their start and end apart: 25, of which 9 were waited for; matrix products, arithmetic and copies ran while one was open for 0% of the time, Pallas kernels for 17%

profile of v4, /device:TPU:1, one launch (start us, length us, event | category | flops | bytes accessed | tf_op | source)
XLA Modules:
  0.0 121.5 jit_solution(13880463970979608898)
XLA Ops:
  1.0 3.4 %collective-permute-start.5 = (bf16[9,4,960]{2,1,0:T(4,128)(2,1)S(1)}, bf16[9,4,960]{2,1,0:T(4,128)(2,1)S(1)}, u32[]{:S(2)}, u32[]{:S(2)}) collective-permute-start(bf16[9,4,960]{2,1,0:T(4,128)(2,1)S(1)} %reshape.11), channel_id=1, source_target_pairs={{0,96},{32,0},{64,32},{96,64},{1,97},{33,1},{65,33},{97,65},{2,98}... | collective-permute-start | bytes 207368 | tf_op jit(solution)/shard_map/basis_a_x/ppermute | solution.py:178
  5.6 3.8 %collective-permute-start.2 = (bf16[40,320]{1,0:T(8,128)(2,1)}, bf16[40,320]{1,0:T(8,128)(2,1)S(1)}, u32[]{:S(2)}, u32[]{:S(2)}) collective-permute-start(bf16[40,320]{1,0:T(8,128)(2,1)} %bitcast.29), channel_id=1, source_target_pairs={{0,3},{1,0},{2,1},{3,2},{4,7},{5,4},{6,5},{7,6},{8,11},{9,8},{10,9... | collective-permute-start | bytes 76808 | tf_op jit(solution)/shard_map/basis_g_z/ppermute | solution.py:178
  9.3 1.2 collective-permute-done.2
  10.5 3.2 %collective-permute-done.1 = bf16[40,320]{1,0:T(8,128)(2,1)S(1)} collective-permute-done((bf16[40,320]{1,0:T(8,128)(2,1)}, bf16[40,320]{1,0:T(8,128)(2,1)S(1)}, u32[]{:S(2)}, u32[]{:S(2)}) %collective-permute-start.1) | collective-permute-done | bytes 25632 | tf_op jit(solution)/shard_map/basis_g_z/ppermute | solution.py:178
  13.8 1.2 collective-permute-done
  15.2 3.6 %collective-permute-start.15 = (bf16[8,320,512]{2,1,0:T(8,128)(2,1)}, bf16[8,320,512]{2,1,0:T(8,128)(2,1)}, u32[]{:S(2)}, u32[]{:S(2)}) collective-permute-start(bf16[8,320,512]{2,1,0:T(8,128)(2,1)} %bitcast.19), channel_id=1, source_target_pairs={{0,4},{4,0},{1,5},{5,1},{2,6},{6,2},{3,7},{7,3},{8,12},{12,8},{9,1... | collective-permute-start | bytes 7864328 | tf_op jit(solution)/shard_map/basis_a_y/ppermute | solution.py:178
  18.8 4.6 %all-to-all-start = ((bf16[8,320,512]{2,1,0:T(8,128)(2,1)}), bf16[8,320,512]{2,1,0:T(8,128)(2,1)}, u32[]{:S(2)}, u32[]{:S(2)}) async-start(bf16[8,320,512]{2,1,0:T(8,128)(2,1)} %bitcast.22), calls=%async_computation | async-start | bytes 5242880 | tf_op jit(solution)/shard_map/exchange_grads/all_to_all | solution.py:203
  23.5 2.1 %collective-permute-start.11 = (bf16[40,1280]{1,0:T(8,128)(2,1)S(1)}, bf16[40,1280]{1,0:T(8,128)(2,1)S(1)}, u32[]{:S(2)}, u32[]{:S(2)}) collective-permute-start(bf16[40,1280]{1,0:T(8,128)(2,1)S(1)} %concatenate.7), channel_id=1, source_target_pairs={{0,96},{32,0},{64,32},{96,64},{1,97},{33,1},{65,33},{97,65},{2,98}... | collective-permute-start | bytes 307208 | tf_op jit(solution)/shard_map/basis_g_x/ppermute | solution.py:178
  25.6 2.7 %collective-permute-start.8 = (bf16[9,16,960]{2,1,0:T(8,128)(2,1)S(1)}, bf16[9,16,960]{2,1,0:T(8,128)(2,1)S(1)}, u32[]{:S(2)}, u32[]{:S(2)}) collective-permute-start(bf16[9,16,960]{2,1,0:T(8,128)(2,1)S(1)} %pad_maximum_fusion.1.refs_1_), channel_id=1, source_target_pairs={{0,24},{8,0},{16,8},{24,16},{1,25},{9,1},{17,9},{25,17},{2,26},{10... | collective-permute-start | bytes 829448 | tf_op jit(solution)/shard_map/basis_a_y/ppermute | solution.py:178
  29.4 1.2 %collective-permute-start.10 = (bf16[40,1280]{1,0:T(8,128)(2,1)S(1)}, bf16[40,1280]{1,0:T(8,128)(2,1)S(1)}, u32[]{:S(2)}, u32[]{:S(2)}) collective-permute-start(bf16[40,1280]{1,0:T(8,128)(2,1)S(1)} %concatenate.7), channel_id=1, source_target_pairs={{0,64},{32,96},{64,0},{96,32},{1,65},{33,97},{65,1},{97,33},{2,66}... | collective-permute-start | bytes 307208 | tf_op jit(solution)/shard_map/basis_g_x/ppermute | solution.py:178
  30.7 4.1 %collective-permute-done.10 = bf16[40,1280]{1,0:T(8,128)(2,1)S(1)} collective-permute-done((bf16[40,1280]{1,0:T(8,128)(2,1)S(1)}, bf16[40,1280]{1,0:T(8,128)(2,1)S(1)}, u32[]{:S(2)}, u32[]{:S(2)}) %collective-permute-start.10) | collective-permute-done | bytes 102432 | tf_op jit(solution)/shard_map/basis_g_x/ppermute | solution.py:178
  35.0 4.9 %collective-permute-done.9 = bf16[40,1280]{1,0:T(8,128)(2,1)S(1)} collective-permute-done((bf16[40,1280]{1,0:T(8,128)(2,1)S(1)}, bf16[40,1280]{1,0:T(8,128)(2,1)S(1)}, u32[]{:S(2)}, u32[]{:S(2)}) %collective-permute-start.9) | collective-permute-done | bytes 102432 | tf_op jit(solution)/shard_map/basis_g_x/ppermute | solution.py:178
  42.0 3.3 %collective-permute-done.6.refs_2_ = bf16[9,16,960]{2,1,0:T(8,128)(2,1)S(1)} collective-permute-done((bf16[9,16,960]{2,1,0:T(8,128)(2,1)S(1)}, bf16[9,16,960]{2,1,0:T(8,128)(2,1)S(1)}, u32[]{:S(2)}, u32[]{:S(2)}) %collective-permute-start.6) | collective-permute-done | bytes 276512 | tf_op jit(solution)/shard_map/basis_a_y/ppermute | solution.py:178
  50.5 10.7 %conv_taps.2 = (bf16[4,64,512]{2,1,0:T(8,128)(2,1)}, bf16[4,64,512]{2,1,0:T(8,128)(2,1)}) custom-call(s32[2]{0:T(128)S(1)} %pad_add_fusion.1.refs_0_, bf16[9,16,960]{2,1,0:T(8,128)(2,1)S(1)} %pad_maximum_fusion.1.refs_1_, bf16[9,16,960]{2,1,0:T(8,128)(2,1)S(1)} %copy-done.8, bf16[9,16,960]{2,1,0:T(8,128)(2,1)S(1)} %copy-done.5, ...), custom_call_target="tpu_custom_call" | custom-call | tf_op jit(solution)/shard_map/coeff_parts/conv_taps/pallas_call | solution.py:81
  61.3 1.4 %collective-permute-start.17 = (bf16[4,64,512]{2,1,0:T(8,128)(2,1)}, bf16[4,64,512]{2,1,0:T(8,128)(2,1)}, u32[]{:S(2)}, u32[]{:S(2)}) collective-permute-start(bf16[4,64,512]{2,1,0:T(8,128)(2,1)} %get-tuple-element.65), channel_id=1, source_target_pairs={{0,1},{1,2},{2,3},{3,0},{4,5},{5,6},{6,7},{7,4},{8,9},{9,10},{10,1... | collective-permute-start | bytes 786440 | tf_op jit(solution)/shard_map/coeff_parts/ppermute | solution.py:178
  62.6 2.5 %collective-permute-start.16 = (bf16[4,64,512]{2,1,0:T(8,128)(2,1)}, bf16[4,64,512]{2,1,0:T(8,128)(2,1)}, u32[]{:S(2)}, u32[]{:S(2)}) collective-permute-start(bf16[4,64,512]{2,1,0:T(8,128)(2,1)} %get-tuple-element.64), channel_id=1, source_target_pairs={{0,2},{1,3},{2,0},{3,1},{4,6},{5,7},{6,4},{7,5},{8,10},{9,11},{10,... | collective-permute-start | bytes 786440 | tf_op jit(solution)/shard_map/coeff_parts/ppermute | solution.py:178
  68.1 10.0 %conv_taps.3 = (bf16[4,64,512]{2,1,0:T(8,128)(2,1)S(1)}, f32[4,64,512]{2,1,0:T(8,128)S(1)}) custom-call(s32[2]{0:T(128)S(1)} %pad_add_fusion.2.refs_0_, bf16[9,16,960]{2,1,0:T(8,128)(2,1)S(1)} %pad_maximum_fusion.1.refs_1_, bf16[9,16,960]{2,1,0:T(8,128)(2,1)S(1)} %copy-done.9, bf16[9,16,960]{2,1,0:T(8,128)(2,1)S(1)} %copy-done.6, ...), custom_call_target="tpu_custom_call" | custom-call | tf_op jit(solution)/shard_map/coeff_parts/conv_taps/pallas_call | solution.py:81
  79.7 2.4 %collective-permute-start.19 = (bf16[8,320,512]{2,1,0:T(8,128)(2,1)}, bf16[8,320,512]{2,1,0:T(8,128)(2,1)}, u32[]{:S(2)}, u32[]{:S(2)}) collective-permute-start(bf16[8,320,512]{2,1,0:T(8,128)(2,1)} %all-to-all-done.refs_5_), channel_id=1, source_target_pairs={{0,4},{4,0},{1,5},{5,1},{2,6},{6,2},{3,7},{7,3},{8,12},{12,8},{9,1... | collective-permute-start | bytes 7864328 | tf_op jit(solution)/shard_map/exchange_cores/ppermute | solution.py:178
  82.1 1.2 collective-permute-start.18
  84.1 6.0 %collective-permute-done.18.refs_4_ = bf16[4,64,512]{2,1,0:T(8,128)(2,1)S(1)} collective-permute-done((bf16[4,64,512]{2,1,0:T(8,128)(2,1)}, bf16[4,64,512]{2,1,0:T(8,128)(2,1)S(1)}, u32[]{:S(2)}, u32[]{:S(2)}) %collective-permute-start.18) | collective-permute-done | bytes 262176 | tf_op jit(solution)/shard_map/ppermute | solution.py:178
  91.1 1.5 %collective-permute-done.23.refs_14_ = bf16[4,40,1280]{2,1,0:T(8,128)(2,1)S(1)} collective-permute-done((bf16[4,40,1280]{2,1,0:T(8,128)(2,1)}, bf16[4,40,1280]{2,1,0:T(8,128)(2,1)S(1)}, u32[]{:S(2)}, u32[]{:S(2)}) %collective-permute-start.23) | collective-permute-done | bytes 409632 | tf_op jit(solution)/shard_map/exchange_cores/ppermute | solution.py:178
  92.6 1.0 copy-done.11
  93.7 8.2 %squared_sums.1 = f32[16,4,1280]{2,1,0:T(4,128)S(1)} custom-call(s32[4]{0:T(128)S(1)} %pad_add_fusion.refs_0_, f32[4,64,512]{2,1,0:T(8,128)S(1)} %copy-done.11, bf16[4,64,512]{2,1,0:T(8,128)(2,1)} %collective-permute-done.16.refs_2_, bf16[4,64,512]{2,1,0:T(8,128)(2,1)} %collective-permute-done.17.refs_3_, ...), custom_call_target="tpu_custom_call" | custom-call | tf_op jit(solution)/shard_map/squared_sums/pallas_call | solution.py:157
  102.2 18.5 %all_to_all.10 = f32[64,1,1280]{2,1,0:T(1,128)S(1)} all-to-all(f32[64,1,1280]{2,1,0:T(1,128)S(1)} %reshape.13), channel_id=1, replica_groups=mesh['x'=4,'y'=4,'core'=2,'z'=4] {'x','y','z'}, dimensions={0} | all-to-all | bytes 655360 | tf_op jit(solution)/shard_map/sum_examples/all_to_all | solution.py:236
  (69 shorter events, 18.7 us)
Async XLA Ops:
  1.0 13.9 %collective-permute-start.5 = (bf16[9,4,960]{2,1,0:T(4,128)(2,1)S(1)}, bf16[9,4,960]{2,1,0:T(4,128)(2,1)S(1)}, u32[]{:S(2)}, u32[]{:S(2)}) collective-permute-start(bf16[9,4,960]{2,1,0:T(4,128)(2,1)S(1)} %reshape.11), channel_id=1, source_target_pairs={{0,96},{32,0},{64,32},{96,64},{1,97},{33,1},{65,33},{97,65},{2,98}... | collective-permute-start | bytes 207368 | tf_op jit(solution)/shard_map/basis_a_x/ppermute | solution.py:178
  4.4 10.5 %collective-permute-start.4 = (bf16[9,4,960]{2,1,0:T(4,128)(2,1)S(1)}, bf16[9,4,960]{2,1,0:T(4,128)(2,1)S(1)}, u32[]{:S(2)}, u32[]{:S(2)}) collective-permute-start(bf16[9,4,960]{2,1,0:T(4,128)(2,1)S(1)} %reshape.11), channel_id=1, source_target_pairs={{0,64},{32,96},{64,0},{96,32},{1,65},{33,97},{65,1},{97,33},{2,66}... | collective-permute-start | bytes 207368 | tf_op jit(solution)/shard_map/basis_a_x/ppermute | solution.py:178
  4.9 10.0 %collective-permute-start.3 = (bf16[9,4,960]{2,1,0:T(4,128)(2,1)S(1)}, bf16[9,4,960]{2,1,0:T(4,128)(2,1)S(1)}, u32[]{:S(2)}, u32[]{:S(2)}) collective-permute-start(bf16[9,4,960]{2,1,0:T(4,128)(2,1)S(1)} %reshape.11), channel_id=1, source_target_pairs={{0,32},{32,64},{64,96},{96,0},{1,33},{33,65},{65,97},{97,1},{2,34}... | collective-permute-start | bytes 207368 | tf_op jit(solution)/shard_map/basis_a_x/ppermute | solution.py:178
  5.6 5.0 %collective-permute-start.2 = (bf16[40,320]{1,0:T(8,128)(2,1)}, bf16[40,320]{1,0:T(8,128)(2,1)S(1)}, u32[]{:S(2)}, u32[]{:S(2)}) collective-permute-start(bf16[40,320]{1,0:T(8,128)(2,1)} %bitcast.29), channel_id=1, source_target_pairs={{0,3},{1,0},{2,1},{3,2},{4,7},{5,4},{6,5},{7,6},{8,11},{9,8},{10,9... | collective-permute-start | bytes 76808 | tf_op jit(solution)/shard_map/basis_g_z/ppermute | solution.py:178
  9.3 4.5 %collective-permute-start.1 = (bf16[40,320]{1,0:T(8,128)(2,1)}, bf16[40,320]{1,0:T(8,128)(2,1)S(1)}, u32[]{:S(2)}, u32[]{:S(2)}) collective-permute-start(bf16[40,320]{1,0:T(8,128)(2,1)} %bitcast.30), channel_id=1, source_target_pairs={{0,2},{1,3},{2,0},{3,1},{4,6},{5,7},{6,4},{7,5},{8,10},{9,11},{10,... | collective-permute-start | bytes 76808 | tf_op jit(solution)/shard_map/basis_g_z/ppermute | solution.py:178
  10.5 4.4 %collective-permute-start = (bf16[40,320]{1,0:T(8,128)(2,1)}, bf16[40,320]{1,0:T(8,128)(2,1)S(1)}, u32[]{:S(2)}, u32[]{:S(2)}) collective-permute-start(bf16[40,320]{1,0:T(8,128)(2,1)} %bitcast.31), channel_id=1, source_target_pairs={{0,1},{1,2},{2,3},{3,0},{4,5},{5,6},{6,7},{7,4},{8,9},{9,10},{10,1... | collective-permute-start | bytes 76808 | tf_op jit(solution)/shard_map/basis_g_z/ppermute | solution.py:178
  15.2 32.4 %collective-permute-start.15 = (bf16[8,320,512]{2,1,0:T(8,128)(2,1)}, bf16[8,320,512]{2,1,0:T(8,128)(2,1)}, u32[]{:S(2)}, u32[]{:S(2)}) collective-permute-start(bf16[8,320,512]{2,1,0:T(8,128)(2,1)} %bitcast.19), channel_id=1, source_target_pairs={{0,4},{4,0},{1,5},{5,1},{2,6},{6,2},{3,7},{7,3},{8,12},{12,8},{9,1... | collective-permute-start | bytes 7864328 | tf_op jit(solution)/shard_map/basis_a_y/ppermute | solution.py:178
  18.8 60.8 %all-to-all-start = ((bf16[8,320,512]{2,1,0:T(8,128)(2,1)}), bf16[8,320,512]{2,1,0:T(8,128)(2,1)}, u32[]{:S(2)}, u32[]{:S(2)}) async-start(bf16[8,320,512]{2,1,0:T(8,128)(2,1)} %bitcast.22), calls=%async_computation | async-start | bytes 5242880 | tf_op jit(solution)/shard_map/exchange_grads/all_to_all | solution.py:203
  23.5 5.9 %collective-permute-start.11 = (bf16[40,1280]{1,0:T(8,128)(2,1)S(1)}, bf16[40,1280]{1,0:T(8,128)(2,1)S(1)}, u32[]{:S(2)}, u32[]{:S(2)}) collective-permute-start(bf16[40,1280]{1,0:T(8,128)(2,1)S(1)} %concatenate.7), channel_id=1, source_target_pairs={{0,96},{32,0},{64,32},{96,64},{1,97},{33,1},{65,33},{97,65},{2,98}... | collective-permute-start | bytes 307208 | tf_op jit(solution)/shard_map/basis_g_x/ppermute | solution.py:178
  25.6 14.9 %collective-permute-start.8 = (bf16[9,16,960]{2,1,0:T(8,128)(2,1)S(1)}, bf16[9,16,960]{2,1,0:T(8,128)(2,1)S(1)}, u32[]{:S(2)}, u32[]{:S(2)}) collective-permute-start(bf16[9,16,960]{2,1,0:T(8,128)(2,1)S(1)} %pad_maximum_fusion.1.refs_1_), channel_id=1, source_target_pairs={{0,24},{8,0},{16,8},{24,16},{1,25},{9,1},{17,9},{25,17},{2,26},{10... | collective-permute-start | bytes 829448 | tf_op jit(solution)/shard_map/basis_a_y/ppermute | solution.py:178
  28.4 12.9 %collective-permute-start.7 = (bf16[9,16,960]{2,1,0:T(8,128)(2,1)S(1)}, bf16[9,16,960]{2,1,0:T(8,128)(2,1)S(1)}, u32[]{:S(2)}, u32[]{:S(2)}) collective-permute-start(bf16[9,16,960]{2,1,0:T(8,128)(2,1)S(1)} %pad_maximum_fusion.1.refs_1_), channel_id=1, source_target_pairs={{0,16},{8,24},{16,0},{24,8},{1,17},{9,25},{17,1},{25,9},{2,18},{10... | collective-permute-start | bytes 829448 | tf_op jit(solution)/shard_map/basis_a_y/ppermute | solution.py:178
  28.7 16.5 %collective-permute-start.6 = (bf16[9,16,960]{2,1,0:T(8,128)(2,1)S(1)}, bf16[9,16,960]{2,1,0:T(8,128)(2,1)S(1)}, u32[]{:S(2)}, u32[]{:S(2)}) collective-permute-start(bf16[9,16,960]{2,1,0:T(8,128)(2,1)S(1)} %pad_maximum_fusion.1.refs_1_), channel_id=1, source_target_pairs={{0,8},{8,16},{16,24},{24,0},{1,9},{9,17},{17,25},{25,1},{2,10},{10... | collective-permute-start | bytes 829448 | tf_op jit(solution)/shard_map/basis_a_y/ppermute | solution.py:178
  29.4 5.3 %collective-permute-start.10 = (bf16[40,1280]{1,0:T(8,128)(2,1)S(1)}, bf16[40,1280]{1,0:T(8,128)(2,1)S(1)}, u32[]{:S(2)}, u32[]{:S(2)}) collective-permute-start(bf16[40,1280]{1,0:T(8,128)(2,1)S(1)} %concatenate.7), channel_id=1, source_target_pairs={{0,64},{32,96},{64,0},{96,32},{1,65},{33,97},{65,1},{97,33},{2,66}... | collective-permute-start | bytes 307208 | tf_op jit(solution)/shard_map/basis_g_x/ppermute | solution.py:178
  34.7 5.1 %collective-permute-start.9 = (bf16[40,1280]{1,0:T(8,128)(2,1)S(1)}, bf16[40,1280]{1,0:T(8,128)(2,1)S(1)}, u32[]{:S(2)}, u32[]{:S(2)}) collective-permute-start(bf16[40,1280]{1,0:T(8,128)(2,1)S(1)} %concatenate.7), channel_id=1, source_target_pairs={{0,32},{32,64},{64,96},{96,0},{1,33},{33,65},{65,97},{97,1},{2,34}... | collective-permute-start | bytes 307208 | tf_op jit(solution)/shard_map/basis_g_x/ppermute | solution.py:178
  46.0 33.6 %collective-permute-start.14 = (bf16[4,40,1280]{2,1,0:T(8,128)(2,1)S(1)}, bf16[4,40,1280]{2,1,0:T(8,128)(2,1)}, u32[]{:S(2)}, u32[]{:S(2)}) collective-permute-start(bf16[4,40,1280]{2,1,0:T(8,128)(2,1)S(1)} %pad_maximum_fusion.refs_7_), channel_id=1, source_target_pairs={{0,24},{8,0},{16,8},{24,16},{1,25},{9,1},{17,9},{25,17},{2,26},{10... | collective-permute-start | bytes 1228808 | tf_op jit(solution)/shard_map/basis_g_y/ppermute | solution.py:178
  46.5 33.2 %collective-permute-start.13 = (bf16[4,40,1280]{2,1,0:T(8,128)(2,1)S(1)}, bf16[4,40,1280]{2,1,0:T(8,128)(2,1)}, u32[]{:S(2)}, u32[]{:S(2)}) collective-permute-start(bf16[4,40,1280]{2,1,0:T(8,128)(2,1)S(1)} %pad_maximum_fusion.refs_7_), channel_id=1, source_target_pairs={{0,16},{8,24},{16,0},{24,8},{1,17},{9,25},{17,1},{25,9},{2,18},{10... | collective-permute-start | bytes 1228808 | tf_op jit(solution)/shard_map/basis_g_y/ppermute | solution.py:178
  46.5 33.1 %collective-permute-start.12 = (bf16[4,40,1280]{2,1,0:T(8,128)(2,1)S(1)}, bf16[4,40,1280]{2,1,0:T(8,128)(2,1)}, u32[]{:S(2)}, u32[]{:S(2)}) collective-permute-start(bf16[4,40,1280]{2,1,0:T(8,128)(2,1)S(1)} %pad_maximum_fusion.refs_7_), channel_id=1, source_target_pairs={{0,8},{8,16},{16,24},{24,0},{1,9},{9,17},{17,25},{25,1},{2,10},{10... | collective-permute-start | bytes 1228808 | tf_op jit(solution)/shard_map/basis_g_y/ppermute | solution.py:178
  61.3 18.4 %collective-permute-start.17 = (bf16[4,64,512]{2,1,0:T(8,128)(2,1)}, bf16[4,64,512]{2,1,0:T(8,128)(2,1)}, u32[]{:S(2)}, u32[]{:S(2)}) collective-permute-start(bf16[4,64,512]{2,1,0:T(8,128)(2,1)} %get-tuple-element.65), channel_id=1, source_target_pairs={{0,1},{1,2},{2,3},{3,0},{4,5},{5,6},{6,7},{7,4},{8,9},{9,10},{10,1... | collective-permute-start | bytes 786440 | tf_op jit(solution)/shard_map/coeff_parts/ppermute | solution.py:178
  62.6 17.1 %collective-permute-start.16 = (bf16[4,64,512]{2,1,0:T(8,128)(2,1)}, bf16[4,64,512]{2,1,0:T(8,128)(2,1)}, u32[]{:S(2)}, u32[]{:S(2)}) collective-permute-start(bf16[4,64,512]{2,1,0:T(8,128)(2,1)} %get-tuple-element.64), channel_id=1, source_target_pairs={{0,2},{1,3},{2,0},{3,1},{4,6},{5,7},{6,4},{7,5},{8,10},{9,11},{10,... | collective-permute-start | bytes 786440 | tf_op jit(solution)/shard_map/coeff_parts/ppermute | solution.py:178
  79.7 12.9 %collective-permute-start.19 = (bf16[8,320,512]{2,1,0:T(8,128)(2,1)}, bf16[8,320,512]{2,1,0:T(8,128)(2,1)}, u32[]{:S(2)}, u32[]{:S(2)}) collective-permute-start(bf16[8,320,512]{2,1,0:T(8,128)(2,1)} %all-to-all-done.refs_5_), channel_id=1, source_target_pairs={{0,4},{4,0},{1,5},{5,1},{2,6},{6,2},{3,7},{7,3},{8,12},{12,8},{9,1... | collective-permute-start | bytes 7864328 | tf_op jit(solution)/shard_map/exchange_cores/ppermute | solution.py:178
  82.1 8.1 %collective-permute-start.18 = (bf16[4,64,512]{2,1,0:T(8,128)(2,1)}, bf16[4,64,512]{2,1,0:T(8,128)(2,1)S(1)}, u32[]{:S(2)}, u32[]{:S(2)}) collective-permute-start(bf16[4,64,512]{2,1,0:T(8,128)(2,1)} %copy-done.12), channel_id=1, source_target_pairs={{0,3},{1,0},{2,1},{3,2},{4,7},{5,4},{6,5},{7,6},{8,11},{9,8},{10,9... | collective-permute-start | bytes 786440 | tf_op jit(solution)/shard_map/ppermute | solution.py:178
  83.3 7.8 %collective-permute-start.20 = (bf16[4,40,1280]{2,1,0:T(8,128)(2,1)S(1)}, bf16[4,40,1280]{2,1,0:T(8,128)(2,1)S(1)}, u32[]{:S(2)}, u32[]{:S(2)}) collective-permute-start(bf16[4,40,1280]{2,1,0:T(8,128)(2,1)S(1)} %pad_maximum_fusion.refs_7_), channel_id=1, source_target_pairs={{0,4},{4,0},{1,5},{5,1},{2,6},{6,2},{3,7},{7,3},{8,12},{12,8},{9,1... | collective-permute-start | bytes 1228808 | tf_op jit(solution)/shard_map/exchange_cores/ppermute | solution.py:178
  83.6 7.5 %collective-permute-start.21 = (bf16[4,40,1280]{2,1,0:T(8,128)(2,1)}, bf16[4,40,1280]{2,1,0:T(8,128)(2,1)S(1)}, u32[]{:S(2)}, u32[]{:S(2)}) collective-permute-start(bf16[4,40,1280]{2,1,0:T(8,128)(2,1)} %collective-permute-done.12.refs_8_), channel_id=1, source_target_pairs={{0,4},{4,0},{1,5},{5,1},{2,6},{6,2},{3,7},{7,3},{8,12},{12,8},{9,1... | collective-permute-start | bytes 1228808 | tf_op jit(solution)/shard_map/exchange_cores/ppermute | solution.py:178
  83.8 7.3 %collective-permute-start.22 = (bf16[4,40,1280]{2,1,0:T(8,128)(2,1)}, bf16[4,40,1280]{2,1,0:T(8,128)(2,1)S(1)}, u32[]{:S(2)}, u32[]{:S(2)}) collective-permute-start(bf16[4,40,1280]{2,1,0:T(8,128)(2,1)} %collective-permute-done.13.refs_9_), channel_id=1, source_target_pairs={{0,4},{4,0},{1,5},{5,1},{2,6},{6,2},{3,7},{7,3},{8,12},{12,8},{9,1... | collective-permute-start | bytes 1228808 | tf_op jit(solution)/shard_map/exchange_cores/ppermute | solution.py:178
  (15 other events, 53.6 us)

commit v5 on v4

v5 whole, which is shorter than its diff:
```python
import jax
import jax.numpy as jnp
from jax import lax
from jax.experimental import pallas as pl
from jax.experimental.pallas import tpu as pltpu
from jax.sharding import Mesh, PartitionSpec as P

SIDE = 8
POS = SIDE * SIDE * SIDE
AB = 9
ALL = ("x", "y", "core", "z")
NT = (((1,), (1,)), ((), ()))
VMEM = pl.BlockSpec(memory_space=pltpu.VMEM)
SMEM = pl.BlockSpec(memory_space=pltpu.SMEM)


def lane_coords():
    p = lax.broadcasted_iota(jnp.int32, (1, POS), 1)
    return p // 64, (p // 8) % 8, p % 8


def shifted(y, ab, i, j):
    a, b = ab // 3 - 1, ab % 3 - 1
    s = a * 64 + b * 8
    if s == 0:
        return y
    ok = None
    for v, o in ((i, a), (j, b)):
        if o != 0:
            m = (v + o >= 0) & (v + o < SIDE)
            ok = m if ok is None else ok & m
    return jnp.where(ok, pltpu.roll(y, (-s) % POS, 1), 0.0)


def conv_kernel(idx_ref, b_ref, x_ref, x_oth_ref, *refs):
    *o_refs, xc_ref = refs
    i, j, k = lane_coords()
    h = x_ref.shape[1]
    per = o_refs[0].shape[0] // 2
    ranks = b_ref.shape[1]
    zero = jnp.zeros((), x_ref.dtype)
    b = b_ref[...].reshape(AB * ranks, 3 * h)
    for n in range(2 * per * len(o_refs)):
        o, m = n // (2 * per), n % (2 * per)
        x = (x_ref if m < per else x_oth_ref)[idx_ref[o] * per + m % per]
        xc_ref[n % 2, :h] = jnp.where(k >= 1, pltpu.roll(x, 1, 1), zero)
        xc_ref[n % 2, h : 2 * h] = x
        xc_ref[n % 2, 2 * h :] = jnp.where(k <= SIDE - 2, pltpu.roll(x, POS - 1, 1), zero)
        y = jnp.dot(b, xc_ref[n % 2], preferred_element_type=jnp.float32)
        acc = None
        for ab in range(AB):
            t = shifted(y[ab * ranks : (ab + 1) * ranks], ab, i, j)
            acc = t if acc is None else acc + t
        o_refs[o][m] = acc.astype(o_refs[o].dtype)


def conv(idx, taps, x, x_oth, per, dtypes):
    ranks = taps.shape[1]
    return pl.pallas_call(
        conv_kernel,
        out_shape=[jax.ShapeDtypeStruct((2 * per, ranks, POS), d) for d in dtypes],
        in_specs=[SMEM] + [VMEM] * 3,
        out_specs=[VMEM] * len(dtypes),
        scratch_shapes=[pltpu.VMEM((2, 3 * x.shape[1], POS), jnp.bfloat16)],
        compiler_params=pltpu.CompilerParams(vmem_limit_bytes=16 << 20),
        name="conv_taps",
    )(idx, taps, x, x_oth)


def squares_kernel(idx_ref, c_ref, g_ref, g_oth_ref, *refs, scale):
    *bg_refs, o_ref, hi_ref, m_ref, sq_ref = refs
    x, y, core, z = idx_ref[0], idx_ref[1], idx_ref[2], idx_ref[3]
    side, width = len(bg_refs) // 2, bg_refs[0].shape[1]
    examples, ranks = c_ref.shape[0], c_ref.shape[1]
    per = examples // 2
    tensor = g_ref.shape[0] // per

    def chip(rx, ry):
        return ((x + side - rx) % side) * side + (y + side - ry) % side

    for n in range(examples):
        c = c_ref[n]
        hi_ref[n] = c.astype(jnp.bfloat16)
        hi = hi_ref[n]
        lo = (c - hi.astype(jnp.float32)).astype(jnp.bfloat16)
        both = jnp.concatenate([hi, lo], axis=0)
        src = g_ref if n < per else g_oth_ref
        g = jnp.concatenate([src[((z + tensor - t) % tensor) * per + n % per] for t in range(tensor)], axis=0)
        m = lax.dot_general(both, g, NT, preferred_element_type=jnp.float32)
        m_ref[n * ranks : (n + 1) * ranks] = (m[:ranks] + m[ranks:]).astype(jnp.bfloat16)
    m = m_ref[...]
    for half in range(2):
        for ry in range(side):
            bg = bg_refs[half * side + ry][...].reshape(side * width, -1)
            p = lax.dot_general(bg, m, NT, preferred_element_type=jnp.float32)
            p = p * p
            while p.shape[1] > 2 * ranks:
                p = p[:, : p.shape[1] // 2] + p[:, p.shape[1] // 2 :]
            p = (p + pltpu.roll(p, ranks, 1)) * scale
            for rx in range(side):
                at = (chip(rx, ry) * 2 + (core + half) % 2) * width
                sq_ref[pl.ds(pl.multiple_of(at, 8), width), :] = p[rx * width : (rx + 1) * width]
    sq = sq_ref[...].T[:ranks]
    low = ranks // (side * side)
    for b in range(side * side):
        o_ref[chip(b % side, b // side)] = sq[b * low : (b + 1) * low]


def squares(idx, c, g, g_oth, bg, bg_oth, scale):
    examples, ranks = c.shape[0], c.shape[1]
    side, width, hidden = bg[0].shape
    chips = side * side

    def kernel(*refs):
        squares_kernel(*refs, scale=scale)

    return pl.pallas_call(
        kernel,
        out_shape=jax.ShapeDtypeStruct((chips, ranks // chips, 2 * chips * width), jnp.float32),
        in_specs=[SMEM] + [VMEM] * (3 + 2 * side),
        out_specs=VMEM,
        scratch_shapes=[
            pltpu.VMEM((examples, ranks, POS), jnp.bfloat16),
            pltpu.VMEM((examples * ranks, hidden), jnp.bfloat16),
            pltpu.VMEM((2 * chips * width, 2 * ranks), jnp.float32),
        ],
        compiler_params=pltpu.CompilerParams(vmem_limit_bytes=16 << 20),
        name="squared_sums",
    )(idx, c, g, g_oth, *bg, *bg_oth)


def shift(v, axis, s):
    n = lax.axis_size(axis)
    return lax.ppermute(v, axis, [(i, (i + s) % n) for i in range(n)])


def around(v, axis):
    return [v] + [shift(v, axis, s) for s in range(1, lax.axis_size(axis))]


def body(patch_rows, out_grads, basis_a, basis_g):
    coords = [lax.axis_index(a).astype(jnp.int32) for a in ALL]
    z = coords[3]
    x = patch_rows.transpose(0, 2, 1)
    grads = out_grads.transpose(0, 2, 1)
    here, channels = x.shape[0], x.shape[1]
    tensor = lax.axis_size("z")
    per = here // tensor

    with jax.named_scope("basis_a_x"):
        own = basis_a.reshape(AB, 3, channels, -1).transpose(0, 3, 1, 2)
        own = own.reshape(AB, own.shape[1], 3 * channels)
        ba = around(own, "x")
    with jax.named_scope("basis_g_z"):
        bg = around(basis_g.T, "z")
    with jax.named_scope("exchange_grads"):
        grads, bg, ba = lax.optimization_barrier((grads, bg, ba))
        g = lax.all_to_all(grads, "z", 0, 0, tiled=True)
    with jax.named_scope("basis_a_y"):
        ba = jnp.concatenate(ba, axis=1)
        bg, give, _ = lax.optimization_barrier((bg, x, ba))
        x_oth = shift(give, "core", 1)
        ba = around(ba, "y")
    with jax.named_scope("basis_g_x"):
        bg = around(jnp.concatenate(bg, axis=1), "x")

    def parts(shifts, dtypes):
        return conv(jnp.stack([(z + s) % tensor for s in shifts]), jnp.concatenate(ba, axis=1), x, x_oth, per, dtypes)

    ba, bg = lax.optimization_barrier((ba, bg))
    with jax.named_scope("basis_g_y"):
        bg = around(jnp.stack(bg), "y")
    with jax.named_scope("coeff_parts"):
        bf16 = jnp.bfloat16
        *sent, mine = parts((2, 1, 3, 0), (bf16, bf16, bf16, jnp.float32))
        received = [shift(v, "z", s) for v, s in zip(sent, (2, 1, 3))]
    with jax.named_scope("exchange_cores"):
        g, bg, received[1] = lax.optimization_barrier((g, bg, received[1]))
        g_oth = shift(g, "core", 1)
        bg_oth = [shift(v, "core", 1) for v in bg]

    total_coeff = mine
    for r in received:
        total_coeff = total_coeff + r.astype(jnp.float32)
    examples = here * lax.axis_size(("x", "y", "core"))
    total = squares(jnp.stack(coords), total_coeff, g, g_oth, bg, bg_oth, 1.0 / examples)

    with jax.named_scope("sum_examples"):
        rows = total.reshape(-1, 1, total.shape[2])
        got = lax.all_to_all(rows, ("x", "y", "z"), 0, 0, tiled=True)
        return jnp.sum(got, axis=0)


def solution(mesh):
    tensor = mesh.shape["tensor"]
    fine = Mesh(mesh.devices.reshape(4, -1, 2, tensor), ALL)
    dp = ("x", "y", "core")
    in_specs = (P(dp, None, "z"), P(dp, None, "z"), P(None, "z", dp), P("z", dp))
    return jax.shard_map(body, mesh=fine, in_specs=in_specs, out_specs=P(ALL, None), check_vma=False)
```

time: 122 us -> 117 us (0.959)
  Pallas kernels: 28.9 us -> 19 us
  starting transfers between devices: 34.5 us -> 42 us
  local copies, waits for them, and re-layouts: 12.7 us -> 6.99 us
  other arithmetic: 0.69 us -> 4.09 us
    ppermute x24, starting transfers between devices: 30 us -> 37.9 us  [shift(): return lax.ppermute(v, axis, [(i, (i + s) % n) for i in range(n)])]
    pallas_call x2 -> x1, Pallas kernels: 20.7 us -> 12.9 us  [conv(): pl.pallas_call(conv_kernel, out_shape=[jax.ShapeDtypeStruct((2 * per, ran...]
    unnamed x28 -> x20, local copies, waits for them, and re-layouts: 10.5 us -> 4.85 us
    pallas_call x1, Pallas kernels: 8.16 us -> 6.14 us  [squares(): pl.pallas_call(kernel, out_shape=jax.ShapeDtypeStruct((chips, ranks // ch...]
    concatenate x0 -> x1, other arithmetic: none -> 1.28 us  [parts(): jnp.concatenate(ba, axis=1)]
    add x0 -> x1, other arithmetic: none -> 1.24 us  [body(): total_coeff = total_coeff + r.astype(jnp.float32)]
  transfers between devices with their start and end apart: 25 -> 25, of which waited for: 9 -> 11; matrix products, arithmetic and copies ran while one was open for 0% -> 3% of each run, Pallas kernels for 17% -> 11%
where the time goes in v5:
time: 117 us; the launch traced here: 116 us
  starting transfers between devices  42 us (36%)
  waiting for transfers between devices  26 us (22%)
  Pallas kernels  19 us (16%)
  blocking collectives  17.7 us (15%)
  local copies, waits for them, and re-layouts  6.99 us (6%)
  other arithmetic  4.09 us (3%)
    ppermute x24, starting transfers between devices, shift(): return lax.ppermute(v, axis, [(i, (i + s) % n) for i in range(n)])  37.9 us
    ppermute x24, waiting for transfers between devices, shift(): return lax.ppermute(v, axis, [(i, (i + s) % n) for i in range(n)])  26 us
    all_to_all x1, blocking collectives, body(): got = lax.all_to_all(rows, ('x', 'y', 'z'), 0, 0, tiled=True)  17.7 us
    pallas_call x1, Pallas kernels, conv(): pl.pallas_call(conv_kernel, out_shape=[jax.ShapeDtypeStruct((2 * per, ran...  12.9 us
    pallas_call x1, Pallas kernels, squares(): pl.pallas_call(kernel, out_shape=jax.ShapeDtypeStruct((chips, ranks // ch...  6.14 us
    unnamed x20, local copies, waits for them, and re-layouts  4.85 us
    all_to_all x1, starting transfers between devices, body(): g = lax.all_to_all(grads, 'z', 0, 0, tiled=True)  4.08 us
  transfers between devices with their start and end apart: 25, of which 11 were waited for; matrix products, arithmetic and copies ran while one was open for 3% of the time, Pallas kernels for 11%

profile of v5, /device:TPU:1, one launch (start us, length us, event | category | flops | bytes accessed | tf_op | source)
XLA Modules:
  0.0 115.9 jit_solution(2710848814765501373)
XLA Ops:
  1.0 2.1 %collective-permute-start.3 = (bf16[9,4,960]{2,1,0:T(4,128)(2,1)S(1)}, bf16[9,4,960]{2,1,0:T(4,128)(2,1)S(1)}, u32[]{:S(2)}, u32[]{:S(2)}) collective-permute-start(bf16[9,4,960]{2,1,0:T(4,128)(2,1)S(1)} %reshape.11), channel_id=1, source_target_pairs={{0,32},{32,64},{64,96},{96,0},{1,33},{33,65},{65,97},{97,1},{2,34}... | collective-permute-start | bytes 207368 | tf_op jit(solution)/shard_map/basis_a_x/ppermute | solution.py:134
  3.2 2.5 %collective-permute-start.4 = (bf16[9,4,960]{2,1,0:T(4,128)(2,1)S(1)}, bf16[9,4,960]{2,1,0:T(4,128)(2,1)S(1)}, u32[]{:S(2)}, u32[]{:S(2)}) collective-permute-start(bf16[9,4,960]{2,1,0:T(4,128)(2,1)S(1)} %reshape.11), channel_id=1, source_target_pairs={{0,64},{32,96},{64,0},{96,32},{1,65},{33,97},{65,1},{97,33},{2,66}... | collective-permute-start | bytes 207368 | tf_op jit(solution)/shard_map/basis_a_x/ppermute | solution.py:134
  6.8 1.6 %collective-permute-start = (bf16[40,320]{1,0:T(8,128)(2,1)}, bf16[40,320]{1,0:T(8,128)(2,1)S(1)}, u32[]{:S(2)}, u32[]{:S(2)}) collective-permute-start(bf16[40,320]{1,0:T(8,128)(2,1)} %bitcast.27), channel_id=1, source_target_pairs={{0,1},{1,2},{2,3},{3,0},{4,5},{5,6},{6,7},{7,4},{8,9},{9,10},{10,1... | collective-permute-start | bytes 76808 | tf_op jit(solution)/shard_map/basis_g_z/ppermute | solution.py:134
  8.4 3.3 %collective-permute-start.1 = (bf16[40,320]{1,0:T(8,128)(2,1)}, bf16[40,320]{1,0:T(8,128)(2,1)S(1)}, u32[]{:S(2)}, u32[]{:S(2)}) collective-permute-start(bf16[40,320]{1,0:T(8,128)(2,1)} %bitcast.28), channel_id=1, source_target_pairs={{0,2},{1,3},{2,0},{3,1},{4,6},{5,7},{6,4},{7,5},{8,10},{9,11},{10,... | collective-permute-start | bytes 76808 | tf_op jit(solution)/shard_map/basis_g_z/ppermute | solution.py:134
  12.0 1.8 %collective-permute-start.2 = (bf16[40,320]{1,0:T(8,128)(2,1)}, bf16[40,320]{1,0:T(8,128)(2,1)S(1)}, u32[]{:S(2)}, u32[]{:S(2)}) collective-permute-start(bf16[40,320]{1,0:T(8,128)(2,1)} %bitcast.29), channel_id=1, source_target_pairs={{0,3},{1,0},{2,1},{3,2},{4,7},{5,4},{6,5},{7,6},{8,11},{9,8},{10,9... | collective-permute-start | bytes 76808 | tf_op jit(solution)/shard_map/basis_g_z/ppermute | solution.py:134
  13.8 1.5 %collective-permute-done.2 = bf16[40,320]{1,0:T(8,128)(2,1)S(1)} collective-permute-done((bf16[40,320]{1,0:T(8,128)(2,1)}, bf16[40,320]{1,0:T(8,128)(2,1)S(1)}, u32[]{:S(2)}, u32[]{:S(2)}) %collective-permute-start.2) | collective-permute-done | bytes 25632 | tf_op jit(solution)/shard_map/basis_g_z/ppermute | solution.py:134
  15.5 3.5 %collective-permute-start.12 = (bf16[8,320,512]{2,1,0:T(8,128)(2,1)}, bf16[8,320,512]{2,1,0:T(8,128)(2,1)}, u32[]{:S(2)}, u32[]{:S(2)}) collective-permute-start(bf16[8,320,512]{2,1,0:T(8,128)(2,1)} %bitcast.19), channel_id=1, source_target_pairs={{0,4},{4,0},{1,5},{5,1},{2,6},{6,2},{3,7},{7,3},{8,12},{12,8},{9,1... | collective-permute-start | bytes 7864328 | tf_op jit(solution)/shard_map/basis_a_y/ppermute | solution.py:134
  19.0 4.1 %all-to-all-start = ((bf16[8,320,512]{2,1,0:T(8,128)(2,1)}), bf16[8,320,512]{2,1,0:T(8,128)(2,1)S(1)}, u32[]{:S(2)}, u32[]{:S(2)}) async-start(bf16[8,320,512]{2,1,0:T(8,128)(2,1)} %bitcast.21), calls=%async_computation | async-start | bytes 5242880 | tf_op jit(solution)/shard_map/exchange_grads/all_to_all | solution.py:158
  23.5 1.3 %collective-permute-start.6 = (bf16[9,16,960]{2,1,0:T(8,128)(2,1)S(1)}, bf16[9,16,960]{2,1,0:T(8,128)(2,1)S(1)}, u32[]{:S(2)}, u32[]{:S(2)}) collective-permute-start(bf16[9,16,960]{2,1,0:T(8,128)(2,1)S(1)} %pad_maximum_fusion.2), channel_id=1, source_target_pairs={{0,8},{8,16},{16,24},{24,0},{1,9},{9,17},{17,25},{25,1},{2,10},{10... | collective-permute-start | bytes 829448 | tf_op jit(solution)/shard_map/basis_a_y/ppermute | solution.py:134
  24.8 2.6 %collective-permute-start.7 = (bf16[9,16,960]{2,1,0:T(8,128)(2,1)S(1)}, bf16[9,16,960]{2,1,0:T(8,128)(2,1)}, u32[]{:S(2)}, u32[]{:S(2)}) collective-permute-start(bf16[9,16,960]{2,1,0:T(8,128)(2,1)S(1)} %pad_maximum_fusion.2), channel_id=1, source_target_pairs={{0,16},{8,24},{16,0},{24,8},{1,17},{9,25},{17,1},{25,9},{2,18},{10... | collective-permute-start | bytes 829448 | tf_op jit(solution)/shard_map/basis_a_y/ppermute | solution.py:134
  28.9 2.0 %collective-permute-start.11 = (bf16[40,1280]{1,0:T(8,128)(2,1)S(1)}, bf16[40,1280]{1,0:T(8,128)(2,1)S(1)}, u32[]{:S(2)}, u32[]{:S(2)}) collective-permute-start(bf16[40,1280]{1,0:T(8,128)(2,1)S(1)} %concatenate.10), channel_id=1, source_target_pairs={{0,96},{32,0},{64,32},{96,64},{1,97},{33,1},{65,33},{97,65},{2,98}... | collective-permute-start | bytes 307208 | tf_op jit(solution)/shard_map/basis_g_x/ppermute | solution.py:134
  30.9 1.8 %collective-permute-done.11 = bf16[40,1280]{1,0:T(8,128)(2,1)S(1)} collective-permute-done((bf16[40,1280]{1,0:T(8,128)(2,1)S(1)}, bf16[40,1280]{1,0:T(8,128)(2,1)S(1)}, u32[]{:S(2)}, u32[]{:S(2)}) %collective-permute-start.11) | collective-permute-done | bytes 102432 | tf_op jit(solution)/shard_map/basis_g_x/ppermute | solution.py:134
  33.2 5.2 %collective-permute-done.9 = bf16[40,1280]{1,0:T(8,128)(2,1)} collective-permute-done((bf16[40,1280]{1,0:T(8,128)(2,1)S(1)}, bf16[40,1280]{1,0:T(8,128)(2,1)}, u32[]{:S(2)}, u32[]{:S(2)}) %collective-permute-start.9) | collective-permute-done | bytes 102432 | tf_op jit(solution)/shard_map/basis_g_x/ppermute | solution.py:134
  38.4 1.9 %collective-permute-done.7 = bf16[9,16,960]{2,1,0:T(8,128)(2,1)} collective-permute-done((bf16[9,16,960]{2,1,0:T(8,128)(2,1)S(1)}, bf16[9,16,960]{2,1,0:T(8,128)(2,1)}, u32[]{:S(2)}, u32[]{:S(2)}) %collective-permute-start.7) | collective-permute-done | bytes 276512 | tf_op jit(solution)/shard_map/basis_a_y/ppermute | solution.py:134
  42.4 3.0 %collective-permute-start.15 = (bf16[4,40,1280]{2,1,0:T(8,128)(2,1)S(1)}, bf16[4,40,1280]{2,1,0:T(8,128)(2,1)S(1)}, u32[]{:S(2)}, u32[]{:S(2)}) collective-permute-start(bf16[4,40,1280]{2,1,0:T(8,128)(2,1)S(1)} %pad_maximum_fusion.1.refs_4_), channel_id=1, source_target_pairs={{0,16},{8,24},{16,0},{24,8},{1,17},{9,25},{17,1},{25,9},{2,18},{10... | collective-permute-start | bytes 1228808 | tf_op jit(solution)/shard_map/basis_g_y/ppermute | solution.py:134
  46.9 12.9 %conv_taps.1 = (bf16[4,64,512]{2,1,0:T(8,128)(2,1)S(1)}, bf16[4,64,512]{2,1,0:T(8,128)(2,1)}, bf16[4,64,512]{2,1,0:T(8,128)(2,1)S(1)}, f32[4,64,512]{2,1,0:T(8,128)S(1)}) custom-call(s32[4]{0:T(128)S(1)} %pad_add_fusion.1.idx_ref, bf16[9,64,960]{2,1,0:T(8,128)(2,1)S(1)} %pad_maximum_fusion.b_ref, bf16[8,320,512]{2,1,0:T(8,128)(2,1)S(1)} %bitcast.20, ...), custom_call_target="tpu_custom_call" | custom-call | tf_op jit(solution)/shard_map/coeff_parts/conv_taps/pallas_call | solution.py:59
  61.2 1.3 %collective-permute-start.17 = (bf16[4,64,512]{2,1,0:T(8,128)(2,1)}, bf16[4,64,512]{2,1,0:T(8,128)(2,1)}, u32[]{:S(2)}, u32[]{:S(2)}) collective-permute-start(bf16[4,64,512]{2,1,0:T(8,128)(2,1)} %get-tuple-element.61), channel_id=1, source_target_pairs={{0,1},{1,2},{2,3},{3,0},{4,5},{5,6},{6,7},{7,4},{8,9},{9,10},{10,1... | collective-permute-start | bytes 786440 | tf_op jit(solution)/shard_map/coeff_parts/ppermute | solution.py:134
  63.9 4.0 %collective-permute-done.17 = bf16[4,64,512]{2,1,0:T(8,128)(2,1)} collective-permute-done((bf16[4,64,512]{2,1,0:T(8,128)(2,1)}, bf16[4,64,512]{2,1,0:T(8,128)(2,1)}, u32[]{:S(2)}, u32[]{:S(2)}) %collective-permute-start.17) | collective-permute-done | bytes 262176 | tf_op jit(solution)/shard_map/coeff_parts/ppermute | solution.py:134
  67.9 3.9 %collective-permute-start.19 = (bf16[8,320,512]{2,1,0:T(8,128)(2,1)S(1)}, bf16[8,320,512]{2,1,0:T(8,128)(2,1)}, u32[]{:S(2)}, u32[]{:S(2)}) collective-permute-start(bf16[8,320,512]{2,1,0:T(8,128)(2,1)S(1)} %all-to-all-done.refs_2_), channel_id=1, source_target_pairs={{0,4},{4,0},{1,5},{5,1},{2,6},{6,2},{3,7},{7,3},{8,12},{12,8},{9,1... | collective-permute-start | bytes 7864328 | tf_op jit(solution)/shard_map/exchange_cores/ppermute | solution.py:134
  71.9 1.8 %collective-permute-start.13 = (bf16[4,64,512]{2,1,0:T(8,128)(2,1)}, bf16[4,64,512]{2,1,0:T(8,128)(2,1)}, u32[]{:S(2)}, u32[]{:S(2)}) collective-permute-start(bf16[4,64,512]{2,1,0:T(8,128)(2,1)} %copy-done.6), channel_id=1, source_target_pairs={{0,2},{1,3},{2,0},{3,1},{4,6},{5,7},{6,4},{7,5},{8,10},{9,11},{10,... | collective-permute-start | bytes 786440 | tf_op jit(solution)/shard_map/coeff_parts/ppermute | solution.py:134
  75.1 6.5 %collective-permute-done.13 = bf16[4,64,512]{2,1,0:T(8,128)(2,1)} collective-permute-done((bf16[4,64,512]{2,1,0:T(8,128)(2,1)}, bf16[4,64,512]{2,1,0:T(8,128)(2,1)}, u32[]{:S(2)}, u32[]{:S(2)}) %collective-permute-start.13) | collective-permute-done | bytes 262176 | tf_op jit(solution)/shard_map/coeff_parts/ppermute | solution.py:134
  82.4 4.0 %collective-permute-done.18 = bf16[4,64,512]{2,1,0:T(8,128)(2,1)} collective-permute-done((bf16[4,64,512]{2,1,0:T(8,128)(2,1)}, bf16[4,64,512]{2,1,0:T(8,128)(2,1)}, u32[]{:S(2)}, u32[]{:S(2)}) %collective-permute-start.18) | collective-permute-done | bytes 262176 | tf_op jit(solution)/shard_map/coeff_parts/ppermute | solution.py:134
  90.9 6.1 %squared_sums.1 = f32[16,4,1280]{2,1,0:T(4,128)S(1)} custom-call(s32[4]{0:T(128)S(1)} %pad_add_fusion.refs_0_, f32[4,64,512]{2,1,0:T(8,128)S(1)} %convert_add_fusion.refs_1_, bf16[8,320,512]{2,1,0:T(8,128)(2,1)S(1)} %all-to-all-done.refs_2_, bf16[8,320,512]{2,1,0:T(8,128)(2,1)} %collective-permute-done.19.refs_3_, ...), custom_call_target="tpu_custom_call" | custom-call | tf_op jit(solution)/shard_map/squared_sums/pallas_call | solution.py:117
  97.4 17.7 %all_to_all.10 = f32[64,1,1280]{2,1,0:T(1,128)S(1)} all-to-all(f32[64,1,1280]{2,1,0:T(1,128)S(1)} %reshape.13), channel_id=1, replica_groups=mesh['x'=4,'y'=4,'core'=2,'z'=4] {'x','y','z'}, dimensions={0} | all-to-all | bytes 655360 | tf_op jit(solution)/shard_map/sum_examples/all_to_all | solution.py:190
  (61 shorter events, 19.6 us)
Async XLA Ops:
  1.0 14.2 %collective-permute-start.3 = (bf16[9,4,960]{2,1,0:T(4,128)(2,1)S(1)}, bf16[9,4,960]{2,1,0:T(4,128)(2,1)S(1)}, u32[]{:S(2)}, u32[]{:S(2)}) collective-permute-start(bf16[9,4,960]{2,1,0:T(4,128)(2,1)S(1)} %reshape.11), channel_id=1, source_target_pairs={{0,32},{32,64},{64,96},{96,0},{1,33},{33,65},{65,97},{97,1},{2,34}... | collective-permute-start | bytes 207368 | tf_op jit(solution)/shard_map/basis_a_x/ppermute | solution.py:134
  3.2 12.1 %collective-permute-start.4 = (bf16[9,4,960]{2,1,0:T(4,128)(2,1)S(1)}, bf16[9,4,960]{2,1,0:T(4,128)(2,1)S(1)}, u32[]{:S(2)}, u32[]{:S(2)}) collective-permute-start(bf16[9,4,960]{2,1,0:T(4,128)(2,1)S(1)} %reshape.11), channel_id=1, source_target_pairs={{0,64},{32,96},{64,0},{96,32},{1,65},{33,97},{65,1},{97,33},{2,66}... | collective-permute-start | bytes 207368 | tf_op jit(solution)/shard_map/basis_a_x/ppermute | solution.py:134
  5.6 9.7 %collective-permute-start.5 = (bf16[9,4,960]{2,1,0:T(4,128)(2,1)S(1)}, bf16[9,4,960]{2,1,0:T(4,128)(2,1)S(1)}, u32[]{:S(2)}, u32[]{:S(2)}) collective-permute-start(bf16[9,4,960]{2,1,0:T(4,128)(2,1)S(1)} %reshape.11), channel_id=1, source_target_pairs={{0,96},{32,0},{64,32},{96,64},{1,97},{33,1},{65,33},{97,65},{2,98}... | collective-permute-start | bytes 207368 | tf_op jit(solution)/shard_map/basis_a_x/ppermute | solution.py:134
  6.8 5.2 %collective-permute-start = (bf16[40,320]{1,0:T(8,128)(2,1)}, bf16[40,320]{1,0:T(8,128)(2,1)S(1)}, u32[]{:S(2)}, u32[]{:S(2)}) collective-permute-start(bf16[40,320]{1,0:T(8,128)(2,1)} %bitcast.27), channel_id=1, source_target_pairs={{0,1},{1,2},{2,3},{3,0},{4,5},{5,6},{6,7},{7,4},{8,9},{9,10},{10,1... | collective-permute-start | bytes 76808 | tf_op jit(solution)/shard_map/basis_g_z/ppermute | solution.py:134
  8.4 5.4 %collective-permute-start.1 = (bf16[40,320]{1,0:T(8,128)(2,1)}, bf16[40,320]{1,0:T(8,128)(2,1)S(1)}, u32[]{:S(2)}, u32[]{:S(2)}) collective-permute-start(bf16[40,320]{1,0:T(8,128)(2,1)} %bitcast.28), channel_id=1, source_target_pairs={{0,2},{1,3},{2,0},{3,1},{4,6},{5,7},{6,4},{7,5},{8,10},{9,11},{10,... | collective-permute-start | bytes 76808 | tf_op jit(solution)/shard_map/basis_g_z/ppermute | solution.py:134
  12.0 3.2 %collective-permute-start.2 = (bf16[40,320]{1,0:T(8,128)(2,1)}, bf16[40,320]{1,0:T(8,128)(2,1)S(1)}, u32[]{:S(2)}, u32[]{:S(2)}) collective-permute-start(bf16[40,320]{1,0:T(8,128)(2,1)} %bitcast.29), channel_id=1, source_target_pairs={{0,3},{1,0},{2,1},{3,2},{4,7},{5,4},{6,5},{7,6},{8,11},{9,8},{10,9... | collective-permute-start | bytes 76808 | tf_op jit(solution)/shard_map/basis_g_z/ppermute | solution.py:134
  15.5 31.4 %collective-permute-start.12 = (bf16[8,320,512]{2,1,0:T(8,128)(2,1)}, bf16[8,320,512]{2,1,0:T(8,128)(2,1)}, u32[]{:S(2)}, u32[]{:S(2)}) collective-permute-start(bf16[8,320,512]{2,1,0:T(8,128)(2,1)} %bitcast.19), channel_id=1, source_target_pairs={{0,4},{4,0},{1,5},{5,1},{2,6},{6,2},{3,7},{7,3},{8,12},{12,8},{9,1... | collective-permute-start | bytes 7864328 | tf_op jit(solution)/shard_map/basis_a_y/ppermute | solution.py:134
  19.0 45.0 %all-to-all-start = ((bf16[8,320,512]{2,1,0:T(8,128)(2,1)}), bf16[8,320,512]{2,1,0:T(8,128)(2,1)S(1)}, u32[]{:S(2)}, u32[]{:S(2)}) async-start(bf16[8,320,512]{2,1,0:T(8,128)(2,1)} %bitcast.21), calls=%async_computation | async-start | bytes 5242880 | tf_op jit(solution)/shard_map/exchange_grads/all_to_all | solution.py:158
  23.1 5.7 %collective-permute-start.10 = (bf16[40,1280]{1,0:T(8,128)(2,1)S(1)}, bf16[40,1280]{1,0:T(8,128)(2,1)S(1)}, u32[]{:S(2)}, u32[]{:S(2)}) collective-permute-start(bf16[40,1280]{1,0:T(8,128)(2,1)S(1)} %concatenate.10), channel_id=1, source_target_pairs={{0,64},{32,96},{64,0},{96,32},{1,65},{33,97},{65,1},{97,33},{2,66}... | collective-permute-start | bytes 307208 | tf_op jit(solution)/shard_map/basis_g_x/ppermute | solution.py:134
  23.5 14.9 %collective-permute-start.6 = (bf16[9,16,960]{2,1,0:T(8,128)(2,1)S(1)}, bf16[9,16,960]{2,1,0:T(8,128)(2,1)S(1)}, u32[]{:S(2)}, u32[]{:S(2)}) collective-permute-start(bf16[9,16,960]{2,1,0:T(8,128)(2,1)S(1)} %pad_maximum_fusion.2), channel_id=1, source_target_pairs={{0,8},{8,16},{16,24},{24,0},{1,9},{9,17},{17,25},{25,1},{2,10},{10... | collective-permute-start | bytes 829448 | tf_op jit(solution)/shard_map/basis_a_y/ppermute | solution.py:134
  24.8 15.5 %collective-permute-start.7 = (bf16[9,16,960]{2,1,0:T(8,128)(2,1)S(1)}, bf16[9,16,960]{2,1,0:T(8,128)(2,1)}, u32[]{:S(2)}, u32[]{:S(2)}) collective-permute-start(bf16[9,16,960]{2,1,0:T(8,128)(2,1)S(1)} %pad_maximum_fusion.2), channel_id=1, source_target_pairs={{0,16},{8,24},{16,0},{24,8},{1,17},{9,25},{17,1},{25,9},{2,18},{10... | collective-permute-start | bytes 829448 | tf_op jit(solution)/shard_map/basis_a_y/ppermute | solution.py:134
  27.4 12.9 %collective-permute-start.8 = (bf16[9,16,960]{2,1,0:T(8,128)(2,1)S(1)}, bf16[9,16,960]{2,1,0:T(8,128)(2,1)}, u32[]{:S(2)}, u32[]{:S(2)}) collective-permute-start(bf16[9,16,960]{2,1,0:T(8,128)(2,1)S(1)} %pad_maximum_fusion.2), channel_id=1, source_target_pairs={{0,24},{8,0},{16,8},{24,16},{1,25},{9,1},{17,9},{25,17},{2,26},{10... | collective-permute-start | bytes 829448 | tf_op jit(solution)/shard_map/basis_a_y/ppermute | solution.py:134
  28.9 3.8 %collective-permute-start.11 = (bf16[40,1280]{1,0:T(8,128)(2,1)S(1)}, bf16[40,1280]{1,0:T(8,128)(2,1)S(1)}, u32[]{:S(2)}, u32[]{:S(2)}) collective-permute-start(bf16[40,1280]{1,0:T(8,128)(2,1)S(1)} %concatenate.10), channel_id=1, source_target_pairs={{0,96},{32,0},{64,32},{96,64},{1,97},{33,1},{65,33},{97,65},{2,98}... | collective-permute-start | bytes 307208 | tf_op jit(solution)/shard_map/basis_g_x/ppermute | solution.py:134
  32.7 5.7 %collective-permute-start.9 = (bf16[40,1280]{1,0:T(8,128)(2,1)S(1)}, bf16[40,1280]{1,0:T(8,128)(2,1)}, u32[]{:S(2)}, u32[]{:S(2)}) collective-permute-start(bf16[40,1280]{1,0:T(8,128)(2,1)S(1)} %concatenate.10), channel_id=1, source_target_pairs={{0,32},{32,64},{64,96},{96,0},{1,33},{33,65},{65,97},{97,1},{2,34}... | collective-permute-start | bytes 307208 | tf_op jit(solution)/shard_map/basis_g_x/ppermute | solution.py:134
  41.3 21.1 %collective-permute-start.14 = (bf16[4,40,1280]{2,1,0:T(8,128)(2,1)S(1)}, bf16[4,40,1280]{2,1,0:T(8,128)(2,1)S(1)}, u32[]{:S(2)}, u32[]{:S(2)}) collective-permute-start(bf16[4,40,1280]{2,1,0:T(8,128)(2,1)S(1)} %pad_maximum_fusion.1.refs_4_), channel_id=1, source_target_pairs={{0,8},{8,16},{16,24},{24,0},{1,9},{9,17},{17,25},{25,1},{2,10},{10... | collective-permute-start | bytes 1228808 | tf_op jit(solution)/shard_map/basis_g_y/ppermute | solution.py:134
  42.4 20.2 %collective-permute-start.15 = (bf16[4,40,1280]{2,1,0:T(8,128)(2,1)S(1)}, bf16[4,40,1280]{2,1,0:T(8,128)(2,1)S(1)}, u32[]{:S(2)}, u32[]{:S(2)}) collective-permute-start(bf16[4,40,1280]{2,1,0:T(8,128)(2,1)S(1)} %pad_maximum_fusion.1.refs_4_), channel_id=1, source_target_pairs={{0,16},{8,24},{16,0},{24,8},{1,17},{9,25},{17,1},{25,9},{2,18},{10... | collective-permute-start | bytes 1228808 | tf_op jit(solution)/shard_map/basis_g_y/ppermute | solution.py:134
  45.3 18.6 %collective-permute-start.16 = (bf16[4,40,1280]{2,1,0:T(8,128)(2,1)S(1)}, bf16[4,40,1280]{2,1,0:T(8,128)(2,1)}, u32[]{:S(2)}, u32[]{:S(2)}) collective-permute-start(bf16[4,40,1280]{2,1,0:T(8,128)(2,1)S(1)} %pad_maximum_fusion.1.refs_4_), channel_id=1, source_target_pairs={{0,24},{8,0},{16,8},{24,16},{1,25},{9,1},{17,9},{25,17},{2,26},{10... | collective-permute-start | bytes 1228808 | tf_op jit(solution)/shard_map/basis_g_y/ppermute | solution.py:134
  61.2 6.7 %collective-permute-start.17 = (bf16[4,64,512]{2,1,0:T(8,128)(2,1)}, bf16[4,64,512]{2,1,0:T(8,128)(2,1)}, u32[]{:S(2)}, u32[]{:S(2)}) collective-permute-start(bf16[4,64,512]{2,1,0:T(8,128)(2,1)} %get-tuple-element.61), channel_id=1, source_target_pairs={{0,1},{1,2},{2,3},{3,0},{4,5},{5,6},{6,7},{7,4},{8,9},{9,10},{10,1... | collective-permute-start | bytes 786440 | tf_op jit(solution)/shard_map/coeff_parts/ppermute | solution.py:134
  67.9 20.9 %collective-permute-start.19 = (bf16[8,320,512]{2,1,0:T(8,128)(2,1)S(1)}, bf16[8,320,512]{2,1,0:T(8,128)(2,1)}, u32[]{:S(2)}, u32[]{:S(2)}) collective-permute-start(bf16[8,320,512]{2,1,0:T(8,128)(2,1)S(1)} %all-to-all-done.refs_2_), channel_id=1, source_target_pairs={{0,4},{4,0},{1,5},{5,1},{2,6},{6,2},{3,7},{7,3},{8,12},{12,8},{9,1... | collective-permute-start | bytes 7864328 | tf_op jit(solution)/shard_map/exchange_cores/ppermute | solution.py:134
  71.9 9.8 %collective-permute-start.13 = (bf16[4,64,512]{2,1,0:T(8,128)(2,1)}, bf16[4,64,512]{2,1,0:T(8,128)(2,1)}, u32[]{:S(2)}, u32[]{:S(2)}) collective-permute-start(bf16[4,64,512]{2,1,0:T(8,128)(2,1)} %copy-done.6), channel_id=1, source_target_pairs={{0,2},{1,3},{2,0},{3,1},{4,6},{5,7},{6,4},{7,5},{8,10},{9,11},{10,... | collective-permute-start | bytes 786440 | tf_op jit(solution)/shard_map/coeff_parts/ppermute | solution.py:134
  73.6 12.7 %collective-permute-start.18 = (bf16[4,64,512]{2,1,0:T(8,128)(2,1)}, bf16[4,64,512]{2,1,0:T(8,128)(2,1)}, u32[]{:S(2)}, u32[]{:S(2)}) collective-permute-start(bf16[4,64,512]{2,1,0:T(8,128)(2,1)} %copy-done.5), channel_id=1, source_target_pairs={{0,3},{1,0},{2,1},{3,2},{4,7},{5,4},{6,5},{7,6},{8,11},{9,8},{10,9... | collective-permute-start | bytes 786440 | tf_op jit(solution)/shard_map/coeff_parts/ppermute | solution.py:134
  74.5 14.0 %collective-permute-start.20 = (bf16[4,40,1280]{2,1,0:T(8,128)(2,1)S(1)}, bf16[4,40,1280]{2,1,0:T(8,128)(2,1)}, u32[]{:S(2)}, u32[]{:S(2)}) collective-permute-start(bf16[4,40,1280]{2,1,0:T(8,128)(2,1)S(1)} %pad_maximum_fusion.1.refs_4_), channel_id=1, source_target_pairs={{0,4},{4,0},{1,5},{5,1},{2,6},{6,2},{3,7},{7,3},{8,12},{12,8},{9,1... | collective-permute-start | bytes 1228808 | tf_op jit(solution)/shard_map/exchange_cores/ppermute | solution.py:134
  75.1 13.4 %collective-permute-start.21 = (bf16[4,40,1280]{2,1,0:T(8,128)(2,1)}, bf16[4,40,1280]{2,1,0:T(8,128)(2,1)}, u32[]{:S(2)}, u32[]{:S(2)}) collective-permute-start(bf16[4,40,1280]{2,1,0:T(8,128)(2,1)} %copy-done.1), channel_id=1, source_target_pairs={{0,4},{4,0},{1,5},{5,1},{2,6},{6,2},{3,7},{7,3},{8,12},{12,8},{9,1... | collective-permute-start | bytes 1228808 | tf_op jit(solution)/shard_map/exchange_cores/ppermute | solution.py:134
  81.6 6.9 %collective-permute-start.22 = (bf16[4,40,1280]{2,1,0:T(8,128)(2,1)}, bf16[4,40,1280]{2,1,0:T(8,128)(2,1)}, u32[]{:S(2)}, u32[]{:S(2)}) collective-permute-start(bf16[4,40,1280]{2,1,0:T(8,128)(2,1)} %copy-done.3), channel_id=1, source_target_pairs={{0,4},{4,0},{1,5},{5,1},{2,6},{6,2},{3,7},{7,3},{8,12},{12,8},{9,1... | collective-permute-start | bytes 1228808 | tf_op jit(solution)/shard_map/exchange_cores/ppermute | solution.py:134
  (11 other events, 38.1 us)

commit v6 on v5

--- a/solution.py
+++ b/solution.py
@@ -175,9 +175,11 @@
         *sent, mine = parts((2, 1, 3, 0), (bf16, bf16, bf16, jnp.float32))
         received = [shift(v, "z", s) for v, s in zip(sent, (2, 1, 3))]
     with jax.named_scope("exchange_cores"):
-        g, bg, received[1] = lax.optimization_barrier((g, bg, received[1]))
+        g, bg, _ = lax.optimization_barrier((g, bg, sent[0]))
         g_oth = shift(g, "core", 1)
-        bg_oth = [shift(v, "core", 1) for v in bg]
+        first = shift(bg[0], "core", 1)
+        rest, first = lax.optimization_barrier((bg[1:], first))
+        bg_oth = [first] + [shift(v, "core", 1) for v in rest]
 
     total_coeff = mine
     for r in received:

time: 117 us -> 111 us (0.949)
  waiting for transfers between devices: 26 us -> 18.9 us
  starting transfers between devices: 42 us -> 44.9 us
  local copies, waits for them, and re-layouts: 6.99 us -> 8.62 us
  blocking collectives: 17.7 us -> 16.1 us
    ppermute x24, waiting for transfers between devices: 26 us -> 18.9 us  [shift(): return lax.ppermute(v, axis, [(i, (i + s) % n) for i in range(n)])]
    ppermute x24, starting transfers between devices: 37.9 us -> 40.9 us  [shift(): return lax.ppermute(v, axis, [(i, (i + s) % n) for i in range(n)])]
    unnamed x20, local copies, waits for them, and re-layouts: 4.85 us -> 6.48 us
    all_to_all x1, blocking collectives: 17.7 us -> 16.1 us  [body(): got = lax.all_to_all(rows, ('x', 'y', 'z'), 0, 0, tiled=True)]
  transfers between devices with their start and end apart: 25 -> 25, of which waited for: 11 -> 9; matrix products, arithmetic and copies ran while one was open for 3% -> 3% of each run, Pallas kernels for 11% -> 11%
where the time goes in v6:
time: 111 us
  starting transfers between devices  44.9 us (40%)
  waiting for transfers between devices  18.9 us (17%)
  Pallas kernels  18.7 us (17%)
  blocking collectives  16.1 us (15%)
  local copies, waits for them, and re-layouts  8.62 us (8%)
  other arithmetic  3.14 us (3%)
    ppermute x24, starting transfers between devices, shift(): return lax.ppermute(v, axis, [(i, (i + s) % n) for i in range(n)])  40.9 us
    ppermute x24, waiting for transfers between devices, shift(): return lax.ppermute(v, axis, [(i, (i + s) % n) for i in range(n)])  18.9 us
    all_to_all x1, blocking collectives, body(): got = lax.all_to_all(rows, ('x', 'y', 'z'), 0, 0, tiled=True)  16.1 us
    pallas_call x1, Pallas kernels, conv(): pl.pallas_call(conv_kernel, out_shape=[jax.ShapeDtypeStruct((2 * per, ran...  12.5 us
    unnamed x20, local copies, waits for them, and re-layouts  6.48 us
    pallas_call x1, Pallas kernels, squares(): pl.pallas_call(kernel, out_shape=jax.ShapeDtypeStruct((chips, ranks // ch...  6.26 us
    all_to_all x1, starting transfers between devices, body(): g = lax.all_to_all(grads, 'z', 0, 0, tiled=True)  4.08 us
  transfers between devices with their start and end apart: 25, of which 9 were waited for; matrix products, arithmetic and copies ran while one was open for 3% of the time, Pallas kernels for 11%

profile of v6, /device:TPU:1, one launch (start us, length us, event | category | flops | bytes accessed | tf_op | source)
XLA Modules:
  0.0 110.6 jit_solution(9120842680231481332)
XLA Ops:
  1.0 2.1 %collective-permute-start.3 = (bf16[9,4,960]{2,1,0:T(4,128)(2,1)S(1)}, bf16[9,4,960]{2,1,0:T(4,128)(2,1)S(1)}, u32[]{:S(2)}, u32[]{:S(2)}) collective-permute-start(bf16[9,4,960]{2,1,0:T(4,128)(2,1)S(1)} %reshape.11), channel_id=1, source_target_pairs={{0,32},{32,64},{64,96},{96,0},{1,33},{33,65},{65,97},{97,1},{2,34}... | collective-permute-start | bytes 207368 | tf_op jit(solution)/shard_map/basis_a_x/ppermute | solution.py:134
  3.2 2.5 %collective-permute-start.4 = (bf16[9,4,960]{2,1,0:T(4,128)(2,1)S(1)}, bf16[9,4,960]{2,1,0:T(4,128)(2,1)S(1)}, u32[]{:S(2)}, u32[]{:S(2)}) collective-permute-start(bf16[9,4,960]{2,1,0:T(4,128)(2,1)S(1)} %reshape.11), channel_id=1, source_target_pairs={{0,64},{32,96},{64,0},{96,32},{1,65},{33,97},{65,1},{97,33},{2,66}... | collective-permute-start | bytes 207368 | tf_op jit(solution)/shard_map/basis_a_x/ppermute | solution.py:134
  6.8 1.6 %collective-permute-start = (bf16[40,320]{1,0:T(8,128)(2,1)}, bf16[40,320]{1,0:T(8,128)(2,1)S(1)}, u32[]{:S(2)}, u32[]{:S(2)}) collective-permute-start(bf16[40,320]{1,0:T(8,128)(2,1)} %bitcast.28), channel_id=1, source_target_pairs={{0,1},{1,2},{2,3},{3,0},{4,5},{5,6},{6,7},{7,4},{8,9},{9,10},{10,1... | collective-permute-start | bytes 76808 | tf_op jit(solution)/shard_map/basis_g_z/ppermute | solution.py:134
  8.4 3.3 %collective-permute-start.1 = (bf16[40,320]{1,0:T(8,128)(2,1)}, bf16[40,320]{1,0:T(8,128)(2,1)S(1)}, u32[]{:S(2)}, u32[]{:S(2)}) collective-permute-start(bf16[40,320]{1,0:T(8,128)(2,1)} %bitcast.29), channel_id=1, source_target_pairs={{0,2},{1,3},{2,0},{3,1},{4,6},{5,7},{6,4},{7,5},{8,10},{9,11},{10,... | collective-permute-start | bytes 76808 | tf_op jit(solution)/shard_map/basis_g_z/ppermute | solution.py:134
  12.0 1.8 %collective-permute-start.2 = (bf16[40,320]{1,0:T(8,128)(2,1)}, bf16[40,320]{1,0:T(8,128)(2,1)S(1)}, u32[]{:S(2)}, u32[]{:S(2)}) collective-permute-start(bf16[40,320]{1,0:T(8,128)(2,1)} %bitcast.30), channel_id=1, source_target_pairs={{0,3},{1,0},{2,1},{3,2},{4,7},{5,4},{6,5},{7,6},{8,11},{9,8},{10,9... | collective-permute-start | bytes 76808 | tf_op jit(solution)/shard_map/basis_g_z/ppermute | solution.py:134
  13.8 1.5 %collective-permute-done.2 = bf16[40,320]{1,0:T(8,128)(2,1)S(1)} collective-permute-done((bf16[40,320]{1,0:T(8,128)(2,1)}, bf16[40,320]{1,0:T(8,128)(2,1)S(1)}, u32[]{:S(2)}, u32[]{:S(2)}) %collective-permute-start.2) | collective-permute-done | bytes 25632 | tf_op jit(solution)/shard_map/basis_g_z/ppermute | solution.py:134
  15.5 3.5 %collective-permute-start.12 = (bf16[8,320,512]{2,1,0:T(8,128)(2,1)}, bf16[8,320,512]{2,1,0:T(8,128)(2,1)}, u32[]{:S(2)}, u32[]{:S(2)}) collective-permute-start(bf16[8,320,512]{2,1,0:T(8,128)(2,1)} %bitcast.19), channel_id=1, source_target_pairs={{0,4},{4,0},{1,5},{5,1},{2,6},{6,2},{3,7},{7,3},{8,12},{12,8},{9,1... | collective-permute-start | bytes 7864328 | tf_op jit(solution)/shard_map/basis_a_y/ppermute | solution.py:134
  18.9 4.1 %all-to-all-start = ((bf16[8,320,512]{2,1,0:T(8,128)(2,1)}), bf16[8,320,512]{2,1,0:T(8,128)(2,1)S(1)}, u32[]{:S(2)}, u32[]{:S(2)}) async-start(bf16[8,320,512]{2,1,0:T(8,128)(2,1)} %bitcast.21), calls=%async_computation | async-start | bytes 5242880 | tf_op jit(solution)/shard_map/exchange_grads/all_to_all | solution.py:158
  24.8 2.6 %collective-permute-start.7 = (bf16[9,16,960]{2,1,0:T(8,128)(2,1)S(1)}, bf16[9,16,960]{2,1,0:T(8,128)(2,1)S(1)}, u32[]{:S(2)}, u32[]{:S(2)}) collective-permute-start(bf16[9,16,960]{2,1,0:T(8,128)(2,1)S(1)} %pad_maximum_fusion.2), channel_id=1, source_target_pairs={{0,16},{8,24},{16,0},{24,8},{1,17},{9,25},{17,1},{25,9},{2,18},{10... | collective-permute-start | bytes 829448 | tf_op jit(solution)/shard_map/basis_a_y/ppermute | solution.py:134
  29.1 4.5 %collective-permute-done.10 = bf16[40,1280]{1,0:T(8,128)(2,1)S(1)} collective-permute-done((bf16[40,1280]{1,0:T(8,128)(2,1)S(1)}, bf16[40,1280]{1,0:T(8,128)(2,1)S(1)}, u32[]{:S(2)}, u32[]{:S(2)}) %collective-permute-start.10) | collective-permute-done | bytes 102432 | tf_op jit(solution)/shard_map/basis_g_x/ppermute | solution.py:134
  33.6 2.3 %collective-permute-start.11 = (bf16[40,1280]{1,0:T(8,128)(2,1)S(1)}, bf16[40,1280]{1,0:T(8,128)(2,1)S(1)}, u32[]{:S(2)}, u32[]{:S(2)}) collective-permute-start(bf16[40,1280]{1,0:T(8,128)(2,1)S(1)} %concatenate.10), channel_id=1, source_target_pairs={{0,96},{32,0},{64,32},{96,64},{1,97},{33,1},{65,33},{97,65},{2,98}... | collective-permute-start | bytes 307208 | tf_op jit(solution)/shard_map/basis_g_x/ppermute | solution.py:134
  35.9 1.7 %collective-permute-done.11 = bf16[40,1280]{1,0:T(8,128)(2,1)S(1)} collective-permute-done((bf16[40,1280]{1,0:T(8,128)(2,1)S(1)}, bf16[40,1280]{1,0:T(8,128)(2,1)S(1)}, u32[]{:S(2)}, u32[]{:S(2)}) %collective-permute-start.11) | collective-permute-done | bytes 102432 | tf_op jit(solution)/shard_map/basis_g_x/ppermute | solution.py:134
  37.6 2.7 %collective-permute-done.7 = bf16[9,16,960]{2,1,0:T(8,128)(2,1)S(1)} collective-permute-done((bf16[9,16,960]{2,1,0:T(8,128)(2,1)S(1)}, bf16[9,16,960]{2,1,0:T(8,128)(2,1)S(1)}, u32[]{:S(2)}, u32[]{:S(2)}) %collective-permute-start.7) | collective-permute-done | bytes 276512 | tf_op jit(solution)/shard_map/basis_a_y/ppermute | solution.py:134
  42.1 3.0 %collective-permute-start.17 = (bf16[4,40,1280]{2,1,0:T(8,128)(2,1)S(1)}, bf16[4,40,1280]{2,1,0:T(8,128)(2,1)}, u32[]{:S(2)}, u32[]{:S(2)}) collective-permute-start(bf16[4,40,1280]{2,1,0:T(8,128)(2,1)S(1)} %pad_maximum_fusion.1.refs_4_), channel_id=1, source_target_pairs={{0,16},{8,24},{16,0},{24,8},{1,17},{9,25},{17,1},{25,9},{2,18},{10... | collective-permute-start | bytes 1228808 | tf_op jit(solution)/shard_map/basis_g_y/ppermute | solution.py:134
  46.6 1.7 %copy-done = bf16[8,512,320]{1,2,0:T(8,128)(2,1)S(1)} copy-done((bf16[8,512,320]{1,2,0:T(8,128)(2,1)S(1)}, bf16[8,512,320]{1,2,0:T(8,128)(2,1)}, u32[]{:S(2)}) %copy-start) | copy-done | bytes 2621464
  48.3 12.5 %conv_taps.1 = (bf16[4,64,512]{2,1,0:T(8,128)(2,1)S(1)}, bf16[4,64,512]{2,1,0:T(8,128)(2,1)S(1)}, bf16[4,64,512]{2,1,0:T(8,128)(2,1)S(1)}, f32[4,64,512]{2,1,0:T(8,128)S(1)}) custom-call(s32[4]{0:T(128)S(1)} %pad_add_fusion.1.idx_ref, bf16[9,64,960]{2,1,0:T(8,128)(2,1)S(1)} %pad_maximum_fusion.b_ref, bf16[8,320,512]{2,1,0:T(8,128)(2,1)S(1)} %bitcast.20, ...), custom_call_target="tpu_custom_call" | custom-call | tf_op jit(solution)/shard_map/coeff_parts/conv_taps/pallas_call | solution.py:59
  63.0 2.6 %collective-permute-start.19 = (bf16[8,320,512]{2,1,0:T(8,128)(2,1)S(1)}, bf16[8,320,512]{2,1,0:T(8,128)(2,1)}, u32[]{:S(2)}, u32[]{:S(2)}) collective-permute-start(bf16[8,320,512]{2,1,0:T(8,128)(2,1)S(1)} %all-to-all-done.refs_2_), channel_id=1, source_target_pairs={{0,4},{4,0},{1,5},{5,1},{2,6},{6,2},{3,7},{7,3},{8,12},{12,8},{9,1... | collective-permute-start | bytes 7864328 | tf_op jit(solution)/shard_map/exchange_cores/ppermute | solution.py:134
  65.7 2.7 %collective-permute-start.15 = (bf16[4,64,512]{2,1,0:T(8,128)(2,1)}, bf16[4,64,512]{2,1,0:T(8,128)(2,1)}, u32[]{:S(2)}, u32[]{:S(2)}) collective-permute-start(bf16[4,64,512]{2,1,0:T(8,128)(2,1)} %copy-done.5), channel_id=1, source_target_pairs={{0,3},{1,0},{2,1},{3,2},{4,7},{5,4},{6,5},{7,6},{8,11},{9,8},{10,9... | collective-permute-start | bytes 786440 | tf_op jit(solution)/shard_map/coeff_parts/ppermute | solution.py:134
  68.4 1.8 %collective-permute-start.13 = (bf16[4,64,512]{2,1,0:T(8,128)(2,1)}, bf16[4,64,512]{2,1,0:T(8,128)(2,1)}, u32[]{:S(2)}, u32[]{:S(2)}) collective-permute-start(bf16[4,64,512]{2,1,0:T(8,128)(2,1)} %copy-done.3), channel_id=1, source_target_pairs={{0,2},{1,3},{2,0},{3,1},{4,6},{5,7},{6,4},{7,5},{8,10},{9,11},{10,... | collective-permute-start | bytes 786440 | tf_op jit(solution)/shard_map/coeff_parts/ppermute | solution.py:134
  72.2 7.3 %collective-permute-done.15 = bf16[4,64,512]{2,1,0:T(8,128)(2,1)} collective-permute-done((bf16[4,64,512]{2,1,0:T(8,128)(2,1)}, bf16[4,64,512]{2,1,0:T(8,128)(2,1)}, u32[]{:S(2)}, u32[]{:S(2)}) %collective-permute-start.15) | collective-permute-done | bytes 262176 | tf_op jit(solution)/shard_map/coeff_parts/ppermute | solution.py:134
  79.5 1.4 %collective-permute-start.22 = (bf16[4,40,1280]{2,1,0:T(8,128)(2,1)}, bf16[4,40,1280]{2,1,0:T(8,128)(2,1)}, u32[]{:S(2)}, u32[]{:S(2)}) collective-permute-start(bf16[4,40,1280]{2,1,0:T(8,128)(2,1)} %collective-permute-done.17.refs_6_), channel_id=1, source_target_pairs={{0,4},{4,0},{1,5},{5,1},{2,6},{6,2},{3,7},{7,3},{8,12},{12,8},{9,1... | collective-permute-start | bytes 1228808 | tf_op jit(solution)/shard_map/exchange_cores/ppermute | solution.py:134
  80.9 3.4 %collective-permute-start.23 = (bf16[4,40,1280]{2,1,0:T(8,128)(2,1)}, bf16[4,40,1280]{2,1,0:T(8,128)(2,1)}, u32[]{:S(2)}, u32[]{:S(2)}) collective-permute-start(bf16[4,40,1280]{2,1,0:T(8,128)(2,1)} %collective-permute-done.18.refs_7_), channel_id=1, source_target_pairs={{0,4},{4,0},{1,5},{5,1},{2,6},{6,2},{3,7},{7,3},{8,12},{12,8},{9,1... | collective-permute-start | bytes 1228808 | tf_op jit(solution)/shard_map/exchange_cores/ppermute | solution.py:134
  87.0 6.3 %squared_sums.1 = f32[16,4,1280]{2,1,0:T(4,128)S(1)} custom-call(s32[4]{0:T(128)S(1)} %pad_add_fusion.refs_0_, f32[4,64,512]{2,1,0:T(8,128)S(1)} %convert_add_fusion.refs_1_, bf16[8,320,512]{2,1,0:T(8,128)(2,1)S(1)} %all-to-all-done.refs_2_, bf16[8,320,512]{2,1,0:T(8,128)(2,1)} %collective-permute-done.19.refs_3_, ...), custom_call_target="tpu_custom_call" | custom-call | tf_op jit(solution)/shard_map/squared_sums/pallas_call | solution.py:117
  93.7 16.1 %all_to_all.10 = f32[64,1,1280]{2,1,0:T(1,128)S(1)} all-to-all(f32[64,1,1280]{2,1,0:T(1,128)S(1)} %reshape.13), channel_id=1, replica_groups=mesh['x'=4,'y'=4,'core'=2,'z'=4] {'x','y','z'}, dimensions={0} | all-to-all | bytes 655360 | tf_op jit(solution)/shard_map/sum_examples/all_to_all | solution.py:192
  (61 shorter events, 17.7 us)
Async XLA Ops:
  1.0 14.2 %collective-permute-start.3 = (bf16[9,4,960]{2,1,0:T(4,128)(2,1)S(1)}, bf16[9,4,960]{2,1,0:T(4,128)(2,1)S(1)}, u32[]{:S(2)}, u32[]{:S(2)}) collective-permute-start(bf16[9,4,960]{2,1,0:T(4,128)(2,1)S(1)} %reshape.11), channel_id=1, source_target_pairs={{0,32},{32,64},{64,96},{96,0},{1,33},{33,65},{65,97},{97,1},{2,34}... | collective-permute-start | bytes 207368 | tf_op jit(solution)/shard_map/basis_a_x/ppermute | solution.py:134
  3.2 12.1 %collective-permute-start.4 = (bf16[9,4,960]{2,1,0:T(4,128)(2,1)S(1)}, bf16[9,4,960]{2,1,0:T(4,128)(2,1)S(1)}, u32[]{:S(2)}, u32[]{:S(2)}) collective-permute-start(bf16[9,4,960]{2,1,0:T(4,128)(2,1)S(1)} %reshape.11), channel_id=1, source_target_pairs={{0,64},{32,96},{64,0},{96,32},{1,65},{33,97},{65,1},{97,33},{2,66}... | collective-permute-start | bytes 207368 | tf_op jit(solution)/shard_map/basis_a_x/ppermute | solution.py:134
  5.6 9.7 %collective-permute-start.5 = (bf16[9,4,960]{2,1,0:T(4,128)(2,1)S(1)}, bf16[9,4,960]{2,1,0:T(4,128)(2,1)S(1)}, u32[]{:S(2)}, u32[]{:S(2)}) collective-permute-start(bf16[9,4,960]{2,1,0:T(4,128)(2,1)S(1)} %reshape.11), channel_id=1, source_target_pairs={{0,96},{32,0},{64,32},{96,64},{1,97},{33,1},{65,33},{97,65},{2,98}... | collective-permute-start | bytes 207368 | tf_op jit(solution)/shard_map/basis_a_x/ppermute | solution.py:134
  6.8 5.2 %collective-permute-start = (bf16[40,320]{1,0:T(8,128)(2,1)}, bf16[40,320]{1,0:T(8,128)(2,1)S(1)}, u32[]{:S(2)}, u32[]{:S(2)}) collective-permute-start(bf16[40,320]{1,0:T(8,128)(2,1)} %bitcast.28), channel_id=1, source_target_pairs={{0,1},{1,2},{2,3},{3,0},{4,5},{5,6},{6,7},{7,4},{8,9},{9,10},{10,1... | collective-permute-start | bytes 76808 | tf_op jit(solution)/shard_map/basis_g_z/ppermute | solution.py:134
  8.4 5.4 %collective-permute-start.1 = (bf16[40,320]{1,0:T(8,128)(2,1)}, bf16[40,320]{1,0:T(8,128)(2,1)S(1)}, u32[]{:S(2)}, u32[]{:S(2)}) collective-permute-start(bf16[40,320]{1,0:T(8,128)(2,1)} %bitcast.29), channel_id=1, source_target_pairs={{0,2},{1,3},{2,0},{3,1},{4,6},{5,7},{6,4},{7,5},{8,10},{9,11},{10,... | collective-permute-start | bytes 76808 | tf_op jit(solution)/shard_map/basis_g_z/ppermute | solution.py:134
  15.5 31.1 %collective-permute-start.12 = (bf16[8,320,512]{2,1,0:T(8,128)(2,1)}, bf16[8,320,512]{2,1,0:T(8,128)(2,1)}, u32[]{:S(2)}, u32[]{:S(2)}) collective-permute-start(bf16[8,320,512]{2,1,0:T(8,128)(2,1)} %bitcast.19), channel_id=1, source_target_pairs={{0,4},{4,0},{1,5},{5,1},{2,6},{6,2},{3,7},{7,3},{8,12},{12,8},{9,1... | collective-permute-start | bytes 7864328 | tf_op jit(solution)/shard_map/basis_a_y/ppermute | solution.py:134
  18.9 44.1 %all-to-all-start = ((bf16[8,320,512]{2,1,0:T(8,128)(2,1)}), bf16[8,320,512]{2,1,0:T(8,128)(2,1)S(1)}, u32[]{:S(2)}, u32[]{:S(2)}) async-start(bf16[8,320,512]{2,1,0:T(8,128)(2,1)} %bitcast.21), calls=%async_computation | async-start | bytes 5242880 | tf_op jit(solution)/shard_map/exchange_grads/all_to_all | solution.py:158
  23.1 5.4 %collective-permute-start.9 = (bf16[40,1280]{1,0:T(8,128)(2,1)S(1)}, bf16[40,1280]{1,0:T(8,128)(2,1)S(1)}, u32[]{:S(2)}, u32[]{:S(2)}) collective-permute-start(bf16[40,1280]{1,0:T(8,128)(2,1)S(1)} %concatenate.10), channel_id=1, source_target_pairs={{0,32},{32,64},{64,96},{96,0},{1,33},{33,65},{65,97},{97,1},{2,34}... | collective-permute-start | bytes 307208 | tf_op jit(solution)/shard_map/basis_g_x/ppermute | solution.py:134
  23.5 14.1 %collective-permute-start.6 = (bf16[9,16,960]{2,1,0:T(8,128)(2,1)S(1)}, bf16[9,16,960]{2,1,0:T(8,128)(2,1)S(1)}, u32[]{:S(2)}, u32[]{:S(2)}) collective-permute-start(bf16[9,16,960]{2,1,0:T(8,128)(2,1)S(1)} %pad_maximum_fusion.2), channel_id=1, source_target_pairs={{0,8},{8,16},{16,24},{24,0},{1,9},{9,17},{17,25},{25,1},{2,10},{10... | collective-permute-start | bytes 829448 | tf_op jit(solution)/shard_map/basis_a_y/ppermute | solution.py:134
  24.8 15.4 %collective-permute-start.7 = (bf16[9,16,960]{2,1,0:T(8,128)(2,1)S(1)}, bf16[9,16,960]{2,1,0:T(8,128)(2,1)S(1)}, u32[]{:S(2)}, u32[]{:S(2)}) collective-permute-start(bf16[9,16,960]{2,1,0:T(8,128)(2,1)S(1)} %pad_maximum_fusion.2), channel_id=1, source_target_pairs={{0,16},{8,24},{16,0},{24,8},{1,17},{9,25},{17,1},{25,9},{2,18},{10... | collective-permute-start | bytes 829448 | tf_op jit(solution)/shard_map/basis_a_y/ppermute | solution.py:134
  27.4 12.8 %collective-permute-start.8 = (bf16[9,16,960]{2,1,0:T(8,128)(2,1)S(1)}, bf16[9,16,960]{2,1,0:T(8,128)(2,1)S(1)}, u32[]{:S(2)}, u32[]{:S(2)}) collective-permute-start(bf16[9,16,960]{2,1,0:T(8,128)(2,1)S(1)} %pad_maximum_fusion.2), channel_id=1, source_target_pairs={{0,24},{8,0},{16,8},{24,16},{1,25},{9,1},{17,9},{25,17},{2,26},{10... | collective-permute-start | bytes 829448 | tf_op jit(solution)/shard_map/basis_a_y/ppermute | solution.py:134
  28.6 5.0 %collective-permute-start.10 = (bf16[40,1280]{1,0:T(8,128)(2,1)S(1)}, bf16[40,1280]{1,0:T(8,128)(2,1)S(1)}, u32[]{:S(2)}, u32[]{:S(2)}) collective-permute-start(bf16[40,1280]{1,0:T(8,128)(2,1)S(1)} %concatenate.10), channel_id=1, source_target_pairs={{0,64},{32,96},{64,0},{96,32},{1,65},{33,97},{65,1},{97,33},{2,66}... | collective-permute-start | bytes 307208 | tf_op jit(solution)/shard_map/basis_g_x/ppermute | solution.py:134
  33.6 4.0 %collective-permute-start.11 = (bf16[40,1280]{1,0:T(8,128)(2,1)S(1)}, bf16[40,1280]{1,0:T(8,128)(2,1)S(1)}, u32[]{:S(2)}, u32[]{:S(2)}) collective-permute-start(bf16[40,1280]{1,0:T(8,128)(2,1)S(1)} %concatenate.10), channel_id=1, source_target_pairs={{0,96},{32,0},{64,32},{96,64},{1,97},{33,1},{65,33},{97,65},{2,98}... | collective-permute-start | bytes 307208 | tf_op jit(solution)/shard_map/basis_g_x/ppermute | solution.py:134
  41.1 21.8 %collective-permute-start.16 = (bf16[4,40,1280]{2,1,0:T(8,128)(2,1)S(1)}, bf16[4,40,1280]{2,1,0:T(8,128)(2,1)}, u32[]{:S(2)}, u32[]{:S(2)}) collective-permute-start(bf16[4,40,1280]{2,1,0:T(8,128)(2,1)S(1)} %pad_maximum_fusion.1.refs_4_), channel_id=1, source_target_pairs={{0,8},{8,16},{16,24},{24,0},{1,9},{9,17},{17,25},{25,1},{2,10},{10... | collective-permute-start | bytes 1228808 | tf_op jit(solution)/shard_map/basis_g_y/ppermute | solution.py:134
  42.1 20.9 %collective-permute-start.17 = (bf16[4,40,1280]{2,1,0:T(8,128)(2,1)S(1)}, bf16[4,40,1280]{2,1,0:T(8,128)(2,1)}, u32[]{:S(2)}, u32[]{:S(2)}) collective-permute-start(bf16[4,40,1280]{2,1,0:T(8,128)(2,1)S(1)} %pad_maximum_fusion.1.refs_4_), channel_id=1, source_target_pairs={{0,16},{8,24},{16,0},{24,8},{1,17},{9,25},{17,1},{25,9},{2,18},{10... | collective-permute-start | bytes 1228808 | tf_op jit(solution)/shard_map/basis_g_y/ppermute | solution.py:134
  45.0 18.0 %collective-permute-start.18 = (bf16[4,40,1280]{2,1,0:T(8,128)(2,1)S(1)}, bf16[4,40,1280]{2,1,0:T(8,128)(2,1)}, u32[]{:S(2)}, u32[]{:S(2)}) collective-permute-start(bf16[4,40,1280]{2,1,0:T(8,128)(2,1)S(1)} %pad_maximum_fusion.1.refs_4_), channel_id=1, source_target_pairs={{0,24},{8,0},{16,8},{24,16},{1,25},{9,1},{17,9},{25,17},{2,26},{10... | collective-permute-start | bytes 1228808 | tf_op jit(solution)/shard_map/basis_g_y/ppermute | solution.py:134
  63.0 23.0 %collective-permute-start.19 = (bf16[8,320,512]{2,1,0:T(8,128)(2,1)S(1)}, bf16[8,320,512]{2,1,0:T(8,128)(2,1)}, u32[]{:S(2)}, u32[]{:S(2)}) collective-permute-start(bf16[8,320,512]{2,1,0:T(8,128)(2,1)S(1)} %all-to-all-done.refs_2_), channel_id=1, source_target_pairs={{0,4},{4,0},{1,5},{5,1},{2,6},{6,2},{3,7},{7,3},{8,12},{12,8},{9,1... | collective-permute-start | bytes 7864328 | tf_op jit(solution)/shard_map/exchange_cores/ppermute | solution.py:134
  65.6 5.0 %collective-permute-start.20 = (bf16[4,40,1280]{2,1,0:T(8,128)(2,1)S(1)}, bf16[4,40,1280]{2,1,0:T(8,128)(2,1)S(1)}, u32[]{:S(2)}, u32[]{:S(2)}) collective-permute-start(bf16[4,40,1280]{2,1,0:T(8,128)(2,1)S(1)} %pad_maximum_fusion.1.refs_4_), channel_id=1, source_target_pairs={{0,4},{4,0},{1,5},{5,1},{2,6},{6,2},{3,7},{7,3},{8,12},{12,8},{9,1... | collective-permute-start | bytes 1228808 | tf_op jit(solution)/shard_map/exchange_cores/ppermute | solution.py:134
  65.7 13.7 %collective-permute-start.15 = (bf16[4,64,512]{2,1,0:T(8,128)(2,1)}, bf16[4,64,512]{2,1,0:T(8,128)(2,1)}, u32[]{:S(2)}, u32[]{:S(2)}) collective-permute-start(bf16[4,64,512]{2,1,0:T(8,128)(2,1)} %copy-done.5), channel_id=1, source_target_pairs={{0,3},{1,0},{2,1},{3,2},{4,7},{5,4},{6,5},{7,6},{8,11},{9,8},{10,9... | collective-permute-start | bytes 786440 | tf_op jit(solution)/shard_map/coeff_parts/ppermute | solution.py:134
  68.4 12.5 %collective-permute-start.14 = (bf16[4,64,512]{2,1,0:T(8,128)(2,1)}, bf16[4,64,512]{2,1,0:T(8,128)(2,1)}, u32[]{:S(2)}, u32[]{:S(2)}) collective-permute-start(bf16[4,64,512]{2,1,0:T(8,128)(2,1)} %copy-done.4), channel_id=1, source_target_pairs={{0,1},{1,2},{2,3},{3,0},{4,5},{5,6},{6,7},{7,4},{8,9},{9,10},{10,1... | collective-permute-start | bytes 786440 | tf_op jit(solution)/shard_map/coeff_parts/ppermute | solution.py:134
  68.4 15.9 %collective-permute-start.13 = (bf16[4,64,512]{2,1,0:T(8,128)(2,1)}, bf16[4,64,512]{2,1,0:T(8,128)(2,1)}, u32[]{:S(2)}, u32[]{:S(2)}) collective-permute-start(bf16[4,64,512]{2,1,0:T(8,128)(2,1)} %copy-done.3), channel_id=1, source_target_pairs={{0,2},{1,3},{2,0},{3,1},{4,6},{5,7},{6,4},{7,5},{8,10},{9,11},{10,... | collective-permute-start | bytes 786440 | tf_op jit(solution)/shard_map/coeff_parts/ppermute | solution.py:134
  71.4 14.2 %collective-permute-start.21 = (bf16[4,40,1280]{2,1,0:T(8,128)(2,1)}, bf16[4,40,1280]{2,1,0:T(8,128)(2,1)}, u32[]{:S(2)}, u32[]{:S(2)}) collective-permute-start(bf16[4,40,1280]{2,1,0:T(8,128)(2,1)} %collective-permute-done.16.refs_5_), channel_id=1, source_target_pairs={{0,4},{4,0},{1,5},{5,1},{2,6},{6,2},{3,7},{7,3},{8,12},{12,8},{9,1... | collective-permute-start | bytes 1228808 | tf_op jit(solution)/shard_map/exchange_cores/ppermute | solution.py:134
  79.5 6.2 %collective-permute-start.22 = (bf16[4,40,1280]{2,1,0:T(8,128)(2,1)}, bf16[4,40,1280]{2,1,0:T(8,128)(2,1)}, u32[]{:S(2)}, u32[]{:S(2)}) collective-permute-start(bf16[4,40,1280]{2,1,0:T(8,128)(2,1)} %collective-permute-done.17.refs_6_), channel_id=1, source_target_pairs={{0,4},{4,0},{1,5},{5,1},{2,6},{6,2},{3,7},{7,3},{8,12},{12,8},{9,1... | collective-permute-start | bytes 1228808 | tf_op jit(solution)/shard_map/exchange_cores/ppermute | solution.py:134
  80.9 5.1 %collective-permute-start.23 = (bf16[4,40,1280]{2,1,0:T(8,128)(2,1)}, bf16[4,40,1280]{2,1,0:T(8,128)(2,1)}, u32[]{:S(2)}, u32[]{:S(2)}) collective-permute-start(bf16[4,40,1280]{2,1,0:T(8,128)(2,1)} %collective-permute-done.18.refs_7_), channel_id=1, source_target_pairs={{0,4},{4,0},{1,5},{5,1},{2,6},{6,2},{3,7},{7,3},{8,12},{12,8},{9,1... | collective-permute-start | bytes 1228808 | tf_op jit(solution)/shard_map/exchange_cores/ppermute | solution.py:134
  (11 other events, 20.7 us)

commit v7 on v6

--- a/solution.py
+++ b/solution.py
@@ -151,29 +151,30 @@
         own = basis_a.reshape(AB, 3, channels, -1).transpose(0, 3, 1, 2)
         own = own.reshape(AB, own.shape[1], 3 * channels)
         ba = around(own, "x")
-    with jax.named_scope("basis_g_z"):
-        bg = around(basis_g.T, "z")
-    with jax.named_scope("exchange_grads"):
-        grads, bg, ba = lax.optimization_barrier((grads, bg, ba))
-        g = lax.all_to_all(grads, "z", 0, 0, tiled=True)
+    with jax.named_scope("basis_g_x"):
+        bg = around(basis_g.T, "x")
+
+    ba, bg = lax.optimization_barrier((ba, bg))
     with jax.named_scope("basis_a_y"):
         ba = jnp.concatenate(ba, axis=1)
-        bg, give, _ = lax.optimization_barrier((bg, x, ba))
+        bg, ba = lax.optimization_barrier((bg, ba))
+        ba = around(ba, "y")
+    with jax.named_scope("basis_g_z"):
+        bg = around(jnp.stack(bg), "z")
+
+    ba, bg, grads, give = lax.optimization_barrier((ba, bg, grads, x))
+    with jax.named_scope("exchange_inputs"):
         x_oth = shift(give, "core", 1)
-        ba = around(ba, "y")
-    with jax.named_scope("basis_g_x"):
-        bg = around(jnp.concatenate(bg, axis=1), "x")
-
-    def parts(shifts, dtypes):
-        return conv(jnp.stack([(z + s) % tensor for s in shifts]), jnp.concatenate(ba, axis=1), x, x_oth, per, dtypes)
-
-    ba, bg = lax.optimization_barrier((ba, bg))
+    with jax.named_scope("exchange_grads"):
+        g = lax.all_to_all(grads, "z", 0, 0, tiled=True)
     with jax.named_scope("basis_g_y"):
-        bg = around(jnp.stack(bg), "y")
+        bg = around(jnp.concatenate(bg, axis=2), "y")
     with jax.named_scope("coeff_parts"):
         bf16 = jnp.bfloat16
-        *sent, mine = parts((2, 1, 3, 0), (bf16, bf16, bf16, jnp.float32))
-        received = [shift(v, "z", s) for v, s in zip(sent, (2, 1, 3))]
+        shifts = (2, 1, 3, 0)
+        taps, blocks = jnp.concatenate(ba, axis=1), jnp.stack([(z + s) % tensor for s in shifts])
+        *sent, mine = conv(blocks, taps, x, x_oth, per, (bf16, bf16, bf16, jnp.float32))
+        received = [shift(v, "z", s) for v, s in zip(sent, shifts)]
     with jax.named_scope("exchange_cores"):
         g, bg, _ = lax.optimization_barrier((g, bg, sent[0]))
         g_oth = shift(g, "core", 1)

time: 111 us -> 116 us (1.045)
  waiting for transfers between devices: 18.9 us -> 29.2 us
  starting transfers between devices: 44.9 us -> 39.8 us
  blocking collectives: 16.1 us -> 14.1 us
    all_to_all x1, waiting for transfers between devices: 0.01 us -> 8.86 us  [body(): g = lax.all_to_all(grads, 'z', 0, 0, tiled=True)]
    ppermute x24, starting transfers between devices: 40.9 us -> 35.5 us  [shift(): return lax.ppermute(v, axis, [(i, (i + s) % n) for i in range(n)])]
    all_to_all x1, blocking collectives: 16.1 us -> 14.1 us  [body(): got = lax.all_to_all(rows, ('x', 'y', 'z'), 0, 0, tiled=True)]
    ppermute x24, waiting for transfers between devices: 18.9 us -> 20.4 us  [shift(): return lax.ppermute(v, axis, [(i, (i + s) % n) for i in range(n)])]
    unnamed x20 -> x24, local copies, waits for them, and re-layouts: 6.48 us -> 5.65 us
  transfers between devices with their start and end apart: 25 -> 25, of which waited for: 9 -> 12; matrix products, arithmetic and copies ran while one was open for 3% -> 4% of each run, Pallas kernels for 11% -> 11%
where the time goes in v7:
time: 116 us; the launch traced here: 115 us
  starting transfers between devices  39.8 us (34%)
  waiting for transfers between devices  29.2 us (25%)
  Pallas kernels  18.7 us (16%)
  blocking collectives  14.1 us (12%)
  local copies, waits for them, and re-layouts  8.9 us (8%)
  other arithmetic  3.87 us (3%)
    ppermute x24, starting transfers between devices, shift(): return lax.ppermute(v, axis, [(i, (i + s) % n) for i in range(n)])  35.5 us
    ppermute x24, waiting for transfers between devices, shift(): return lax.ppermute(v, axis, [(i, (i + s) % n) for i in range(n)])  20.4 us
    all_to_all x1, blocking collectives, body(): got = lax.all_to_all(rows, ('x', 'y', 'z'), 0, 0, tiled=True)  14.1 us
    pallas_call x1, Pallas kernels, conv(): pl.pallas_call(conv_kernel, out_shape=[jax.ShapeDtypeStruct((2 * per, ran...  12.5 us
    all_to_all x1, waiting for transfers between devices, body(): g = lax.all_to_all(grads, 'z', 0, 0, tiled=True)  8.86 us
    pallas_call x1, Pallas kernels, squares(): pl.pallas_call(kernel, out_shape=jax.ShapeDtypeStruct((chips, ranks // ch...  6.26 us
    unnamed x24, local copies, waits for them, and re-layouts  5.65 us
    all_to_all x1, starting transfers between devices, body(): g = lax.all_to_all(grads, 'z', 0, 0, tiled=True)  4.23 us
  transfers between devices with their start and end apart: 25, of which 12 were waited for; matrix products, arithmetic and copies ran while one was open for 4% of the time, Pallas kernels for 11%

profile of v7, /device:TPU:1, one launch (start us, length us, event | category | flops | bytes accessed | tf_op | source)
XLA Modules:
  0.0 114.8 jit_solution(14236599798180567223)
XLA Ops:
  1.0 2.1 %collective-permute-start = (bf16[9,4,960]{2,1,0:T(4,128)(2,1)S(1)}, bf16[9,4,960]{2,1,0:T(4,128)(2,1)S(1)}, u32[]{:S(2)}, u32[]{:S(2)}) collective-permute-start(bf16[9,4,960]{2,1,0:T(4,128)(2,1)S(1)} %reshape.11), channel_id=1, source_target_pairs={{0,32},{32,64},{64,96},{96,0},{1,33},{33,65},{65,97},{97,1},{2,34}... | collective-permute-start | bytes 207368 | tf_op jit(solution)/shard_map/basis_a_x/ppermute | solution.py:134
  3.2 2.5 %collective-permute-start.1 = (bf16[9,4,960]{2,1,0:T(4,128)(2,1)S(1)}, bf16[9,4,960]{2,1,0:T(4,128)(2,1)S(1)}, u32[]{:S(2)}, u32[]{:S(2)}) collective-permute-start(bf16[9,4,960]{2,1,0:T(4,128)(2,1)S(1)} %reshape.11), channel_id=1, source_target_pairs={{0,64},{32,96},{64,0},{96,32},{1,65},{33,97},{65,1},{97,33},{2,66}... | collective-permute-start | bytes 207368 | tf_op jit(solution)/shard_map/basis_a_x/ppermute | solution.py:134
  7.9 3.0 %collective-permute-done.3 = bf16[40,320]{1,0:T(8,128)(2,1)S(1)} collective-permute-done((bf16[40,320]{1,0:T(8,128)(2,1)}, bf16[40,320]{1,0:T(8,128)(2,1)S(1)}, u32[]{:S(2)}, u32[]{:S(2)}) %collective-permute-start.3) | collective-permute-done | bytes 25632 | tf_op jit(solution)/shard_map/basis_g_x/ppermute | solution.py:134
  11.5 2.6 %collective-permute-done.5 = bf16[40,320]{1,0:T(8,128)(2,1)S(1)} collective-permute-done((bf16[40,320]{1,0:T(8,128)(2,1)}, bf16[40,320]{1,0:T(8,128)(2,1)S(1)}, u32[]{:S(2)}, u32[]{:S(2)}) %collective-permute-start.5) | collective-permute-done | bytes 25632 | tf_op jit(solution)/shard_map/basis_g_x/ppermute | solution.py:134
  15.7 2.6 %collective-permute-start.7 = (bf16[9,16,960]{2,1,0:T(8,128)(2,1)S(1)}, bf16[9,16,960]{2,1,0:T(8,128)(2,1)S(1)}, u32[]{:S(2)}, u32[]{:S(2)}) collective-permute-start(bf16[9,16,960]{2,1,0:T(8,128)(2,1)S(1)} %pad_maximum_fusion.1), channel_id=1, source_target_pairs={{0,16},{8,24},{16,0},{24,8},{1,17},{9,25},{17,1},{25,9},{2,18},{10... | collective-permute-start | bytes 829448 | tf_op jit(solution)/shard_map/basis_a_y/ppermute | solution.py:134
  20.1 1.7 %collective-permute-start.9 = (bf16[4,40,320]{2,1,0:T(8,128)(2,1)S(1)}, bf16[4,40,320]{2,1,0:T(8,128)(2,1)S(1)}, u32[]{:S(2)}, u32[]{:S(2)}) collective-permute-start(bf16[4,40,320]{2,1,0:T(8,128)(2,1)S(1)} %pad_maximum_fusion.2), channel_id=1, source_target_pairs={{0,1},{1,2},{2,3},{3,0},{4,5},{5,6},{6,7},{7,4},{8,9},{9,10},{10,1... | collective-permute-start | bytes 307208 | tf_op jit(solution)/shard_map/basis_g_z/ppermute | solution.py:134
  21.8 3.3 %collective-permute-start.10 = (bf16[4,40,320]{2,1,0:T(8,128)(2,1)S(1)}, bf16[4,40,320]{2,1,0:T(8,128)(2,1)S(1)}, u32[]{:S(2)}, u32[]{:S(2)}) collective-permute-start(bf16[4,40,320]{2,1,0:T(8,128)(2,1)S(1)} %pad_maximum_fusion.2), channel_id=1, source_target_pairs={{0,2},{1,3},{2,0},{3,1},{4,6},{5,7},{6,4},{7,5},{8,10},{9,11},{10,... | collective-permute-start | bytes 307208 | tf_op jit(solution)/shard_map/basis_g_z/ppermute | solution.py:134
  25.1 1.4 %collective-permute-done.9 = bf16[4,40,320]{2,1,0:T(8,128)(2,1)S(1)} collective-permute-done((bf16[4,40,320]{2,1,0:T(8,128)(2,1)S(1)}, bf16[4,40,320]{2,1,0:T(8,128)(2,1)S(1)}, u32[]{:S(2)}, u32[]{:S(2)}) %collective-permute-start.9) | collective-permute-done | bytes 102432 | tf_op jit(solution)/shard_map/basis_g_z/ppermute | solution.py:134
  26.5 1.5 %collective-permute-start.11 = (bf16[4,40,320]{2,1,0:T(8,128)(2,1)S(1)}, bf16[4,40,320]{2,1,0:T(8,128)(2,1)S(1)}, u32[]{:S(2)}, u32[]{:S(2)}) collective-permute-start(bf16[4,40,320]{2,1,0:T(8,128)(2,1)S(1)} %pad_maximum_fusion.2), channel_id=1, source_target_pairs={{0,3},{1,0},{2,1},{3,2},{4,7},{5,4},{6,5},{7,6},{8,11},{9,8},{10,9... | collective-permute-start | bytes 307208 | tf_op jit(solution)/shard_map/basis_g_z/ppermute | solution.py:134
  28.7 1.8 %collective-permute-done.11 = bf16[4,40,320]{2,1,0:T(8,128)(2,1)S(1)} collective-permute-done((bf16[4,40,320]{2,1,0:T(8,128)(2,1)S(1)}, bf16[4,40,320]{2,1,0:T(8,128)(2,1)S(1)}, u32[]{:S(2)}, u32[]{:S(2)}) %collective-permute-start.11) | collective-permute-done | bytes 102432 | tf_op jit(solution)/shard_map/basis_g_z/ppermute | solution.py:134
  30.6 6.0 %collective-permute-start.12 = (bf16[8,320,512]{2,1,0:T(8,128)(2,1)}, bf16[8,320,512]{2,1,0:T(8,128)(2,1)}, u32[]{:S(2)}, u32[]{:S(2)}) collective-permute-start(bf16[8,320,512]{2,1,0:T(8,128)(2,1)} %bitcast.19), channel_id=1, source_target_pairs={{0,4},{4,0},{1,5},{5,1},{2,6},{6,2},{3,7},{7,3},{8,12},{12,8},{9,1... | collective-permute-start | bytes 7864328 | tf_op jit(solution)/shard_map/exchange_inputs/ppermute | solution.py:134
  36.6 4.2 %all-to-all-start = ((bf16[8,320,512]{2,1,0:T(8,128)(2,1)}), bf16[8,320,512]{2,1,0:T(8,128)(2,1)S(1)}, u32[]{:S(2)}, u32[]{:S(2)}) async-start(bf16[8,320,512]{2,1,0:T(8,128)(2,1)} %bitcast.21), calls=%async_computation | async-start | bytes 5242880 | tf_op jit(solution)/shard_map/exchange_grads/all_to_all | solution.py:169
  43.0 2.0 %collective-permute-start.18 = (bf16[4,40,1280]{2,1,0:T(8,128)(2,1)S(1)}, bf16[4,40,1280]{2,1,0:T(8,128)(2,1)}, u32[]{:S(2)}, u32[]{:S(2)}) collective-permute-start(bf16[4,40,1280]{2,1,0:T(8,128)(2,1)S(1)} %concatenate.11.refs_4_), channel_id=1, source_target_pairs={{0,24},{8,0},{16,8},{24,16},{1,25},{9,1},{17,9},{25,17},{2,26},{10... | collective-permute-start | bytes 1228808 | tf_op jit(solution)/shard_map/basis_g_y/ppermute | solution.py:134
  46.4 1.7 %copy-done = bf16[8,512,320]{1,2,0:T(8,128)(2,1)S(1)} copy-done((bf16[8,512,320]{1,2,0:T(8,128)(2,1)S(1)}, bf16[8,512,320]{1,2,0:T(8,128)(2,1)}, u32[]{:S(2)}) %copy-start) | copy-done | bytes 2621464
  48.1 12.5 %conv_taps.1 = (bf16[4,64,512]{2,1,0:T(8,128)(2,1)S(1)}, bf16[4,64,512]{2,1,0:T(8,128)(2,1)S(1)}, bf16[4,64,512]{2,1,0:T(8,128)(2,1)S(1)}, f32[4,64,512]{2,1,0:T(8,128)S(1)}) custom-call(s32[4]{0:T(128)S(1)} %pad_add_fusion.1.idx_ref, bf16[9,64,960]{2,1,0:T(8,128)(2,1)S(1)} %pad_maximum_fusion.b_ref, bf16[8,320,512]{2,1,0:T(8,128)(2,1)S(1)} %bitcast.20, ...), custom_call_target="tpu_custom_call" | custom-call | tf_op jit(solution)/shard_map/coeff_parts/conv_taps/pallas_call | solution.py:59
  62.9 8.9 %all-to-all-done.refs_2_ = bf16[8,320,512]{2,1,0:T(8,128)(2,1)S(1)} async-done(((bf16[8,320,512]{2,1,0:T(8,128)(2,1)}), bf16[8,320,512]{2,1,0:T(8,128)(2,1)S(1)}, u32[]{:S(2)}, u32[]{:S(2)}) %all-to-all-start) | async-done | bytes 2621472 | tf_op jit(solution)/shard_map/exchange_grads/all_to_all | solution.py:169
  71.7 2.0 %collective-permute-start.19 = (bf16[8,320,512]{2,1,0:T(8,128)(2,1)S(1)}, bf16[8,320,512]{2,1,0:T(8,128)(2,1)}, u32[]{:S(2)}, u32[]{:S(2)}) collective-permute-start(bf16[8,320,512]{2,1,0:T(8,128)(2,1)S(1)} %all-to-all-done.refs_2_), channel_id=1, source_target_pairs={{0,4},{4,0},{1,5},{5,1},{2,6},{6,2},{3,7},{7,3},{8,12},{12,8},{9,1... | collective-permute-start | bytes 7864328 | tf_op jit(solution)/shard_map/exchange_cores/ppermute | solution.py:134
  75.8 2.9 %collective-permute-done.20.refs_8_ = bf16[4,40,1280]{2,1,0:T(8,128)(2,1)S(1)} collective-permute-done((bf16[4,40,1280]{2,1,0:T(8,128)(2,1)S(1)}, bf16[4,40,1280]{2,1,0:T(8,128)(2,1)S(1)}, u32[]{:S(2)}, u32[]{:S(2)}) %collective-permute-start.20) | collective-permute-done | bytes 409632 | tf_op jit(solution)/shard_map/exchange_cores/ppermute | solution.py:134
  79.6 1.8 %collective-permute-done.15 = bf16[4,64,512]{2,1,0:T(8,128)(2,1)} collective-permute-done((bf16[4,64,512]{2,1,0:T(8,128)(2,1)}, bf16[4,64,512]{2,1,0:T(8,128)(2,1)}, u32[]{:S(2)}, u32[]{:S(2)}) %collective-permute-start.15) | collective-permute-done | bytes 262176 | tf_op jit(solution)/shard_map/coeff_parts/ppermute | solution.py:134
  81.4 2.3 %collective-permute-start.22 = (bf16[4,40,1280]{2,1,0:T(8,128)(2,1)}, bf16[4,40,1280]{2,1,0:T(8,128)(2,1)}, u32[]{:S(2)}, u32[]{:S(2)}) collective-permute-start(bf16[4,40,1280]{2,1,0:T(8,128)(2,1)} %collective-permute-done.17.refs_6_), channel_id=1, source_target_pairs={{0,4},{4,0},{1,5},{5,1},{2,6},{6,2},{3,7},{7,3},{8,12},{12,8},{9,1... | collective-permute-start | bytes 1228808 | tf_op jit(solution)/shard_map/exchange_cores/ppermute | solution.py:134
  83.7 5.1 %collective-permute-done.14 = bf16[4,64,512]{2,1,0:T(8,128)(2,1)} collective-permute-done((bf16[4,64,512]{2,1,0:T(8,128)(2,1)}, bf16[4,64,512]{2,1,0:T(8,128)(2,1)}, u32[]{:S(2)}, u32[]{:S(2)}) %collective-permute-start.14) | collective-permute-done | bytes 262176 | tf_op jit(solution)/shard_map/coeff_parts/ppermute | solution.py:134
  88.8 1.7 %collective-permute-start.23 = (bf16[4,40,1280]{2,1,0:T(8,128)(2,1)}, bf16[4,40,1280]{2,1,0:T(8,128)(2,1)}, u32[]{:S(2)}, u32[]{:S(2)}) collective-permute-start(bf16[4,40,1280]{2,1,0:T(8,128)(2,1)} %collective-permute-done.18.refs_7_), channel_id=1, source_target_pairs={{0,4},{4,0},{1,5},{5,1},{2,6},{6,2},{3,7},{7,3},{8,12},{12,8},{9,1... | collective-permute-start | bytes 1228808 | tf_op jit(solution)/shard_map/exchange_cores/ppermute | solution.py:134
  93.2 6.3 %squared_sums.1 = f32[16,4,1280]{2,1,0:T(4,128)S(1)} custom-call(s32[4]{0:T(128)S(1)} %pad_add_fusion.refs_0_, f32[4,64,512]{2,1,0:T(8,128)S(1)} %convert_add_fusion.refs_1_, bf16[8,320,512]{2,1,0:T(8,128)(2,1)S(1)} %all-to-all-done.refs_2_, bf16[8,320,512]{2,1,0:T(8,128)(2,1)} %collective-permute-done.19.refs_3_, ...), custom_call_target="tpu_custom_call" | custom-call | tf_op jit(solution)/shard_map/squared_sums/pallas_call | solution.py:117
  99.9 14.1 %all_to_all.10 = f32[64,1,1280]{2,1,0:T(1,128)S(1)} all-to-all(f32[64,1,1280]{2,1,0:T(1,128)S(1)} %reshape.13), channel_id=1, replica_groups=mesh['x'=4,'y'=4,'core'=2,'z'=4] {'x','y','z'}, dimensions={0} | all-to-all | bytes 655360 | tf_op jit(solution)/shard_map/sum_examples/all_to_all | solution.py:193
  (65 shorter events, 20.9 us)
Async XLA Ops:
  1.0 13.0 %collective-permute-start = (bf16[9,4,960]{2,1,0:T(4,128)(2,1)S(1)}, bf16[9,4,960]{2,1,0:T(4,128)(2,1)S(1)}, u32[]{:S(2)}, u32[]{:S(2)}) collective-permute-start(bf16[9,4,960]{2,1,0:T(4,128)(2,1)S(1)} %reshape.11), channel_id=1, source_target_pairs={{0,32},{32,64},{64,96},{96,0},{1,33},{33,65},{65,97},{97,1},{2,34}... | collective-permute-start | bytes 207368 | tf_op jit(solution)/shard_map/basis_a_x/ppermute | solution.py:134
  3.2 10.9 %collective-permute-start.1 = (bf16[9,4,960]{2,1,0:T(4,128)(2,1)S(1)}, bf16[9,4,960]{2,1,0:T(4,128)(2,1)S(1)}, u32[]{:S(2)}, u32[]{:S(2)}) collective-permute-start(bf16[9,4,960]{2,1,0:T(4,128)(2,1)S(1)} %reshape.11), channel_id=1, source_target_pairs={{0,64},{32,96},{64,0},{96,32},{1,65},{33,97},{65,1},{97,33},{2,66}... | collective-permute-start | bytes 207368 | tf_op jit(solution)/shard_map/basis_a_x/ppermute | solution.py:134
  5.6 8.5 %collective-permute-start.2 = (bf16[9,4,960]{2,1,0:T(4,128)(2,1)S(1)}, bf16[9,4,960]{2,1,0:T(4,128)(2,1)S(1)}, u32[]{:S(2)}, u32[]{:S(2)}) collective-permute-start(bf16[9,4,960]{2,1,0:T(4,128)(2,1)S(1)} %reshape.11), channel_id=1, source_target_pairs={{0,96},{32,0},{64,32},{96,64},{1,97},{33,1},{65,33},{97,65},{2,98}... | collective-permute-start | bytes 207368 | tf_op jit(solution)/shard_map/basis_a_x/ppermute | solution.py:134
  6.8 4.2 %collective-permute-start.3 = (bf16[40,320]{1,0:T(8,128)(2,1)}, bf16[40,320]{1,0:T(8,128)(2,1)S(1)}, u32[]{:S(2)}, u32[]{:S(2)}) collective-permute-start(bf16[40,320]{1,0:T(8,128)(2,1)} %bitcast.24), channel_id=1, source_target_pairs={{0,32},{32,64},{64,96},{96,0},{1,33},{33,65},{65,97},{97,1},{2,34}... | collective-permute-start | bytes 76808 | tf_op jit(solution)/shard_map/basis_g_x/ppermute | solution.py:134
  7.1 4.5 %collective-permute-start.4 = (bf16[40,320]{1,0:T(8,128)(2,1)}, bf16[40,320]{1,0:T(8,128)(2,1)S(1)}, u32[]{:S(2)}, u32[]{:S(2)}) collective-permute-start(bf16[40,320]{1,0:T(8,128)(2,1)} %bitcast.25), channel_id=1, source_target_pairs={{0,64},{32,96},{64,0},{96,32},{1,65},{33,97},{65,1},{97,33},{2,66}... | collective-permute-start | bytes 76808 | tf_op jit(solution)/shard_map/basis_g_x/ppermute | solution.py:134
  14.3 16.3 %collective-permute-start.6 = (bf16[9,16,960]{2,1,0:T(8,128)(2,1)S(1)}, bf16[9,16,960]{2,1,0:T(8,128)(2,1)S(1)}, u32[]{:S(2)}, u32[]{:S(2)}) collective-permute-start(bf16[9,16,960]{2,1,0:T(8,128)(2,1)S(1)} %pad_maximum_fusion.1), channel_id=1, source_target_pairs={{0,8},{8,16},{16,24},{24,0},{1,9},{9,17},{17,25},{25,1},{2,10},{10... | collective-permute-start | bytes 829448 | tf_op jit(solution)/shard_map/basis_a_y/ppermute | solution.py:134
  15.7 14.9 %collective-permute-start.7 = (bf16[9,16,960]{2,1,0:T(8,128)(2,1)S(1)}, bf16[9,16,960]{2,1,0:T(8,128)(2,1)S(1)}, u32[]{:S(2)}, u32[]{:S(2)}) collective-permute-start(bf16[9,16,960]{2,1,0:T(8,128)(2,1)S(1)} %pad_maximum_fusion.1), channel_id=1, source_target_pairs={{0,16},{8,24},{16,0},{24,8},{1,17},{9,25},{17,1},{25,9},{2,18},{10... | collective-permute-start | bytes 829448 | tf_op jit(solution)/shard_map/basis_a_y/ppermute | solution.py:134
  18.3 12.3 %collective-permute-start.8 = (bf16[9,16,960]{2,1,0:T(8,128)(2,1)S(1)}, bf16[9,16,960]{2,1,0:T(8,128)(2,1)S(1)}, u32[]{:S(2)}, u32[]{:S(2)}) collective-permute-start(bf16[9,16,960]{2,1,0:T(8,128)(2,1)S(1)} %pad_maximum_fusion.1), channel_id=1, source_target_pairs={{0,24},{8,0},{16,8},{24,16},{1,25},{9,1},{17,9},{25,17},{2,26},{10... | collective-permute-start | bytes 829448 | tf_op jit(solution)/shard_map/basis_a_y/ppermute | solution.py:134
  20.1 6.4 %collective-permute-start.9 = (bf16[4,40,320]{2,1,0:T(8,128)(2,1)S(1)}, bf16[4,40,320]{2,1,0:T(8,128)(2,1)S(1)}, u32[]{:S(2)}, u32[]{:S(2)}) collective-permute-start(bf16[4,40,320]{2,1,0:T(8,128)(2,1)S(1)} %pad_maximum_fusion.2), channel_id=1, source_target_pairs={{0,1},{1,2},{2,3},{3,0},{4,5},{5,6},{6,7},{7,4},{8,9},{9,10},{10,1... | collective-permute-start | bytes 307208 | tf_op jit(solution)/shard_map/basis_g_z/ppermute | solution.py:134
  21.8 6.9 %collective-permute-start.10 = (bf16[4,40,320]{2,1,0:T(8,128)(2,1)S(1)}, bf16[4,40,320]{2,1,0:T(8,128)(2,1)S(1)}, u32[]{:S(2)}, u32[]{:S(2)}) collective-permute-start(bf16[4,40,320]{2,1,0:T(8,128)(2,1)S(1)} %pad_maximum_fusion.2), channel_id=1, source_target_pairs={{0,2},{1,3},{2,0},{3,1},{4,6},{5,7},{6,4},{7,5},{8,10},{9,11},{10,... | collective-permute-start | bytes 307208 | tf_op jit(solution)/shard_map/basis_g_z/ppermute | solution.py:134
  26.5 4.0 %collective-permute-start.11 = (bf16[4,40,320]{2,1,0:T(8,128)(2,1)S(1)}, bf16[4,40,320]{2,1,0:T(8,128)(2,1)S(1)}, u32[]{:S(2)}, u32[]{:S(2)}) collective-permute-start(bf16[4,40,320]{2,1,0:T(8,128)(2,1)S(1)} %pad_maximum_fusion.2), channel_id=1, source_target_pairs={{0,3},{1,0},{2,1},{3,2},{4,7},{5,4},{6,5},{7,6},{8,11},{9,8},{10,9... | collective-permute-start | bytes 307208 | tf_op jit(solution)/shard_map/basis_g_z/ppermute | solution.py:134
  30.6 15.8 %collective-permute-start.12 = (bf16[8,320,512]{2,1,0:T(8,128)(2,1)}, bf16[8,320,512]{2,1,0:T(8,128)(2,1)}, u32[]{:S(2)}, u32[]{:S(2)}) collective-permute-start(bf16[8,320,512]{2,1,0:T(8,128)(2,1)} %bitcast.19), channel_id=1, source_target_pairs={{0,4},{4,0},{1,5},{5,1},{2,6},{6,2},{3,7},{7,3},{8,12},{12,8},{9,1... | collective-permute-start | bytes 7864328 | tf_op jit(solution)/shard_map/exchange_inputs/ppermute | solution.py:134
  36.6 35.1 %all-to-all-start = ((bf16[8,320,512]{2,1,0:T(8,128)(2,1)}), bf16[8,320,512]{2,1,0:T(8,128)(2,1)S(1)}, u32[]{:S(2)}, u32[]{:S(2)}) async-start(bf16[8,320,512]{2,1,0:T(8,128)(2,1)} %bitcast.21), calls=%async_computation | async-start | bytes 5242880 | tf_op jit(solution)/shard_map/exchange_grads/all_to_all | solution.py:169
  42.0 20.7 %collective-permute-start.16 = (bf16[4,40,1280]{2,1,0:T(8,128)(2,1)S(1)}, bf16[4,40,1280]{2,1,0:T(8,128)(2,1)}, u32[]{:S(2)}, u32[]{:S(2)}) collective-permute-start(bf16[4,40,1280]{2,1,0:T(8,128)(2,1)S(1)} %concatenate.11.refs_4_), channel_id=1, source_target_pairs={{0,8},{8,16},{16,24},{24,0},{1,9},{9,17},{17,25},{25,1},{2,10},{10... | collective-permute-start | bytes 1228808 | tf_op jit(solution)/shard_map/basis_g_y/ppermute | solution.py:134
  42.5 20.2 %collective-permute-start.17 = (bf16[4,40,1280]{2,1,0:T(8,128)(2,1)S(1)}, bf16[4,40,1280]{2,1,0:T(8,128)(2,1)}, u32[]{:S(2)}, u32[]{:S(2)}) collective-permute-start(bf16[4,40,1280]{2,1,0:T(8,128)(2,1)S(1)} %concatenate.11.refs_4_), channel_id=1, source_target_pairs={{0,16},{8,24},{16,0},{24,8},{1,17},{9,25},{17,1},{25,9},{2,18},{10... | collective-permute-start | bytes 1228808 | tf_op jit(solution)/shard_map/basis_g_y/ppermute | solution.py:134
  43.0 19.9 %collective-permute-start.18 = (bf16[4,40,1280]{2,1,0:T(8,128)(2,1)S(1)}, bf16[4,40,1280]{2,1,0:T(8,128)(2,1)}, u32[]{:S(2)}, u32[]{:S(2)}) collective-permute-start(bf16[4,40,1280]{2,1,0:T(8,128)(2,1)S(1)} %concatenate.11.refs_4_), channel_id=1, source_target_pairs={{0,24},{8,0},{16,8},{24,16},{1,25},{9,1},{17,9},{25,17},{2,26},{10... | collective-permute-start | bytes 1228808 | tf_op jit(solution)/shard_map/basis_g_y/ppermute | solution.py:134
  71.7 20.5 %collective-permute-start.19 = (bf16[8,320,512]{2,1,0:T(8,128)(2,1)S(1)}, bf16[8,320,512]{2,1,0:T(8,128)(2,1)}, u32[]{:S(2)}, u32[]{:S(2)}) collective-permute-start(bf16[8,320,512]{2,1,0:T(8,128)(2,1)S(1)} %all-to-all-done.refs_2_), channel_id=1, source_target_pairs={{0,4},{4,0},{1,5},{5,1},{2,6},{6,2},{3,7},{7,3},{8,12},{12,8},{9,1... | collective-permute-start | bytes 7864328 | tf_op jit(solution)/shard_map/exchange_cores/ppermute | solution.py:134
  73.7 5.0 %collective-permute-start.20 = (bf16[4,40,1280]{2,1,0:T(8,128)(2,1)S(1)}, bf16[4,40,1280]{2,1,0:T(8,128)(2,1)S(1)}, u32[]{:S(2)}, u32[]{:S(2)}) collective-permute-start(bf16[4,40,1280]{2,1,0:T(8,128)(2,1)S(1)} %concatenate.11.refs_4_), channel_id=1, source_target_pairs={{0,4},{4,0},{1,5},{5,1},{2,6},{6,2},{3,7},{7,3},{8,12},{12,8},{9,1... | collective-permute-start | bytes 1228808 | tf_op jit(solution)/shard_map/exchange_cores/ppermute | solution.py:134
  73.7 7.7 %collective-permute-start.15 = (bf16[4,64,512]{2,1,0:T(8,128)(2,1)}, bf16[4,64,512]{2,1,0:T(8,128)(2,1)}, u32[]{:S(2)}, u32[]{:S(2)}) collective-permute-start(bf16[4,64,512]{2,1,0:T(8,128)(2,1)} %copy-done.5), channel_id=1, source_target_pairs={{0,3},{1,0},{2,1},{3,2},{4,7},{5,4},{6,5},{7,6},{8,11},{9,8},{10,9... | collective-permute-start | bytes 786440 | tf_op jit(solution)/shard_map/coeff_parts/ppermute | solution.py:134
  74.6 14.2 %collective-permute-start.14 = (bf16[4,64,512]{2,1,0:T(8,128)(2,1)}, bf16[4,64,512]{2,1,0:T(8,128)(2,1)}, u32[]{:S(2)}, u32[]{:S(2)}) collective-permute-start(bf16[4,64,512]{2,1,0:T(8,128)(2,1)} %copy-done.4), channel_id=1, source_target_pairs={{0,1},{1,2},{2,3},{3,0},{4,5},{5,6},{6,7},{7,4},{8,9},{9,10},{10,1... | collective-permute-start | bytes 786440 | tf_op jit(solution)/shard_map/coeff_parts/ppermute | solution.py:134
  75.2 15.4 %collective-permute-start.13 = (bf16[4,64,512]{2,1,0:T(8,128)(2,1)}, bf16[4,64,512]{2,1,0:T(8,128)(2,1)}, u32[]{:S(2)}, u32[]{:S(2)}) collective-permute-start(bf16[4,64,512]{2,1,0:T(8,128)(2,1)} %copy-done.3), channel_id=1, source_target_pairs={{0,2},{1,3},{2,0},{3,1},{4,6},{5,7},{6,4},{7,5},{8,10},{9,11},{10,... | collective-permute-start | bytes 786440 | tf_op jit(solution)/shard_map/coeff_parts/ppermute | solution.py:134
  79.5 12.3 %collective-permute-start.21 = (bf16[4,40,1280]{2,1,0:T(8,128)(2,1)}, bf16[4,40,1280]{2,1,0:T(8,128)(2,1)}, u32[]{:S(2)}, u32[]{:S(2)}) collective-permute-start(bf16[4,40,1280]{2,1,0:T(8,128)(2,1)} %collective-permute-done.16.refs_5_), channel_id=1, source_target_pairs={{0,4},{4,0},{1,5},{5,1},{2,6},{6,2},{3,7},{7,3},{8,12},{12,8},{9,1... | collective-permute-start | bytes 1228808 | tf_op jit(solution)/shard_map/exchange_cores/ppermute | solution.py:134
  81.4 10.4 %collective-permute-start.22 = (bf16[4,40,1280]{2,1,0:T(8,128)(2,1)}, bf16[4,40,1280]{2,1,0:T(8,128)(2,1)}, u32[]{:S(2)}, u32[]{:S(2)}) collective-permute-start(bf16[4,40,1280]{2,1,0:T(8,128)(2,1)} %collective-permute-done.17.refs_6_), channel_id=1, source_target_pairs={{0,4},{4,0},{1,5},{5,1},{2,6},{6,2},{3,7},{7,3},{8,12},{12,8},{9,1... | collective-permute-start | bytes 1228808 | tf_op jit(solution)/shard_map/exchange_cores/ppermute | solution.py:134
  88.8 3.4 %collective-permute-start.23 = (bf16[4,40,1280]{2,1,0:T(8,128)(2,1)}, bf16[4,40,1280]{2,1,0:T(8,128)(2,1)}, u32[]{:S(2)}, u32[]{:S(2)}) collective-permute-start(bf16[4,40,1280]{2,1,0:T(8,128)(2,1)} %collective-permute-done.18.refs_7_), channel_id=1, source_target_pairs={{0,4},{4,0},{1,5},{5,1},{2,6},{6,2},{3,7},{7,3},{8,12},{12,8},{9,1... | collective-permute-start | bytes 1228808 | tf_op jit(solution)/shard_map/exchange_cores/ppermute | solution.py:134
  (13 other events, 50.7 us)

commit v8 on v6

v8 whole, which is shorter than its diff:
```python
import jax
import jax.numpy as jnp
from jax import lax
from jax.experimental import pallas as pl
from jax.experimental.pallas import tpu as pltpu
from jax.sharding import Mesh, PartitionSpec as P

SIDE = 8
POS = SIDE * SIDE * SIDE
AB = 9
ALL = ("x", "y", "core", "z")
NT = (((1,), (1,)), ((), ()))
VMEM = pl.BlockSpec(memory_space=pltpu.VMEM)
SMEM = pl.BlockSpec(memory_space=pltpu.SMEM)


def lane_coords():
    p = lax.broadcasted_iota(jnp.int32, (1, POS), 1)
    return p // 64, (p // 8) % 8, p % 8


def shifted(y, ab, i, j):
    a, b = ab // 3 - 1, ab % 3 - 1
    s = a * 64 + b * 8
    if s == 0:
        return y
    ok = None
    for v, o in ((i, a), (j, b)):
        if o != 0:
            m = (v + o >= 0) & (v + o < SIDE)
            ok = m if ok is None else ok & m
    return jnp.where(ok, pltpu.roll(y, (-s) % POS, 1), 0.0)


def conv_kernel(idx_ref, b_ref, x_ref, x_oth_ref, o_ref, rest_ref, xc_ref):
    i, j, k = lane_coords()
    h = x_ref.shape[1]
    blocks, per, ranks = o_ref.shape[0], o_ref.shape[1] // 2, b_ref.shape[1]
    zero = jnp.zeros((), x_ref.dtype)
    b = b_ref[...].reshape(AB * ranks, 3 * h)
    for n in range(2 * per * blocks):
        o, m = n // (2 * per), n % (2 * per)
        block = (idx_ref[0] + o) % blocks
        x = (x_ref if m < per else x_oth_ref)[block * per + m % per]
        xc_ref[n % 2, :h] = jnp.where(k >= 1, pltpu.roll(x, 1, 1), zero)
        xc_ref[n % 2, h : 2 * h] = x
        xc_ref[n % 2, 2 * h :] = jnp.where(k <= SIDE - 2, pltpu.roll(x, POS - 1, 1), zero)
        y = jnp.dot(b, xc_ref[n % 2], preferred_element_type=jnp.float32)
        acc = None
        for ab in range(AB):
            t = shifted(y[ab * ranks : (ab + 1) * ranks], ab, i, j)
            acc = t if acc is None else acc + t
        o_ref[block, m] = acc.astype(o_ref.dtype)
        if o == 0:
            rest_ref[m] = acc - o_ref[block, m].astype(jnp.float32)


def conv(z, taps, x, x_oth, blocks):
    ranks, per = taps.shape[1], x.shape[0] // blocks
    return pl.pallas_call(
        conv_kernel,
        out_shape=[
            jax.ShapeDtypeStruct((blocks, 2 * per, ranks, POS), jnp.bfloat16),
            jax.ShapeDtypeStruct((2 * per, ranks, POS), jnp.float32),
        ],
        in_specs=[SMEM] + [VMEM] * 3,
        out_specs=[VMEM] * 2,
        scratch_shapes=[pltpu.VMEM((2, 3 * x.shape[1], POS), jnp.bfloat16)],
        compiler_params=pltpu.CompilerParams(vmem_limit_bytes=16 << 20),
        name="conv_taps",
    )(z, taps, x, x_oth)


def squares_kernel(idx_ref, c_ref, rest_ref, g_ref, g_oth_ref, *refs, scale):
    *bg_refs, o_ref, hi_ref, m_ref, sq_ref = refs
    x, y, core = idx_ref[0], idx_ref[1], idx_ref[2]
    side, width = len(bg_refs) // 2, bg_refs[0].shape[1]
    tensor, examples, ranks = c_ref.shape[0], c_ref.shape[1], c_ref.shape[2]
    per = examples // 2

    def chip(rx, ry):
        return ((x + side - rx) % side) * side + (y + side - ry) % side

    low_half = lax.broadcasted_iota(jnp.int32, (1, 2 * ranks), 1) < ranks
    pair = None
    for n in range(examples):
        c = rest_ref[n]
        for t in range(tensor):
            c = c + c_ref[t, n].astype(jnp.float32)
        hi_ref[n] = c.astype(jnp.bfloat16)
        hi = hi_ref[n]
        lo = (c - hi.astype(jnp.float32)).astype(jnp.bfloat16)
        both = jnp.concatenate([hi, lo], axis=0)
        src = g_ref if n < per else g_oth_ref
        g = jnp.concatenate([src[t * per + n % per] for t in range(tensor)], axis=0)
        m = lax.dot_general(g, both, NT, preferred_element_type=jnp.float32)
        m = m + pltpu.roll(m, ranks, 1)
        if n % 2 == 0:
            pair = m
        else:
            m_ref[:, (n - 1) * ranks : (n + 1) * ranks] = jnp.where(low_half, pair, m).astype(jnp.bfloat16)
    m = m_ref[...]
    for half in range(2):
        for ry in range(side):
            bg = bg_refs[half * side + ry][...].reshape(side * width, -1)
            p = jnp.dot(bg, m, preferred_element_type=jnp.float32)
            p = p * p
            while p.shape[1] > 2 * ranks:
                p = p[:, : p.shape[1] // 2] + p[:, p.shape[1] // 2 :]
            p = (p + pltpu.roll(p, ranks, 1)) * scale
            for rx in range(side):
                at = (chip(rx, ry) * 2 + (core + half) % 2) * width
                sq_ref[pl.ds(pl.multiple_of(at, 8), width), :] = p[rx * width : (rx + 1) * width]
    sq = sq_ref[...].T[:ranks]
    low = ranks // (side * side)
    for b in range(side * side):
        o_ref[chip(b % side, b // side)] = sq[b * low : (b + 1) * low]


def squares(idx, c, rest, g, g_oth, bg, bg_oth, scale):
    examples, ranks = rest.shape[0], rest.shape[1]
    side, width, hidden = bg[0].shape
    chips = side * side

    def kernel(*refs):
        squares_kernel(*refs, scale=scale)

    return pl.pallas_call(
        kernel,
        out_shape=jax.ShapeDtypeStruct((chips, ranks // chips, 2 * chips * width), jnp.float32),
        in_specs=[SMEM] + [VMEM] * (4 + 2 * side),
        out_specs=VMEM,
        scratch_shapes=[
            pltpu.VMEM((examples, ranks, POS), jnp.bfloat16),
            pltpu.VMEM((hidden, examples * ranks), jnp.bfloat16),
            pltpu.VMEM((2 * chips * width, 2 * ranks), jnp.float32),
        ],
        compiler_params=pltpu.CompilerParams(vmem_limit_bytes=16 << 20),
        name="squared_sums",
    )(idx, c, rest, g, g_oth, *bg, *bg_oth)


def shift(v, axis, s):
    n = lax.axis_size(axis)
    return lax.ppermute(v, axis, [(i, (i + s) % n) for i in range(n)])


def around(v, axis):
    return [v] + [shift(v, axis, s) for s in range(1, lax.axis_size(axis))]


def body(patch_rows, out_grads, basis_a, basis_g):
    coords = [lax.axis_index(a).astype(jnp.int32) for a in ALL]
    z = coords[3]
    x = patch_rows.transpose(0, 2, 1)
    grads = out_grads.transpose(0, 2, 1)
    here, channels = x.shape[0], x.shape[1]
    tensor = lax.axis_size("z")
    per = here // tensor

    with jax.named_scope("basis_a_x"):
        own = basis_a.reshape(AB, 3, channels, -1).transpose(0, 3, 1, 2)
        own = own.reshape(AB, own.shape[1], 3 * channels)
        ba = around(own, "x")
    with jax.named_scope("basis_g_z"):
        bg = basis_g.T
        bg = lax.all_to_all(jnp.broadcast_to(bg[None], (tensor, *bg.shape)), "z", 0, 0, tiled=True)
    with jax.named_scope("exchange_grads"):
        grads, bg, ba = lax.optimization_barrier((grads, bg, ba))
        g = lax.all_to_all(grads, "z", 0, 0, tiled=True)
    with jax.named_scope("basis_a_y"):
        ba = jnp.concatenate(ba, axis=1)
        bg, give, _ = lax.optimization_barrier((bg, x, ba))
        x_oth = shift(give, "core", 1)
        ba = around(ba, "y")
    with jax.named_scope("basis_g_x"):
        bg = around(jnp.concatenate(list(bg), axis=1), "x")

    ba, bg = lax.optimization_barrier((ba, bg))
    with jax.named_scope("basis_g_y"):
        bg = around(jnp.stack(bg), "y")
    with jax.named_scope("coeff_parts"):
        sent, rest = conv(z.reshape(1), jnp.concatenate(ba, axis=1), x, x_oth, tensor)
        received = lax.all_to_all(sent, "z", 0, 0, tiled=True)
    with jax.named_scope("exchange_cores"):
        g, bg, _ = lax.optimization_barrier((g, bg, sent))
        g_oth = shift(g, "core", 1)
        first = shift(bg[0], "core", 1)
        later, first = lax.optimization_barrier((bg[1:], first))
        bg_oth = [first] + [shift(v, "core", 1) for v in later]

    examples = here * lax.axis_size(("x", "y", "core"))
    total = squares(jnp.stack(coords), received, rest, g, g_oth, bg, bg_oth, 1.0 / examples)

    with jax.named_scope("sum_examples"):
        rows = total.reshape(-1, 1, total.shape[2])
        got = lax.all_to_all(rows, ("x", "y", "z"), 0, 0, tiled=True)
        return jnp.sum(got, axis=0)


def solution(mesh):
    tensor = mesh.shape["tensor"]
    fine = Mesh(mesh.devices.reshape(4, -1, 2, tensor), ALL)
    dp = ("x", "y", "core")
    in_specs = (P(dp, None, "z"), P(dp, None, "z"), P(None, "z", dp), P("z", dp))
    return jax.shard_map(body, mesh=fine, in_specs=in_specs, out_specs=P(ALL, None), check_vma=False)
```

time: 111 us -> 111 us (level); the launches traced: 111 us -> 109 us
  waiting for transfers between devices: 18.9 us -> 34.8 us
  starting transfers between devices: 44.9 us -> 29.8 us
  blocking collectives: 16.1 us -> 14.7 us
  other arithmetic: 3.14 us -> 1.89 us
  local copies, waits for them, and re-layouts: 8.62 us -> 9.82 us
    ppermute x24 -> x18, starting transfers between devices: 40.9 us -> 15.2 us  [shift(): return lax.ppermute(v, axis, [(i, (i + s) % n) for i in range(n)])]
    all_to_all x0 -> x2, waiting for transfers between devices: none -> 12.5 us  [the longest x1 12.5 us: body(): received = lax.all_to_all(sent, 'z', 0, 0, tiled=True)]
    all_to_all x0 -> x2, starting transfers between devices: none -> 10.1 us  [the longest x1 5.86 us: body(): lax.all_to_all(jnp.broadcast_to(bg[None], (tensor, *bg.shape)), 'z', 0, 0...]
    ppermute x24 -> x18, waiting for transfers between devices: 18.9 us -> 22.3 us  [shift(): return lax.ppermute(v, axis, [(i, (i + s) % n) for i in range(n)])]
    broadcast_in_dim x0 -> x1, local copies, waits for them, and re-layouts: none -> 1.41 us  [body(): jnp.broadcast_to(bg[None], (tensor, *bg.shape))]
    all_to_all x1, blocking collectives: 16.1 us -> 14.7 us  [body(): got = lax.all_to_all(rows, ('x', 'y', 'z'), 0, 0, tiled=True)]
    add x1 -> x0, other arithmetic: 1.24 us -> none  [body(): total_coeff = total_coeff + r.astype(jnp.float32)]
  transfers between devices with their start and end apart: 25 -> 21, of which waited for: 9 -> 11; matrix products, arithmetic and copies ran while one was open for 3% -> 2% of each run, Pallas kernels for 11% -> 11%
where the time goes in v8:
time: 111 us; the launch traced here: 109 us
  waiting for transfers between devices  34.8 us (31%)
  starting transfers between devices  29.8 us (27%)
  Pallas kernels  17.8 us (16%)
  blocking collectives  14.7 us (13%)
  local copies, waits for them, and re-layouts  9.82 us (9%)
  other arithmetic  1.89 us (2%)
    ppermute x18, waiting for transfers between devices, shift(): return lax.ppermute(v, axis, [(i, (i + s) % n) for i in range(n)])  22.3 us
    ppermute x18, starting transfers between devices, shift(): return lax.ppermute(v, axis, [(i, (i + s) % n) for i in range(n)])  15.2 us
    all_to_all x1, blocking collectives, body(): got = lax.all_to_all(rows, ('x', 'y', 'z'), 0, 0, tiled=True)  14.7 us
    all_to_all x1, waiting for transfers between devices, body(): received = lax.all_to_all(sent, 'z', 0, 0, tiled=True)  12.5 us
    pallas_call x1, Pallas kernels, conv(): pl.pallas_call(conv_kernel, out_shape=[jax.ShapeDtypeStruct((blocks, 2 *...  12.2 us
    unnamed x20, local copies, waits for them, and re-layouts  6.25 us
    all_to_all x1, starting transfers between devices, body(): lax.all_to_all(jnp.broadcast_to(bg[None], (tensor, *bg.shape)), 'z', 0, 0...  5.86 us
    pallas_call x1, Pallas kernels, squares(): pl.pallas_call(kernel, out_shape=jax.ShapeDtypeStruct((chips, ranks // ch...  5.53 us
  transfers between devices with their start and end apart: 21, of which 11 were waited for; matrix products, arithmetic and copies ran while one was open for 2% of the time, Pallas kernels for 11%

profile of v8, /device:TPU:1, one launch (start us, length us, event | category | flops | bytes accessed | tf_op | source)
XLA Modules:
  0.0 109.0 jit_solution(3341517914043644274)
XLA Ops:
  0.0 1.4 %broadcast_in_dim.2 = bf16[4,40,320]{2,1,0:T(8,128)(2,1)} broadcast(bf16[40,320]{1,0:T(8,128)(2,1)} %bitcast.32), dimensions={1,2} | broadcast | bytes 128000 | tf_op jit(solution)/shard_map/basis_g_z/broadcast_in_dim | solution.py:167
  1.4 5.9 %all-to-all-start = ((bf16[4,40,320]{2,1,0:T(8,128)(2,1)}), bf16[4,40,320]{2,1,0:T(8,128)(2,1)S(1)}, u32[]{:S(2)}, u32[]{:S(2)}) async-start(bf16[4,40,320]{2,1,0:T(8,128)(2,1)} %broadcast_in_dim.2), calls=%async_computation | async-start | bytes 245760 | tf_op jit(solution)/shard_map/basis_g_z/all_to_all | solution.py:167
  8.3 2.5 %collective-permute-start.2 = (bf16[9,4,960]{2,1,0:T(4,128)(2,1)S(1)}, bf16[9,4,960]{2,1,0:T(4,128)(2,1)S(1)}, u32[]{:S(2)}, u32[]{:S(2)}) collective-permute-start(bf16[9,4,960]{2,1,0:T(4,128)(2,1)S(1)} %reshape.13), channel_id=1, source_target_pairs={{0,96},{32,0},{64,32},{96,64},{1,97},{33,1},{65,33},{97,65},{2,98}... | collective-permute-start | bytes 207368 | tf_op jit(solution)/shard_map/basis_a_x/ppermute | solution.py:145
  12.3 3.4 %collective-permute-done.1 = bf16[9,4,960]{2,1,0:T(4,128)(2,1)S(1)} collective-permute-done((bf16[9,4,960]{2,1,0:T(4,128)(2,1)S(1)}, bf16[9,4,960]{2,1,0:T(4,128)(2,1)S(1)}, u32[]{:S(2)}, u32[]{:S(2)}) %collective-permute-start.1) | collective-permute-done | bytes 69152 | tf_op jit(solution)/shard_map/basis_a_x/ppermute | solution.py:145
  16.6 2.5 %collective-permute-start.9 = (bf16[8,320,512]{2,1,0:T(8,128)(2,1)}, bf16[8,320,512]{2,1,0:T(8,128)(2,1)}, u32[]{:S(2)}, u32[]{:S(2)}) collective-permute-start(bf16[8,320,512]{2,1,0:T(8,128)(2,1)} %bitcast.23), channel_id=1, source_target_pairs={{0,4},{4,0},{1,5},{5,1},{2,6},{6,2},{3,7},{7,3},{8,12},{12,8},{9,1... | collective-permute-start | bytes 7864328 | tf_op jit(solution)/shard_map/basis_a_y/ppermute | solution.py:145
  19.0 4.5 %all-to-all-start.2 = ((bf16[8,320,512]{2,1,0:T(8,128)(2,1)}), bf16[8,320,512]{2,1,0:T(8,128)(2,1)S(1)}, u32[]{:S(2)}, u32[]{:S(2)}) async-start(bf16[8,320,512]{2,1,0:T(8,128)(2,1)} %bitcast.25), calls=%async_computation.2 | async-start | bytes 5242880 | tf_op jit(solution)/shard_map/exchange_grads/all_to_all | solution.py:170
  24.0 2.7 %collective-permute-start.5 = (bf16[9,16,960]{2,1,0:T(8,128)(2,1)S(1)}, bf16[9,16,960]{2,1,0:T(8,128)(2,1)S(1)}, u32[]{:S(2)}, u32[]{:S(2)}) collective-permute-start(bf16[9,16,960]{2,1,0:T(8,128)(2,1)S(1)} %pad_maximum_fusion.2), channel_id=1, source_target_pairs={{0,24},{8,0},{16,8},{24,16},{1,25},{9,1},{17,9},{25,17},{2,26},{10... | collective-permute-start | bytes 829448 | tf_op jit(solution)/shard_map/basis_a_y/ppermute | solution.py:145
  27.9 1.0 collective-permute-start.7
  28.9 4.4 %collective-permute-done.7 = bf16[40,1280]{1,0:T(8,128)(2,1)S(1)} collective-permute-done((bf16[40,1280]{1,0:T(8,128)(2,1)S(1)}, bf16[40,1280]{1,0:T(8,128)(2,1)S(1)}, u32[]{:S(2)}, u32[]{:S(2)}) %collective-permute-start.7) | collective-permute-done | bytes 102432 | tf_op jit(solution)/shard_map/basis_g_x/ppermute | solution.py:145
  33.2 1.1 collective-permute-start.6
  34.3 3.9 %collective-permute-done.6 = bf16[40,1280]{1,0:T(8,128)(2,1)S(1)} collective-permute-done((bf16[40,1280]{1,0:T(8,128)(2,1)S(1)}, bf16[40,1280]{1,0:T(8,128)(2,1)S(1)}, u32[]{:S(2)}, u32[]{:S(2)}) %collective-permute-start.6) | collective-permute-done | bytes 102432 | tf_op jit(solution)/shard_map/basis_g_x/ppermute | solution.py:145
  38.7 4.8 %collective-permute-done.3 = bf16[9,16,960]{2,1,0:T(8,128)(2,1)S(1)} collective-permute-done((bf16[9,16,960]{2,1,0:T(8,128)(2,1)S(1)}, bf16[9,16,960]{2,1,0:T(8,128)(2,1)S(1)}, u32[]{:S(2)}, u32[]{:S(2)}) %collective-permute-start.3) | collective-permute-done | bytes 276512 | tf_op jit(solution)/shard_map/basis_a_y/ppermute | solution.py:145
  44.8 1.0 collective-permute-start.10
  45.8 1.4 %pad_maximum_fusion.b_ref = bf16[9,64,960]{2,1,0:T(8,128)(2,1)S(1)} fusion(bf16[9,16,960]{2,1,0:T(8,128)(2,1)} %copy-done.7, bf16[9,16,960]{2,1,0:T(8,128)(2,1)} %copy-done.8, bf16[9,16,960]{2,1,0:T(8,128)(2,1)} %copy-done.9, bf16[9,16,960]{2,1,0:T(8,128)(2,1)} %copy-done.6), kind=kLoop, calls=%fused_computation | loop fusion | flops 4423680 | bytes 2211840 | tf_op jit(solution)/shard_map/coeff_parts/concatenate | solution.py:183
  47.2 1.7 %copy-done = bf16[8,512,320]{1,2,0:T(8,128)(2,1)S(1)} copy-done((bf16[8,512,320]{1,2,0:T(8,128)(2,1)S(1)}, bf16[8,512,320]{1,2,0:T(8,128)(2,1)}, u32[]{:S(2)}) %copy-start) | copy-done | bytes 2621464
  49.0 12.2 %conv_taps.1 = (bf16[4,4,64,512]{3,2,1,0:T(8,128)(2,1)S(1)}, f32[4,64,512]{2,1,0:T(8,128)S(1)}) custom-call(s32[1]{0:T(128)} %bitcast.3.idx_ref, bf16[9,64,960]{2,1,0:T(8,128)(2,1)S(1)} %pad_maximum_fusion.b_ref, bf16[8,320,512]{2,1,0:T(8,128)(2,1)S(1)} %bitcast.24, bf16[8,320,512]{2,1,0:T(8,128)(2,1)} %collective-permute-done.9.x_oth_ref), custom_call_target="tpu_custom_call" | custom-call | tf_op jit(solution)/shard_map/coeff_parts/conv_taps/pallas_call | solution.py:60
  63.0 3.3 %collective-permute-done.10.refs_6_ = bf16[4,40,1280]{2,1,0:T(8,128)(2,1)} collective-permute-done((bf16[4,40,1280]{2,1,0:T(8,128)(2,1)S(1)}, bf16[4,40,1280]{2,1,0:T(8,128)(2,1)}, u32[]{:S(2)}, u32[]{:S(2)}) %collective-permute-start.10) | collective-permute-done | bytes 409632 | tf_op jit(solution)/shard_map/basis_g_y/ppermute | solution.py:145
  66.7 4.2 %all-to-all-start.1 = ((bf16[4,4,64,512]{3,2,1,0:T(8,128)(2,1)}), bf16[4,4,64,512]{3,2,1,0:T(8,128)(2,1)}, u32[]{:S(2)}, u32[]{:S(2)}) async-start(bf16[4,4,64,512]{3,2,1,0:T(8,128)(2,1)} %copy-done.1), calls=%async_computation.1 | async-start | bytes 2097152 | tf_op jit(solution)/shard_map/coeff_parts/all_to_all | solution.py:184
  71.0 1.0 collective-permute-done.14.refs_9_
  72.9 12.5 %all-to-all-done.1.refs_1_ = bf16[4,4,64,512]{3,2,1,0:T(8,128)(2,1)} async-done(((bf16[4,4,64,512]{3,2,1,0:T(8,128)(2,1)}), bf16[4,4,64,512]{3,2,1,0:T(8,128)(2,1)}, u32[]{:S(2)}, u32[]{:S(2)}) %all-to-all-start.1) | async-done | bytes 1048608 | tf_op jit(solution)/shard_map/coeff_parts/all_to_all | solution.py:184
  85.5 1.0 copy-done.3
  86.6 1.0 copy-done.5
  87.6 5.5 %squared_sums.1 = f32[16,4,1280]{2,1,0:T(4,128)S(1)} custom-call(s32[4]{0:T(128)S(1)} %pad_add_fusion.refs_0_, bf16[4,4,64,512]{3,2,1,0:T(8,128)(2,1)} %all-to-all-done.1.refs_1_, f32[4,64,512]{2,1,0:T(8,128)S(1)} %copy-done.3, bf16[8,320,512]{2,1,0:T(8,128)(2,1)S(1)} %all-to-all-done.2.refs_3_, bf16[8,320,512]{2,1,0:T(8,128)(2,1)} %collective-permute-done.13.refs_4_, ...), custom_call_target="tpu_custom_call" | custom-call | tf_op jit(solution)/shard_map/squared_sums/pallas_call | solution.py:128
  93.5 14.7 %all_to_all.20 = f32[64,1,1280]{2,1,0:T(1,128)S(1)} all-to-all(f32[64,1,1280]{2,1,0:T(1,128)S(1)} %reshape.15), channel_id=1, replica_groups=mesh['x'=4,'y'=4,'core'=2,'z'=4] {'x','y','z'}, dimensions={0} | all-to-all | bytes 655360 | tf_op jit(solution)/shard_map/sum_examples/all_to_all | solution.py:197
  (53 shorter events, 11.2 us)
Async XLA Ops:
  1.4 15.0 %all-to-all-start = ((bf16[4,40,320]{2,1,0:T(8,128)(2,1)}), bf16[4,40,320]{2,1,0:T(8,128)(2,1)S(1)}, u32[]{:S(2)}, u32[]{:S(2)}) async-start(bf16[4,40,320]{2,1,0:T(8,128)(2,1)} %broadcast_in_dim.2), calls=%async_computation | async-start | bytes 245760 | tf_op jit(solution)/shard_map/basis_g_z/all_to_all | solution.py:167
  8.3 4.0 %collective-permute-start.2 = (bf16[9,4,960]{2,1,0:T(4,128)(2,1)S(1)}, bf16[9,4,960]{2,1,0:T(4,128)(2,1)S(1)}, u32[]{:S(2)}, u32[]{:S(2)}) collective-permute-start(bf16[9,4,960]{2,1,0:T(4,128)(2,1)S(1)} %reshape.13), channel_id=1, source_target_pairs={{0,96},{32,0},{64,32},{96,64},{1,97},{33,1},{65,33},{97,65},{2,98}... | collective-permute-start | bytes 207368 | tf_op jit(solution)/shard_map/basis_a_x/ppermute | solution.py:145
  10.9 4.8 %collective-permute-start.1 = (bf16[9,4,960]{2,1,0:T(4,128)(2,1)S(1)}, bf16[9,4,960]{2,1,0:T(4,128)(2,1)S(1)}, u32[]{:S(2)}, u32[]{:S(2)}) collective-permute-start(bf16[9,4,960]{2,1,0:T(4,128)(2,1)S(1)} %reshape.13), channel_id=1, source_target_pairs={{0,64},{32,96},{64,0},{96,32},{1,65},{33,97},{65,1},{97,33},{2,66}... | collective-permute-start | bytes 207368 | tf_op jit(solution)/shard_map/basis_a_x/ppermute | solution.py:145
  11.4 5.0 %collective-permute-start = (bf16[9,4,960]{2,1,0:T(4,128)(2,1)S(1)}, bf16[9,4,960]{2,1,0:T(4,128)(2,1)S(1)}, u32[]{:S(2)}, u32[]{:S(2)}) collective-permute-start(bf16[9,4,960]{2,1,0:T(4,128)(2,1)S(1)} %reshape.13), channel_id=1, source_target_pairs={{0,32},{32,64},{64,96},{96,0},{1,33},{33,65},{65,97},{97,1},{2,34}... | collective-permute-start | bytes 207368 | tf_op jit(solution)/shard_map/basis_a_x/ppermute | solution.py:145
  16.6 10.6 %copy-start.6 = (bf16[9,16,960]{2,1,0:T(8,128)(2,1)}, bf16[9,16,960]{2,1,0:T(8,128)(2,1)S(1)}, u32[]{:S(2)}) copy-start(bf16[9,16,960]{2,1,0:T(8,128)(2,1)S(1)} %pad_maximum_fusion.2) | copy-start | bytes 829444
  16.6 30.6 %collective-permute-start.9 = (bf16[8,320,512]{2,1,0:T(8,128)(2,1)}, bf16[8,320,512]{2,1,0:T(8,128)(2,1)}, u32[]{:S(2)}, u32[]{:S(2)}) collective-permute-start(bf16[8,320,512]{2,1,0:T(8,128)(2,1)} %bitcast.23), channel_id=1, source_target_pairs={{0,4},{4,0},{1,5},{5,1},{2,6},{6,2},{3,7},{7,3},{8,12},{12,8},{9,1... | collective-permute-start | bytes 7864328 | tf_op jit(solution)/shard_map/basis_a_y/ppermute | solution.py:145
  19.0 47.2 %all-to-all-start.2 = ((bf16[8,320,512]{2,1,0:T(8,128)(2,1)}), bf16[8,320,512]{2,1,0:T(8,128)(2,1)S(1)}, u32[]{:S(2)}, u32[]{:S(2)}) async-start(bf16[8,320,512]{2,1,0:T(8,128)(2,1)} %bitcast.25), calls=%async_computation.2 | async-start | bytes 5242880 | tf_op jit(solution)/shard_map/exchange_grads/all_to_all | solution.py:170
  23.7 4.2 %collective-permute-start.8 = (bf16[40,1280]{1,0:T(8,128)(2,1)S(1)}, bf16[40,1280]{1,0:T(8,128)(2,1)S(1)}, u32[]{:S(2)}, u32[]{:S(2)}) collective-permute-start(bf16[40,1280]{1,0:T(8,128)(2,1)S(1)} %concatenate.10), channel_id=1, source_target_pairs={{0,96},{32,0},{64,32},{96,64},{1,97},{33,1},{65,33},{97,65},{2,98}... | collective-permute-start | bytes 307208 | tf_op jit(solution)/shard_map/basis_g_x/ppermute | solution.py:145
  24.0 14.7 %collective-permute-start.5 = (bf16[9,16,960]{2,1,0:T(8,128)(2,1)S(1)}, bf16[9,16,960]{2,1,0:T(8,128)(2,1)S(1)}, u32[]{:S(2)}, u32[]{:S(2)}) collective-permute-start(bf16[9,16,960]{2,1,0:T(8,128)(2,1)S(1)} %pad_maximum_fusion.2), channel_id=1, source_target_pairs={{0,24},{8,0},{16,8},{24,16},{1,25},{9,1},{17,9},{25,17},{2,26},{10... | collective-permute-start | bytes 829448 | tf_op jit(solution)/shard_map/basis_a_y/ppermute | solution.py:145
  26.8 12.0 %collective-permute-start.4 = (bf16[9,16,960]{2,1,0:T(8,128)(2,1)S(1)}, bf16[9,16,960]{2,1,0:T(8,128)(2,1)S(1)}, u32[]{:S(2)}, u32[]{:S(2)}) collective-permute-start(bf16[9,16,960]{2,1,0:T(8,128)(2,1)S(1)} %pad_maximum_fusion.2), channel_id=1, source_target_pairs={{0,16},{8,24},{16,0},{24,8},{1,17},{9,25},{17,1},{25,9},{2,18},{10... | collective-permute-start | bytes 829448 | tf_op jit(solution)/shard_map/basis_a_y/ppermute | solution.py:145
  27.1 16.4 %collective-permute-start.3 = (bf16[9,16,960]{2,1,0:T(8,128)(2,1)S(1)}, bf16[9,16,960]{2,1,0:T(8,128)(2,1)S(1)}, u32[]{:S(2)}, u32[]{:S(2)}) collective-permute-start(bf16[9,16,960]{2,1,0:T(8,128)(2,1)S(1)} %pad_maximum_fusion.2), channel_id=1, source_target_pairs={{0,8},{8,16},{16,24},{24,0},{1,9},{9,17},{17,25},{25,1},{2,10},{10... | collective-permute-start | bytes 829448 | tf_op jit(solution)/shard_map/basis_a_y/ppermute | solution.py:145
  27.9 5.3 %collective-permute-start.7 = (bf16[40,1280]{1,0:T(8,128)(2,1)S(1)}, bf16[40,1280]{1,0:T(8,128)(2,1)S(1)}, u32[]{:S(2)}, u32[]{:S(2)}) collective-permute-start(bf16[40,1280]{1,0:T(8,128)(2,1)S(1)} %concatenate.10), channel_id=1, source_target_pairs={{0,64},{32,96},{64,0},{96,32},{1,65},{33,97},{65,1},{97,33},{2,66}... | collective-permute-start | bytes 307208 | tf_op jit(solution)/shard_map/basis_g_x/ppermute | solution.py:145
  33.2 5.0 %collective-permute-start.6 = (bf16[40,1280]{1,0:T(8,128)(2,1)S(1)}, bf16[40,1280]{1,0:T(8,128)(2,1)S(1)}, u32[]{:S(2)}, u32[]{:S(2)}) collective-permute-start(bf16[40,1280]{1,0:T(8,128)(2,1)S(1)} %concatenate.10), channel_id=1, source_target_pairs={{0,32},{32,64},{64,96},{96,0},{1,33},{33,65},{65,97},{97,1},{2,34}... | collective-permute-start | bytes 307208 | tf_op jit(solution)/shard_map/basis_g_x/ppermute | solution.py:145
  38.7 5.5 %copy-start.7 = (bf16[9,16,960]{2,1,0:T(8,128)(2,1)}, bf16[9,16,960]{2,1,0:T(8,128)(2,1)S(1)}, u32[]{:S(2)}) copy-start(bf16[9,16,960]{2,1,0:T(8,128)(2,1)S(1)} %collective-permute-done.5) | copy-start | bytes 829444
  44.3 18.7 %collective-permute-start.12 = (bf16[4,40,1280]{2,1,0:T(8,128)(2,1)S(1)}, bf16[4,40,1280]{2,1,0:T(8,128)(2,1)S(1)}, u32[]{:S(2)}, u32[]{:S(2)}) collective-permute-start(bf16[4,40,1280]{2,1,0:T(8,128)(2,1)S(1)} %pad_maximum_fusion.1.refs_5_), channel_id=1, source_target_pairs={{0,24},{8,0},{16,8},{24,16},{1,25},{9,1},{17,9},{25,17},{2,26},{10... | collective-permute-start | bytes 1228808 | tf_op jit(solution)/shard_map/basis_g_y/ppermute | solution.py:145
  44.4 18.6 %collective-permute-start.11 = (bf16[4,40,1280]{2,1,0:T(8,128)(2,1)S(1)}, bf16[4,40,1280]{2,1,0:T(8,128)(2,1)}, u32[]{:S(2)}, u32[]{:S(2)}) collective-permute-start(bf16[4,40,1280]{2,1,0:T(8,128)(2,1)S(1)} %pad_maximum_fusion.1.refs_5_), channel_id=1, source_target_pairs={{0,16},{8,24},{16,0},{24,8},{1,17},{9,25},{17,1},{25,9},{2,18},{10... | collective-permute-start | bytes 1228808 | tf_op jit(solution)/shard_map/basis_g_y/ppermute | solution.py:145
  44.8 21.4 %collective-permute-start.10 = (bf16[4,40,1280]{2,1,0:T(8,128)(2,1)S(1)}, bf16[4,40,1280]{2,1,0:T(8,128)(2,1)}, u32[]{:S(2)}, u32[]{:S(2)}) collective-permute-start(bf16[4,40,1280]{2,1,0:T(8,128)(2,1)S(1)} %pad_maximum_fusion.1.refs_5_), channel_id=1, source_target_pairs={{0,8},{8,16},{16,24},{24,0},{1,9},{9,17},{17,25},{25,1},{2,10},{10... | collective-permute-start | bytes 1228808 | tf_op jit(solution)/shard_map/basis_g_y/ppermute | solution.py:145
  63.0 22.5 %copy-start.4 = (bf16[4,40,1280]{2,1,0:T(8,128)(2,1)}, bf16[4,40,1280]{2,1,0:T(8,128)(2,1)S(1)}, u32[]{:S(2)}) copy-start(bf16[4,40,1280]{2,1,0:T(8,128)(2,1)S(1)} %collective-permute-done.12.refs_8_) | copy-start | bytes 1228804
  66.2 19.3 %collective-permute-start.13 = (bf16[8,320,512]{2,1,0:T(8,128)(2,1)S(1)}, bf16[8,320,512]{2,1,0:T(8,128)(2,1)}, u32[]{:S(2)}, u32[]{:S(2)}) collective-permute-start(bf16[8,320,512]{2,1,0:T(8,128)(2,1)S(1)} %all-to-all-done.2.refs_3_), channel_id=1, source_target_pairs={{0,4},{4,0},{1,5},{5,1},{2,6},{6,2},{3,7},{7,3},{8,12},{12,8},{9,1... | collective-permute-start | bytes 7864328 | tf_op jit(solution)/shard_map/exchange_cores/ppermute | solution.py:145
  66.7 5.3 %collective-permute-start.14 = (bf16[4,40,1280]{2,1,0:T(8,128)(2,1)S(1)}, bf16[4,40,1280]{2,1,0:T(8,128)(2,1)}, u32[]{:S(2)}, u32[]{:S(2)}) collective-permute-start(bf16[4,40,1280]{2,1,0:T(8,128)(2,1)S(1)} %pad_maximum_fusion.1.refs_5_), channel_id=1, source_target_pairs={{0,4},{4,0},{1,5},{5,1},{2,6},{6,2},{3,7},{7,3},{8,12},{12,8},{9,1... | collective-permute-start | bytes 1228808 | tf_op jit(solution)/shard_map/exchange_cores/ppermute | solution.py:145
  66.7 18.7 %all-to-all-start.1 = ((bf16[4,4,64,512]{3,2,1,0:T(8,128)(2,1)}), bf16[4,4,64,512]{3,2,1,0:T(8,128)(2,1)}, u32[]{:S(2)}, u32[]{:S(2)}) async-start(bf16[4,4,64,512]{3,2,1,0:T(8,128)(2,1)} %copy-done.1), calls=%async_computation.1 | async-start | bytes 2097152 | tf_op jit(solution)/shard_map/coeff_parts/all_to_all | solution.py:184
  72.0 13.5 %collective-permute-start.15 = (bf16[4,40,1280]{2,1,0:T(8,128)(2,1)}, bf16[4,40,1280]{2,1,0:T(8,128)(2,1)}, u32[]{:S(2)}, u32[]{:S(2)}) collective-permute-start(bf16[4,40,1280]{2,1,0:T(8,128)(2,1)} %collective-permute-done.10.refs_6_), channel_id=1, source_target_pairs={{0,4},{4,0},{1,5},{5,1},{2,6},{6,2},{3,7},{7,3},{8,12},{12,8},{9,1... | collective-permute-start | bytes 1228808 | tf_op jit(solution)/shard_map/exchange_cores/ppermute | solution.py:145
  72.4 13.1 %collective-permute-start.16 = (bf16[4,40,1280]{2,1,0:T(8,128)(2,1)}, bf16[4,40,1280]{2,1,0:T(8,128)(2,1)}, u32[]{:S(2)}, u32[]{:S(2)}) collective-permute-start(bf16[4,40,1280]{2,1,0:T(8,128)(2,1)} %collective-permute-done.11.refs_7_), channel_id=1, source_target_pairs={{0,4},{4,0},{1,5},{5,1},{2,6},{6,2},{3,7},{7,3},{8,12},{12,8},{9,1... | collective-permute-start | bytes 1228808 | tf_op jit(solution)/shard_map/exchange_cores/ppermute | solution.py:145
  72.5 13.0 %collective-permute-start.17 = (bf16[4,40,1280]{2,1,0:T(8,128)(2,1)S(1)}, bf16[4,40,1280]{2,1,0:T(8,128)(2,1)}, u32[]{:S(2)}, u32[]{:S(2)}) collective-permute-start(bf16[4,40,1280]{2,1,0:T(8,128)(2,1)S(1)} %collective-permute-done.12.refs_8_), channel_id=1, source_target_pairs={{0,4},{4,0},{1,5},{5,1},{2,6},{6,2},{3,7},{7,3},{8,12},{12,8},{9,1... | collective-permute-start | bytes 1228808 | tf_op jit(solution)/shard_map/exchange_cores/ppermute | solution.py:145
  (7 other events, 11.1 us)

commit v9 on v5

--- a/solution.py
+++ b/solution.py
@@ -67,32 +67,40 @@
     )(idx, taps, x, x_oth)
 
 
-def squares_kernel(idx_ref, c_ref, g_ref, g_oth_ref, *refs, scale):
+def squares_kernel(idx_ref, own_ref, r1_ref, r2_ref, r3_ref, g_ref, g_oth_ref, *refs, scale):
     *bg_refs, o_ref, hi_ref, m_ref, sq_ref = refs
-    x, y, core, z = idx_ref[0], idx_ref[1], idx_ref[2], idx_ref[3]
+    x, y, core = idx_ref[0], idx_ref[1], idx_ref[2]
     side, width = len(bg_refs) // 2, bg_refs[0].shape[1]
-    examples, ranks = c_ref.shape[0], c_ref.shape[1]
+    examples, ranks = own_ref.shape[0], own_ref.shape[1]
     per = examples // 2
     tensor = g_ref.shape[0] // per
 
     def chip(rx, ry):
         return ((x + side - rx) % side) * side + (y + side - ry) % side
 
+    low_half = lax.broadcasted_iota(jnp.int32, (1, 2 * ranks), 1) < ranks
+    pair = None
     for n in range(examples):
-        c = c_ref[n]
+        c = own_ref[n]
+        for r in (r1_ref, r2_ref, r3_ref):
+            c = c + r[n].astype(jnp.float32)
         hi_ref[n] = c.astype(jnp.bfloat16)
         hi = hi_ref[n]
         lo = (c - hi.astype(jnp.float32)).astype(jnp.bfloat16)
         both = jnp.concatenate([hi, lo], axis=0)
         src = g_ref if n < per else g_oth_ref
-        g = jnp.concatenate([src[((z + tensor - t) % tensor) * per + n % per] for t in range(tensor)], axis=0)
-        m = lax.dot_general(both, g, NT, preferred_element_type=jnp.float32)
-        m_ref[n * ranks : (n + 1) * ranks] = (m[:ranks] + m[ranks:]).astype(jnp.bfloat16)
+        g = jnp.concatenate([src[t * per + n % per] for t in range(tensor)], axis=0)
+        m = lax.dot_general(g, both, NT, preferred_element_type=jnp.float32)
+        m = m + pltpu.roll(m, ranks, 1)
+        if n % 2 == 0:
+            pair = m
+        else:
+            m_ref[:, (n - 1) * ranks : (n + 1) * ranks] = jnp.where(low_half, pair, m).astype(jnp.bfloat16)
     m = m_ref[...]
     for half in range(2):
         for ry in range(side):
             bg = bg_refs[half * side + ry][...].reshape(side * width, -1)
-            p = lax.dot_general(bg, m, NT, preferred_element_type=jnp.float32)
+            p = jnp.dot(bg, m, preferred_element_type=jnp.float32)
             p = p * p
             while p.shape[1] > 2 * ranks:
                 p = p[:, : p.shape[1] // 2] + p[:, p.shape[1] // 2 :]
@@ -106,8 +114,8 @@
         o_ref[chip(b % side, b // side)] = sq[b * low : (b + 1) * low]
 
 
-def squares(idx, c, g, g_oth, bg, bg_oth, scale):
-    examples, ranks = c.shape[0], c.shape[1]
+def squares(idx, own, received, g, g_oth, bg, bg_oth, scale):
+    examples, ranks = own.shape[0], own.shape[1]
     side, width, hidden = bg[0].shape
     chips = side * side
 
@@ -117,16 +125,16 @@
     return pl.pallas_call(
         kernel,
         out_shape=jax.ShapeDtypeStruct((chips, ranks // chips, 2 * chips * width), jnp.float32),
-        in_specs=[SMEM] + [VMEM] * (3 + 2 * side),
+        in_specs=[SMEM] + [VMEM] * (6 + 2 * side),
         out_specs=VMEM,
         scratch_shapes=[
             pltpu.VMEM((examples, ranks, POS), jnp.bfloat16),
-            pltpu.VMEM((examples * ranks, hidden), jnp.bfloat16),
+            pltpu.VMEM((hidden, examples * ranks), jnp.bfloat16),
             pltpu.VMEM((2 * chips * width, 2 * ranks), jnp.float32),
         ],
         compiler_params=pltpu.CompilerParams(vmem_limit_bytes=16 << 20),
         name="squared_sums",
-    )(idx, c, g, g_oth, *bg, *bg_oth)
+    )(idx, own, *received, g, g_oth, *bg, *bg_oth)
 
 
 def shift(v, axis, s):
@@ -152,7 +160,8 @@
         own = own.reshape(AB, own.shape[1], 3 * channels)
         ba = around(own, "x")
     with jax.named_scope("basis_g_z"):
-        bg = around(basis_g.T, "z")
+        bg = basis_g.T
+        bg = lax.all_to_all(jnp.broadcast_to(bg[None], (tensor, *bg.shape)), "z", 0, 0, tiled=True)
     with jax.named_scope("exchange_grads"):
         grads, bg, ba = lax.optimization_barrier((grads, bg, ba))
         g = lax.all_to_all(grads, "z", 0, 0, tiled=True)
@@ -162,28 +171,26 @@
         x_oth = shift(give, "core", 1)
         ba = around(ba, "y")
     with jax.named_scope("basis_g_x"):
-        bg = around(jnp.concatenate(bg, axis=1), "x")
-
-    def parts(shifts, dtypes):
-        return conv(jnp.stack([(z + s) % tensor for s in shifts]), jnp.concatenate(ba, axis=1), x, x_oth, per, dtypes)
+        bg = around(jnp.concatenate(list(bg), axis=1), "x")
 
     ba, bg = lax.optimization_barrier((ba, bg))
     with jax.named_scope("basis_g_y"):
         bg = around(jnp.stack(bg), "y")
     with jax.named_scope("coeff_parts"):
         bf16 = jnp.bfloat16
-        *sent, mine = parts((2, 1, 3, 0), (bf16, bf16, bf16, jnp.float32))
-        received = [shift(v, "z", s) for v, s in zip(sent, (2, 1, 3))]
+        blocks = [(z + s) % tensor for s in (2, 1, 3, 0)]
+        far, near = conv(jnp.stack(blocks[:2]), jnp.concatenate(ba, axis=1), x, x_oth, per, (bf16, bf16))
+        received = [shift(far, "z", 2), shift(near, "z", 1)]
+        ba, blocks, _ = lax.optimization_barrier((ba, blocks, far))
+        last, mine = conv(jnp.stack(blocks[2:]), jnp.concatenate(ba, axis=1), x, x_oth, per, (bf16, jnp.float32))
     with jax.named_scope("exchange_cores"):
-        g, bg, received[1] = lax.optimization_barrier((g, bg, received[1]))
+        g, bg, received, mine = lax.optimization_barrier((g, bg, received, mine))
         g_oth = shift(g, "core", 1)
         bg_oth = [shift(v, "core", 1) for v in bg]
-
-    total_coeff = mine
-    for r in received:
-        total_coeff = total_coeff + r.astype(jnp.float32)
+    received.append(shift(last, "z", 3))
+
     examples = here * lax.axis_size(("x", "y", "core"))
-    total = squares(jnp.stack(coords), total_coeff, g, g_oth, bg, bg_oth, 1.0 / examples)
+    total = squares(jnp.stack(coords), mine, received, g, g_oth, bg, bg_oth, 1.0 / examples)
 
     with jax.named_scope("sum_examples"):
         rows = total.reshape(-1, 1, total.shape[2])

time: 117 us -> 113 us (0.966)
  starting transfers between devices: 42 us -> 32.4 us
  local copies, waits for them, and re-layouts: 6.99 us -> 9.54 us
  Pallas kernels: 19 us -> 20.5 us
    ppermute x24 -> x21, starting transfers between devices: 37.9 us -> 22 us  [shift(): return lax.ppermute(v, axis, [(i, (i + s) % n) for i in range(n)])]
    all_to_all x0 -> x1, starting transfers between devices: none -> 5.86 us  [body(): lax.all_to_all(jnp.broadcast_to(bg[None], (tensor, *bg.shape)), 'z', 0, 0...]
    pallas_call x1 -> x2, Pallas kernels: 12.9 us -> 15.2 us  [conv(): pl.pallas_call(conv_kernel, out_shape=[jax.ShapeDtypeStruct((2 * per, ran...]
    concatenate x1 -> x2, other arithmetic: 1.28 us -> 2.74 us  [body(): jnp.concatenate(ba, axis=1)]
    broadcast_in_dim x0 -> x1, local copies, waits for them, and re-layouts: none -> 1.4 us  [body(): jnp.broadcast_to(bg[None], (tensor, *bg.shape))]
    add x1 -> x0, other arithmetic: 1.24 us -> none  [body(): total_coeff = total_coeff + r.astype(jnp.float32)]
    ppermute x24 -> x21, waiting for transfers between devices: 26 us -> 26.6 us  [shift(): return lax.ppermute(v, axis, [(i, (i + s) % n) for i in range(n)])]
  transfers between devices with their start and end apart: 25 -> 23, of which waited for: 11 -> 11; matrix products, arithmetic and copies ran while one was open for 3% -> 5% of each run, Pallas kernels for 11% -> 14%
where the time goes in v9:
time: 113 us; the launch traced here: 112 us
  starting transfers between devices  32.4 us (29%)
  waiting for transfers between devices  26.6 us (24%)
  Pallas kernels  20.5 us (18%)
  blocking collectives  17.9 us (16%)
  local copies, waits for them, and re-layouts  9.54 us (8%)
  other arithmetic  4.32 us (4%)
    ppermute x21, waiting for transfers between devices, shift(): return lax.ppermute(v, axis, [(i, (i + s) % n) for i in range(n)])  26.6 us
    ppermute x21, starting transfers between devices, shift(): return lax.ppermute(v, axis, [(i, (i + s) % n) for i in range(n)])  22 us
    all_to_all x1, blocking collectives, body(): got = lax.all_to_all(rows, ('x', 'y', 'z'), 0, 0, tiled=True)  17.9 us
    pallas_call x2, Pallas kernels, conv(): pl.pallas_call(conv_kernel, out_shape=[jax.ShapeDtypeStruct((2 * per, ran...  15.2 us
    unnamed x20, local copies, waits for them, and re-layouts  5.98 us
    all_to_all x1, starting transfers between devices, body(): lax.all_to_all(jnp.broadcast_to(bg[None], (tensor, *bg.shape)), 'z', 0, 0...  5.86 us
    pallas_call x1, Pallas kernels, squares(): pl.pallas_call(kernel, out_shape=jax.ShapeDtypeStruct((chips, ranks // ch...  5.39 us
    all_to_all x1, starting transfers between devices, body(): g = lax.all_to_all(grads, 'z', 0, 0, tiled=True)  4.55 us
  transfers between devices with their start and end apart: 23, of which 11 were waited for; matrix products, arithmetic and copies ran while one was open for 5% of the time, Pallas kernels for 14%

profile of v9, /device:TPU:1, one launch (start us, length us, event | category | flops | bytes accessed | tf_op | source)
XLA Modules:
  0.0 111.6 jit_solution(3601793015422808948)
XLA Ops:
  0.0 1.4 %broadcast_in_dim.2 = bf16[4,40,320]{2,1,0:T(8,128)(2,1)} broadcast(bf16[40,320]{1,0:T(8,128)(2,1)} %bitcast.36), dimensions={1,2} | broadcast | bytes 128000 | tf_op jit(solution)/shard_map/basis_g_z/broadcast_in_dim | solution.py:164
  1.4 5.9 %all-to-all-start = ((bf16[4,40,320]{2,1,0:T(8,128)(2,1)}), bf16[4,40,320]{2,1,0:T(8,128)(2,1)S(1)}, u32[]{:S(2)}, u32[]{:S(2)}) async-start(bf16[4,40,320]{2,1,0:T(8,128)(2,1)} %broadcast_in_dim.2), calls=%async_computation | async-start | bytes 245760 | tf_op jit(solution)/shard_map/basis_g_z/all_to_all | solution.py:164
  8.3 2.5 %collective-permute-start.2 = (bf16[9,4,960]{2,1,0:T(4,128)(2,1)S(1)}, bf16[9,4,960]{2,1,0:T(4,128)(2,1)S(1)}, u32[]{:S(2)}, u32[]{:S(2)}) collective-permute-start(bf16[9,4,960]{2,1,0:T(4,128)(2,1)S(1)} %reshape.12), channel_id=1, source_target_pairs={{0,96},{32,0},{64,32},{96,64},{1,97},{33,1},{65,33},{97,65},{2,98}... | collective-permute-start | bytes 207368 | tf_op jit(solution)/shard_map/basis_a_x/ppermute | solution.py:142
  12.3 3.4 %collective-permute-done.1 = bf16[9,4,960]{2,1,0:T(4,128)(2,1)S(1)} collective-permute-done((bf16[9,4,960]{2,1,0:T(4,128)(2,1)S(1)}, bf16[9,4,960]{2,1,0:T(4,128)(2,1)S(1)}, u32[]{:S(2)}, u32[]{:S(2)}) %collective-permute-start.1) | collective-permute-done | bytes 69152 | tf_op jit(solution)/shard_map/basis_a_x/ppermute | solution.py:142
  16.6 2.5 %collective-permute-start.12 = (bf16[8,320,512]{2,1,0:T(8,128)(2,1)}, bf16[8,320,512]{2,1,0:T(8,128)(2,1)}, u32[]{:S(2)}, u32[]{:S(2)}) collective-permute-start(bf16[8,320,512]{2,1,0:T(8,128)(2,1)} %bitcast.27), channel_id=1, source_target_pairs={{0,4},{4,0},{1,5},{5,1},{2,6},{6,2},{3,7},{7,3},{8,12},{12,8},{9,1... | collective-permute-start | bytes 7864328 | tf_op jit(solution)/shard_map/basis_a_y/ppermute | solution.py:142
  19.0 4.5 %all-to-all-start.1 = ((bf16[8,320,512]{2,1,0:T(8,128)(2,1)}), bf16[8,320,512]{2,1,0:T(8,128)(2,1)}, u32[]{:S(2)}, u32[]{:S(2)}) async-start(bf16[8,320,512]{2,1,0:T(8,128)(2,1)} %bitcast.30), calls=%async_computation.1 | async-start | bytes 5242880 | tf_op jit(solution)/shard_map/exchange_grads/all_to_all | solution.py:167
  24.1 2.7 %collective-permute-start.5 = (bf16[9,16,960]{2,1,0:T(8,128)(2,1)S(1)}, bf16[9,16,960]{2,1,0:T(8,128)(2,1)S(1)}, u32[]{:S(2)}, u32[]{:S(2)}) collective-permute-start(bf16[9,16,960]{2,1,0:T(8,128)(2,1)S(1)} %pad_maximum_fusion.3), channel_id=1, source_target_pairs={{0,24},{8,0},{16,8},{24,16},{1,25},{9,1},{17,9},{25,17},{2,26},{10... | collective-permute-start | bytes 829448 | tf_op jit(solution)/shard_map/basis_a_y/ppermute | solution.py:142
  28.1 1.0 collective-permute-start.7
  29.1 4.5 %collective-permute-done.7 = bf16[40,1280]{1,0:T(8,128)(2,1)S(1)} collective-permute-done((bf16[40,1280]{1,0:T(8,128)(2,1)S(1)}, bf16[40,1280]{1,0:T(8,128)(2,1)S(1)}, u32[]{:S(2)}, u32[]{:S(2)}) %collective-permute-start.7) | collective-permute-done | bytes 102432 | tf_op jit(solution)/shard_map/basis_g_x/ppermute | solution.py:142
  34.5 4.2 %collective-permute-done.6 = bf16[40,1280]{1,0:T(8,128)(2,1)} collective-permute-done((bf16[40,1280]{1,0:T(8,128)(2,1)S(1)}, bf16[40,1280]{1,0:T(8,128)(2,1)}, u32[]{:S(2)}, u32[]{:S(2)}) %collective-permute-start.6) | collective-permute-done | bytes 102432 | tf_op jit(solution)/shard_map/basis_g_x/ppermute | solution.py:142
  38.8 4.8 %collective-permute-done.3 = bf16[9,16,960]{2,1,0:T(8,128)(2,1)} collective-permute-done((bf16[9,16,960]{2,1,0:T(8,128)(2,1)S(1)}, bf16[9,16,960]{2,1,0:T(8,128)(2,1)}, u32[]{:S(2)}, u32[]{:S(2)}) %collective-permute-start.3) | collective-permute-done | bytes 276512 | tf_op jit(solution)/shard_map/basis_a_y/ppermute | solution.py:142
  45.1 1.0 collective-permute-start.9
  46.2 1.4 %pad_maximum_fusion.b_ref = bf16[9,64,960]{2,1,0:T(8,128)(2,1)S(1)} fusion(bf16[9,16,960]{2,1,0:T(8,128)(2,1)} %copy-done.9, bf16[9,16,960]{2,1,0:T(8,128)(2,1)} %collective-permute-done.4, bf16[9,16,960]{2,1,0:T(8,128)(2,1)} %collective-permute-done.3, bf16[9,16,960]{2,1,0:T(8,128)(2,1)} %copy-done.8), kind=kLoop, calls=%fused_computation | loop fusion | flops 4423680 | bytes 2211840 | tf_op jit(solution)/shard_map/coeff_parts/concatenate | solution.py:182
  47.6 7.9 %conv_taps.2 = (bf16[4,64,512]{2,1,0:T(8,128)(2,1)}, bf16[4,64,512]{2,1,0:T(8,128)(2,1)}) custom-call(s32[2]{0:T(128)S(1)} %pad_add_fusion.1.idx_ref, bf16[9,64,960]{2,1,0:T(8,128)(2,1)S(1)} %pad_maximum_fusion.b_ref, bf16[8,320,512]{2,1,0:T(8,128)(2,1)S(1)} %bitcast.28, bf16[8,320,512]{2,1,0:T(8,128)(2,1)} %collective-permute-done.12.x_oth_ref), custom_call_target="tpu_custom_call" | custom-call | tf_op jit(solution)/shard_map/coeff_parts/conv_taps/pallas_call | solution.py:59
  55.6 1.8 %collective-permute-start.14 = (bf16[4,64,512]{2,1,0:T(8,128)(2,1)}, bf16[4,64,512]{2,1,0:T(8,128)(2,1)}, u32[]{:S(2)}, u32[]{:S(2)}) collective-permute-start(bf16[4,64,512]{2,1,0:T(8,128)(2,1)} %get-tuple-element.56), channel_id=1, source_target_pairs={{0,1},{1,2},{2,3},{3,0},{4,5},{5,6},{6,7},{7,4},{8,9},{9,10},{10,1... | collective-permute-start | bytes 786440 | tf_op jit(solution)/shard_map/coeff_parts/ppermute | solution.py:142
  57.3 2.4 %collective-permute-start.13 = (bf16[4,64,512]{2,1,0:T(8,128)(2,1)}, bf16[4,64,512]{2,1,0:T(8,128)(2,1)}, u32[]{:S(2)}, u32[]{:S(2)}) collective-permute-start(bf16[4,64,512]{2,1,0:T(8,128)(2,1)} %get-tuple-element.55), channel_id=1, source_target_pairs={{0,2},{1,3},{2,0},{3,1},{4,6},{5,7},{6,4},{7,5},{8,10},{9,11},{10,... | collective-permute-start | bytes 786440 | tf_op jit(solution)/shard_map/coeff_parts/ppermute | solution.py:142
  59.8 1.4 %pad_maximum_fusion.1.b_ref = bf16[9,64,960]{2,1,0:T(8,128)(2,1)S(1)} fusion(bf16[9,16,960]{2,1,0:T(8,128)(2,1)} %copy-done.9, bf16[9,16,960]{2,1,0:T(8,128)(2,1)} %collective-permute-done.4, bf16[9,16,960]{2,1,0:T(8,128)(2,1)} %collective-permute-done.3, bf16[9,16,960]{2,1,0:T(8,128)(2,1)} %copy-done.8), kind=kLoop, calls=%fused_computation.1 | loop fusion | flops 4423680 | bytes 2211840 | tf_op jit(solution)/shard_map/coeff_parts/concatenate | solution.py:185
  61.2 7.2 %conv_taps.3 = (bf16[4,64,512]{2,1,0:T(8,128)(2,1)S(1)}, f32[4,64,512]{2,1,0:T(8,128)S(1)}) custom-call(s32[2]{0:T(128)S(1)} %pad_add_fusion.2.idx_ref, bf16[9,64,960]{2,1,0:T(8,128)(2,1)S(1)} %pad_maximum_fusion.1.b_ref, bf16[8,320,512]{2,1,0:T(8,128)(2,1)S(1)} %bitcast.29, bf16[8,320,512]{2,1,0:T(8,128)(2,1)} %collective-permute-done.12.x_oth_ref), custom_call_target="tpu_custom_call" | custom-call | tf_op jit(solution)/shard_map/coeff_parts/conv_taps/pallas_call | solution.py:59
  70.6 2.3 %collective-permute-start.16 = (bf16[8,320,512]{2,1,0:T(8,128)(2,1)}, bf16[8,320,512]{2,1,0:T(8,128)(2,1)S(1)}, u32[]{:S(2)}, u32[]{:S(2)}) collective-permute-start(bf16[8,320,512]{2,1,0:T(8,128)(2,1)} %all-to-all-done.1.refs_5_), channel_id=1, source_target_pairs={{0,4},{4,0},{1,5},{5,1},{2,6},{6,2},{3,7},{7,3},{8,12},{12,8},{9,1... | collective-permute-start | bytes 7864328 | tf_op jit(solution)/shard_map/exchange_cores/ppermute | solution.py:142
  74.0 7.0 %collective-permute-done.15.refs_4_ = bf16[4,64,512]{2,1,0:T(8,128)(2,1)S(1)} collective-permute-done((bf16[4,64,512]{2,1,0:T(8,128)(2,1)}, bf16[4,64,512]{2,1,0:T(8,128)(2,1)S(1)}, u32[]{:S(2)}, u32[]{:S(2)}) %collective-permute-start.15) | collective-permute-done | bytes 262176 | tf_op jit(solution)/shard_map/ppermute | solution.py:142
  84.1 1.0 copy-done.2
  85.1 1.0 copy-done.4
  87.1 5.4 %squared_sums.1 = f32[16,4,1280]{2,1,0:T(4,128)S(1)} custom-call(s32[4]{0:T(128)S(1)} %pad_add_fusion.refs_0_, f32[4,64,512]{2,1,0:T(8,128)S(1)} %copy-done.2, bf16[4,64,512]{2,1,0:T(8,128)(2,1)} %collective-permute-done.13.refs_2_, bf16[4,64,512]{2,1,0:T(8,128)(2,1)} %collective-permute-done.14.refs_3_, bf16[4,64,512]{2,1,0:T(8,128)(2,1)S(1)} %copy-done.6, ...), custom_call_target="tpu_custom_call" | custom-call | tf_op jit(solution)/shard_map/squared_sums/pallas_call | solution.py:125
  92.9 17.9 %all_to_all.15 = f32[64,1,1280]{2,1,0:T(1,128)S(1)} all-to-all(f32[64,1,1280]{2,1,0:T(1,128)S(1)} %reshape.14), channel_id=1, replica_groups=mesh['x'=4,'y'=4,'core'=2,'z'=4] {'x','y','z'}, dimensions={0} | all-to-all | bytes 655360 | tf_op jit(solution)/shard_map/sum_examples/all_to_all | solution.py:197
  (61 shorter events, 16.3 us)
Async XLA Ops:
  1.4 15.0 %all-to-all-start = ((bf16[4,40,320]{2,1,0:T(8,128)(2,1)}), bf16[4,40,320]{2,1,0:T(8,128)(2,1)S(1)}, u32[]{:S(2)}, u32[]{:S(2)}) async-start(bf16[4,40,320]{2,1,0:T(8,128)(2,1)} %broadcast_in_dim.2), calls=%async_computation | async-start | bytes 245760 | tf_op jit(solution)/shard_map/basis_g_z/all_to_all | solution.py:164
  8.3 4.0 %collective-permute-start.2 = (bf16[9,4,960]{2,1,0:T(4,128)(2,1)S(1)}, bf16[9,4,960]{2,1,0:T(4,128)(2,1)S(1)}, u32[]{:S(2)}, u32[]{:S(2)}) collective-permute-start(bf16[9,4,960]{2,1,0:T(4,128)(2,1)S(1)} %reshape.12), channel_id=1, source_target_pairs={{0,96},{32,0},{64,32},{96,64},{1,97},{33,1},{65,33},{97,65},{2,98}... | collective-permute-start | bytes 207368 | tf_op jit(solution)/shard_map/basis_a_x/ppermute | solution.py:142
  10.9 4.8 %collective-permute-start.1 = (bf16[9,4,960]{2,1,0:T(4,128)(2,1)S(1)}, bf16[9,4,960]{2,1,0:T(4,128)(2,1)S(1)}, u32[]{:S(2)}, u32[]{:S(2)}) collective-permute-start(bf16[9,4,960]{2,1,0:T(4,128)(2,1)S(1)} %reshape.12), channel_id=1, source_target_pairs={{0,64},{32,96},{64,0},{96,32},{1,65},{33,97},{65,1},{97,33},{2,66}... | collective-permute-start | bytes 207368 | tf_op jit(solution)/shard_map/basis_a_x/ppermute | solution.py:142
  11.4 5.0 %collective-permute-start = (bf16[9,4,960]{2,1,0:T(4,128)(2,1)S(1)}, bf16[9,4,960]{2,1,0:T(4,128)(2,1)S(1)}, u32[]{:S(2)}, u32[]{:S(2)}) collective-permute-start(bf16[9,4,960]{2,1,0:T(4,128)(2,1)S(1)} %reshape.12), channel_id=1, source_target_pairs={{0,32},{32,64},{64,96},{96,0},{1,33},{33,65},{65,97},{97,1},{2,34}... | collective-permute-start | bytes 207368 | tf_op jit(solution)/shard_map/basis_a_x/ppermute | solution.py:142
  16.6 31.1 %collective-permute-start.12 = (bf16[8,320,512]{2,1,0:T(8,128)(2,1)}, bf16[8,320,512]{2,1,0:T(8,128)(2,1)}, u32[]{:S(2)}, u32[]{:S(2)}) collective-permute-start(bf16[8,320,512]{2,1,0:T(8,128)(2,1)} %bitcast.27), channel_id=1, source_target_pairs={{0,4},{4,0},{1,5},{5,1},{2,6},{6,2},{3,7},{7,3},{8,12},{12,8},{9,1... | collective-permute-start | bytes 7864328 | tf_op jit(solution)/shard_map/basis_a_y/ppermute | solution.py:142
  19.0 50.9 %all-to-all-start.1 = ((bf16[8,320,512]{2,1,0:T(8,128)(2,1)}), bf16[8,320,512]{2,1,0:T(8,128)(2,1)}, u32[]{:S(2)}, u32[]{:S(2)}) async-start(bf16[8,320,512]{2,1,0:T(8,128)(2,1)} %bitcast.30), calls=%async_computation.1 | async-start | bytes 5242880 | tf_op jit(solution)/shard_map/exchange_grads/all_to_all | solution.py:167
  23.6 24.1 %copy-start = (bf16[8,512,320]{1,2,0:T(8,128)(2,1)S(1)}, bf16[8,512,320]{1,2,0:T(8,128)(2,1)}, u32[]{:S(2)}) copy-start(bf16[8,512,320]{1,2,0:T(8,128)(2,1)} %param.4) | copy-start | bytes 7864324
  23.7 4.4 %collective-permute-start.8 = (bf16[40,1280]{1,0:T(8,128)(2,1)S(1)}, bf16[40,1280]{1,0:T(8,128)(2,1)S(1)}, u32[]{:S(2)}, u32[]{:S(2)}) collective-permute-start(bf16[40,1280]{1,0:T(8,128)(2,1)S(1)} %concatenate.13), channel_id=1, source_target_pairs={{0,96},{32,0},{64,32},{96,64},{1,97},{33,1},{65,33},{97,65},{2,98}... | collective-permute-start | bytes 307208 | tf_op jit(solution)/shard_map/basis_g_x/ppermute | solution.py:142
  24.1 14.7 %collective-permute-start.5 = (bf16[9,16,960]{2,1,0:T(8,128)(2,1)S(1)}, bf16[9,16,960]{2,1,0:T(8,128)(2,1)S(1)}, u32[]{:S(2)}, u32[]{:S(2)}) collective-permute-start(bf16[9,16,960]{2,1,0:T(8,128)(2,1)S(1)} %pad_maximum_fusion.3), channel_id=1, source_target_pairs={{0,24},{8,0},{16,8},{24,16},{1,25},{9,1},{17,9},{25,17},{2,26},{10... | collective-permute-start | bytes 829448 | tf_op jit(solution)/shard_map/basis_a_y/ppermute | solution.py:142
  26.8 12.0 %collective-permute-start.4 = (bf16[9,16,960]{2,1,0:T(8,128)(2,1)S(1)}, bf16[9,16,960]{2,1,0:T(8,128)(2,1)}, u32[]{:S(2)}, u32[]{:S(2)}) collective-permute-start(bf16[9,16,960]{2,1,0:T(8,128)(2,1)S(1)} %pad_maximum_fusion.3), channel_id=1, source_target_pairs={{0,16},{8,24},{16,0},{24,8},{1,17},{9,25},{17,1},{25,9},{2,18},{10... | collective-permute-start | bytes 829448 | tf_op jit(solution)/shard_map/basis_a_y/ppermute | solution.py:142
  27.2 16.5 %collective-permute-start.3 = (bf16[9,16,960]{2,1,0:T(8,128)(2,1)S(1)}, bf16[9,16,960]{2,1,0:T(8,128)(2,1)}, u32[]{:S(2)}, u32[]{:S(2)}) collective-permute-start(bf16[9,16,960]{2,1,0:T(8,128)(2,1)S(1)} %pad_maximum_fusion.3), channel_id=1, source_target_pairs={{0,8},{8,16},{16,24},{24,0},{1,9},{9,17},{17,25},{25,1},{2,10},{10... | collective-permute-start | bytes 829448 | tf_op jit(solution)/shard_map/basis_a_y/ppermute | solution.py:142
  28.1 5.4 %collective-permute-start.7 = (bf16[40,1280]{1,0:T(8,128)(2,1)S(1)}, bf16[40,1280]{1,0:T(8,128)(2,1)S(1)}, u32[]{:S(2)}, u32[]{:S(2)}) collective-permute-start(bf16[40,1280]{1,0:T(8,128)(2,1)S(1)} %concatenate.13), channel_id=1, source_target_pairs={{0,64},{32,96},{64,0},{96,32},{1,65},{33,97},{65,1},{97,33},{2,66}... | collective-permute-start | bytes 307208 | tf_op jit(solution)/shard_map/basis_g_x/ppermute | solution.py:142
  33.5 5.1 %collective-permute-start.6 = (bf16[40,1280]{1,0:T(8,128)(2,1)S(1)}, bf16[40,1280]{1,0:T(8,128)(2,1)}, u32[]{:S(2)}, u32[]{:S(2)}) collective-permute-start(bf16[40,1280]{1,0:T(8,128)(2,1)S(1)} %concatenate.13), channel_id=1, source_target_pairs={{0,32},{32,64},{64,96},{96,0},{1,33},{33,65},{65,97},{97,1},{2,34}... | collective-permute-start | bytes 307208 | tf_op jit(solution)/shard_map/basis_g_x/ppermute | solution.py:142
  44.6 25.3 %collective-permute-start.11 = (bf16[4,40,1280]{2,1,0:T(8,128)(2,1)S(1)}, bf16[4,40,1280]{2,1,0:T(8,128)(2,1)S(1)}, u32[]{:S(2)}, u32[]{:S(2)}) collective-permute-start(bf16[4,40,1280]{2,1,0:T(8,128)(2,1)S(1)} %pad_maximum_fusion.2.refs_7_), channel_id=1, source_target_pairs={{0,24},{8,0},{16,8},{24,16},{1,25},{9,1},{17,9},{25,17},{2,26},{10... | collective-permute-start | bytes 1228808 | tf_op jit(solution)/shard_map/basis_g_y/ppermute | solution.py:142
  44.7 25.2 %collective-permute-start.10 = (bf16[4,40,1280]{2,1,0:T(8,128)(2,1)S(1)}, bf16[4,40,1280]{2,1,0:T(8,128)(2,1)}, u32[]{:S(2)}, u32[]{:S(2)}) collective-permute-start(bf16[4,40,1280]{2,1,0:T(8,128)(2,1)S(1)} %pad_maximum_fusion.2.refs_7_), channel_id=1, source_target_pairs={{0,16},{8,24},{16,0},{24,8},{1,17},{9,25},{17,1},{25,9},{2,18},{10... | collective-permute-start | bytes 1228808 | tf_op jit(solution)/shard_map/basis_g_y/ppermute | solution.py:142
  45.1 24.8 %collective-permute-start.9 = (bf16[4,40,1280]{2,1,0:T(8,128)(2,1)S(1)}, bf16[4,40,1280]{2,1,0:T(8,128)(2,1)}, u32[]{:S(2)}, u32[]{:S(2)}) collective-permute-start(bf16[4,40,1280]{2,1,0:T(8,128)(2,1)S(1)} %pad_maximum_fusion.2.refs_7_), channel_id=1, source_target_pairs={{0,8},{8,16},{16,24},{24,0},{1,9},{9,17},{17,25},{25,1},{2,10},{10... | collective-permute-start | bytes 1228808 | tf_op jit(solution)/shard_map/basis_g_y/ppermute | solution.py:142
  55.6 14.4 %collective-permute-start.14 = (bf16[4,64,512]{2,1,0:T(8,128)(2,1)}, bf16[4,64,512]{2,1,0:T(8,128)(2,1)}, u32[]{:S(2)}, u32[]{:S(2)}) collective-permute-start(bf16[4,64,512]{2,1,0:T(8,128)(2,1)} %get-tuple-element.56), channel_id=1, source_target_pairs={{0,1},{1,2},{2,3},{3,0},{4,5},{5,6},{6,7},{7,4},{8,9},{9,10},{10,1... | collective-permute-start | bytes 786440 | tf_op jit(solution)/shard_map/coeff_parts/ppermute | solution.py:142
  57.3 13.2 %collective-permute-start.13 = (bf16[4,64,512]{2,1,0:T(8,128)(2,1)}, bf16[4,64,512]{2,1,0:T(8,128)(2,1)}, u32[]{:S(2)}, u32[]{:S(2)}) collective-permute-start(bf16[4,64,512]{2,1,0:T(8,128)(2,1)} %get-tuple-element.55), channel_id=1, source_target_pairs={{0,2},{1,3},{2,0},{3,1},{4,6},{5,7},{6,4},{7,5},{8,10},{9,11},{10,... | collective-permute-start | bytes 786440 | tf_op jit(solution)/shard_map/coeff_parts/ppermute | solution.py:142
  70.6 13.5 %collective-permute-start.16 = (bf16[8,320,512]{2,1,0:T(8,128)(2,1)}, bf16[8,320,512]{2,1,0:T(8,128)(2,1)S(1)}, u32[]{:S(2)}, u32[]{:S(2)}) collective-permute-start(bf16[8,320,512]{2,1,0:T(8,128)(2,1)} %all-to-all-done.1.refs_5_), channel_id=1, source_target_pairs={{0,4},{4,0},{1,5},{5,1},{2,6},{6,2},{3,7},{7,3},{8,12},{12,8},{9,1... | collective-permute-start | bytes 7864328 | tf_op jit(solution)/shard_map/exchange_cores/ppermute | solution.py:142
  72.9 8.1 %collective-permute-start.15 = (bf16[4,64,512]{2,1,0:T(8,128)(2,1)}, bf16[4,64,512]{2,1,0:T(8,128)(2,1)S(1)}, u32[]{:S(2)}, u32[]{:S(2)}) collective-permute-start(bf16[4,64,512]{2,1,0:T(8,128)(2,1)} %copy-done.7), channel_id=1, source_target_pairs={{0,3},{1,0},{2,1},{3,2},{4,7},{5,4},{6,5},{7,6},{8,11},{9,8},{10,9... | collective-permute-start | bytes 786440 | tf_op jit(solution)/shard_map/ppermute | solution.py:142
  73.2 10.2 %collective-permute-start.17 = (bf16[4,40,1280]{2,1,0:T(8,128)(2,1)S(1)}, bf16[4,40,1280]{2,1,0:T(8,128)(2,1)}, u32[]{:S(2)}, u32[]{:S(2)}) collective-permute-start(bf16[4,40,1280]{2,1,0:T(8,128)(2,1)S(1)} %pad_maximum_fusion.2.refs_7_), channel_id=1, source_target_pairs={{0,4},{4,0},{1,5},{5,1},{2,6},{6,2},{3,7},{7,3},{8,12},{12,8},{9,1... | collective-permute-start | bytes 1228808 | tf_op jit(solution)/shard_map/exchange_cores/ppermute | solution.py:142
  73.5 9.9 %collective-permute-start.18 = (bf16[4,40,1280]{2,1,0:T(8,128)(2,1)}, bf16[4,40,1280]{2,1,0:T(8,128)(2,1)}, u32[]{:S(2)}, u32[]{:S(2)}) collective-permute-start(bf16[4,40,1280]{2,1,0:T(8,128)(2,1)} %collective-permute-done.9.refs_8_), channel_id=1, source_target_pairs={{0,4},{4,0},{1,5},{5,1},{2,6},{6,2},{3,7},{7,3},{8,12},{12,8},{9,1... | collective-permute-start | bytes 1228808 | tf_op jit(solution)/shard_map/exchange_cores/ppermute | solution.py:142
  73.7 9.7 %collective-permute-start.19 = (bf16[4,40,1280]{2,1,0:T(8,128)(2,1)}, bf16[4,40,1280]{2,1,0:T(8,128)(2,1)}, u32[]{:S(2)}, u32[]{:S(2)}) collective-permute-start(bf16[4,40,1280]{2,1,0:T(8,128)(2,1)} %collective-permute-done.10.refs_9_), channel_id=1, source_target_pairs={{0,4},{4,0},{1,5},{5,1},{2,6},{6,2},{3,7},{7,3},{8,12},{12,8},{9,1... | collective-permute-start | bytes 1228808 | tf_op jit(solution)/shard_map/exchange_cores/ppermute | solution.py:142
  81.8 2.3 %collective-permute-start.20 = (bf16[4,40,1280]{2,1,0:T(8,128)(2,1)S(1)}, bf16[4,40,1280]{2,1,0:T(8,128)(2,1)}, u32[]{:S(2)}, u32[]{:S(2)}) collective-permute-start(bf16[4,40,1280]{2,1,0:T(8,128)(2,1)S(1)} %collective-permute-done.11.refs_10_), channel_id=1, source_target_pairs={{0,4},{4,0},{1,5},{5,1},{2,6},{6,2},{3,7},{7,3},{8,12},{12,8},{9,1... | collective-permute-start | bytes 1228808 | tf_op jit(solution)/shard_map/exchange_cores/ppermute | solution.py:142
  (9 other events, 21.4 us)

commit v10 on v9

--- a/solution.py
+++ b/solution.py
@@ -62,7 +62,7 @@
         in_specs=[SMEM] + [VMEM] * 3,
         out_specs=[VMEM] * len(dtypes),
         scratch_shapes=[pltpu.VMEM((2, 3 * x.shape[1], POS), jnp.bfloat16)],
-        compiler_params=pltpu.CompilerParams(vmem_limit_bytes=16 << 20),
+        compiler_params=pltpu.CompilerParams(vmem_limit_bytes=52 << 20),
         name="conv_taps",
     )(idx, taps, x, x_oth)
 
@@ -132,7 +132,7 @@
             pltpu.VMEM((hidden, examples * ranks), jnp.bfloat16),
             pltpu.VMEM((2 * chips * width, 2 * ranks), jnp.float32),
         ],
-        compiler_params=pltpu.CompilerParams(vmem_limit_bytes=16 << 20),
+        compiler_params=pltpu.CompilerParams(vmem_limit_bytes=52 << 20),
         name="squared_sums",
     )(idx, own, *received, g, g_oth, *bg, *bg_oth)
 

time: 113 us -> 107 us (0.947)
  local copies, waits for them, and re-layouts: 9.54 us -> 4.38 us
  other arithmetic: 4.32 us -> 1.01 us
  waiting for transfers between devices: 26.6 us -> 28.9 us
  Pallas kernels: 20.5 us -> 22.1 us
    unnamed x20 -> x8, local copies, waits for them, and re-layouts: 5.98 us -> 0.81 us
    concatenate x2, other arithmetic: 2.74 us -> 0.31 us  [body(): jnp.concatenate(ba, axis=1)]
    ppermute x21, waiting for transfers between devices: 26.6 us -> 28.9 us  [shift(): return lax.ppermute(v, axis, [(i, (i + s) % n) for i in range(n)])]
  transfers between devices with their start and end apart: 23 -> 23, of which waited for: 11 -> 11; matrix products, arithmetic and copies ran while one was open for 5% -> 2% of each run, Pallas kernels for 14% -> 15%
where the time goes in v10:
time: 107 us; the launch traced here: 106 us
  starting transfers between devices  31.6 us (30%)
  waiting for transfers between devices  28.9 us (27%)
  Pallas kernels  22.1 us (21%)
  blocking collectives  17.7 us (17%)
  local copies, waits for them, and re-layouts  4.38 us (4%)
    ppermute x21, waiting for transfers between devices, shift(): return lax.ppermute(v, axis, [(i, (i + s) % n) for i in range(n)])  28.9 us
    ppermute x21, starting transfers between devices, shift(): return lax.ppermute(v, axis, [(i, (i + s) % n) for i in range(n)])  21.2 us
    all_to_all x1, blocking collectives, body(): got = lax.all_to_all(rows, ('x', 'y', 'z'), 0, 0, tiled=True)  17.7 us
    pallas_call x2, Pallas kernels, conv(): pl.pallas_call(conv_kernel, out_shape=[jax.ShapeDtypeStruct((2 * per, ran...  16 us
    pallas_call x1, Pallas kernels, squares(): pl.pallas_call(kernel, out_shape=jax.ShapeDtypeStruct((chips, ranks // ch...  6.1 us
    all_to_all x1, starting transfers between devices, body(): lax.all_to_all(jnp.broadcast_to(bg[None], (tensor, *bg.shape)), 'z', 0, 0...  5.86 us
    all_to_all x1, starting transfers between devices, body(): g = lax.all_to_all(grads, 'z', 0, 0, tiled=True)  4.54 us
  transfers between devices with their start and end apart: 23, of which 11 were waited for; matrix products, arithmetic and copies ran while one was open for 2% of the time, Pallas kernels for 15%

profile of v10, /device:TPU:1, one launch (start us, length us, event | category | flops | bytes accessed | tf_op | source)
XLA Modules:
  0.0 105.9 jit_solution(9551611995741396007)
XLA Ops:
  0.0 1.4 %broadcast_in_dim.2 = bf16[4,40,320]{2,1,0:T(8,128)(2,1)} broadcast(bf16[40,320]{1,0:T(8,128)(2,1)} %bitcast.37), dimensions={1,2} | broadcast | bytes 128000 | tf_op jit(solution)/shard_map/basis_g_z/broadcast_in_dim | solution.py:164
  1.4 5.9 %all-to-all-start = ((bf16[4,40,320]{2,1,0:T(8,128)(2,1)}), bf16[4,40,320]{2,1,0:T(8,128)(2,1)S(1)}, u32[]{:S(2)}, u32[]{:S(2)}) async-start(bf16[4,40,320]{2,1,0:T(8,128)(2,1)} %broadcast_in_dim.2), calls=%async_computation | async-start | bytes 245760 | tf_op jit(solution)/shard_map/basis_g_z/all_to_all | solution.py:164
  7.3 0.9 copy.10
  8.3 2.5 %collective-permute-start.2 = (bf16[9,4,960]{2,1,0:T(4,128)(2,1)S(1)}, bf16[9,4,960]{2,1,0:T(4,128)(2,1)S(1)}, u32[]{:S(2)}, u32[]{:S(2)}) collective-permute-start(bf16[9,4,960]{2,1,0:T(4,128)(2,1)S(1)} %reshape.12), channel_id=1, source_target_pairs={{0,96},{32,0},{64,32},{96,64},{1,97},{33,1},{65,33},{97,65},{2,98}... | collective-permute-start | bytes 207368 | tf_op jit(solution)/shard_map/basis_a_x/ppermute | solution.py:142
  12.3 3.4 %collective-permute-done.1 = bf16[9,4,960]{2,1,0:T(4,128)(2,1)S(1)} collective-permute-done((bf16[9,4,960]{2,1,0:T(4,128)(2,1)S(1)}, bf16[9,4,960]{2,1,0:T(4,128)(2,1)S(1)}, u32[]{:S(2)}, u32[]{:S(2)}) %collective-permute-start.1) | collective-permute-done | bytes 69152 | tf_op jit(solution)/shard_map/basis_a_x/ppermute | solution.py:142
  16.6 2.5 %collective-permute-start.12 = (bf16[8,320,512]{2,1,0:T(8,128)(2,1)}, bf16[8,320,512]{2,1,0:T(8,128)(2,1)}, u32[]{:S(2)}, u32[]{:S(2)}) collective-permute-start(bf16[8,320,512]{2,1,0:T(8,128)(2,1)} %bitcast.27), channel_id=1, source_target_pairs={{0,4},{4,0},{1,5},{5,1},{2,6},{6,2},{3,7},{7,3},{8,12},{12,8},{9,1... | collective-permute-start | bytes 7864328 | tf_op jit(solution)/shard_map/basis_a_y/ppermute | solution.py:142
  19.0 4.5 %all-to-all-start.1 = ((bf16[8,320,512]{2,1,0:T(8,128)(2,1)}), bf16[8,320,512]{2,1,0:T(8,128)(2,1)}, u32[]{:S(2)}, u32[]{:S(2)}) async-start(bf16[8,320,512]{2,1,0:T(8,128)(2,1)} %bitcast.30), calls=%async_computation.1 | async-start | bytes 5242880 | tf_op jit(solution)/shard_map/exchange_grads/all_to_all | solution.py:167
  24.1 2.7 %collective-permute-start.5 = (bf16[9,16,960]{2,1,0:T(8,128)(2,1)S(1)}, bf16[9,16,960]{2,1,0:T(8,128)(2,1)S(1)}, u32[]{:S(2)}, u32[]{:S(2)}) collective-permute-start(bf16[9,16,960]{2,1,0:T(8,128)(2,1)S(1)} %pad_maximum_fusion.3), channel_id=1, source_target_pairs={{0,24},{8,0},{16,8},{24,16},{1,25},{9,1},{17,9},{25,17},{2,26},{10... | collective-permute-start | bytes 829448 | tf_op jit(solution)/shard_map/basis_a_y/ppermute | solution.py:142
  28.1 1.0 collective-permute-start.7
  29.1 4.4 %collective-permute-done.7 = bf16[40,1280]{1,0:T(8,128)(2,1)S(1)} collective-permute-done((bf16[40,1280]{1,0:T(8,128)(2,1)S(1)}, bf16[40,1280]{1,0:T(8,128)(2,1)S(1)}, u32[]{:S(2)}, u32[]{:S(2)}) %collective-permute-start.7) | collective-permute-done | bytes 102432 | tf_op jit(solution)/shard_map/basis_g_x/ppermute | solution.py:142
  33.4 1.0 collective-permute-start.6
  34.5 4.1 %collective-permute-done.6 = bf16[40,1280]{1,0:T(8,128)(2,1)S(1)} collective-permute-done((bf16[40,1280]{1,0:T(8,128)(2,1)S(1)}, bf16[40,1280]{1,0:T(8,128)(2,1)S(1)}, u32[]{:S(2)}, u32[]{:S(2)}) %collective-permute-start.6) | collective-permute-done | bytes 102432 | tf_op jit(solution)/shard_map/basis_g_x/ppermute | solution.py:142
  38.8 4.9 %collective-permute-done.3 = bf16[9,16,960]{2,1,0:T(8,128)(2,1)S(1)} collective-permute-done((bf16[9,16,960]{2,1,0:T(8,128)(2,1)S(1)}, bf16[9,16,960]{2,1,0:T(8,128)(2,1)S(1)}, u32[]{:S(2)}, u32[]{:S(2)}) %collective-permute-start.3) | collective-permute-done | bytes 276512 | tf_op jit(solution)/shard_map/basis_a_y/ppermute | solution.py:142
  44.2 1.0 collective-permute-start.9
  45.5 8.0 %conv_taps.2 = (bf16[4,64,512]{2,1,0:T(8,128)(2,1)S(1)}, bf16[4,64,512]{2,1,0:T(8,128)(2,1)S(1)}) custom-call(s32[2]{0:T(128)S(1)} %pad_add_fusion.1.idx_ref, bf16[9,64,960]{2,1,0:T(8,128)(2,1)S(1)} %pad_maximum_fusion.b_ref, bf16[8,320,512]{2,1,0:T(8,128)(2,1)} %bitcast.28, bf16[8,320,512]{2,1,0:T(8,128)(2,1)} %collective-permute-done.12.x_oth_ref), custom_call_target="tpu_custom_call" | custom-call | tf_op jit(solution)/shard_map/coeff_parts/conv_taps/pallas_call | solution.py:59
  53.5 1.7 %collective-permute-start.14 = (bf16[4,64,512]{2,1,0:T(8,128)(2,1)S(1)}, bf16[4,64,512]{2,1,0:T(8,128)(2,1)S(1)}, u32[]{:S(2)}, u32[]{:S(2)}) collective-permute-start(bf16[4,64,512]{2,1,0:T(8,128)(2,1)S(1)} %get-tuple-element.56), channel_id=1, source_target_pairs={{0,1},{1,2},{2,3},{3,0},{4,5},{5,6},{6,7},{7,4},{8,9},{9,10},{10,1... | collective-permute-start | bytes 786440 | tf_op jit(solution)/shard_map/coeff_parts/ppermute | solution.py:142
  55.2 2.5 %collective-permute-start.13 = (bf16[4,64,512]{2,1,0:T(8,128)(2,1)S(1)}, bf16[4,64,512]{2,1,0:T(8,128)(2,1)S(1)}, u32[]{:S(2)}, u32[]{:S(2)}) collective-permute-start(bf16[4,64,512]{2,1,0:T(8,128)(2,1)S(1)} %get-tuple-element.55), channel_id=1, source_target_pairs={{0,2},{1,3},{2,0},{3,1},{4,6},{5,7},{6,4},{7,5},{8,10},{9,11},{10,... | collective-permute-start | bytes 786440 | tf_op jit(solution)/shard_map/coeff_parts/ppermute | solution.py:142
  57.9 8.0 %conv_taps.3 = (bf16[4,64,512]{2,1,0:T(8,128)(2,1)S(1)}, f32[4,64,512]{2,1,0:T(8,128)S(1)}) custom-call(s32[2]{0:T(128)S(1)} %pad_add_fusion.2.idx_ref, bf16[9,64,960]{2,1,0:T(8,128)(2,1)S(1)} %pad_maximum_fusion.1.b_ref, bf16[8,320,512]{2,1,0:T(8,128)(2,1)} %bitcast.29, bf16[8,320,512]{2,1,0:T(8,128)(2,1)} %collective-permute-done.12.x_oth_ref), custom_call_target="tpu_custom_call" | custom-call | tf_op jit(solution)/shard_map/coeff_parts/conv_taps/pallas_call | solution.py:59
  66.8 1.9 %collective-permute-done.13.refs_2_ = bf16[4,64,512]{2,1,0:T(8,128)(2,1)S(1)} collective-permute-done((bf16[4,64,512]{2,1,0:T(8,128)(2,1)S(1)}, bf16[4,64,512]{2,1,0:T(8,128)(2,1)S(1)}, u32[]{:S(2)}, u32[]{:S(2)}) %collective-permute-start.13) | collective-permute-done | bytes 262176 | tf_op jit(solution)/shard_map/coeff_parts/ppermute | solution.py:142
  68.7 1.9 %collective-permute-start.16 = (bf16[8,320,512]{2,1,0:T(8,128)(2,1)}, bf16[8,320,512]{2,1,0:T(8,128)(2,1)}, u32[]{:S(2)}, u32[]{:S(2)}) collective-permute-start(bf16[8,320,512]{2,1,0:T(8,128)(2,1)} %all-to-all-done.1.refs_5_), channel_id=1, source_target_pairs={{0,4},{4,0},{1,5},{5,1},{2,6},{6,2},{3,7},{7,3},{8,12},{12,8},{9,1... | collective-permute-start | bytes 7864328 | tf_op jit(solution)/shard_map/exchange_cores/ppermute | solution.py:142
  71.1 7.4 %collective-permute-done.15.refs_4_ = bf16[4,64,512]{2,1,0:T(8,128)(2,1)S(1)} collective-permute-done((bf16[4,64,512]{2,1,0:T(8,128)(2,1)S(1)}, bf16[4,64,512]{2,1,0:T(8,128)(2,1)S(1)}, u32[]{:S(2)}, u32[]{:S(2)}) %collective-permute-start.15) | collective-permute-done | bytes 262176 | tf_op jit(solution)/shard_map/ppermute | solution.py:142
  79.4 1.4 %collective-permute-done.20.refs_14_ = bf16[4,40,1280]{2,1,0:T(8,128)(2,1)} collective-permute-done((bf16[4,40,1280]{2,1,0:T(8,128)(2,1)S(1)}, bf16[4,40,1280]{2,1,0:T(8,128)(2,1)}, u32[]{:S(2)}, u32[]{:S(2)}) %collective-permute-start.20) | collective-permute-done | bytes 409632 | tf_op jit(solution)/shard_map/exchange_cores/ppermute | solution.py:142
  80.8 6.1 %squared_sums.1 = f32[16,4,1280]{2,1,0:T(4,128)S(1)} custom-call(s32[4]{0:T(128)S(1)} %pad_add_fusion.refs_0_, f32[4,64,512]{2,1,0:T(8,128)} %copy-done, bf16[4,64,512]{2,1,0:T(8,128)(2,1)S(1)} %collective-permute-done.13.refs_2_, bf16[4,64,512]{2,1,0:T(8,128)(2,1)S(1)} %collective-permute-done.14.refs_3_, ...), custom_call_target="tpu_custom_call" | custom-call | tf_op jit(solution)/shard_map/squared_sums/pallas_call | solution.py:125
  87.3 17.7 %all_to_all.15 = f32[64,1,1280]{2,1,0:T(1,128)S(1)} all-to-all(f32[64,1,1280]{2,1,0:T(1,128)S(1)} %reshape.14), channel_id=1, replica_groups=mesh['x'=4,'y'=4,'core'=2,'z'=4] {'x','y','z'}, dimensions={0} | all-to-all | bytes 655360 | tf_op jit(solution)/shard_map/sum_examples/all_to_all | solution.py:197
  (49 shorter events, 8.9 us)
Async XLA Ops:
  1.4 15.0 %all-to-all-start = ((bf16[4,40,320]{2,1,0:T(8,128)(2,1)}), bf16[4,40,320]{2,1,0:T(8,128)(2,1)S(1)}, u32[]{:S(2)}, u32[]{:S(2)}) async-start(bf16[4,40,320]{2,1,0:T(8,128)(2,1)} %broadcast_in_dim.2), calls=%async_computation | async-start | bytes 245760 | tf_op jit(solution)/shard_map/basis_g_z/all_to_all | solution.py:164
  8.3 4.0 %collective-permute-start.2 = (bf16[9,4,960]{2,1,0:T(4,128)(2,1)S(1)}, bf16[9,4,960]{2,1,0:T(4,128)(2,1)S(1)}, u32[]{:S(2)}, u32[]{:S(2)}) collective-permute-start(bf16[9,4,960]{2,1,0:T(4,128)(2,1)S(1)} %reshape.12), channel_id=1, source_target_pairs={{0,96},{32,0},{64,32},{96,64},{1,97},{33,1},{65,33},{97,65},{2,98}... | collective-permute-start | bytes 207368 | tf_op jit(solution)/shard_map/basis_a_x/ppermute | solution.py:142
  10.9 4.8 %collective-permute-start.1 = (bf16[9,4,960]{2,1,0:T(4,128)(2,1)S(1)}, bf16[9,4,960]{2,1,0:T(4,128)(2,1)S(1)}, u32[]{:S(2)}, u32[]{:S(2)}) collective-permute-start(bf16[9,4,960]{2,1,0:T(4,128)(2,1)S(1)} %reshape.12), channel_id=1, source_target_pairs={{0,64},{32,96},{64,0},{96,32},{1,65},{33,97},{65,1},{97,33},{2,66}... | collective-permute-start | bytes 207368 | tf_op jit(solution)/shard_map/basis_a_x/ppermute | solution.py:142
  11.4 5.0 %collective-permute-start = (bf16[9,4,960]{2,1,0:T(4,128)(2,1)S(1)}, bf16[9,4,960]{2,1,0:T(4,128)(2,1)S(1)}, u32[]{:S(2)}, u32[]{:S(2)}) collective-permute-start(bf16[9,4,960]{2,1,0:T(4,128)(2,1)S(1)} %reshape.12), channel_id=1, source_target_pairs={{0,32},{32,64},{64,96},{96,0},{1,33},{33,65},{65,97},{97,1},{2,34}... | collective-permute-start | bytes 207368 | tf_op jit(solution)/shard_map/basis_a_x/ppermute | solution.py:142
  16.6 29.0 %collective-permute-start.12 = (bf16[8,320,512]{2,1,0:T(8,128)(2,1)}, bf16[8,320,512]{2,1,0:T(8,128)(2,1)}, u32[]{:S(2)}, u32[]{:S(2)}) collective-permute-start(bf16[8,320,512]{2,1,0:T(8,128)(2,1)} %bitcast.27), channel_id=1, source_target_pairs={{0,4},{4,0},{1,5},{5,1},{2,6},{6,2},{3,7},{7,3},{8,12},{12,8},{9,1... | collective-permute-start | bytes 7864328 | tf_op jit(solution)/shard_map/basis_a_y/ppermute | solution.py:142
  19.0 47.7 %all-to-all-start.1 = ((bf16[8,320,512]{2,1,0:T(8,128)(2,1)}), bf16[8,320,512]{2,1,0:T(8,128)(2,1)}, u32[]{:S(2)}, u32[]{:S(2)}) async-start(bf16[8,320,512]{2,1,0:T(8,128)(2,1)} %bitcast.30), calls=%async_computation.1 | async-start | bytes 5242880 | tf_op jit(solution)/shard_map/exchange_grads/all_to_all | solution.py:167
  23.7 4.4 %collective-permute-start.8 = (bf16[40,1280]{1,0:T(8,128)(2,1)S(1)}, bf16[40,1280]{1,0:T(8,128)(2,1)S(1)}, u32[]{:S(2)}, u32[]{:S(2)}) collective-permute-start(bf16[40,1280]{1,0:T(8,128)(2,1)S(1)} %concatenate.13), channel_id=1, source_target_pairs={{0,96},{32,0},{64,32},{96,64},{1,97},{33,1},{65,33},{97,65},{2,98}... | collective-permute-start | bytes 307208 | tf_op jit(solution)/shard_map/basis_g_x/ppermute | solution.py:142
  24.1 14.7 %collective-permute-start.5 = (bf16[9,16,960]{2,1,0:T(8,128)(2,1)S(1)}, bf16[9,16,960]{2,1,0:T(8,128)(2,1)S(1)}, u32[]{:S(2)}, u32[]{:S(2)}) collective-permute-start(bf16[9,16,960]{2,1,0:T(8,128)(2,1)S(1)} %pad_maximum_fusion.3), channel_id=1, source_target_pairs={{0,24},{8,0},{16,8},{24,16},{1,25},{9,1},{17,9},{25,17},{2,26},{10... | collective-permute-start | bytes 829448 | tf_op jit(solution)/shard_map/basis_a_y/ppermute | solution.py:142
  26.8 12.0 %collective-permute-start.4 = (bf16[9,16,960]{2,1,0:T(8,128)(2,1)S(1)}, bf16[9,16,960]{2,1,0:T(8,128)(2,1)S(1)}, u32[]{:S(2)}, u32[]{:S(2)}) collective-permute-start(bf16[9,16,960]{2,1,0:T(8,128)(2,1)S(1)} %pad_maximum_fusion.3), channel_id=1, source_target_pairs={{0,16},{8,24},{16,0},{24,8},{1,17},{9,25},{17,1},{25,9},{2,18},{10... | collective-permute-start | bytes 829448 | tf_op jit(solution)/shard_map/basis_a_y/ppermute | solution.py:142
  27.2 16.5 %collective-permute-start.3 = (bf16[9,16,960]{2,1,0:T(8,128)(2,1)S(1)}, bf16[9,16,960]{2,1,0:T(8,128)(2,1)S(1)}, u32[]{:S(2)}, u32[]{:S(2)}) collective-permute-start(bf16[9,16,960]{2,1,0:T(8,128)(2,1)S(1)} %pad_maximum_fusion.3), channel_id=1, source_target_pairs={{0,8},{8,16},{16,24},{24,0},{1,9},{9,17},{17,25},{25,1},{2,10},{10... | collective-permute-start | bytes 829448 | tf_op jit(solution)/shard_map/basis_a_y/ppermute | solution.py:142
  28.1 5.3 %collective-permute-start.7 = (bf16[40,1280]{1,0:T(8,128)(2,1)S(1)}, bf16[40,1280]{1,0:T(8,128)(2,1)S(1)}, u32[]{:S(2)}, u32[]{:S(2)}) collective-permute-start(bf16[40,1280]{1,0:T(8,128)(2,1)S(1)} %concatenate.13), channel_id=1, source_target_pairs={{0,64},{32,96},{64,0},{96,32},{1,65},{33,97},{65,1},{97,33},{2,66}... | collective-permute-start | bytes 307208 | tf_op jit(solution)/shard_map/basis_g_x/ppermute | solution.py:142
  33.4 5.1 %collective-permute-start.6 = (bf16[40,1280]{1,0:T(8,128)(2,1)S(1)}, bf16[40,1280]{1,0:T(8,128)(2,1)S(1)}, u32[]{:S(2)}, u32[]{:S(2)}) collective-permute-start(bf16[40,1280]{1,0:T(8,128)(2,1)S(1)} %concatenate.13), channel_id=1, source_target_pairs={{0,32},{32,64},{64,96},{96,0},{1,33},{33,65},{65,97},{97,1},{2,34}... | collective-permute-start | bytes 307208 | tf_op jit(solution)/shard_map/basis_g_x/ppermute | solution.py:142
  43.7 23.0 %collective-permute-start.11 = (bf16[4,40,1280]{2,1,0:T(8,128)(2,1)S(1)}, bf16[4,40,1280]{2,1,0:T(8,128)(2,1)S(1)}, u32[]{:S(2)}, u32[]{:S(2)}) collective-permute-start(bf16[4,40,1280]{2,1,0:T(8,128)(2,1)S(1)} %pad_maximum_fusion.2.refs_7_), channel_id=1, source_target_pairs={{0,24},{8,0},{16,8},{24,16},{1,25},{9,1},{17,9},{25,17},{2,26},{10... | collective-permute-start | bytes 1228808 | tf_op jit(solution)/shard_map/basis_g_y/ppermute | solution.py:142
  43.8 22.9 %collective-permute-start.10 = (bf16[4,40,1280]{2,1,0:T(8,128)(2,1)S(1)}, bf16[4,40,1280]{2,1,0:T(8,128)(2,1)}, u32[]{:S(2)}, u32[]{:S(2)}) collective-permute-start(bf16[4,40,1280]{2,1,0:T(8,128)(2,1)S(1)} %pad_maximum_fusion.2.refs_7_), channel_id=1, source_target_pairs={{0,16},{8,24},{16,0},{24,8},{1,17},{9,25},{17,1},{25,9},{2,18},{10... | collective-permute-start | bytes 1228808 | tf_op jit(solution)/shard_map/basis_g_y/ppermute | solution.py:142
  44.2 22.5 %collective-permute-start.9 = (bf16[4,40,1280]{2,1,0:T(8,128)(2,1)S(1)}, bf16[4,40,1280]{2,1,0:T(8,128)(2,1)S(1)}, u32[]{:S(2)}, u32[]{:S(2)}) collective-permute-start(bf16[4,40,1280]{2,1,0:T(8,128)(2,1)S(1)} %pad_maximum_fusion.2.refs_7_), channel_id=1, source_target_pairs={{0,8},{8,16},{16,24},{24,0},{1,9},{9,17},{17,25},{25,1},{2,10},{10... | collective-permute-start | bytes 1228808 | tf_op jit(solution)/shard_map/basis_g_y/ppermute | solution.py:142
  53.5 13.3 %collective-permute-start.14 = (bf16[4,64,512]{2,1,0:T(8,128)(2,1)S(1)}, bf16[4,64,512]{2,1,0:T(8,128)(2,1)S(1)}, u32[]{:S(2)}, u32[]{:S(2)}) collective-permute-start(bf16[4,64,512]{2,1,0:T(8,128)(2,1)S(1)} %get-tuple-element.56), channel_id=1, source_target_pairs={{0,1},{1,2},{2,3},{3,0},{4,5},{5,6},{6,7},{7,4},{8,9},{9,10},{10,1... | collective-permute-start | bytes 786440 | tf_op jit(solution)/shard_map/coeff_parts/ppermute | solution.py:142
  55.2 13.5 %collective-permute-start.13 = (bf16[4,64,512]{2,1,0:T(8,128)(2,1)S(1)}, bf16[4,64,512]{2,1,0:T(8,128)(2,1)S(1)}, u32[]{:S(2)}, u32[]{:S(2)}) collective-permute-start(bf16[4,64,512]{2,1,0:T(8,128)(2,1)S(1)} %get-tuple-element.55), channel_id=1, source_target_pairs={{0,2},{1,3},{2,0},{3,1},{4,6},{5,7},{6,4},{7,5},{8,10},{9,11},{10,... | collective-permute-start | bytes 786440 | tf_op jit(solution)/shard_map/coeff_parts/ppermute | solution.py:142
  66.8 14.1 %copy-start.1 = (bf16[4,40,1280]{2,1,0:T(8,128)(2,1)}, bf16[4,40,1280]{2,1,0:T(8,128)(2,1)S(1)}, u32[]{:S(2)}) copy-start(bf16[4,40,1280]{2,1,0:T(8,128)(2,1)S(1)} %collective-permute-done.11.refs_10_) | copy-start | bytes 1228804
  68.7 12.1 %collective-permute-start.16 = (bf16[8,320,512]{2,1,0:T(8,128)(2,1)}, bf16[8,320,512]{2,1,0:T(8,128)(2,1)}, u32[]{:S(2)}, u32[]{:S(2)}) collective-permute-start(bf16[8,320,512]{2,1,0:T(8,128)(2,1)} %all-to-all-done.1.refs_5_), channel_id=1, source_target_pairs={{0,4},{4,0},{1,5},{5,1},{2,6},{6,2},{3,7},{7,3},{8,12},{12,8},{9,1... | collective-permute-start | bytes 7864328 | tf_op jit(solution)/shard_map/exchange_cores/ppermute | solution.py:142
  70.6 7.9 %collective-permute-start.15 = (bf16[4,64,512]{2,1,0:T(8,128)(2,1)S(1)}, bf16[4,64,512]{2,1,0:T(8,128)(2,1)S(1)}, u32[]{:S(2)}, u32[]{:S(2)}) collective-permute-start(bf16[4,64,512]{2,1,0:T(8,128)(2,1)S(1)} %get-tuple-element.67), channel_id=1, source_target_pairs={{0,3},{1,0},{2,1},{3,2},{4,7},{5,4},{6,5},{7,6},{8,11},{9,8},{10,9... | collective-permute-start | bytes 786440 | tf_op jit(solution)/shard_map/ppermute | solution.py:142
  70.6 8.8 %collective-permute-start.17 = (bf16[4,40,1280]{2,1,0:T(8,128)(2,1)S(1)}, bf16[4,40,1280]{2,1,0:T(8,128)(2,1)S(1)}, u32[]{:S(2)}, u32[]{:S(2)}) collective-permute-start(bf16[4,40,1280]{2,1,0:T(8,128)(2,1)S(1)} %pad_maximum_fusion.2.refs_7_), channel_id=1, source_target_pairs={{0,4},{4,0},{1,5},{5,1},{2,6},{6,2},{3,7},{7,3},{8,12},{12,8},{9,1... | collective-permute-start | bytes 1228808 | tf_op jit(solution)/shard_map/exchange_cores/ppermute | solution.py:142
  70.6 8.8 %collective-permute-start.18 = (bf16[4,40,1280]{2,1,0:T(8,128)(2,1)S(1)}, bf16[4,40,1280]{2,1,0:T(8,128)(2,1)S(1)}, u32[]{:S(2)}, u32[]{:S(2)}) collective-permute-start(bf16[4,40,1280]{2,1,0:T(8,128)(2,1)S(1)} %collective-permute-done.9.refs_8_), channel_id=1, source_target_pairs={{0,4},{4,0},{1,5},{5,1},{2,6},{6,2},{3,7},{7,3},{8,12},{12,8},{9,1... | collective-permute-start | bytes 1228808 | tf_op jit(solution)/shard_map/exchange_cores/ppermute | solution.py:142
  71.1 8.3 %collective-permute-start.19 = (bf16[4,40,1280]{2,1,0:T(8,128)(2,1)}, bf16[4,40,1280]{2,1,0:T(8,128)(2,1)}, u32[]{:S(2)}, u32[]{:S(2)}) collective-permute-start(bf16[4,40,1280]{2,1,0:T(8,128)(2,1)} %collective-permute-done.10.refs_9_), channel_id=1, source_target_pairs={{0,4},{4,0},{1,5},{5,1},{2,6},{6,2},{3,7},{7,3},{8,12},{12,8},{9,1... | collective-permute-start | bytes 1228808 | tf_op jit(solution)/shard_map/exchange_cores/ppermute | solution.py:142
  78.5 2.3 %collective-permute-start.20 = (bf16[4,40,1280]{2,1,0:T(8,128)(2,1)S(1)}, bf16[4,40,1280]{2,1,0:T(8,128)(2,1)}, u32[]{:S(2)}, u32[]{:S(2)}) collective-permute-start(bf16[4,40,1280]{2,1,0:T(8,128)(2,1)S(1)} %collective-permute-done.11.refs_10_), channel_id=1, source_target_pairs={{0,4},{4,0},{1,5},{5,1},{2,6},{6,2},{3,7},{7,3},{8,12},{12,8},{9,1... | collective-permute-start | bytes 1228808 | tf_op jit(solution)/shard_map/exchange_cores/ppermute | solution.py:142
  (3 other events, 3.7 us)

commit v11 on v10

--- a/solution.py
+++ b/solution.py
@@ -179,15 +179,17 @@
     with jax.named_scope("coeff_parts"):
         bf16 = jnp.bfloat16
         blocks = [(z + s) % tensor for s in (2, 1, 3, 0)]
-        far, near = conv(jnp.stack(blocks[:2]), jnp.concatenate(ba, axis=1), x, x_oth, per, (bf16, bf16))
+        near, far = conv(jnp.stack(blocks[1::-1]), jnp.concatenate(ba, axis=1), x, x_oth, per, (bf16, bf16))
         received = [shift(far, "z", 2), shift(near, "z", 1)]
         ba, blocks, _ = lax.optimization_barrier((ba, blocks, far))
-        last, mine = conv(jnp.stack(blocks[2:]), jnp.concatenate(ba, axis=1), x, x_oth, per, (bf16, jnp.float32))
+        (last,) = conv(blocks[2].reshape(1), jnp.concatenate(ba, axis=1), x, x_oth, per, (bf16,))
+        received.append(shift(last, "z", 3))
+        ba, blocks, _ = lax.optimization_barrier((ba, blocks, last))
+        (mine,) = conv(blocks[3].reshape(1), jnp.concatenate(ba, axis=1), x, x_oth, per, (jnp.float32,))
     with jax.named_scope("exchange_cores"):
         g, bg, received, mine = lax.optimization_barrier((g, bg, received, mine))
         g_oth = shift(g, "core", 1)
         bg_oth = [shift(v, "core", 1) for v in bg]
-    received.append(shift(last, "z", 3))
 
     examples = here * lax.axis_size(("x", "y", "core"))
     total = squares(jnp.stack(coords), mine, received, g, g_oth, bg, bg_oth, 1.0 / examples)

time: 107 us -> 107 us (level)
  waiting for transfers between devices: 28.9 us -> 24.3 us
  Pallas kernels: 22.1 us -> 25 us
  starting transfers between devices: 31.6 us -> 33.2 us
  local copies, waits for them, and re-layouts: 4.38 us -> 5.66 us
    ppermute x21, waiting for transfers between devices: 28.9 us -> 24.3 us  [shift(): return lax.ppermute(v, axis, [(i, (i + s) % n) for i in range(n)])]
    pallas_call x2 -> x3, Pallas kernels: 16 us -> 18.9 us  [conv(): pl.pallas_call(conv_kernel, out_shape=[jax.ShapeDtypeStruct((2 * per, ran...]
    ppermute x21, starting transfers between devices: 21.2 us -> 22.8 us  [shift(): return lax.ppermute(v, axis, [(i, (i + s) % n) for i in range(n)])]
    unnamed x8 -> x14, local copies, waits for them, and re-layouts: 0.81 us -> 2.09 us
  transfers between devices with their start and end apart: 23 -> 23, of which waited for: 11 -> 11; matrix products, arithmetic and copies ran while one was open for 2% -> 2% of each run, Pallas kernels for 15% -> 18%
where the time goes in v11:
time: 107 us
  starting transfers between devices  33.2 us (31%)
  Pallas kernels  25 us (23%)
  waiting for transfers between devices  24.3 us (23%)
  blocking collectives  17.3 us (16%)
  local copies, waits for them, and re-layouts  5.66 us (5%)
    ppermute x21, waiting for transfers between devices, shift(): return lax.ppermute(v, axis, [(i, (i + s) % n) for i in range(n)])  24.3 us
    ppermute x21, starting transfers between devices, shift(): return lax.ppermute(v, axis, [(i, (i + s) % n) for i in range(n)])  22.8 us
    pallas_call x3, Pallas kernels, conv(): pl.pallas_call(conv_kernel, out_shape=[jax.ShapeDtypeStruct((2 * per, ran...  18.9 us
    all_to_all x1, blocking collectives, body(): got = lax.all_to_all(rows, ('x', 'y', 'z'), 0, 0, tiled=True)  17.3 us
    pallas_call x1, Pallas kernels, squares(): pl.pallas_call(kernel, out_shape=jax.ShapeDtypeStruct((chips, ranks // ch...  6.09 us
    all_to_all x1, starting transfers between devices, body(): lax.all_to_all(jnp.broadcast_to(bg[None], (tensor, *bg.shape)), 'z', 0, 0...  5.86 us
    all_to_all x1, starting transfers between devices, body(): g = lax.all_to_all(grads, 'z', 0, 0, tiled=True)  4.54 us
  transfers between devices with their start and end apart: 23, of which 11 were waited for; matrix products, arithmetic and copies ran while one was open for 2% of the time, Pallas kernels for 18%

profile of v11, /device:TPU:1, one launch (start us, length us, event | category | flops | bytes accessed | tf_op | source)
XLA Modules:
  0.0 106.7 jit_solution(6725916905091633958)
XLA Ops:
  0.0 1.4 %broadcast_in_dim.2 = bf16[4,40,320]{2,1,0:T(8,128)(2,1)} broadcast(bf16[40,320]{1,0:T(8,128)(2,1)} %bitcast.38), dimensions={1,2} | broadcast | bytes 128000 | tf_op jit(solution)/shard_map/basis_g_z/broadcast_in_dim | solution.py:164
  1.4 5.9 %all-to-all-start = ((bf16[4,40,320]{2,1,0:T(8,128)(2,1)}), bf16[4,40,320]{2,1,0:T(8,128)(2,1)S(1)}, u32[]{:S(2)}, u32[]{:S(2)}) async-start(bf16[4,40,320]{2,1,0:T(8,128)(2,1)} %broadcast_in_dim.2), calls=%async_computation | async-start | bytes 245760 | tf_op jit(solution)/shard_map/basis_g_z/all_to_all | solution.py:164
  7.3 0.9 copy.10
  8.3 2.5 %collective-permute-start.2 = (bf16[9,4,960]{2,1,0:T(4,128)(2,1)S(1)}, bf16[9,4,960]{2,1,0:T(4,128)(2,1)S(1)}, u32[]{:S(2)}, u32[]{:S(2)}) collective-permute-start(bf16[9,4,960]{2,1,0:T(4,128)(2,1)S(1)} %reshape.18), channel_id=1, source_target_pairs={{0,96},{32,0},{64,32},{96,64},{1,97},{33,1},{65,33},{97,65},{2,98}... | collective-permute-start | bytes 207368 | tf_op jit(solution)/shard_map/basis_a_x/ppermute | solution.py:142
  12.3 3.4 %collective-permute-done.1 = bf16[9,4,960]{2,1,0:T(4,128)(2,1)S(1)} collective-permute-done((bf16[9,4,960]{2,1,0:T(4,128)(2,1)S(1)}, bf16[9,4,960]{2,1,0:T(4,128)(2,1)S(1)}, u32[]{:S(2)}, u32[]{:S(2)}) %collective-permute-start.1) | collective-permute-done | bytes 69152 | tf_op jit(solution)/shard_map/basis_a_x/ppermute | solution.py:142
  16.6 2.5 %collective-permute-start.12 = (bf16[8,320,512]{2,1,0:T(8,128)(2,1)}, bf16[8,320,512]{2,1,0:T(8,128)(2,1)}, u32[]{:S(2)}, u32[]{:S(2)}) collective-permute-start(bf16[8,320,512]{2,1,0:T(8,128)(2,1)} %bitcast.27), channel_id=1, source_target_pairs={{0,4},{4,0},{1,5},{5,1},{2,6},{6,2},{3,7},{7,3},{8,12},{12,8},{9,1... | collective-permute-start | bytes 7864328 | tf_op jit(solution)/shard_map/basis_a_y/ppermute | solution.py:142
  19.0 4.5 %all-to-all-start.1 = ((bf16[8,320,512]{2,1,0:T(8,128)(2,1)}), bf16[8,320,512]{2,1,0:T(8,128)(2,1)}, u32[]{:S(2)}, u32[]{:S(2)}) async-start(bf16[8,320,512]{2,1,0:T(8,128)(2,1)} %bitcast.31), calls=%async_computation.1 | async-start | bytes 5242880 | tf_op jit(solution)/shard_map/exchange_grads/all_to_all | solution.py:167
  24.1 2.7 %collective-permute-start.5 = (bf16[9,16,960]{2,1,0:T(8,128)(2,1)S(1)}, bf16[9,16,960]{2,1,0:T(8,128)(2,1)S(1)}, u32[]{:S(2)}, u32[]{:S(2)}) collective-permute-start(bf16[9,16,960]{2,1,0:T(8,128)(2,1)S(1)} %pad_maximum_fusion.4), channel_id=1, source_target_pairs={{0,24},{8,0},{16,8},{24,16},{1,25},{9,1},{17,9},{25,17},{2,26},{10... | collective-permute-start | bytes 829448 | tf_op jit(solution)/shard_map/basis_a_y/ppermute | solution.py:142
  28.1 1.0 collective-permute-start.7
  29.1 4.4 %collective-permute-done.7 = bf16[40,1280]{1,0:T(8,128)(2,1)S(1)} collective-permute-done((bf16[40,1280]{1,0:T(8,128)(2,1)S(1)}, bf16[40,1280]{1,0:T(8,128)(2,1)S(1)}, u32[]{:S(2)}, u32[]{:S(2)}) %collective-permute-start.7) | collective-permute-done | bytes 102432 | tf_op jit(solution)/shard_map/basis_g_x/ppermute | solution.py:142
  33.4 1.0 collective-permute-start.6
  34.5 4.1 %collective-permute-done.6 = bf16[40,1280]{1,0:T(8,128)(2,1)S(1)} collective-permute-done((bf16[40,1280]{1,0:T(8,128)(2,1)S(1)}, bf16[40,1280]{1,0:T(8,128)(2,1)S(1)}, u32[]{:S(2)}, u32[]{:S(2)}) %collective-permute-start.6) | collective-permute-done | bytes 102432 | tf_op jit(solution)/shard_map/basis_g_x/ppermute | solution.py:142
  38.8 4.9 %collective-permute-done.3 = bf16[9,16,960]{2,1,0:T(8,128)(2,1)S(1)} collective-permute-done((bf16[9,16,960]{2,1,0:T(8,128)(2,1)S(1)}, bf16[9,16,960]{2,1,0:T(8,128)(2,1)S(1)}, u32[]{:S(2)}, u32[]{:S(2)}) %collective-permute-start.3) | collective-permute-done | bytes 276512 | tf_op jit(solution)/shard_map/basis_a_y/ppermute | solution.py:142
  44.3 1.1 %collective-permute-start.9 = (bf16[4,40,1280]{2,1,0:T(8,128)(2,1)S(1)}, bf16[4,40,1280]{2,1,0:T(8,128)(2,1)S(1)}, u32[]{:S(2)}, u32[]{:S(2)}) collective-permute-start(bf16[4,40,1280]{2,1,0:T(8,128)(2,1)S(1)} %pad_maximum_fusion.3.refs_7_), channel_id=1, source_target_pairs={{0,8},{8,16},{16,24},{24,0},{1,9},{9,17},{17,25},{25,1},{2,10},{10... | collective-permute-start | bytes 1228808 | tf_op jit(solution)/shard_map/basis_g_y/ppermute | solution.py:142
  45.6 8.0 %conv_taps.3 = (bf16[4,64,512]{2,1,0:T(8,128)(2,1)S(1)}, bf16[4,64,512]{2,1,0:T(8,128)(2,1)S(1)}) custom-call(s32[2]{0:T(128)S(1)} %pad_add_fusion.1.idx_ref, bf16[9,64,960]{2,1,0:T(8,128)(2,1)S(1)} %pad_maximum_fusion.b_ref, bf16[8,320,512]{2,1,0:T(8,128)(2,1)} %bitcast.28, bf16[8,320,512]{2,1,0:T(8,128)(2,1)} %collective-permute-done.12.x_oth_ref), custom_call_target="tpu_custom_call" | custom-call | tf_op jit(solution)/shard_map/coeff_parts/conv_taps/pallas_call | solution.py:59
  53.6 3.2 %collective-permute-start.13 = (bf16[4,64,512]{2,1,0:T(8,128)(2,1)S(1)}, bf16[4,64,512]{2,1,0:T(8,128)(2,1)S(1)}, u32[]{:S(2)}, u32[]{:S(2)}) collective-permute-start(bf16[4,64,512]{2,1,0:T(8,128)(2,1)S(1)} %get-tuple-element.59), channel_id=1, source_target_pairs={{0,2},{1,3},{2,0},{3,1},{4,6},{5,7},{6,4},{7,5},{8,10},{9,11},{10,... | collective-permute-start | bytes 786440 | tf_op jit(solution)/shard_map/coeff_parts/ppermute | solution.py:142
  57.4 5.5 %conv_taps.4 = bf16[4,64,512]{2,1,0:T(8,128)(2,1)S(1)} custom-call(s32[1]{0:T(128)} %bitcast.19.idx_ref, bf16[9,64,960]{2,1,0:T(8,128)(2,1)S(1)} %pad_maximum_fusion.1.b_ref, bf16[8,320,512]{2,1,0:T(8,128)(2,1)} %bitcast.29, bf16[8,320,512]{2,1,0:T(8,128)(2,1)} %collective-permute-done.12.x_oth_ref), custom_call_target="tpu_custom_call" | custom-call | tf_op jit(solution)/shard_map/coeff_parts/conv_taps/pallas_call | solution.py:59
  62.9 2.3 %collective-permute-start.15 = (bf16[4,64,512]{2,1,0:T(8,128)(2,1)S(1)}, bf16[4,64,512]{2,1,0:T(8,128)(2,1)S(1)}, u32[]{:S(2)}, u32[]{:S(2)}) collective-permute-start(bf16[4,64,512]{2,1,0:T(8,128)(2,1)S(1)} %conv_taps.4), channel_id=1, source_target_pairs={{0,3},{1,0},{2,1},{3,2},{4,7},{5,4},{6,5},{7,6},{8,11},{9,8},{10,9... | collective-permute-start | bytes 786440 | tf_op jit(solution)/shard_map/coeff_parts/ppermute | solution.py:142
  65.3 5.5 %conv_taps.5.refs_1_ = f32[4,64,512]{2,1,0:T(8,128)S(1)} custom-call(s32[1]{0:T(128)} %bitcast.20.idx_ref, bf16[9,64,960]{2,1,0:T(8,128)(2,1)S(1)} %pad_maximum_fusion.2.b_ref, bf16[8,320,512]{2,1,0:T(8,128)(2,1)} %bitcast.30, bf16[8,320,512]{2,1,0:T(8,128)(2,1)} %collective-permute-done.12.x_oth_ref), custom_call_target="tpu_custom_call" | custom-call | tf_op jit(solution)/shard_map/coeff_parts/conv_taps/pallas_call | solution.py:59
  70.8 0.8 copy-done
  72.4 2.0 %collective-permute-start.16 = (bf16[8,320,512]{2,1,0:T(8,128)(2,1)}, bf16[8,320,512]{2,1,0:T(8,128)(2,1)}, u32[]{:S(2)}, u32[]{:S(2)}) collective-permute-start(bf16[8,320,512]{2,1,0:T(8,128)(2,1)} %all-to-all-done.1.refs_5_), channel_id=1, source_target_pairs={{0,4},{4,0},{1,5},{5,1},{2,6},{6,2},{3,7},{7,3},{8,12},{12,8},{9,1... | collective-permute-start | bytes 7864328 | tf_op jit(solution)/shard_map/exchange_cores/ppermute | solution.py:142
  75.5 5.1 %collective-permute-done.17.refs_11_ = bf16[4,40,1280]{2,1,0:T(8,128)(2,1)S(1)} collective-permute-done((bf16[4,40,1280]{2,1,0:T(8,128)(2,1)S(1)}, bf16[4,40,1280]{2,1,0:T(8,128)(2,1)S(1)}, u32[]{:S(2)}, u32[]{:S(2)}) %collective-permute-start.17) | collective-permute-done | bytes 409632 | tf_op jit(solution)/shard_map/exchange_cores/ppermute | solution.py:142
  82.1 6.1 %squared_sums.1 = f32[16,4,1280]{2,1,0:T(4,128)S(1)} custom-call(s32[4]{0:T(128)S(1)} %pad_add_fusion.refs_0_, f32[4,64,512]{2,1,0:T(8,128)} %copy-done, bf16[4,64,512]{2,1,0:T(8,128)(2,1)S(1)} %collective-permute-done.13.refs_2_, bf16[4,64,512]{2,1,0:T(8,128)(2,1)S(1)} %collective-permute-done.14.refs_3_, ...), custom_call_target="tpu_custom_call" | custom-call | tf_op jit(solution)/shard_map/squared_sums/pallas_call | solution.py:125
  88.6 17.3 %all_to_all.15 = f32[64,1,1280]{2,1,0:T(1,128)S(1)} all-to-all(f32[64,1,1280]{2,1,0:T(1,128)S(1)} %reshape.22), channel_id=1, replica_groups=mesh['x'=4,'y'=4,'core'=2,'z'=4] {'x','y','z'}, dimensions={0} | all-to-all | bytes 655360 | tf_op jit(solution)/shard_map/sum_examples/all_to_all | solution.py:199
  (56 shorter events, 10.5 us)
Async XLA Ops:
  1.4 15.0 %all-to-all-start = ((bf16[4,40,320]{2,1,0:T(8,128)(2,1)}), bf16[4,40,320]{2,1,0:T(8,128)(2,1)S(1)}, u32[]{:S(2)}, u32[]{:S(2)}) async-start(bf16[4,40,320]{2,1,0:T(8,128)(2,1)} %broadcast_in_dim.2), calls=%async_computation | async-start | bytes 245760 | tf_op jit(solution)/shard_map/basis_g_z/all_to_all | solution.py:164
  8.3 4.0 %collective-permute-start.2 = (bf16[9,4,960]{2,1,0:T(4,128)(2,1)S(1)}, bf16[9,4,960]{2,1,0:T(4,128)(2,1)S(1)}, u32[]{:S(2)}, u32[]{:S(2)}) collective-permute-start(bf16[9,4,960]{2,1,0:T(4,128)(2,1)S(1)} %reshape.18), channel_id=1, source_target_pairs={{0,96},{32,0},{64,32},{96,64},{1,97},{33,1},{65,33},{97,65},{2,98}... | collective-permute-start | bytes 207368 | tf_op jit(solution)/shard_map/basis_a_x/ppermute | solution.py:142
  10.9 4.8 %collective-permute-start.1 = (bf16[9,4,960]{2,1,0:T(4,128)(2,1)S(1)}, bf16[9,4,960]{2,1,0:T(4,128)(2,1)S(1)}, u32[]{:S(2)}, u32[]{:S(2)}) collective-permute-start(bf16[9,4,960]{2,1,0:T(4,128)(2,1)S(1)} %reshape.18), channel_id=1, source_target_pairs={{0,64},{32,96},{64,0},{96,32},{1,65},{33,97},{65,1},{97,33},{2,66}... | collective-permute-start | bytes 207368 | tf_op jit(solution)/shard_map/basis_a_x/ppermute | solution.py:142
  11.4 5.0 %collective-permute-start = (bf16[9,4,960]{2,1,0:T(4,128)(2,1)S(1)}, bf16[9,4,960]{2,1,0:T(4,128)(2,1)S(1)}, u32[]{:S(2)}, u32[]{:S(2)}) collective-permute-start(bf16[9,4,960]{2,1,0:T(4,128)(2,1)S(1)} %reshape.18), channel_id=1, source_target_pairs={{0,32},{32,64},{64,96},{96,0},{1,33},{33,65},{65,97},{97,1},{2,34}... | collective-permute-start | bytes 207368 | tf_op jit(solution)/shard_map/basis_a_x/ppermute | solution.py:142
  16.6 29.0 %collective-permute-start.12 = (bf16[8,320,512]{2,1,0:T(8,128)(2,1)}, bf16[8,320,512]{2,1,0:T(8,128)(2,1)}, u32[]{:S(2)}, u32[]{:S(2)}) collective-permute-start(bf16[8,320,512]{2,1,0:T(8,128)(2,1)} %bitcast.27), channel_id=1, source_target_pairs={{0,4},{4,0},{1,5},{5,1},{2,6},{6,2},{3,7},{7,3},{8,12},{12,8},{9,1... | collective-permute-start | bytes 7864328 | tf_op jit(solution)/shard_map/basis_a_y/ppermute | solution.py:142
  19.0 53.4 %all-to-all-start.1 = ((bf16[8,320,512]{2,1,0:T(8,128)(2,1)}), bf16[8,320,512]{2,1,0:T(8,128)(2,1)}, u32[]{:S(2)}, u32[]{:S(2)}) async-start(bf16[8,320,512]{2,1,0:T(8,128)(2,1)} %bitcast.31), calls=%async_computation.1 | async-start | bytes 5242880 | tf_op jit(solution)/shard_map/exchange_grads/all_to_all | solution.py:167
  23.7 4.4 %collective-permute-start.8 = (bf16[40,1280]{1,0:T(8,128)(2,1)S(1)}, bf16[40,1280]{1,0:T(8,128)(2,1)S(1)}, u32[]{:S(2)}, u32[]{:S(2)}) collective-permute-start(bf16[40,1280]{1,0:T(8,128)(2,1)S(1)} %concatenate.16), channel_id=1, source_target_pairs={{0,96},{32,0},{64,32},{96,64},{1,97},{33,1},{65,33},{97,65},{2,98}... | collective-permute-start | bytes 307208 | tf_op jit(solution)/shard_map/basis_g_x/ppermute | solution.py:142
  24.1 14.7 %collective-permute-start.5 = (bf16[9,16,960]{2,1,0:T(8,128)(2,1)S(1)}, bf16[9,16,960]{2,1,0:T(8,128)(2,1)S(1)}, u32[]{:S(2)}, u32[]{:S(2)}) collective-permute-start(bf16[9,16,960]{2,1,0:T(8,128)(2,1)S(1)} %pad_maximum_fusion.4), channel_id=1, source_target_pairs={{0,24},{8,0},{16,8},{24,16},{1,25},{9,1},{17,9},{25,17},{2,26},{10... | collective-permute-start | bytes 829448 | tf_op jit(solution)/shard_map/basis_a_y/ppermute | solution.py:142
  26.8 12.0 %collective-permute-start.4 = (bf16[9,16,960]{2,1,0:T(8,128)(2,1)S(1)}, bf16[9,16,960]{2,1,0:T(8,128)(2,1)S(1)}, u32[]{:S(2)}, u32[]{:S(2)}) collective-permute-start(bf16[9,16,960]{2,1,0:T(8,128)(2,1)S(1)} %pad_maximum_fusion.4), channel_id=1, source_target_pairs={{0,16},{8,24},{16,0},{24,8},{1,17},{9,25},{17,1},{25,9},{2,18},{10... | collective-permute-start | bytes 829448 | tf_op jit(solution)/shard_map/basis_a_y/ppermute | solution.py:142
  27.2 16.5 %collective-permute-start.3 = (bf16[9,16,960]{2,1,0:T(8,128)(2,1)S(1)}, bf16[9,16,960]{2,1,0:T(8,128)(2,1)S(1)}, u32[]{:S(2)}, u32[]{:S(2)}) collective-permute-start(bf16[9,16,960]{2,1,0:T(8,128)(2,1)S(1)} %pad_maximum_fusion.4), channel_id=1, source_target_pairs={{0,8},{8,16},{16,24},{24,0},{1,9},{9,17},{17,25},{25,1},{2,10},{10... | collective-permute-start | bytes 829448 | tf_op jit(solution)/shard_map/basis_a_y/ppermute | solution.py:142
  28.1 5.3 %collective-permute-start.7 = (bf16[40,1280]{1,0:T(8,128)(2,1)S(1)}, bf16[40,1280]{1,0:T(8,128)(2,1)S(1)}, u32[]{:S(2)}, u32[]{:S(2)}) collective-permute-start(bf16[40,1280]{1,0:T(8,128)(2,1)S(1)} %concatenate.16), channel_id=1, source_target_pairs={{0,64},{32,96},{64,0},{96,32},{1,65},{33,97},{65,1},{97,33},{2,66}... | collective-permute-start | bytes 307208 | tf_op jit(solution)/shard_map/basis_g_x/ppermute | solution.py:142
  33.4 5.1 %collective-permute-start.6 = (bf16[40,1280]{1,0:T(8,128)(2,1)S(1)}, bf16[40,1280]{1,0:T(8,128)(2,1)S(1)}, u32[]{:S(2)}, u32[]{:S(2)}) collective-permute-start(bf16[40,1280]{1,0:T(8,128)(2,1)S(1)} %concatenate.16), channel_id=1, source_target_pairs={{0,32},{32,64},{64,96},{96,0},{1,33},{33,65},{65,97},{97,1},{2,34}... | collective-permute-start | bytes 307208 | tf_op jit(solution)/shard_map/basis_g_x/ppermute | solution.py:142
  43.7 13.5 %copy-start.1 = (bf16[9,16,960]{2,1,0:T(8,128)(2,1)}, bf16[9,16,960]{2,1,0:T(8,128)(2,1)S(1)}, u32[]{:S(2)}) copy-start(bf16[9,16,960]{2,1,0:T(8,128)(2,1)S(1)} %collective-permute-done.3) | copy-start | bytes 829444
  43.7 19.1 %collective-permute-start.11 = (bf16[4,40,1280]{2,1,0:T(8,128)(2,1)S(1)}, bf16[4,40,1280]{2,1,0:T(8,128)(2,1)}, u32[]{:S(2)}, u32[]{:S(2)}) collective-permute-start(bf16[4,40,1280]{2,1,0:T(8,128)(2,1)S(1)} %pad_maximum_fusion.3.refs_7_), channel_id=1, source_target_pairs={{0,24},{8,0},{16,8},{24,16},{1,25},{9,1},{17,9},{25,17},{2,26},{10... | collective-permute-start | bytes 1228808 | tf_op jit(solution)/shard_map/basis_g_y/ppermute | solution.py:142
  43.9 27.7 %collective-permute-start.10 = (bf16[4,40,1280]{2,1,0:T(8,128)(2,1)S(1)}, bf16[4,40,1280]{2,1,0:T(8,128)(2,1)S(1)}, u32[]{:S(2)}, u32[]{:S(2)}) collective-permute-start(bf16[4,40,1280]{2,1,0:T(8,128)(2,1)S(1)} %pad_maximum_fusion.3.refs_7_), channel_id=1, source_target_pairs={{0,16},{8,24},{16,0},{24,8},{1,17},{9,25},{17,1},{25,9},{2,18},{10... | collective-permute-start | bytes 1228808 | tf_op jit(solution)/shard_map/basis_g_y/ppermute | solution.py:142
  44.3 28.1 %collective-permute-start.9 = (bf16[4,40,1280]{2,1,0:T(8,128)(2,1)S(1)}, bf16[4,40,1280]{2,1,0:T(8,128)(2,1)S(1)}, u32[]{:S(2)}, u32[]{:S(2)}) collective-permute-start(bf16[4,40,1280]{2,1,0:T(8,128)(2,1)S(1)} %pad_maximum_fusion.3.refs_7_), channel_id=1, source_target_pairs={{0,8},{8,16},{16,24},{24,0},{1,9},{9,17},{17,25},{25,1},{2,10},{10... | collective-permute-start | bytes 1228808 | tf_op jit(solution)/shard_map/basis_g_y/ppermute | solution.py:142
  53.6 18.9 %collective-permute-start.13 = (bf16[4,64,512]{2,1,0:T(8,128)(2,1)S(1)}, bf16[4,64,512]{2,1,0:T(8,128)(2,1)S(1)}, u32[]{:S(2)}, u32[]{:S(2)}) collective-permute-start(bf16[4,64,512]{2,1,0:T(8,128)(2,1)S(1)} %get-tuple-element.59), channel_id=1, source_target_pairs={{0,2},{1,3},{2,0},{3,1},{4,6},{5,7},{6,4},{7,5},{8,10},{9,11},{10,... | collective-permute-start | bytes 786440 | tf_op jit(solution)/shard_map/coeff_parts/ppermute | solution.py:142
  56.8 15.6 %collective-permute-start.14 = (bf16[4,64,512]{2,1,0:T(8,128)(2,1)S(1)}, bf16[4,64,512]{2,1,0:T(8,128)(2,1)S(1)}, u32[]{:S(2)}, u32[]{:S(2)}) collective-permute-start(bf16[4,64,512]{2,1,0:T(8,128)(2,1)S(1)} %get-tuple-element.60), channel_id=1, source_target_pairs={{0,1},{1,2},{2,3},{3,0},{4,5},{5,6},{6,7},{7,4},{8,9},{9,10},{10,1... | collective-permute-start | bytes 786440 | tf_op jit(solution)/shard_map/coeff_parts/ppermute | solution.py:142
  62.9 9.6 %collective-permute-start.15 = (bf16[4,64,512]{2,1,0:T(8,128)(2,1)S(1)}, bf16[4,64,512]{2,1,0:T(8,128)(2,1)S(1)}, u32[]{:S(2)}, u32[]{:S(2)}) collective-permute-start(bf16[4,64,512]{2,1,0:T(8,128)(2,1)S(1)} %conv_taps.4), channel_id=1, source_target_pairs={{0,3},{1,0},{2,1},{3,2},{4,7},{5,4},{6,5},{7,6},{8,11},{9,8},{10,9... | collective-permute-start | bytes 786440 | tf_op jit(solution)/shard_map/coeff_parts/ppermute | solution.py:142
  72.4 9.2 %collective-permute-start.16 = (bf16[8,320,512]{2,1,0:T(8,128)(2,1)}, bf16[8,320,512]{2,1,0:T(8,128)(2,1)}, u32[]{:S(2)}, u32[]{:S(2)}) collective-permute-start(bf16[8,320,512]{2,1,0:T(8,128)(2,1)} %all-to-all-done.1.refs_5_), channel_id=1, source_target_pairs={{0,4},{4,0},{1,5},{5,1},{2,6},{6,2},{3,7},{7,3},{8,12},{12,8},{9,1... | collective-permute-start | bytes 7864328 | tf_op jit(solution)/shard_map/exchange_cores/ppermute | solution.py:142
  74.4 6.2 %collective-permute-start.17 = (bf16[4,40,1280]{2,1,0:T(8,128)(2,1)S(1)}, bf16[4,40,1280]{2,1,0:T(8,128)(2,1)S(1)}, u32[]{:S(2)}, u32[]{:S(2)}) collective-permute-start(bf16[4,40,1280]{2,1,0:T(8,128)(2,1)S(1)} %pad_maximum_fusion.3.refs_7_), channel_id=1, source_target_pairs={{0,4},{4,0},{1,5},{5,1},{2,6},{6,2},{3,7},{7,3},{8,12},{12,8},{9,1... | collective-permute-start | bytes 1228808 | tf_op jit(solution)/shard_map/exchange_cores/ppermute | solution.py:142
  74.5 6.7 %collective-permute-start.18 = (bf16[4,40,1280]{2,1,0:T(8,128)(2,1)S(1)}, bf16[4,40,1280]{2,1,0:T(8,128)(2,1)S(1)}, u32[]{:S(2)}, u32[]{:S(2)}) collective-permute-start(bf16[4,40,1280]{2,1,0:T(8,128)(2,1)S(1)} %collective-permute-done.9.refs_8_), channel_id=1, source_target_pairs={{0,4},{4,0},{1,5},{5,1},{2,6},{6,2},{3,7},{7,3},{8,12},{12,8},{9,1... | collective-permute-start | bytes 1228808 | tf_op jit(solution)/shard_map/exchange_cores/ppermute | solution.py:142
  74.9 6.2 %collective-permute-start.19 = (bf16[4,40,1280]{2,1,0:T(8,128)(2,1)}, bf16[4,40,1280]{2,1,0:T(8,128)(2,1)S(1)}, u32[]{:S(2)}, u32[]{:S(2)}) collective-permute-start(bf16[4,40,1280]{2,1,0:T(8,128)(2,1)} %copy-done.3), channel_id=1, source_target_pairs={{0,4},{4,0},{1,5},{5,1},{2,6},{6,2},{3,7},{7,3},{8,12},{12,8},{9,1... | collective-permute-start | bytes 1228808 | tf_op jit(solution)/shard_map/exchange_cores/ppermute | solution.py:142
  75.0 6.6 %collective-permute-start.20 = (bf16[4,40,1280]{2,1,0:T(8,128)(2,1)}, bf16[4,40,1280]{2,1,0:T(8,128)(2,1)}, u32[]{:S(2)}, u32[]{:S(2)}) collective-permute-start(bf16[4,40,1280]{2,1,0:T(8,128)(2,1)} %collective-permute-done.11.refs_10_), channel_id=1, source_target_pairs={{0,4},{4,0},{1,5},{5,1},{2,6},{6,2},{3,7},{7,3},{8,12},{12,8},{9,1... | collective-permute-start | bytes 1228808 | tf_op jit(solution)/shard_map/exchange_cores/ppermute | solution.py:142
  (6 other events, 12.3 us)

commit v12 on v10

--- a/solution.py
+++ b/solution.py
@@ -184,7 +184,7 @@
         ba, blocks, _ = lax.optimization_barrier((ba, blocks, far))
         last, mine = conv(jnp.stack(blocks[2:]), jnp.concatenate(ba, axis=1), x, x_oth, per, (bf16, jnp.float32))
     with jax.named_scope("exchange_cores"):
-        g, bg, received, mine = lax.optimization_barrier((g, bg, received, mine))
+        g, bg, received[0], last = lax.optimization_barrier((g, bg, received[0], last))
         g_oth = shift(g, "core", 1)
         bg_oth = [shift(v, "core", 1) for v in bg]
     received.append(shift(last, "z", 3))

time: 107 us -> 106 us (level)
  waiting for transfers between devices: 28.9 us -> 26.1 us
  starting transfers between devices: 31.6 us -> 33.2 us
    ppermute x21, waiting for transfers between devices: 28.9 us -> 26.1 us  [shift(): return lax.ppermute(v, axis, [(i, (i + s) % n) for i in range(n)])]
    ppermute x21, starting transfers between devices: 21.2 us -> 22.8 us  [shift(): return lax.ppermute(v, axis, [(i, (i + s) % n) for i in range(n)])]
  transfers between devices with their start and end apart: 23 -> 23, of which waited for: 11 -> 10; matrix products, arithmetic and copies ran while one was open for 2% -> 2% of each run, Pallas kernels for 15% -> 15%
where the time goes in v12:
time: 106 us
  starting transfers between devices  33.2 us (31%)
  waiting for transfers between devices  26.1 us (25%)
  Pallas kernels  22.1 us (21%)
  blocking collectives  18.7 us (18%)
  local copies, waits for them, and re-layouts  4.41 us (4%)
    ppermute x21, waiting for transfers between devices, shift(): return lax.ppermute(v, axis, [(i, (i + s) % n) for i in range(n)])  26.1 us
    ppermute x21, starting transfers between devices, shift(): return lax.ppermute(v, axis, [(i, (i + s) % n) for i in range(n)])  22.8 us
    all_to_all x1, blocking collectives, body(): got = lax.all_to_all(rows, ('x', 'y', 'z'), 0, 0, tiled=True)  18.7 us
    pallas_call x2, Pallas kernels, conv(): pl.pallas_call(conv_kernel, out_shape=[jax.ShapeDtypeStruct((2 * per, ran...  16 us
    pallas_call x1, Pallas kernels, squares(): pl.pallas_call(kernel, out_shape=jax.ShapeDtypeStruct((chips, ranks // ch...  6.1 us
    all_to_all x1, starting transfers between devices, body(): lax.all_to_all(jnp.broadcast_to(bg[None], (tensor, *bg.shape)), 'z', 0, 0...  5.86 us
    all_to_all x1, starting transfers between devices, body(): g = lax.all_to_all(grads, 'z', 0, 0, tiled=True)  4.55 us
  transfers between devices with their start and end apart: 23, of which 10 were waited for; matrix products, arithmetic and copies ran while one was open for 2% of the time, Pallas kernels for 15%

profile of v12, /device:TPU:1, one launch (start us, length us, event | category | flops | bytes accessed | tf_op | source)
XLA Modules:
  0.0 105.7 jit_solution(16907475022490190745)
XLA Ops:
  0.0 1.4 %broadcast_in_dim.2 = bf16[4,40,320]{2,1,0:T(8,128)(2,1)} broadcast(bf16[40,320]{1,0:T(8,128)(2,1)} %bitcast.37), dimensions={1,2} | broadcast | bytes 128000 | tf_op jit(solution)/shard_map/basis_g_z/broadcast_in_dim | solution.py:164
  1.4 5.9 %all-to-all-start = ((bf16[4,40,320]{2,1,0:T(8,128)(2,1)}), bf16[4,40,320]{2,1,0:T(8,128)(2,1)S(1)}, u32[]{:S(2)}, u32[]{:S(2)}) async-start(bf16[4,40,320]{2,1,0:T(8,128)(2,1)} %broadcast_in_dim.2), calls=%async_computation | async-start | bytes 245760 | tf_op jit(solution)/shard_map/basis_g_z/all_to_all | solution.py:164
  7.3 0.9 copy.10
  8.3 2.5 %collective-permute-start.2 = (bf16[9,4,960]{2,1,0:T(4,128)(2,1)S(1)}, bf16[9,4,960]{2,1,0:T(4,128)(2,1)S(1)}, u32[]{:S(2)}, u32[]{:S(2)}) collective-permute-start(bf16[9,4,960]{2,1,0:T(4,128)(2,1)S(1)} %reshape.12), channel_id=1, source_target_pairs={{0,96},{32,0},{64,32},{96,64},{1,97},{33,1},{65,33},{97,65},{2,98}... | collective-permute-start | bytes 207368 | tf_op jit(solution)/shard_map/basis_a_x/ppermute | solution.py:142
  12.3 3.4 %collective-permute-done.1 = bf16[9,4,960]{2,1,0:T(4,128)(2,1)S(1)} collective-permute-done((bf16[9,4,960]{2,1,0:T(4,128)(2,1)S(1)}, bf16[9,4,960]{2,1,0:T(4,128)(2,1)S(1)}, u32[]{:S(2)}, u32[]{:S(2)}) %collective-permute-start.1) | collective-permute-done | bytes 69152 | tf_op jit(solution)/shard_map/basis_a_x/ppermute | solution.py:142
  16.6 2.5 %collective-permute-start.9 = (bf16[8,320,512]{2,1,0:T(8,128)(2,1)}, bf16[8,320,512]{2,1,0:T(8,128)(2,1)}, u32[]{:S(2)}, u32[]{:S(2)}) collective-permute-start(bf16[8,320,512]{2,1,0:T(8,128)(2,1)} %bitcast.27), channel_id=1, source_target_pairs={{0,4},{4,0},{1,5},{5,1},{2,6},{6,2},{3,7},{7,3},{8,12},{12,8},{9,1... | collective-permute-start | bytes 7864328 | tf_op jit(solution)/shard_map/basis_a_y/ppermute | solution.py:142
  19.1 4.6 %all-to-all-start.1 = ((bf16[8,320,512]{2,1,0:T(8,128)(2,1)}), bf16[8,320,512]{2,1,0:T(8,128)(2,1)}, u32[]{:S(2)}, u32[]{:S(2)}) async-start(bf16[8,320,512]{2,1,0:T(8,128)(2,1)} %bitcast.30), calls=%async_computation.1 | async-start | bytes 5242880 | tf_op jit(solution)/shard_map/exchange_grads/all_to_all | solution.py:167
  24.1 2.7 %collective-permute-start.5 = (bf16[9,16,960]{2,1,0:T(8,128)(2,1)S(1)}, bf16[9,16,960]{2,1,0:T(8,128)(2,1)S(1)}, u32[]{:S(2)}, u32[]{:S(2)}) collective-permute-start(bf16[9,16,960]{2,1,0:T(8,128)(2,1)S(1)} %pad_maximum_fusion.3), channel_id=1, source_target_pairs={{0,24},{8,0},{16,8},{24,16},{1,25},{9,1},{17,9},{25,17},{2,26},{10... | collective-permute-start | bytes 829448 | tf_op jit(solution)/shard_map/basis_a_y/ppermute | solution.py:142
  28.2 1.0 collective-permute-start.7
  29.1 4.4 %collective-permute-done.7 = bf16[40,1280]{1,0:T(8,128)(2,1)S(1)} collective-permute-done((bf16[40,1280]{1,0:T(8,128)(2,1)S(1)}, bf16[40,1280]{1,0:T(8,128)(2,1)S(1)}, u32[]{:S(2)}, u32[]{:S(2)}) %collective-permute-start.7) | collective-permute-done | bytes 102432 | tf_op jit(solution)/shard_map/basis_g_x/ppermute | solution.py:142
  33.5 1.0 collective-permute-start.6
  34.5 4.1 %collective-permute-done.6 = bf16[40,1280]{1,0:T(8,128)(2,1)S(1)} collective-permute-done((bf16[40,1280]{1,0:T(8,128)(2,1)S(1)}, bf16[40,1280]{1,0:T(8,128)(2,1)S(1)}, u32[]{:S(2)}, u32[]{:S(2)}) %collective-permute-start.6) | collective-permute-done | bytes 102432 | tf_op jit(solution)/shard_map/basis_g_x/ppermute | solution.py:142
  38.8 4.8 %collective-permute-done.3 = bf16[9,16,960]{2,1,0:T(8,128)(2,1)S(1)} collective-permute-done((bf16[9,16,960]{2,1,0:T(8,128)(2,1)S(1)}, bf16[9,16,960]{2,1,0:T(8,128)(2,1)S(1)}, u32[]{:S(2)}, u32[]{:S(2)}) %collective-permute-start.3) | collective-permute-done | bytes 276512 | tf_op jit(solution)/shard_map/basis_a_y/ppermute | solution.py:142
  44.3 1.0 collective-permute-start.10
  45.6 8.0 %conv_taps.2 = (bf16[4,64,512]{2,1,0:T(8,128)(2,1)S(1)}, bf16[4,64,512]{2,1,0:T(8,128)(2,1)S(1)}) custom-call(s32[2]{0:T(128)S(1)} %pad_add_fusion.1.idx_ref, bf16[9,64,960]{2,1,0:T(8,128)(2,1)S(1)} %pad_maximum_fusion.b_ref, bf16[8,320,512]{2,1,0:T(8,128)(2,1)} %bitcast.28, bf16[8,320,512]{2,1,0:T(8,128)(2,1)} %collective-permute-done.9.x_oth_ref), custom_call_target="tpu_custom_call" | custom-call | tf_op jit(solution)/shard_map/coeff_parts/conv_taps/pallas_call | solution.py:59
  53.5 3.4 %collective-permute-start.13 = (bf16[4,64,512]{2,1,0:T(8,128)(2,1)S(1)}, bf16[4,64,512]{2,1,0:T(8,128)(2,1)S(1)}, u32[]{:S(2)}, u32[]{:S(2)}) collective-permute-start(bf16[4,64,512]{2,1,0:T(8,128)(2,1)S(1)} %get-tuple-element.49), channel_id=1, source_target_pairs={{0,2},{1,3},{2,0},{3,1},{4,6},{5,7},{6,4},{7,5},{8,10},{9,11},{10,... | collective-permute-start | bytes 786440 | tf_op jit(solution)/shard_map/coeff_parts/ppermute | solution.py:142
  57.2 8.0 %conv_taps.3 = (bf16[4,64,512]{2,1,0:T(8,128)(2,1)S(1)}, f32[4,64,512]{2,1,0:T(8,128)S(1)}) custom-call(s32[2]{0:T(128)S(1)} %pad_add_fusion.2.idx_ref, bf16[9,64,960]{2,1,0:T(8,128)(2,1)S(1)} %pad_maximum_fusion.1.b_ref, bf16[8,320,512]{2,1,0:T(8,128)(2,1)} %bitcast.29, bf16[8,320,512]{2,1,0:T(8,128)(2,1)} %collective-permute-done.9.x_oth_ref), custom_call_target="tpu_custom_call" | custom-call | tf_op jit(solution)/shard_map/coeff_parts/conv_taps/pallas_call | solution.py:59
  66.0 1.4 %collective-permute-start.16 = (bf16[8,320,512]{2,1,0:T(8,128)(2,1)}, bf16[8,320,512]{2,1,0:T(8,128)(2,1)}, u32[]{:S(2)}, u32[]{:S(2)}) collective-permute-start(bf16[8,320,512]{2,1,0:T(8,128)(2,1)} %all-to-all-done.1.refs_5_), channel_id=1, source_target_pairs={{0,4},{4,0},{1,5},{5,1},{2,6},{6,2},{3,7},{7,3},{8,12},{12,8},{9,1... | collective-permute-start | bytes 7864328 | tf_op jit(solution)/shard_map/exchange_cores/ppermute | solution.py:142
  67.8 2.4 %collective-permute-start.15 = (bf16[4,64,512]{2,1,0:T(8,128)(2,1)S(1)}, bf16[4,64,512]{2,1,0:T(8,128)(2,1)S(1)}, u32[]{:S(2)}, u32[]{:S(2)}) collective-permute-start(bf16[4,64,512]{2,1,0:T(8,128)(2,1)S(1)} %get-tuple-element.65), channel_id=1, source_target_pairs={{0,3},{1,0},{2,1},{3,2},{4,7},{5,4},{6,5},{7,6},{8,11},{9,8},{10,9... | collective-permute-start | bytes 786440 | tf_op jit(solution)/shard_map/ppermute | solution.py:142
  70.8 5.8 %collective-permute-done.14.refs_3_ = bf16[4,64,512]{2,1,0:T(8,128)(2,1)S(1)} collective-permute-done((bf16[4,64,512]{2,1,0:T(8,128)(2,1)S(1)}, bf16[4,64,512]{2,1,0:T(8,128)(2,1)S(1)}, u32[]{:S(2)}, u32[]{:S(2)}) %collective-permute-start.14) | collective-permute-done | bytes 262176 | tf_op jit(solution)/shard_map/coeff_parts/ppermute | solution.py:142
  76.6 0.9 collective-permute-start.19
  77.5 2.1 %collective-permute-done.19.refs_13_ = bf16[4,40,1280]{2,1,0:T(8,128)(2,1)} collective-permute-done((bf16[4,40,1280]{2,1,0:T(8,128)(2,1)}, bf16[4,40,1280]{2,1,0:T(8,128)(2,1)}, u32[]{:S(2)}, u32[]{:S(2)}) %collective-permute-start.19) | collective-permute-done | bytes 409632 | tf_op jit(solution)/shard_map/exchange_cores/ppermute | solution.py:142
  79.7 6.1 %squared_sums.1 = f32[16,4,1280]{2,1,0:T(4,128)S(1)} custom-call(s32[4]{0:T(128)S(1)} %pad_add_fusion.refs_0_, f32[4,64,512]{2,1,0:T(8,128)} %copy-done, bf16[4,64,512]{2,1,0:T(8,128)(2,1)S(1)} %collective-permute-done.13.refs_2_, bf16[4,64,512]{2,1,0:T(8,128)(2,1)S(1)} %collective-permute-done.14.refs_3_, ...), custom_call_target="tpu_custom_call" | custom-call | tf_op jit(solution)/shard_map/squared_sums/pallas_call | solution.py:125
  86.2 18.7 %all_to_all.15 = f32[64,1,1280]{2,1,0:T(1,128)S(1)} all-to-all(f32[64,1,1280]{2,1,0:T(1,128)S(1)} %reshape.14), channel_id=1, replica_groups=mesh['x'=4,'y'=4,'core'=2,'z'=4] {'x','y','z'}, dimensions={0} | all-to-all | bytes 655360 | tf_op jit(solution)/shard_map/sum_examples/all_to_all | solution.py:197
  (47 shorter events, 8.6 us)
Async XLA Ops:
  1.4 15.0 %all-to-all-start = ((bf16[4,40,320]{2,1,0:T(8,128)(2,1)}), bf16[4,40,320]{2,1,0:T(8,128)(2,1)S(1)}, u32[]{:S(2)}, u32[]{:S(2)}) async-start(bf16[4,40,320]{2,1,0:T(8,128)(2,1)} %broadcast_in_dim.2), calls=%async_computation | async-start | bytes 245760 | tf_op jit(solution)/shard_map/basis_g_z/all_to_all | solution.py:164
  8.3 4.0 %collective-permute-start.2 = (bf16[9,4,960]{2,1,0:T(4,128)(2,1)S(1)}, bf16[9,4,960]{2,1,0:T(4,128)(2,1)S(1)}, u32[]{:S(2)}, u32[]{:S(2)}) collective-permute-start(bf16[9,4,960]{2,1,0:T(4,128)(2,1)S(1)} %reshape.12), channel_id=1, source_target_pairs={{0,96},{32,0},{64,32},{96,64},{1,97},{33,1},{65,33},{97,65},{2,98}... | collective-permute-start | bytes 207368 | tf_op jit(solution)/shard_map/basis_a_x/ppermute | solution.py:142
  10.9 4.8 %collective-permute-start.1 = (bf16[9,4,960]{2,1,0:T(4,128)(2,1)S(1)}, bf16[9,4,960]{2,1,0:T(4,128)(2,1)S(1)}, u32[]{:S(2)}, u32[]{:S(2)}) collective-permute-start(bf16[9,4,960]{2,1,0:T(4,128)(2,1)S(1)} %reshape.12), channel_id=1, source_target_pairs={{0,64},{32,96},{64,0},{96,32},{1,65},{33,97},{65,1},{97,33},{2,66}... | collective-permute-start | bytes 207368 | tf_op jit(solution)/shard_map/basis_a_x/ppermute | solution.py:142
  11.4 5.0 %collective-permute-start = (bf16[9,4,960]{2,1,0:T(4,128)(2,1)S(1)}, bf16[9,4,960]{2,1,0:T(4,128)(2,1)S(1)}, u32[]{:S(2)}, u32[]{:S(2)}) collective-permute-start(bf16[9,4,960]{2,1,0:T(4,128)(2,1)S(1)} %reshape.12), channel_id=1, source_target_pairs={{0,32},{32,64},{64,96},{96,0},{1,33},{33,65},{65,97},{97,1},{2,34}... | collective-permute-start | bytes 207368 | tf_op jit(solution)/shard_map/basis_a_x/ppermute | solution.py:142
  16.6 29.0 %collective-permute-start.9 = (bf16[8,320,512]{2,1,0:T(8,128)(2,1)}, bf16[8,320,512]{2,1,0:T(8,128)(2,1)}, u32[]{:S(2)}, u32[]{:S(2)}) collective-permute-start(bf16[8,320,512]{2,1,0:T(8,128)(2,1)} %bitcast.27), channel_id=1, source_target_pairs={{0,4},{4,0},{1,5},{5,1},{2,6},{6,2},{3,7},{7,3},{8,12},{12,8},{9,1... | collective-permute-start | bytes 7864328 | tf_op jit(solution)/shard_map/basis_a_y/ppermute | solution.py:142
  19.1 47.0 %all-to-all-start.1 = ((bf16[8,320,512]{2,1,0:T(8,128)(2,1)}), bf16[8,320,512]{2,1,0:T(8,128)(2,1)}, u32[]{:S(2)}, u32[]{:S(2)}) async-start(bf16[8,320,512]{2,1,0:T(8,128)(2,1)} %bitcast.30), calls=%async_computation.1 | async-start | bytes 5242880 | tf_op jit(solution)/shard_map/exchange_grads/all_to_all | solution.py:167
  23.8 4.4 %collective-permute-start.8 = (bf16[40,1280]{1,0:T(8,128)(2,1)S(1)}, bf16[40,1280]{1,0:T(8,128)(2,1)S(1)}, u32[]{:S(2)}, u32[]{:S(2)}) collective-permute-start(bf16[40,1280]{1,0:T(8,128)(2,1)S(1)} %concatenate.13), channel_id=1, source_target_pairs={{0,96},{32,0},{64,32},{96,64},{1,97},{33,1},{65,33},{97,65},{2,98}... | collective-permute-start | bytes 307208 | tf_op jit(solution)/shard_map/basis_g_x/ppermute | solution.py:142
  24.1 14.7 %collective-permute-start.5 = (bf16[9,16,960]{2,1,0:T(8,128)(2,1)S(1)}, bf16[9,16,960]{2,1,0:T(8,128)(2,1)S(1)}, u32[]{:S(2)}, u32[]{:S(2)}) collective-permute-start(bf16[9,16,960]{2,1,0:T(8,128)(2,1)S(1)} %pad_maximum_fusion.3), channel_id=1, source_target_pairs={{0,24},{8,0},{16,8},{24,16},{1,25},{9,1},{17,9},{25,17},{2,26},{10... | collective-permute-start | bytes 829448 | tf_op jit(solution)/shard_map/basis_a_y/ppermute | solution.py:142
  26.8 12.0 %collective-permute-start.4 = (bf16[9,16,960]{2,1,0:T(8,128)(2,1)S(1)}, bf16[9,16,960]{2,1,0:T(8,128)(2,1)S(1)}, u32[]{:S(2)}, u32[]{:S(2)}) collective-permute-start(bf16[9,16,960]{2,1,0:T(8,128)(2,1)S(1)} %pad_maximum_fusion.3), channel_id=1, source_target_pairs={{0,16},{8,24},{16,0},{24,8},{1,17},{9,25},{17,1},{25,9},{2,18},{10... | collective-permute-start | bytes 829448 | tf_op jit(solution)/shard_map/basis_a_y/ppermute | solution.py:142
  27.2 16.5 %collective-permute-start.3 = (bf16[9,16,960]{2,1,0:T(8,128)(2,1)S(1)}, bf16[9,16,960]{2,1,0:T(8,128)(2,1)S(1)}, u32[]{:S(2)}, u32[]{:S(2)}) collective-permute-start(bf16[9,16,960]{2,1,0:T(8,128)(2,1)S(1)} %pad_maximum_fusion.3), channel_id=1, source_target_pairs={{0,8},{8,16},{16,24},{24,0},{1,9},{9,17},{17,25},{25,1},{2,10},{10... | collective-permute-start | bytes 829448 | tf_op jit(solution)/shard_map/basis_a_y/ppermute | solution.py:142
  28.2 5.3 %collective-permute-start.7 = (bf16[40,1280]{1,0:T(8,128)(2,1)S(1)}, bf16[40,1280]{1,0:T(8,128)(2,1)S(1)}, u32[]{:S(2)}, u32[]{:S(2)}) collective-permute-start(bf16[40,1280]{1,0:T(8,128)(2,1)S(1)} %concatenate.13), channel_id=1, source_target_pairs={{0,64},{32,96},{64,0},{96,32},{1,65},{33,97},{65,1},{97,33},{2,66}... | collective-permute-start | bytes 307208 | tf_op jit(solution)/shard_map/basis_g_x/ppermute | solution.py:142
  33.5 5.1 %collective-permute-start.6 = (bf16[40,1280]{1,0:T(8,128)(2,1)S(1)}, bf16[40,1280]{1,0:T(8,128)(2,1)S(1)}, u32[]{:S(2)}, u32[]{:S(2)}) collective-permute-start(bf16[40,1280]{1,0:T(8,128)(2,1)S(1)} %concatenate.13), channel_id=1, source_target_pairs={{0,32},{32,64},{64,96},{96,0},{1,33},{33,65},{65,97},{97,1},{2,34}... | collective-permute-start | bytes 307208 | tf_op jit(solution)/shard_map/basis_g_x/ppermute | solution.py:142
  43.8 22.2 %collective-permute-start.12 = (bf16[4,40,1280]{2,1,0:T(8,128)(2,1)S(1)}, bf16[4,40,1280]{2,1,0:T(8,128)(2,1)S(1)}, u32[]{:S(2)}, u32[]{:S(2)}) collective-permute-start(bf16[4,40,1280]{2,1,0:T(8,128)(2,1)S(1)} %pad_maximum_fusion.2.refs_7_), channel_id=1, source_target_pairs={{0,24},{8,0},{16,8},{24,16},{1,25},{9,1},{17,9},{25,17},{2,26},{10... | collective-permute-start | bytes 1228808 | tf_op jit(solution)/shard_map/basis_g_y/ppermute | solution.py:142
  43.8 22.2 %collective-permute-start.11 = (bf16[4,40,1280]{2,1,0:T(8,128)(2,1)S(1)}, bf16[4,40,1280]{2,1,0:T(8,128)(2,1)}, u32[]{:S(2)}, u32[]{:S(2)}) collective-permute-start(bf16[4,40,1280]{2,1,0:T(8,128)(2,1)S(1)} %pad_maximum_fusion.2.refs_7_), channel_id=1, source_target_pairs={{0,16},{8,24},{16,0},{24,8},{1,17},{9,25},{17,1},{25,9},{2,18},{10... | collective-permute-start | bytes 1228808 | tf_op jit(solution)/shard_map/basis_g_y/ppermute | solution.py:142
  44.3 21.7 %collective-permute-start.10 = (bf16[4,40,1280]{2,1,0:T(8,128)(2,1)S(1)}, bf16[4,40,1280]{2,1,0:T(8,128)(2,1)S(1)}, u32[]{:S(2)}, u32[]{:S(2)}) collective-permute-start(bf16[4,40,1280]{2,1,0:T(8,128)(2,1)S(1)} %pad_maximum_fusion.2.refs_7_), channel_id=1, source_target_pairs={{0,8},{8,16},{16,24},{24,0},{1,9},{9,17},{17,25},{25,1},{2,10},{10... | collective-permute-start | bytes 1228808 | tf_op jit(solution)/shard_map/basis_g_y/ppermute | solution.py:142
  53.5 12.5 %collective-permute-start.13 = (bf16[4,64,512]{2,1,0:T(8,128)(2,1)S(1)}, bf16[4,64,512]{2,1,0:T(8,128)(2,1)S(1)}, u32[]{:S(2)}, u32[]{:S(2)}) collective-permute-start(bf16[4,64,512]{2,1,0:T(8,128)(2,1)S(1)} %get-tuple-element.49), channel_id=1, source_target_pairs={{0,2},{1,3},{2,0},{3,1},{4,6},{5,7},{6,4},{7,5},{8,10},{9,11},{10,... | collective-permute-start | bytes 786440 | tf_op jit(solution)/shard_map/coeff_parts/ppermute | solution.py:142
  66.0 13.7 %copy-start.1 = (bf16[4,40,1280]{2,1,0:T(8,128)(2,1)}, bf16[4,40,1280]{2,1,0:T(8,128)(2,1)S(1)}, u32[]{:S(2)}) copy-start(bf16[4,40,1280]{2,1,0:T(8,128)(2,1)S(1)} %collective-permute-done.12.refs_10_) | copy-start | bytes 1228804
  66.0 13.6 %collective-permute-start.16 = (bf16[8,320,512]{2,1,0:T(8,128)(2,1)}, bf16[8,320,512]{2,1,0:T(8,128)(2,1)}, u32[]{:S(2)}, u32[]{:S(2)}) collective-permute-start(bf16[8,320,512]{2,1,0:T(8,128)(2,1)} %all-to-all-done.1.refs_5_), channel_id=1, source_target_pairs={{0,4},{4,0},{1,5},{5,1},{2,6},{6,2},{3,7},{7,3},{8,12},{12,8},{9,1... | collective-permute-start | bytes 7864328 | tf_op jit(solution)/shard_map/exchange_cores/ppermute | solution.py:142
  67.5 9.1 %collective-permute-start.14 = (bf16[4,64,512]{2,1,0:T(8,128)(2,1)S(1)}, bf16[4,64,512]{2,1,0:T(8,128)(2,1)S(1)}, u32[]{:S(2)}, u32[]{:S(2)}) collective-permute-start(bf16[4,64,512]{2,1,0:T(8,128)(2,1)S(1)} %get-tuple-element.64), channel_id=1, source_target_pairs={{0,1},{1,2},{2,3},{3,0},{4,5},{5,6},{6,7},{7,4},{8,9},{9,10},{10,1... | collective-permute-start | bytes 786440 | tf_op jit(solution)/shard_map/coeff_parts/ppermute | solution.py:142
  67.8 9.6 %collective-permute-start.15 = (bf16[4,64,512]{2,1,0:T(8,128)(2,1)S(1)}, bf16[4,64,512]{2,1,0:T(8,128)(2,1)S(1)}, u32[]{:S(2)}, u32[]{:S(2)}) collective-permute-start(bf16[4,64,512]{2,1,0:T(8,128)(2,1)S(1)} %get-tuple-element.65), channel_id=1, source_target_pairs={{0,3},{1,0},{2,1},{3,2},{4,7},{5,4},{6,5},{7,6},{8,11},{9,8},{10,9... | collective-permute-start | bytes 786440 | tf_op jit(solution)/shard_map/ppermute | solution.py:142
  70.2 7.3 %collective-permute-start.17 = (bf16[4,40,1280]{2,1,0:T(8,128)(2,1)S(1)}, bf16[4,40,1280]{2,1,0:T(8,128)(2,1)S(1)}, u32[]{:S(2)}, u32[]{:S(2)}) collective-permute-start(bf16[4,40,1280]{2,1,0:T(8,128)(2,1)S(1)} %pad_maximum_fusion.2.refs_7_), channel_id=1, source_target_pairs={{0,4},{4,0},{1,5},{5,1},{2,6},{6,2},{3,7},{7,3},{8,12},{12,8},{9,1... | collective-permute-start | bytes 1228808 | tf_op jit(solution)/shard_map/exchange_cores/ppermute | solution.py:142
  70.8 6.7 %collective-permute-start.18 = (bf16[4,40,1280]{2,1,0:T(8,128)(2,1)S(1)}, bf16[4,40,1280]{2,1,0:T(8,128)(2,1)}, u32[]{:S(2)}, u32[]{:S(2)}) collective-permute-start(bf16[4,40,1280]{2,1,0:T(8,128)(2,1)S(1)} %collective-permute-done.10.refs_8_), channel_id=1, source_target_pairs={{0,4},{4,0},{1,5},{5,1},{2,6},{6,2},{3,7},{7,3},{8,12},{12,8},{9,1... | collective-permute-start | bytes 1228808 | tf_op jit(solution)/shard_map/exchange_cores/ppermute | solution.py:142
  76.6 3.1 %collective-permute-start.19 = (bf16[4,40,1280]{2,1,0:T(8,128)(2,1)}, bf16[4,40,1280]{2,1,0:T(8,128)(2,1)}, u32[]{:S(2)}, u32[]{:S(2)}) collective-permute-start(bf16[4,40,1280]{2,1,0:T(8,128)(2,1)} %collective-permute-done.11.refs_9_), channel_id=1, source_target_pairs={{0,4},{4,0},{1,5},{5,1},{2,6},{6,2},{3,7},{7,3},{8,12},{12,8},{9,1... | collective-permute-start | bytes 1228808 | tf_op jit(solution)/shard_map/exchange_cores/ppermute | solution.py:142
  77.4 2.2 %collective-permute-start.20 = (bf16[4,40,1280]{2,1,0:T(8,128)(2,1)S(1)}, bf16[4,40,1280]{2,1,0:T(8,128)(2,1)}, u32[]{:S(2)}, u32[]{:S(2)}) collective-permute-start(bf16[4,40,1280]{2,1,0:T(8,128)(2,1)S(1)} %collective-permute-done.12.refs_10_), channel_id=1, source_target_pairs={{0,4},{4,0},{1,5},{5,1},{2,6},{6,2},{3,7},{7,3},{8,12},{12,8},{9,1... | collective-permute-start | bytes 1228808 | tf_op jit(solution)/shard_map/exchange_cores/ppermute | solution.py:142
  (2 other events, 3.0 us)

commit v13 on v12

--- a/solution.py
+++ b/solution.py
@@ -193,9 +193,9 @@
     total = squares(jnp.stack(coords), mine, received, g, g_oth, bg, bg_oth, 1.0 / examples)
 
     with jax.named_scope("sum_examples"):
-        rows = total.reshape(-1, 1, total.shape[2])
+        rows = total.reshape(-1, 1, total.shape[2]).astype(jnp.bfloat16)
         got = lax.all_to_all(rows, ("x", "y", "z"), 0, 0, tiled=True)
-        return jnp.sum(got, axis=0)
+        return jnp.sum(got.astype(jnp.float32), axis=0)
 
 
 def solution(mesh):

time: 106 us -> 107 us (level)
  starting transfers between devices: 33.2 us -> 42.4 us
  waiting for transfers between devices: 26.1 us -> 17.7 us
  blocking collectives: 18.7 us -> 16.2 us
  other arithmetic: 1.01 us -> 2.75 us
    ppermute x21, starting transfers between devices: 22.8 us -> 31.9 us  [shift(): return lax.ppermute(v, axis, [(i, (i + s) % n) for i in range(n)])]
    ppermute x21, waiting for transfers between devices: 26.1 us -> 17.7 us  [shift(): return lax.ppermute(v, axis, [(i, (i + s) % n) for i in range(n)])]
    all_to_all x1, blocking collectives: 18.7 us -> 16.2 us  [body(): got = lax.all_to_all(rows, ('x', 'y', 'z'), 0, 0, tiled=True)]
    convert_element_type x0 -> x2, other arithmetic: none -> 1.65 us  [body(): rows = total.reshape(-1, 1, total.shape[2]).astype(jnp.bfloat16)]
  transfers between devices with their start and end apart: 23 -> 23, of which waited for: 10 -> 9; matrix products, arithmetic and copies ran while one was open for 2% -> 2% of each run, Pallas kernels for 15% -> 15%
where the time goes in v13:
time: 107 us; the launch traced here: 106 us
  starting transfers between devices  42.4 us (40%)
  Pallas kernels  22.1 us (21%)
  waiting for transfers between devices  17.7 us (17%)
  blocking collectives  16.2 us (15%)
  local copies, waits for them, and re-layouts  4.71 us (4%)
  other arithmetic  2.75 us (3%)
    ppermute x21, starting transfers between devices, shift(): return lax.ppermute(v, axis, [(i, (i + s) % n) for i in range(n)])  31.9 us
    ppermute x21, waiting for transfers between devices, shift(): return lax.ppermute(v, axis, [(i, (i + s) % n) for i in range(n)])  17.7 us
    all_to_all x1, blocking collectives, body(): got = lax.all_to_all(rows, ('x', 'y', 'z'), 0, 0, tiled=True)  16.2 us
    pallas_call x2, Pallas kernels, conv(): pl.pallas_call(conv_kernel, out_shape=[jax.ShapeDtypeStruct((2 * per, ran...  16 us
    pallas_call x1, Pallas kernels, squares(): pl.pallas_call(kernel, out_shape=jax.ShapeDtypeStruct((chips, ranks // ch...  6.09 us
    all_to_all x1, starting transfers between devices, body(): lax.all_to_all(jnp.broadcast_to(bg[None], (tensor, *bg.shape)), 'z', 0, 0...  5.86 us
    all_to_all x1, starting transfers between devices, body(): g = lax.all_to_all(grads, 'z', 0, 0, tiled=True)  4.57 us
  transfers between devices with their start and end apart: 23, of which 9 were waited for; matrix products, arithmetic and copies ran while one was open for 2% of the time, Pallas kernels for 15%

profile of v13, /device:TPU:1, one launch (start us, length us, event | category | flops | bytes accessed | tf_op | source)
XLA Modules:
  0.0 106.0 jit_solution(2507757316346558191)
XLA Ops:
  0.0 1.4 %broadcast_in_dim.2 = bf16[4,40,320]{2,1,0:T(8,128)(2,1)} broadcast(bf16[40,320]{1,0:T(8,128)(2,1)} %bitcast.37), dimensions={1,2} | broadcast | bytes 128000 | tf_op jit(solution)/shard_map/basis_g_z/broadcast_in_dim | solution.py:164
  1.4 5.9 %all-to-all-start = ((bf16[4,40,320]{2,1,0:T(8,128)(2,1)}), bf16[4,40,320]{2,1,0:T(8,128)(2,1)S(1)}, u32[]{:S(2)}, u32[]{:S(2)}) async-start(bf16[4,40,320]{2,1,0:T(8,128)(2,1)} %broadcast_in_dim.2), calls=%async_computation | async-start | bytes 245760 | tf_op jit(solution)/shard_map/basis_g_z/all_to_all | solution.py:164
  9.6 2.5 %collective-permute-start.1 = (bf16[9,4,960]{2,1,0:T(4,128)(2,1)S(1)}, bf16[9,4,960]{2,1,0:T(4,128)(2,1)S(1)}, u32[]{:S(2)}, u32[]{:S(2)}) collective-permute-start(bf16[9,4,960]{2,1,0:T(4,128)(2,1)S(1)} %reshape.23), channel_id=1, source_target_pairs={{0,64},{32,96},{64,0},{96,32},{1,65},{33,97},{65,1},{97,33},{2,66}... | collective-permute-start | bytes 207368 | tf_op jit(solution)/shard_map/basis_a_x/ppermute | solution.py:142
  13.2 1.5 %collective-permute-done.1 = bf16[9,4,960]{2,1,0:T(4,128)(2,1)S(1)} collective-permute-done((bf16[9,4,960]{2,1,0:T(4,128)(2,1)S(1)}, bf16[9,4,960]{2,1,0:T(4,128)(2,1)S(1)}, u32[]{:S(2)}, u32[]{:S(2)}) %collective-permute-start.1) | collective-permute-done | bytes 69152 | tf_op jit(solution)/shard_map/basis_a_x/ppermute | solution.py:142
  14.7 1.5 %collective-permute-done.2 = bf16[9,4,960]{2,1,0:T(4,128)(2,1)S(1)} collective-permute-done((bf16[9,4,960]{2,1,0:T(4,128)(2,1)S(1)}, bf16[9,4,960]{2,1,0:T(4,128)(2,1)S(1)}, u32[]{:S(2)}, u32[]{:S(2)}) %collective-permute-start.2) | collective-permute-done | bytes 69152 | tf_op jit(solution)/shard_map/basis_a_x/ppermute | solution.py:142
  16.4 1.8 %collective-permute-start.9 = (bf16[8,320,512]{2,1,0:T(8,128)(2,1)}, bf16[8,320,512]{2,1,0:T(8,128)(2,1)}, u32[]{:S(2)}, u32[]{:S(2)}) collective-permute-start(bf16[8,320,512]{2,1,0:T(8,128)(2,1)} %bitcast.27), channel_id=1, source_target_pairs={{0,4},{4,0},{1,5},{5,1},{2,6},{6,2},{3,7},{7,3},{8,12},{12,8},{9,1... | collective-permute-start | bytes 7864328 | tf_op jit(solution)/shard_map/basis_a_y/ppermute | solution.py:142
  18.2 4.6 %all-to-all-start.1 = ((bf16[8,320,512]{2,1,0:T(8,128)(2,1)}), bf16[8,320,512]{2,1,0:T(8,128)(2,1)}, u32[]{:S(2)}, u32[]{:S(2)}) async-start(bf16[8,320,512]{2,1,0:T(8,128)(2,1)} %bitcast.30), calls=%async_computation.1 | async-start | bytes 5242880 | tf_op jit(solution)/shard_map/exchange_grads/all_to_all | solution.py:167
  24.7 2.6 %collective-permute-start.4 = (bf16[9,16,960]{2,1,0:T(8,128)(2,1)S(1)}, bf16[9,16,960]{2,1,0:T(8,128)(2,1)S(1)}, u32[]{:S(2)}, u32[]{:S(2)}) collective-permute-start(bf16[9,16,960]{2,1,0:T(8,128)(2,1)S(1)} %pad_maximum_fusion.3), channel_id=1, source_target_pairs={{0,16},{8,24},{16,0},{24,8},{1,17},{9,25},{17,1},{25,9},{2,18},{10... | collective-permute-start | bytes 829448 | tf_op jit(solution)/shard_map/basis_a_y/ppermute | solution.py:142
  28.5 3.0 %collective-permute-start.7 = (bf16[40,1280]{1,0:T(8,128)(2,1)S(1)}, bf16[40,1280]{1,0:T(8,128)(2,1)S(1)}, u32[]{:S(2)}, u32[]{:S(2)}) collective-permute-start(bf16[40,1280]{1,0:T(8,128)(2,1)S(1)} %concatenate.13), channel_id=1, source_target_pairs={{0,64},{32,96},{64,0},{96,32},{1,65},{33,97},{65,1},{97,33},{2,66}... | collective-permute-start | bytes 307208 | tf_op jit(solution)/shard_map/basis_g_x/ppermute | solution.py:142
  31.5 2.0 %collective-permute-done.7 = bf16[40,1280]{1,0:T(8,128)(2,1)S(1)} collective-permute-done((bf16[40,1280]{1,0:T(8,128)(2,1)S(1)}, bf16[40,1280]{1,0:T(8,128)(2,1)S(1)}, u32[]{:S(2)}, u32[]{:S(2)}) %collective-permute-start.7) | collective-permute-done | bytes 102432 | tf_op jit(solution)/shard_map/basis_g_x/ppermute | solution.py:142
  33.6 2.1 %collective-permute-start.8 = (bf16[40,1280]{1,0:T(8,128)(2,1)S(1)}, bf16[40,1280]{1,0:T(8,128)(2,1)S(1)}, u32[]{:S(2)}, u32[]{:S(2)}) collective-permute-start(bf16[40,1280]{1,0:T(8,128)(2,1)S(1)} %concatenate.13), channel_id=1, source_target_pairs={{0,96},{32,0},{64,32},{96,64},{1,97},{33,1},{65,33},{97,65},{2,98}... | collective-permute-start | bytes 307208 | tf_op jit(solution)/shard_map/basis_g_x/ppermute | solution.py:142
  35.7 1.8 %collective-permute-done.8 = bf16[40,1280]{1,0:T(8,128)(2,1)S(1)} collective-permute-done((bf16[40,1280]{1,0:T(8,128)(2,1)S(1)}, bf16[40,1280]{1,0:T(8,128)(2,1)S(1)}, u32[]{:S(2)}, u32[]{:S(2)}) %collective-permute-start.8) | collective-permute-done | bytes 102432 | tf_op jit(solution)/shard_map/basis_g_x/ppermute | solution.py:142
  37.5 2.7 %collective-permute-done.4 = bf16[9,16,960]{2,1,0:T(8,128)(2,1)S(1)} collective-permute-done((bf16[9,16,960]{2,1,0:T(8,128)(2,1)S(1)}, bf16[9,16,960]{2,1,0:T(8,128)(2,1)S(1)}, u32[]{:S(2)}, u32[]{:S(2)}) %collective-permute-start.4) | collective-permute-done | bytes 276512 | tf_op jit(solution)/shard_map/basis_a_y/ppermute | solution.py:142
  41.3 3.0 %collective-permute-start.11 = (bf16[4,40,1280]{2,1,0:T(8,128)(2,1)S(1)}, bf16[4,40,1280]{2,1,0:T(8,128)(2,1)S(1)}, u32[]{:S(2)}, u32[]{:S(2)}) collective-permute-start(bf16[4,40,1280]{2,1,0:T(8,128)(2,1)S(1)} %pad_maximum_fusion.2.refs_7_), channel_id=1, source_target_pairs={{0,16},{8,24},{16,0},{24,8},{1,17},{9,25},{17,1},{25,9},{2,18},{10... | collective-permute-start | bytes 1228808 | tf_op jit(solution)/shard_map/basis_g_y/ppermute | solution.py:142
  44.8 8.0 %conv_taps.2 = (bf16[4,64,512]{2,1,0:T(8,128)(2,1)S(1)}, bf16[4,64,512]{2,1,0:T(8,128)(2,1)S(1)}) custom-call(s32[2]{0:T(128)S(1)} %pad_add_fusion.1.idx_ref, bf16[9,64,960]{2,1,0:T(8,128)(2,1)S(1)} %pad_maximum_fusion.b_ref, bf16[8,320,512]{2,1,0:T(8,128)(2,1)} %bitcast.28, bf16[8,320,512]{2,1,0:T(8,128)(2,1)} %collective-permute-done.9.x_oth_ref), custom_call_target="tpu_custom_call" | custom-call | tf_op jit(solution)/shard_map/coeff_parts/conv_taps/pallas_call | solution.py:59
  52.7 3.5 %collective-permute-start.13 = (bf16[4,64,512]{2,1,0:T(8,128)(2,1)S(1)}, bf16[4,64,512]{2,1,0:T(8,128)(2,1)S(1)}, u32[]{:S(2)}, u32[]{:S(2)}) collective-permute-start(bf16[4,64,512]{2,1,0:T(8,128)(2,1)S(1)} %get-tuple-element.49), channel_id=1, source_target_pairs={{0,2},{1,3},{2,0},{3,1},{4,6},{5,7},{6,4},{7,5},{8,10},{9,11},{10,... | collective-permute-start | bytes 786440 | tf_op jit(solution)/shard_map/coeff_parts/ppermute | solution.py:142
  56.4 8.0 %conv_taps.3 = (bf16[4,64,512]{2,1,0:T(8,128)(2,1)S(1)}, f32[4,64,512]{2,1,0:T(8,128)S(1)}) custom-call(s32[2]{0:T(128)S(1)} %pad_add_fusion.2.idx_ref, bf16[9,64,960]{2,1,0:T(8,128)(2,1)S(1)} %pad_maximum_fusion.1.b_ref, bf16[8,320,512]{2,1,0:T(8,128)(2,1)} %bitcast.29, bf16[8,320,512]{2,1,0:T(8,128)(2,1)} %collective-permute-done.9.x_oth_ref), custom_call_target="tpu_custom_call" | custom-call | tf_op jit(solution)/shard_map/coeff_parts/conv_taps/pallas_call | solution.py:59
  65.3 2.8 %collective-permute-start.16 = (bf16[8,320,512]{2,1,0:T(8,128)(2,1)}, bf16[8,320,512]{2,1,0:T(8,128)(2,1)}, u32[]{:S(2)}, u32[]{:S(2)}) collective-permute-start(bf16[8,320,512]{2,1,0:T(8,128)(2,1)} %all-to-all-done.1.refs_5_), channel_id=1, source_target_pairs={{0,4},{4,0},{1,5},{5,1},{2,6},{6,2},{3,7},{7,3},{8,12},{12,8},{9,1... | collective-permute-start | bytes 7864328 | tf_op jit(solution)/shard_map/exchange_cores/ppermute | solution.py:142
  68.3 2.4 %collective-permute-start.15 = (bf16[4,64,512]{2,1,0:T(8,128)(2,1)S(1)}, bf16[4,64,512]{2,1,0:T(8,128)(2,1)S(1)}, u32[]{:S(2)}, u32[]{:S(2)}) collective-permute-start(bf16[4,64,512]{2,1,0:T(8,128)(2,1)S(1)} %get-tuple-element.65), channel_id=1, source_target_pairs={{0,3},{1,0},{2,1},{3,2},{4,7},{5,4},{6,5},{7,6},{8,11},{9,8},{10,9... | collective-permute-start | bytes 786440 | tf_op jit(solution)/shard_map/ppermute | solution.py:142
  71.4 5.8 %collective-permute-done.14.refs_3_ = bf16[4,64,512]{2,1,0:T(8,128)(2,1)S(1)} collective-permute-done((bf16[4,64,512]{2,1,0:T(8,128)(2,1)S(1)}, bf16[4,64,512]{2,1,0:T(8,128)(2,1)S(1)}, u32[]{:S(2)}, u32[]{:S(2)}) %collective-permute-start.14) | collective-permute-done | bytes 262176 | tf_op jit(solution)/shard_map/coeff_parts/ppermute | solution.py:142
  78.1 1.9 %collective-permute-done.19.refs_13_ = bf16[4,40,1280]{2,1,0:T(8,128)(2,1)} collective-permute-done((bf16[4,40,1280]{2,1,0:T(8,128)(2,1)S(1)}, bf16[4,40,1280]{2,1,0:T(8,128)(2,1)}, u32[]{:S(2)}, u32[]{:S(2)}) %collective-permute-start.19) | collective-permute-done | bytes 409632 | tf_op jit(solution)/shard_map/exchange_cores/ppermute | solution.py:142
  80.3 6.1 %squared_sums.1 = f32[16,4,1280]{2,1,0:T(4,128)S(1)} custom-call(s32[4]{0:T(128)S(1)} %pad_add_fusion.refs_0_, f32[4,64,512]{2,1,0:T(8,128)} %copy-done, bf16[4,64,512]{2,1,0:T(8,128)(2,1)S(1)} %collective-permute-done.13.refs_2_, bf16[4,64,512]{2,1,0:T(8,128)(2,1)S(1)} %collective-permute-done.14.refs_3_, ...), custom_call_target="tpu_custom_call" | custom-call | tf_op jit(solution)/shard_map/squared_sums/pallas_call | solution.py:125
  87.1 1.6 %reduce.1 = bf16[64,1280]{1,0:T(8,128)(2,1)S(1)} reduce(bf16[64,1,1280]{2,1,0:T(2,128)(2,1)S(1)} %convert_element_type.20, bf16[]{:T(256)} %broadcast.5), dimensions={1}, to_apply=%convert_element_type.20.reduce_sub_computation | reduce | bytes 327682 | tf_op jit(solution)/shard_map/sum_examples/convert_element_type | solution.py:196
  88.7 16.2 %all_to_all.15 = bf16[64,2,640]{2,1,0:T(2,128)(2,1)S(1)} all-to-all(bf16[64,2,640]{2,1,0:T(2,128)(2,1)S(1)} %reshape.24), channel_id=1, replica_groups=mesh['x'=4,'y'=4,'core'=2,'z'=4] {'x','y','z'}, dimensions={0} | all-to-all | bytes 327680 | tf_op jit(solution)/shard_map/sum_examples/all_to_all | solution.py:197
  (52 shorter events, 13.3 us)
Async XLA Ops:
  1.4 14.7 %all-to-all-start = ((bf16[4,40,320]{2,1,0:T(8,128)(2,1)}), bf16[4,40,320]{2,1,0:T(8,128)(2,1)S(1)}, u32[]{:S(2)}, u32[]{:S(2)}) async-start(bf16[4,40,320]{2,1,0:T(8,128)(2,1)} %broadcast_in_dim.2), calls=%async_computation | async-start | bytes 245760 | tf_op jit(solution)/shard_map/basis_g_z/all_to_all | solution.py:164
  8.3 4.9 %collective-permute-start = (bf16[9,4,960]{2,1,0:T(4,128)(2,1)S(1)}, bf16[9,4,960]{2,1,0:T(4,128)(2,1)S(1)}, u32[]{:S(2)}, u32[]{:S(2)}) collective-permute-start(bf16[9,4,960]{2,1,0:T(4,128)(2,1)S(1)} %reshape.23), channel_id=1, source_target_pairs={{0,32},{32,64},{64,96},{96,0},{1,33},{33,65},{65,97},{97,1},{2,34}... | collective-permute-start | bytes 207368 | tf_op jit(solution)/shard_map/basis_a_x/ppermute | solution.py:142
  9.6 5.1 %collective-permute-start.1 = (bf16[9,4,960]{2,1,0:T(4,128)(2,1)S(1)}, bf16[9,4,960]{2,1,0:T(4,128)(2,1)S(1)}, u32[]{:S(2)}, u32[]{:S(2)}) collective-permute-start(bf16[9,4,960]{2,1,0:T(4,128)(2,1)S(1)} %reshape.23), channel_id=1, source_target_pairs={{0,64},{32,96},{64,0},{96,32},{1,65},{33,97},{65,1},{97,33},{2,66}... | collective-permute-start | bytes 207368 | tf_op jit(solution)/shard_map/basis_a_x/ppermute | solution.py:142
  12.0 4.1 %collective-permute-start.2 = (bf16[9,4,960]{2,1,0:T(4,128)(2,1)S(1)}, bf16[9,4,960]{2,1,0:T(4,128)(2,1)S(1)}, u32[]{:S(2)}, u32[]{:S(2)}) collective-permute-start(bf16[9,4,960]{2,1,0:T(4,128)(2,1)S(1)} %reshape.23), channel_id=1, source_target_pairs={{0,96},{32,0},{64,32},{96,64},{1,97},{33,1},{65,33},{97,65},{2,98}... | collective-permute-start | bytes 207368 | tf_op jit(solution)/shard_map/basis_a_x/ppermute | solution.py:142
  16.4 28.4 %collective-permute-start.9 = (bf16[8,320,512]{2,1,0:T(8,128)(2,1)}, bf16[8,320,512]{2,1,0:T(8,128)(2,1)}, u32[]{:S(2)}, u32[]{:S(2)}) collective-permute-start(bf16[8,320,512]{2,1,0:T(8,128)(2,1)} %bitcast.27), channel_id=1, source_target_pairs={{0,4},{4,0},{1,5},{5,1},{2,6},{6,2},{3,7},{7,3},{8,12},{12,8},{9,1... | collective-permute-start | bytes 7864328 | tf_op jit(solution)/shard_map/basis_a_y/ppermute | solution.py:142
  18.2 47.1 %all-to-all-start.1 = ((bf16[8,320,512]{2,1,0:T(8,128)(2,1)}), bf16[8,320,512]{2,1,0:T(8,128)(2,1)}, u32[]{:S(2)}, u32[]{:S(2)}) async-start(bf16[8,320,512]{2,1,0:T(8,128)(2,1)} %bitcast.30), calls=%async_computation.1 | async-start | bytes 5242880 | tf_op jit(solution)/shard_map/exchange_grads/all_to_all | solution.py:167
  22.9 5.6 %collective-permute-start.6 = (bf16[40,1280]{1,0:T(8,128)(2,1)S(1)}, bf16[40,1280]{1,0:T(8,128)(2,1)S(1)}, u32[]{:S(2)}, u32[]{:S(2)}) collective-permute-start(bf16[40,1280]{1,0:T(8,128)(2,1)S(1)} %concatenate.13), channel_id=1, source_target_pairs={{0,32},{32,64},{64,96},{96,0},{1,33},{33,65},{65,97},{97,1},{2,34}... | collective-permute-start | bytes 307208 | tf_op jit(solution)/shard_map/basis_g_x/ppermute | solution.py:142
  23.4 14.1 %collective-permute-start.3 = (bf16[9,16,960]{2,1,0:T(8,128)(2,1)S(1)}, bf16[9,16,960]{2,1,0:T(8,128)(2,1)S(1)}, u32[]{:S(2)}, u32[]{:S(2)}) collective-permute-start(bf16[9,16,960]{2,1,0:T(8,128)(2,1)S(1)} %pad_maximum_fusion.3), channel_id=1, source_target_pairs={{0,8},{8,16},{16,24},{24,0},{1,9},{9,17},{17,25},{25,1},{2,10},{10... | collective-permute-start | bytes 829448 | tf_op jit(solution)/shard_map/basis_a_y/ppermute | solution.py:142
  24.7 15.5 %collective-permute-start.4 = (bf16[9,16,960]{2,1,0:T(8,128)(2,1)S(1)}, bf16[9,16,960]{2,1,0:T(8,128)(2,1)S(1)}, u32[]{:S(2)}, u32[]{:S(2)}) collective-permute-start(bf16[9,16,960]{2,1,0:T(8,128)(2,1)S(1)} %pad_maximum_fusion.3), channel_id=1, source_target_pairs={{0,16},{8,24},{16,0},{24,8},{1,17},{9,25},{17,1},{25,9},{2,18},{10... | collective-permute-start | bytes 829448 | tf_op jit(solution)/shard_map/basis_a_y/ppermute | solution.py:142
  27.3 12.9 %collective-permute-start.5 = (bf16[9,16,960]{2,1,0:T(8,128)(2,1)S(1)}, bf16[9,16,960]{2,1,0:T(8,128)(2,1)S(1)}, u32[]{:S(2)}, u32[]{:S(2)}) collective-permute-start(bf16[9,16,960]{2,1,0:T(8,128)(2,1)S(1)} %pad_maximum_fusion.3), channel_id=1, source_target_pairs={{0,24},{8,0},{16,8},{24,16},{1,25},{9,1},{17,9},{25,17},{2,26},{10... | collective-permute-start | bytes 829448 | tf_op jit(solution)/shard_map/basis_a_y/ppermute | solution.py:142
  28.5 5.0 %collective-permute-start.7 = (bf16[40,1280]{1,0:T(8,128)(2,1)S(1)}, bf16[40,1280]{1,0:T(8,128)(2,1)S(1)}, u32[]{:S(2)}, u32[]{:S(2)}) collective-permute-start(bf16[40,1280]{1,0:T(8,128)(2,1)S(1)} %concatenate.13), channel_id=1, source_target_pairs={{0,64},{32,96},{64,0},{96,32},{1,65},{33,97},{65,1},{97,33},{2,66}... | collective-permute-start | bytes 307208 | tf_op jit(solution)/shard_map/basis_g_x/ppermute | solution.py:142
  33.6 3.9 %collective-permute-start.8 = (bf16[40,1280]{1,0:T(8,128)(2,1)S(1)}, bf16[40,1280]{1,0:T(8,128)(2,1)S(1)}, u32[]{:S(2)}, u32[]{:S(2)}) collective-permute-start(bf16[40,1280]{1,0:T(8,128)(2,1)S(1)} %concatenate.13), channel_id=1, source_target_pairs={{0,96},{32,0},{64,32},{96,64},{1,97},{33,1},{65,33},{97,65},{2,98}... | collective-permute-start | bytes 307208 | tf_op jit(solution)/shard_map/basis_g_x/ppermute | solution.py:142
  40.2 25.0 %collective-permute-start.10 = (bf16[4,40,1280]{2,1,0:T(8,128)(2,1)S(1)}, bf16[4,40,1280]{2,1,0:T(8,128)(2,1)S(1)}, u32[]{:S(2)}, u32[]{:S(2)}) collective-permute-start(bf16[4,40,1280]{2,1,0:T(8,128)(2,1)S(1)} %pad_maximum_fusion.2.refs_7_), channel_id=1, source_target_pairs={{0,8},{8,16},{16,24},{24,0},{1,9},{9,17},{17,25},{25,1},{2,10},{10... | collective-permute-start | bytes 1228808 | tf_op jit(solution)/shard_map/basis_g_y/ppermute | solution.py:142
  41.3 23.9 %collective-permute-start.11 = (bf16[4,40,1280]{2,1,0:T(8,128)(2,1)S(1)}, bf16[4,40,1280]{2,1,0:T(8,128)(2,1)S(1)}, u32[]{:S(2)}, u32[]{:S(2)}) collective-permute-start(bf16[4,40,1280]{2,1,0:T(8,128)(2,1)S(1)} %pad_maximum_fusion.2.refs_7_), channel_id=1, source_target_pairs={{0,16},{8,24},{16,0},{24,8},{1,17},{9,25},{17,1},{25,9},{2,18},{10... | collective-permute-start | bytes 1228808 | tf_op jit(solution)/shard_map/basis_g_y/ppermute | solution.py:142
  44.3 21.0 %collective-permute-start.12 = (bf16[4,40,1280]{2,1,0:T(8,128)(2,1)S(1)}, bf16[4,40,1280]{2,1,0:T(8,128)(2,1)}, u32[]{:S(2)}, u32[]{:S(2)}) collective-permute-start(bf16[4,40,1280]{2,1,0:T(8,128)(2,1)S(1)} %pad_maximum_fusion.2.refs_7_), channel_id=1, source_target_pairs={{0,24},{8,0},{16,8},{24,16},{1,25},{9,1},{17,9},{25,17},{2,26},{10... | collective-permute-start | bytes 1228808 | tf_op jit(solution)/shard_map/basis_g_y/ppermute | solution.py:142
  52.7 12.6 %collective-permute-start.13 = (bf16[4,64,512]{2,1,0:T(8,128)(2,1)S(1)}, bf16[4,64,512]{2,1,0:T(8,128)(2,1)S(1)}, u32[]{:S(2)}, u32[]{:S(2)}) collective-permute-start(bf16[4,64,512]{2,1,0:T(8,128)(2,1)S(1)} %get-tuple-element.49), channel_id=1, source_target_pairs={{0,2},{1,3},{2,0},{3,1},{4,6},{5,7},{6,4},{7,5},{8,10},{9,11},{10,... | collective-permute-start | bytes 786440 | tf_op jit(solution)/shard_map/coeff_parts/ppermute | solution.py:142
  65.3 15.1 %copy-start.1 = (bf16[4,40,1280]{2,1,0:T(8,128)(2,1)}, bf16[4,40,1280]{2,1,0:T(8,128)(2,1)S(1)}, u32[]{:S(2)}) copy-start(bf16[4,40,1280]{2,1,0:T(8,128)(2,1)S(1)} %collective-permute-done.11.refs_9_) | copy-start | bytes 1228804
  65.3 15.0 %collective-permute-start.16 = (bf16[8,320,512]{2,1,0:T(8,128)(2,1)}, bf16[8,320,512]{2,1,0:T(8,128)(2,1)}, u32[]{:S(2)}, u32[]{:S(2)}) collective-permute-start(bf16[8,320,512]{2,1,0:T(8,128)(2,1)} %all-to-all-done.1.refs_5_), channel_id=1, source_target_pairs={{0,4},{4,0},{1,5},{5,1},{2,6},{6,2},{3,7},{7,3},{8,12},{12,8},{9,1... | collective-permute-start | bytes 7864328 | tf_op jit(solution)/shard_map/exchange_cores/ppermute | solution.py:142
  68.1 9.1 %collective-permute-start.14 = (bf16[4,64,512]{2,1,0:T(8,128)(2,1)S(1)}, bf16[4,64,512]{2,1,0:T(8,128)(2,1)S(1)}, u32[]{:S(2)}, u32[]{:S(2)}) collective-permute-start(bf16[4,64,512]{2,1,0:T(8,128)(2,1)S(1)} %get-tuple-element.64), channel_id=1, source_target_pairs={{0,1},{1,2},{2,3},{3,0},{4,5},{5,6},{6,7},{7,4},{8,9},{9,10},{10,1... | collective-permute-start | bytes 786440 | tf_op jit(solution)/shard_map/coeff_parts/ppermute | solution.py:142
  68.3 9.7 %collective-permute-start.15 = (bf16[4,64,512]{2,1,0:T(8,128)(2,1)S(1)}, bf16[4,64,512]{2,1,0:T(8,128)(2,1)S(1)}, u32[]{:S(2)}, u32[]{:S(2)}) collective-permute-start(bf16[4,64,512]{2,1,0:T(8,128)(2,1)S(1)} %get-tuple-element.65), channel_id=1, source_target_pairs={{0,3},{1,0},{2,1},{3,2},{4,7},{5,4},{6,5},{7,6},{8,11},{9,8},{10,9... | collective-permute-start | bytes 786440 | tf_op jit(solution)/shard_map/ppermute | solution.py:142
  70.7 7.3 %collective-permute-start.17 = (bf16[4,40,1280]{2,1,0:T(8,128)(2,1)S(1)}, bf16[4,40,1280]{2,1,0:T(8,128)(2,1)S(1)}, u32[]{:S(2)}, u32[]{:S(2)}) collective-permute-start(bf16[4,40,1280]{2,1,0:T(8,128)(2,1)S(1)} %pad_maximum_fusion.2.refs_7_), channel_id=1, source_target_pairs={{0,4},{4,0},{1,5},{5,1},{2,6},{6,2},{3,7},{7,3},{8,12},{12,8},{9,1... | collective-permute-start | bytes 1228808 | tf_op jit(solution)/shard_map/exchange_cores/ppermute | solution.py:142
  71.4 6.7 %collective-permute-start.18 = (bf16[4,40,1280]{2,1,0:T(8,128)(2,1)S(1)}, bf16[4,40,1280]{2,1,0:T(8,128)(2,1)}, u32[]{:S(2)}, u32[]{:S(2)}) collective-permute-start(bf16[4,40,1280]{2,1,0:T(8,128)(2,1)S(1)} %collective-permute-done.10.refs_8_), channel_id=1, source_target_pairs={{0,4},{4,0},{1,5},{5,1},{2,6},{6,2},{3,7},{7,3},{8,12},{12,8},{9,1... | collective-permute-start | bytes 1228808 | tf_op jit(solution)/shard_map/exchange_cores/ppermute | solution.py:142
  77.1 2.9 %collective-permute-start.19 = (bf16[4,40,1280]{2,1,0:T(8,128)(2,1)S(1)}, bf16[4,40,1280]{2,1,0:T(8,128)(2,1)}, u32[]{:S(2)}, u32[]{:S(2)}) collective-permute-start(bf16[4,40,1280]{2,1,0:T(8,128)(2,1)S(1)} %collective-permute-done.11.refs_9_), channel_id=1, source_target_pairs={{0,4},{4,0},{1,5},{5,1},{2,6},{6,2},{3,7},{7,3},{8,12},{12,8},{9,1... | collective-permute-start | bytes 1228808 | tf_op jit(solution)/shard_map/exchange_cores/ppermute | solution.py:142
  78.0 2.3 %collective-permute-start.20 = (bf16[4,40,1280]{2,1,0:T(8,128)(2,1)}, bf16[4,40,1280]{2,1,0:T(8,128)(2,1)}, u32[]{:S(2)}, u32[]{:S(2)}) collective-permute-start(bf16[4,40,1280]{2,1,0:T(8,128)(2,1)} %collective-permute-done.12.refs_10_), channel_id=1, source_target_pairs={{0,4},{4,0},{1,5},{5,1},{2,6},{6,2},{3,7},{7,3},{8,12},{12,8},{9,1... | collective-permute-start | bytes 1228808 | tf_op jit(solution)/shard_map/exchange_cores/ppermute | solution.py:142
  (2 other events, 3.0 us)
